TPU v7x, 32 devices: a whole 2x2x4 slice. The times are simulated.
32 devices in a mesh: dp: 4 (over y, x), expert: 4 (over z), fsdp: 2 (over core).
Axes of the slice: x: 2, y: 2, z: 4, core: 2. Of those that a mesh axis runs over, the one named last changes fastest.
Arguments:
- inputs: bfloat16 [2, 32, 1024, 512], P(None, ('dp', 'expert', 'fsdp')), may hold values from -6 to 6
- lengths: int32 [2, 32], replicated, may hold values from 256 to 1024, as said below
- routes: int32 [1, 2, 32, 1024, 8], P(None, None, ('dp', 'expert', 'fsdp')), may hold values from 0 to 23, all different within a row; in each aligned block of 1024 rows (0 to 1023, 1024 to 2047, ..., all dimensions but the last counted through in order) at most 384 rows name the same one
- ln1_gain: bfloat16 [1, 512], P(None, 'fsdp'), may hold values from 0.5 to 1.5
- ln1_bias: bfloat16 [1, 512], P(None, 'fsdp'), may hold values from -0.5 to 0.5
- kv_weight: bfloat16 [1, 512, 128], P(None, 'fsdp'), may hold values from -0.25 to 0.25
- router_weight: bfloat16 [1, 512, 24], P(None, 'fsdp'), may hold values from -0.125 to 0.125
- query_weight: bfloat16 [1, 24, 512, 64], P(None, 'expert', 'fsdp'), may hold values from -0.5 to 0.5
- out_weight: bfloat16 [1, 24, 512, 64], P(None, 'expert', 'fsdp'), may hold values from -1.5 to 1.5
- ln2_gain: bfloat16 [1, 512], P(None, 'fsdp'), may hold values from 0.5 to 1.5
- ln2_bias: bfloat16 [1, 512], P(None, 'fsdp'), may hold values from -0.5 to 0.5
- up_weight: bfloat16 [1, 512, 2048], P(None, 'fsdp'), may hold values from -0.25 to 0.25
- up_bias: bfloat16 [1, 2048], P(None, 'fsdp'), may hold values from -0.5 to 0.5
- down_weight: bfloat16 [1, 2048, 512], P(None, 'fsdp'), may hold values from -0.125 to 0.125
- down_bias: bfloat16 [1, 512], P(None, 'fsdp'), may hold values from -0.5 to 0.5
- out_cotangent: float32 [2, 32, 1024, 512], P(None, ('dp', 'expert', 'fsdp')), may hold values from -6 to 6
Outputs:
- outputs: float32 [2, 32, 1024, 512], P(None, ('dp', 'expert', 'fsdp'))
- input_grad: float32 [2, 32, 1024, 512], P(None, ('dp', 'expert', 'fsdp'))
- ln1_gain_grad: float32 [1, 512], P(None, ('dp', 'expert', 'fsdp'))
- ln1_bias_grad: float32 [1, 512], P(None, ('dp', 'expert', 'fsdp'))
- kv_weight_grad: float32 [1, 512, 128], P(None, ('dp', 'expert', 'fsdp'))
- router_weight_grad: float32 [1, 512, 24], P(None, ('dp', 'expert', 'fsdp'))
- query_weight_grad: float32 [1, 24, 512, 64], P(None, 'expert', ('dp', 'fsdp'))
- out_weight_grad: float32 [1, 24, 512, 64], P(None, 'expert', ('dp', 'fsdp'))
- ln2_gain_grad: float32 [1, 512], P(None, ('dp', 'expert', 'fsdp'))
- ln2_bias_grad: float32 [1, 512], P(None, ('dp', 'expert', 'fsdp'))
- up_weight_grad: float32 [1, 512, 2048], P(None, ('dp', 'expert', 'fsdp'))
- up_bias_grad: float32 [1, 2048], P(None, ('dp', 'expert', 'fsdp'))
- down_weight_grad: float32 [1, 2048, 512], P(None, ('dp', 'expert', 'fsdp'))
- down_bias_grad: float32 [1, 512], P(None, ('dp', 'expert', 'fsdp'))
Inputs may be any that keep to these rules, and one draw needn't show every extreme that they name: `lengths`: one value or more in every micro-batch is exactly 1024, one exactly 256. `routes`: each token names 8 different experts; among the 1024 slots of one sequence in one layer and micro-batch at most 384 name the same expert, a bound that some block reaches.
All inputs are finite; a program needn't handle non-finite values.
Results may differ from a plain program's by a relative error of at most 0.017.
Values may be sent and summed in bfloat16 or wider, within the bound.
No kernel may reach another device: no remote copies, remote signals or barrier semaphores. Data moves between devices by JAX's collectives and lax.ppermute only.
A program may use at most 448 MiB of HBM per device.

v0:
```python
import math

import jax
import jax.numpy as jnp
from jax import lax
from jax.sharding import PartitionSpec as P

CAP = 384


EPSILON = 1e-05
NEGATIVE = -1e30
GELU_SCALE = 0.7978845608028654
GELU_CUBIC = 0.044715


def gelu_slope(values):
    inner = GELU_SCALE * (values + GELU_CUBIC * values * values * values)
    bent = jnp.tanh(inner)
    return 0.5 * (1.0 + bent) + 0.5 * values * (1.0 - bent * bent) * GELU_SCALE * (
        1.0 + 3.0 * GELU_CUBIC * values * values
    )


def layer_normalize(values, gain_vec, shift_vec):
    center = values - jnp.mean(values, -1, keepdims=True)
    spread = lax.rsqrt(jnp.mean(center * center, -1, keepdims=True) + EPSILON)
    normalized_rows = center * spread
    return (normalized_rows * gain_vec + shift_vec, normalized_rows, spread)


def norm_back(grad_in, normalized_rows, spread, gain_vec):
    scaled = grad_in * gain_vec
    back_grad = spread * (
        scaled
        - jnp.mean(scaled, -1, keepdims=True)
        - normalized_rows * jnp.mean(scaled * normalized_rows, -1, keepdims=True)
    )
    return (back_grad, jnp.sum(grad_in * normalized_rows, 0), jnp.sum(grad_in, 0))


def accumulate(store, slot_key, value):
    store[slot_key] = store.get(slot_key, 0.0) + value


def slot_table(route_now, experts, capacity):
    row_total = route_now.shape[0]
    pick_count = route_now.shape[1]
    chosen = route_now[:, :, None] == lax.broadcasted_iota(jnp.int32, (1, 1, experts), 2)
    member = jnp.sum(chosen.astype(jnp.int32), 1).astype(jnp.bfloat16)
    earlier = (
        lax.broadcasted_iota(jnp.int32, (row_total, row_total), 1)
        < lax.broadcasted_iota(jnp.int32, (row_total, row_total), 0)
    ).astype(jnp.bfloat16)
    before = jnp.dot(earlier, member, preferred_element_type=jnp.float32)
    place_ids = jnp.sum(jnp.where(chosen, before[:, None, :], 0.0), 2).astype(jnp.int32)
    target = (route_now * capacity + place_ids).reshape(-1)
    source = lax.broadcasted_iota(jnp.int32, (row_total * pick_count,), 0)
    slot_rows = (
        jnp.full((experts * capacity,), row_total * pick_count, jnp.int32).at[target].set(source)
    )
    return (slot_rows, target)


def allowed_keys(positions, seq_lengths, seq_span):
    column = lax.broadcasted_iota(jnp.int32, positions.shape + (seq_span,), 3)
    return (column <= positions[..., None]) & (column < seq_lengths[:, None, None, None])


def expert_forward(rows_in, place_in, kv_all, seq_lengths, head_query, head_out):
    head_width = head_query.shape[2]
    scaling = 1.0 / math.sqrt(head_width)
    queries = jnp.einsum(
        "sicd,idh->sich", rows_in, head_query, preferred_element_type=jnp.float32
    ).astype(jnp.bfloat16)
    scores = (
        jnp.einsum(
            "sich,sjh->sicj", queries, kv_all[:, :, :head_width], preferred_element_type=jnp.float32
        )
        * scaling
    )
    scores = jnp.where(allowed_keys(place_in, seq_lengths, kv_all.shape[1]), scores, NEGATIVE)
    row_max = jnp.max(scores, -1, keepdims=True)
    weights = jnp.exp(scores - row_max)
    row_sum = jnp.sum(weights, -1, keepdims=True)
    prob_b = (weights / row_sum).astype(jnp.bfloat16)
    context = jnp.einsum(
        "sicj,sjh->sich", prob_b, kv_all[:, :, head_width:], preferred_element_type=jnp.float32
    ).astype(jnp.bfloat16)
    answer = jnp.einsum(
        "sich,idh->sicd", context, head_out, preferred_element_type=jnp.float32
    ).astype(jnp.bfloat16)
    return (answer, queries, context, row_max[..., 0] + jnp.log(row_sum[..., 0]))


def expert_backward(
    grad_answer,
    rows_in,
    place_in,
    kv_all,
    seq_lengths,
    head_query,
    head_out,
    queries,
    context,
    log_total,
):
    head_width = head_query.shape[2]
    scaling = 1.0 / math.sqrt(head_width)
    key_part = kv_all[:, :, :head_width]
    value_part = kv_all[:, :, head_width:]
    grad_context = jnp.einsum(
        "sicd,idh->sich", grad_answer, head_out, preferred_element_type=jnp.float32
    ).astype(jnp.bfloat16)
    grad_out_w = jnp.einsum(
        "sicd,sich->idh", grad_answer, context, preferred_element_type=jnp.float32
    )
    scores = (
        jnp.einsum("sich,sjh->sicj", queries, key_part, preferred_element_type=jnp.float32)
        * scaling
    )
    allowed = allowed_keys(place_in, seq_lengths, kv_all.shape[1])
    prob_rows = jnp.where(
        allowed, jnp.exp(jnp.where(allowed, scores, NEGATIVE) - log_total[..., None]), 0.0
    )
    grad_probs = jnp.einsum(
        "sich,sjh->sicj", grad_context, value_part, preferred_element_type=jnp.float32
    )
    grad_scores = (
        prob_rows * (grad_probs - jnp.sum(prob_rows * grad_probs, -1, keepdims=True))
    ).astype(jnp.bfloat16)
    grad_queries = (
        jnp.einsum("sicj,sjh->sich", grad_scores, key_part, preferred_element_type=jnp.float32)
        * scaling
    ).astype(jnp.bfloat16)
    grad_keys = (
        jnp.einsum("sicj,sich->sjh", grad_scores, queries, preferred_element_type=jnp.float32)
        * scaling
    )
    grad_values = jnp.einsum(
        "sicj,sich->sjh",
        prob_rows.astype(jnp.bfloat16),
        grad_context,
        preferred_element_type=jnp.float32,
    )
    grad_query_w = jnp.einsum(
        "sicd,sich->idh", rows_in, grad_queries, preferred_element_type=jnp.float32
    )
    grad_rows = jnp.einsum(
        "sich,idh->sicd", grad_queries, head_query, preferred_element_type=jnp.float32
    ).astype(jnp.bfloat16)
    return (grad_rows, jnp.concatenate([grad_keys, grad_values], -1), grad_query_w, grad_out_w)


def local(
    inputs,
    lengths,
    routes,
    ln1_gain,
    ln1_bias,
    kv_weight,
    router_weight,
    query_weight,
    out_weight,
    ln2_gain,
    ln2_bias,
    up_weight,
    up_bias,
    down_weight,
    down_bias,
    out_cotangent,
):
    micro_count = inputs.shape[0]
    row_count = inputs.shape[2]
    model_width = inputs.shape[3]
    layer_count = kv_weight.shape[0]
    experts = router_weight.shape[2]
    head_width = query_weight.shape[3]
    pick_count = routes.shape[4]
    group_size = lax.axis_size("expert")
    halves = lax.axis_size("fsdp")
    group_base = lax.axis_index("dp") * group_size
    group_ids = (
        group_base + lax.broadcasted_iota(jnp.int32, (group_size,), 0)
    ) * halves + lax.axis_index("fsdp")
    seq_index = (group_base + lax.axis_index("expert")) * halves + lax.axis_index("fsdp")
    positions = lax.broadcasted_iota(jnp.int32, (row_count,), 0)
    shared_local = (
        ln1_gain,
        ln1_bias,
        kv_weight,
        router_weight,
        ln2_gain,
        ln2_bias,
        up_weight,
        up_bias,
        down_weight,
        down_bias,
    )
    totals = {}
    head_totals = {}
    results = []
    input_grads = []
    for micro_at in range(micro_count):
        shared = (
            lax.all_gather(shared_local[0], "fsdp", axis=1, tiled=True),
            lax.all_gather(shared_local[1], "fsdp", axis=1, tiled=True),
            lax.all_gather(shared_local[2], "fsdp", axis=1, tiled=True),
            lax.all_gather(shared_local[3], "fsdp", axis=1, tiled=True),
            lax.all_gather(shared_local[4], "fsdp", axis=1, tiled=True),
            lax.all_gather(shared_local[5], "fsdp", axis=1, tiled=True),
            lax.all_gather(shared_local[6], "fsdp", axis=1, tiled=True),
            lax.all_gather(shared_local[7], "fsdp", axis=1, tiled=True),
            lax.all_gather(shared_local[8], "fsdp", axis=1, tiled=True),
            lax.all_gather(shared_local[9], "fsdp", axis=1, tiled=True),
        )
        head_query, head_out = (
            lax.all_gather(query_weight, "fsdp", axis=2, tiled=True),
            lax.all_gather(out_weight, "fsdp", axis=2, tiled=True),
        )
        own_length = lax.dynamic_index_in_dim(lengths[micro_at], seq_index, 0, keepdims=False)
        valid_rows = (positions < own_length).astype(jnp.float32)
        layer_state = inputs[micro_at, 0].astype(jnp.float32)
        layer_at = 0
        (
            norm_gain_vector,
            norm_shift,
            kv_proj,
            router_proj,
            ffn_gain,
            ffn_shift,
            up_proj,
            up_shift,
            down_proj,
            down_shift,
        ) = [element[layer_at] for element in shared]
        route_now = routes[layer_at, micro_at, 0]
        slot_rows, target = slot_table(route_now, experts, CAP)
        normalized_rows, centered_input, inverse_deviation_input = layer_normalize(
            layer_state, norm_gain_vector.astype(jnp.float32), norm_shift.astype(jnp.float32)
        )
        hidden = normalized_rows.astype(jnp.bfloat16)
        kv_local = jnp.dot(hidden, kv_proj, preferred_element_type=jnp.float32).astype(jnp.bfloat16)
        logits = jnp.dot(hidden, router_proj, preferred_element_type=jnp.float32)
        gate_probs = jax.nn.softmax(jnp.take_along_axis(logits, route_now, 1), -1)
        source_row = slot_rows // pick_count
        send_rows = jnp.concatenate([hidden, jnp.zeros((1, model_width), jnp.bfloat16)], 0)[
            source_row
        ]
        send_place = jnp.concatenate([positions, jnp.full((1,), row_count - 1, jnp.int32)], 0)[
            source_row
        ]
        kv_all = lax.all_gather(kv_local, "expert", axis=0, tiled=True).reshape(
            group_size, row_count, 2 * head_width
        )
        seq_lengths = lengths[micro_at][group_ids]
        rows_in = lax.all_to_all(
            send_rows.reshape(group_size, experts // group_size, CAP, model_width),
            "expert",
            split_axis=0,
            concat_axis=0,
            tiled=True,
        )
        place_in = lax.all_to_all(
            send_place.reshape(group_size, experts // group_size, CAP),
            "expert",
            split_axis=0,
            concat_axis=0,
            tiled=True,
        )
        answer, queries, context, log_total = expert_forward(
            rows_in, place_in, kv_all, seq_lengths, head_query[layer_at], head_out[layer_at]
        )
        answer = lax.all_to_all(answer, "expert", split_axis=0, concat_axis=0, tiled=True)
        per_route = (
            answer.reshape(experts * CAP, model_width)[target]
            .reshape(row_count, pick_count, model_width)
            .astype(jnp.float32)
        )
        mixed_state = layer_state + jnp.sum(gate_probs[:, :, None] * per_route, 1)
        normalized_middle, centered_middle, inverse_deviation_middle = layer_normalize(
            mixed_state, ffn_gain.astype(jnp.float32), ffn_shift.astype(jnp.float32)
        )
        hidden_mid = normalized_middle.astype(jnp.bfloat16)
        before_act = jnp.dot(
            hidden_mid, up_proj, preferred_element_type=jnp.float32
        ) + up_shift.astype(jnp.float32)
        active = jax.nn.gelu(before_act, approximate=True).astype(jnp.bfloat16)
        layer_state = (
            mixed_state
            + jnp.dot(active, down_proj, preferred_element_type=jnp.float32)
            + down_shift.astype(jnp.float32)
        )
        kept_list = [
            (
                route_now,
                slot_rows,
                target,
                centered_input,
                inverse_deviation_input,
                hidden,
                gate_probs,
                per_route,
                kv_all,
                seq_lengths,
                rows_in,
                place_in,
                queries,
                context,
                log_total,
                centered_middle,
                inverse_deviation_middle,
                hidden_mid,
                before_act,
                active,
            )
        ]
        results.append(layer_state)
        grad_state = out_cotangent[micro_at, 0] * valid_rows[:, None]
        for layer_at in reversed(range(layer_count)):
            (
                norm_gain_vector,
                norm_shift,
                kv_proj,
                router_proj,
                ffn_gain,
                ffn_shift,
                up_proj,
                up_shift,
                down_proj,
                down_shift,
            ) = [element[layer_at] for element in shared]
            (
                route_now,
                slot_rows,
                target,
                centered_input,
                inverse_deviation_input,
                hidden,
                gate_probs,
                per_route,
                kv_all,
                seq_lengths,
                rows_in,
                place_in,
                queries,
                context,
                log_total,
                centered_middle,
                inverse_deviation_middle,
                hidden_mid,
                before_act,
                active,
            ) = kept_list[layer_at]
            grad_down = grad_state.astype(jnp.bfloat16)
            accumulate(
                totals,
                (layer_at, 8),
                jnp.dot(active.T, grad_down, preferred_element_type=jnp.float32),
            )
            accumulate(totals, (layer_at, 9), jnp.sum(grad_down.astype(jnp.float32), 0))
            grad_pre = (
                jnp.dot(grad_down, down_proj.T, preferred_element_type=jnp.float32)
                * gelu_slope(before_act)
            ).astype(jnp.bfloat16)
            accumulate(
                totals,
                (layer_at, 6),
                jnp.dot(hidden_mid.T, grad_pre, preferred_element_type=jnp.float32),
            )
            accumulate(totals, (layer_at, 7), jnp.sum(grad_pre.astype(jnp.float32), 0))
            back_mid, gain_mid, shift_mid = norm_back(
                jnp.dot(grad_pre, up_proj.T, preferred_element_type=jnp.float32),
                centered_middle,
                inverse_deviation_middle,
                ffn_gain.astype(jnp.float32),
            )
            accumulate(totals, (layer_at, 4), gain_mid)
            accumulate(totals, (layer_at, 5), shift_mid)
            grad_mid = grad_state + back_mid
            grad_answer = (
                (gate_probs[:, :, None] * grad_mid[:, None, :])
                .astype(jnp.bfloat16)
                .reshape(row_count * pick_count, model_width)
            )
            grad_gate = jnp.sum(per_route * grad_mid[:, None, :], 2)
            grad_pick = gate_probs * (grad_gate - jnp.sum(gate_probs * grad_gate, 1, keepdims=True))
            chosen = (
                route_now[:, :, None] == lax.broadcasted_iota(jnp.int32, (1, 1, experts), 2)
            ).astype(jnp.float32)
            grad_logits = jnp.sum(chosen * grad_pick[:, :, None], 1)
            send_grads = jnp.concatenate(
                [grad_answer, jnp.zeros((1, model_width), jnp.bfloat16)], 0
            )[slot_rows]
            grad_in = lax.all_to_all(
                send_grads.reshape(group_size, experts // group_size, CAP, model_width),
                "expert",
                split_axis=0,
                concat_axis=0,
                tiled=True,
            )
            grad_rows, grad_kv, grad_query_w, grad_out_w = expert_backward(
                grad_in,
                rows_in,
                place_in,
                kv_all,
                seq_lengths,
                head_query[layer_at],
                head_out[layer_at],
                queries,
                context,
                log_total,
            )
            accumulate(head_totals, (layer_at, 0), grad_query_w)
            accumulate(head_totals, (layer_at, 1), grad_out_w)
            grad_rows = lax.all_to_all(grad_rows, "expert", split_axis=0, concat_axis=0, tiled=True)
            grad_kv = lax.psum_scatter(
                grad_kv.reshape(group_size * row_count, 2 * head_width).astype(jnp.bfloat16),
                "expert",
                scatter_dimension=0,
                tiled=True,
            ).astype(jnp.float32)
            grad_kv = grad_kv.astype(jnp.bfloat16)
            routed_back = jnp.sum(
                grad_rows.reshape(experts * CAP, model_width)[target]
                .reshape(row_count, pick_count, model_width)
                .astype(jnp.float32),
                1,
            )
            hidden_gradient = (
                routed_back
                + jnp.dot(grad_kv, kv_proj.T, preferred_element_type=jnp.float32)
                + jnp.dot(
                    grad_logits, router_proj.T.astype(jnp.float32), precision=lax.Precision.HIGHEST
                )
            )
            accumulate(
                totals,
                (layer_at, 2),
                jnp.dot(hidden.T, grad_kv, preferred_element_type=jnp.float32),
            )
            accumulate(
                totals,
                (layer_at, 3),
                jnp.dot(hidden.astype(jnp.float32).T, grad_logits, precision=lax.Precision.HIGHEST),
            )
            back_in, gain_in, shift_in = norm_back(
                hidden_gradient,
                centered_input,
                inverse_deviation_input,
                norm_gain_vector.astype(jnp.float32),
            )
            accumulate(totals, (layer_at, 0), gain_in)
            accumulate(totals, (layer_at, 1), shift_in)
            grad_state = grad_mid + back_in
        input_grads.append(grad_state)
    stacked = [jnp.stack([totals[0, member]]) for member in range(10)]
    summed = (
        lax.psum_scatter(stacked[0], ("dp", "expert", "fsdp"), scatter_dimension=1, tiled=True),
        lax.psum_scatter(stacked[1], ("dp", "expert", "fsdp"), scatter_dimension=1, tiled=True),
        lax.psum_scatter(stacked[2], ("dp", "expert", "fsdp"), scatter_dimension=1, tiled=True),
        lax.psum_scatter(stacked[3], ("dp", "expert", "fsdp"), scatter_dimension=1, tiled=True),
        lax.psum_scatter(stacked[4], ("dp", "expert", "fsdp"), scatter_dimension=1, tiled=True),
        lax.psum_scatter(stacked[5], ("dp", "expert", "fsdp"), scatter_dimension=1, tiled=True),
        lax.psum_scatter(stacked[6], ("dp", "expert", "fsdp"), scatter_dimension=1, tiled=True),
        lax.psum_scatter(stacked[7], ("dp", "expert", "fsdp"), scatter_dimension=1, tiled=True),
        lax.psum_scatter(stacked[8], ("dp", "expert", "fsdp"), scatter_dimension=1, tiled=True),
        lax.psum_scatter(stacked[9], ("dp", "expert", "fsdp"), scatter_dimension=1, tiled=True),
    )
    query_grad = jnp.stack([head_totals[0, 0]])
    out_grad = jnp.stack([head_totals[0, 1]])
    query_grad, out_grad = (
        lax.psum_scatter(
            query_grad.astype(jnp.bfloat16), ("dp", "fsdp"), scatter_dimension=2, tiled=True
        ).astype(jnp.float32),
        lax.psum_scatter(
            out_grad.astype(jnp.bfloat16), ("dp", "fsdp"), scatter_dimension=2, tiled=True
        ).astype(jnp.float32),
    )
    return (
        jnp.stack(results)[:, None],
        jnp.stack(input_grads)[:, None],
        summed[0],
        summed[1],
        summed[2],
        summed[3],
        query_grad,
        out_grad,
        summed[4],
        summed[5],
        summed[6],
        summed[7],
        summed[8],
        summed[9],
    )


def solution(mesh):
    return jax.shard_map(
        local,
        mesh=mesh,
        in_specs=(
            P(None, ("dp", "expert", "fsdp"), None, None),
            P(),
            P(None, None, ("dp", "expert", "fsdp"), None, None),
            P(None, "fsdp"),
            P(None, "fsdp"),
            P(None, "fsdp", None),
            P(None, "fsdp", None),
            P(None, "expert", "fsdp", None),
            P(None, "expert", "fsdp", None),
            P(None, "fsdp"),
            P(None, "fsdp"),
            P(None, "fsdp", None),
            P(None, "fsdp"),
            P(None, "fsdp", None),
            P(None, "fsdp"),
            P(None, ("dp", "expert", "fsdp"), None, None),
        ),
        out_specs=(
            P(None, ("dp", "expert", "fsdp"), None, None),
            P(None, ("dp", "expert", "fsdp"), None, None),
            P(None, ("dp", "expert", "fsdp")),
            P(None, ("dp", "expert", "fsdp")),
            P(None, ("dp", "expert", "fsdp"), None),
            P(None, ("dp", "expert", "fsdp"), None),
            P(None, "expert", ("dp", "fsdp"), None),
            P(None, "expert", ("dp", "fsdp"), None),
            P(None, ("dp", "expert", "fsdp")),
            P(None, ("dp", "expert", "fsdp")),
            P(None, ("dp", "expert", "fsdp"), None),
            P(None, ("dp", "expert", "fsdp")),
            P(None, ("dp", "expert", "fsdp"), None),
            P(None, ("dp", "expert", "fsdp")),
        ),
        check_vma=False,
    )
```

profile of v0, /device:TPU:0, one launch (start us, length us, event | category | flops | bytes accessed | tf_op | source)
XLA Modules:
  0.0 3537.8 jit_solution(11145771118091234782)
XLA Ops:
  11.5 30.5 scatter_custom_fusion.1
  42.6 51.2 %gather_fusion.4 = s32[9216]{0:T(1024)S(1)} fusion(s32[1025]{0:T(1024)S(1)} %copy-done, s32[9216]{0:T(1024)S(1)} %get-tuple-element.116), kind=kCustom, calls=%fused_computation.6 | custom fusion | bytes 110592 | tf_op jit(solution)/shard_map/gather | solution.py:250
  103.3 30.5 scatter_custom_fusion
  138.0 51.2 %gather_fusion = s32[9216]{0:T(1024)S(1)} fusion(s32[1025]{0:T(1024)S(1)} %copy-done, s32[9216]{0:T(1024)S(1)} %get-tuple-element.114), kind=kCustom, calls=%fused_computation.2 | custom fusion | bytes 110592 | tf_op jit(solution)/shard_map/gather | solution.py:250
  197.7 37.8 %gather_fusion.6 = bf16[9216,512]{1,0:T(8,128)(2,1)} fusion(bf16[1025,512]{1,0:T(8,128)(2,1)S(1)} %concatenate.23, s32[9216]{0:T(1024)S(1)} %get-tuple-element.116), kind=kCustom, calls=%fused_computation.8 | custom fusion | bytes 18911232 | tf_op jit(solution)/shard_map/gather | solution.py:247
  242.6 37.7 %gather_fusion.2 = bf16[9216,512]{1,0:T(8,128)(2,1)} fusion(bf16[1025,512]{1,0:T(8,128)(2,1)S(1)} %concatenate.22, s32[9216]{0:T(1024)S(1)} %get-tuple-element.114), kind=kCustom, calls=%fused_computation.4 | custom fusion | bytes 18911232 | tf_op jit(solution)/shard_map/gather | solution.py:247
  280.4 166.9 %all-to-all-done.4 = bf16[4,6,384,512]{3,2,1,0:T(8,128)(2,1)} async-done(((bf16[4,6,384,512]{3,2,1,0:T(8,128)(2,1)}), bf16[4,6,384,512]{3,2,1,0:T(8,128)(2,1)}, u32[]{:S(2)}, u32[]{:S(2)}) %all-to-all-start.4) | async-done | bytes 9437216 | tf_op jit(solution)/shard_map/all_to_all | solution.py:257
  471.6 61.6 %all-gather.11.cloned.1.call-done = bf16[4096,128]{1,0:T(8,128)(2,1)} async-done(((bf16[1024,128]{1,0:T(8,128)(2,1)}), bf16[4096,128]{1,0:T(8,128)(2,1)}) %all-gather.11.cloned.1.call-update) | async-done | bytes 1048592 | tf_op jit(solution)/shard_map/all_gather | solution.py:253
  533.2 16.9 fusion.279
  550.1 16.0 fusion.3
  566.2 14.4 fusion.136
  586.6 8.2 copy.163
  594.7 80.3 %all-to-all-done.1 = bf16[4,6,384,512]{3,2,1,0:T(8,128)(2,1)} async-done(((bf16[4,6,384,512]{3,2,1,0:T(8,128)(2,1)}), bf16[4,6,384,512]{3,2,1,0:T(8,128)(2,1)}, u32[]{:S(2)}, u32[]{:S(2)}) %all-to-all-start.1) | async-done | bytes 9437216 | tf_op jit(solution)/shard_map/all_to_all | solution.py:257
  689.5 71.3 %all-gather.5.cloned.1.call-done = bf16[4096,128]{1,0:T(8,128)(2,1)} async-done(((bf16[1024,128]{1,0:T(8,128)(2,1)}), bf16[4096,128]{1,0:T(8,128)(2,1)}) %all-gather.5.cloned.1.call-update) | async-done | bytes 1048592 | tf_op jit(solution)/shard_map/all_gather | solution.py:253
  760.9 16.9 fusion.278
  777.7 16.0 fusion.2
  793.8 14.3 fusion.137
  814.2 8.2 copy.154
  822.5 80.3 %all-to-all-done.5 = bf16[4,6,384,512]{3,2,1,0:T(8,128)(2,1)} async-done(((bf16[4,6,384,512]{3,2,1,0:T(8,128)(2,1)}), bf16[4,6,384,512]{3,2,1,0:T(8,128)(2,1)}, u32[]{:S(2)}, u32[]{:S(2)}) %all-to-all-start.5) | async-done | bytes 9437216 | tf_op jit(solution)/shard_map/all_to_all | solution.py:274
  921.5 65.6 %gather_fusion.13 = f32[8192]{0:T(1024)S(1)} fusion(f32[1024,24]{0,1:T(8,128)S(1)} %fusion.253, s32[8192]{0:T(1024)S(1)} %reshape.773), kind=kCustom, calls=%fused_computation.1.clone | custom fusion | bytes 131072 | tf_op jit(solution)/shard_map/jit(take_along_axis)/gather | solution.py:245
  989.7 65.5 %gather_fusion.12 = f32[8192]{0:T(1024)S(1)} fusion(f32[1024,24]{0,1:T(8,128)S(1)} %fusion.255, s32[8192]{0:T(1024)S(1)} %copy-done.1), kind=kCustom, calls=%fused_computation.clone | custom fusion | bytes 131072 | tf_op jit(solution)/shard_map/jit(take_along_axis)/gather | solution.py:245
  1058.6 39.0 %gather_fusion.7 = bf16[8192,512]{1,0:T(8,128)(2,1)} fusion(bf16[9216,512]{1,0:T(8,128)(2,1)} %bitcast.52, s32[8192]{0:T(1024)S(1)} %broadcast_clamp_fusion), kind=kCustom, calls=%fused_computation.9 | custom fusion | bytes 16809984 | tf_op jit(solution)/shard_map/gather | solution.py:276
  1097.6 9.3 fusion.12
  1113.8 38.8 %gather_fusion.3 = bf16[8192,512]{1,0:T(8,128)(2,1)} fusion(bf16[9216,512]{1,0:T(8,128)(2,1)} %bitcast.25, s32[8192]{0:T(1024)S(1)} %broadcast_clamp_fusion.1), kind=kCustom, calls=%fused_computation.5 | custom fusion | bytes 16809984 | tf_op jit(solution)/shard_map/gather | solution.py:276
  1152.6 8.5 fusion.10
  1164.6 8.1 fusion.120
  1178.6 10.7 convert_reduce_fusion.2
  1196.6 8.2 convert_reduce_fusion.3
  1217.1 42.5 %gather_fusion.10 = bf16[9216,512]{1,0:T(8,128)(2,1)} fusion(bf16[8193,512]{1,0:T(8,128)(2,1)} %concatenate.26, s32[9216]{0:T(1024)S(1)} %copy-done.91), kind=kCustom, calls=%fused_computation.12 | custom fusion | bytes 18911232 | tf_op jit(solution)/shard_map/gather | solution.py:392
  1270.9 42.4 %gather_fusion.8 = bf16[9216,512]{1,0:T(8,128)(2,1)} fusion(bf16[8193,512]{1,0:T(8,128)(2,1)} %concatenate.24, s32[9216]{0:T(1024)S(1)} %copy-done.92), kind=kCustom, calls=%fused_computation.10 | custom fusion | bytes 18911232 | tf_op jit(solution)/shard_map/gather | solution.py:392
  1313.4 157.1 %all-to-all-done.8 = bf16[4,6,384,512]{3,2,1,0:T(8,128)(2,1)} async-done(((bf16[4,6,384,512]{3,2,1,0:T(8,128)(2,1)}), bf16[4,6,384,512]{3,2,1,0:T(8,128)(2,1)}, u32[]{:S(2)}, u32[]{:S(2)}) %all-to-all-start.8) | async-done | bytes 9437216 | tf_op jit(solution)/shard_map/all_to_all | solution.py:395
  1483.5 30.6 multiply_reduce_fusion
  1514.1 31.5 multiply_convert_fusion
  1545.6 9.8 multiply_convert_fusion.2
  1561.4 8.2 copy.175
  1569.7 112.0 %all-to-all-done.6 = bf16[4,6,384,512]{3,2,1,0:T(8,128)(2,1)} async-done(((bf16[4,6,384,512]{3,2,1,0:T(8,128)(2,1)}), bf16[4,6,384,512]{3,2,1,0:T(8,128)(2,1)}, u32[]{:S(2)}, u32[]{:S(2)}) %all-to-all-start.6) | async-done | bytes 9437216 | tf_op jit(solution)/shard_map/all_to_all | solution.py:395
  1694.7 30.6 multiply_reduce_fusion.1
  1725.3 31.6 multiply_convert_fusion.1
  1756.9 9.8 multiply_convert_fusion.3
  1772.8 8.4 copy.167
  1781.2 14.9 fusion.162
  1796.2 96.8 %all-to-all-done.9 = bf16[4,6,384,512]{3,2,1,0:T(8,128)(2,1)} async-done(((bf16[4,6,384,512]{3,2,1,0:T(8,128)(2,1)}), bf16[4,6,384,512]{3,2,1,0:T(8,128)(2,1)}, u32[]{:S(2)}, u32[]{:S(2)}) %all-to-all-start.9) | async-done | bytes 9437216 | tf_op jit(solution)/shard_map/all_to_all | solution.py:416
  1898.8 8.4 fusion.171
  1908.8 8.3 fusion.170
  1917.1 15.0 fusion.165
  1950.7 10.3 fusion.265
  1990.6 118.2 %reduce-scatter.31.cloned.1.call-done = bf16[1024,128]{1,0:T(8,128)(2,1)} async-done(((bf16[4096,128]{1,0:T(8,128)(2,1)}), bf16[1024,128]{1,0:T(8,128)(2,1)}) %reduce-scatter.31.cloned.1.call-update) | async-done | bytes 262160 | tf_op jit(solution)/shard_map/reduce_scatter | solution.py:417
  2111.5 38.8 %gather_fusion.11 = bf16[8192,512]{1,0:T(8,128)(2,1)} fusion(bf16[9216,512]{1,0:T(8,128)(2,1)} %bitcast.86, s32[8192]{0:T(1024)S(1)} %copy-done.74), kind=kCustom, calls=%fused_computation.13 | custom fusion | bytes 16809984 | tf_op jit(solution)/shard_map/gather | solution.py:425
  2150.3 10.3 convert_reduce_fusion
  2160.6 39.0 %gather_fusion.9 = bf16[8192,512]{1,0:T(8,128)(2,1)} fusion(bf16[9216,512]{1,0:T(8,128)(2,1)} %bitcast.68, s32[8192]{0:T(1024)S(1)} %copy-done.72), kind=kCustom, calls=%fused_computation.11 | custom fusion | bytes 16809984 | tf_op jit(solution)/shard_map/gather | solution.py:425
  2199.6 10.2 convert_reduce_fusion.1
  2224.4 11.5 add_bitcast_fusion
  2249.6 7.9 add_bitcast_fusion.3
  2266.8 109.4 %reduce-scatter.53.cloned.1.call-done = f32[16,1]{1,0:T(8,128)} async-done(((f32[512,1]{1,0:T(8,128)}), f32[16,1]{1,0:T(8,128)}) %reduce-scatter.53.cloned.1.call-update) | async-done | bytes 80
  2377.5 131.1 %reduce-scatter.51.cloned.1.call-done = f32[16,1]{1,0:T(8,128)} async-done(((f32[512,1]{1,0:T(8,128)}), f32[16,1]{1,0:T(8,128)}) %reduce-scatter.51.cloned.1.call-update) | async-done | bytes 80
  2509.9 132.2 %reduce-scatter.55.cloned.1.call-done = f32[64,1]{1,0:T(8,128)} async-done(((f32[2048,1]{1,0:T(8,128)}), f32[64,1]{1,0:T(8,128)}) %reduce-scatter.55.cloned.1.call-update) | async-done | bytes 272
  2643.4 32.0 reduce-scatter.49.cloned.1.call-done
  2678.8 33.4 reduce-scatter.47.cloned.1.call-done
  2728.3 119.9 %reduce-scatter.45.cloned.1.call-done = f32[16,1]{1,0:T(8,128)} async-done(((f32[512,1]{1,0:T(8,128)}), f32[16,1]{1,0:T(8,128)}) %reduce-scatter.45.cloned.1.call-update) | async-done | bytes 80
  2849.5 130.7 %reduce-scatter.43.cloned.1.call-done = f32[16,1]{1,0:T(8,128)} async-done(((f32[512,1]{1,0:T(8,128)}), f32[16,1]{1,0:T(8,128)}) %reduce-scatter.43.cloned.1.call-update) | async-done | bytes 80
  2981.5 131.6 %reduce-scatter.37.cloned.1.call-done = f32[1,16,24]{2,0,1:T(1,128)} async-done(((f32[1,512,24]{2,0,1:T(1,128)}), f32[1,16,24]{2,0,1:T(1,128)}) %reduce-scatter.37.cloned.1.call-update) | async-done | bytes 1552 | tf_op jit(solution)/shard_map/reduce_scatter | solution.py:462
  3113.1 141.8 %reduce-scatter.41.cloned.1.call-done = f32[1,64,512]{2,1,0:T(8,128)} async-done(((f32[1,2048,512]{2,1,0:T(8,128)}), f32[1,64,512]{2,1,0:T(8,128)}) %reduce-scatter.41.cloned.1.call-update) | async-done | bytes 131088 | tf_op jit(solution)/shard_map/reduce_scatter | solution.py:467
  3255.0 142.2 %reduce-scatter.39.cloned.1.call-done = f32[1,16,2048]{2,1,0:T(8,128)} async-done(((f32[1,512,2048]{2,1,0:T(8,128)}), f32[1,16,2048]{2,1,0:T(8,128)}) %reduce-scatter.39.cloned.1.call-update) | async-done | bytes 131088 | tf_op jit(solution)/shard_map/reduce_scatter | solution.py:465
  3397.2 133.0 %reduce-scatter.35.cloned.1.call-done = f32[1,16,128]{2,1,0:T(8,128)} async-done(((f32[1,512,128]{2,1,0:T(8,128)}), f32[1,16,128]{2,1,0:T(8,128)}) %reduce-scatter.35.cloned.1.call-update) | async-done | bytes 8208 | tf_op jit(solution)/shard_map/reduce_scatter | solution.py:461
  (535 shorter events, 313.9 us)
Async XLA Ops:
  11.0 82.7 %copy-start.14 = (s32[1,1,1,1024,8]{4,3,2,1,0:T(8,128)}, s32[1,1,1,1024,8]{4,3,2,1,0:T(8,128)S(1)}, u32[]{:S(2)}) copy-start(s32[1,1,1,1024,8]{4,3,2,1,0:T(8,128)S(1)} %copy.215) | copy-start | bytes 98308
  11.4 82.3 %copy-start.100 = (s32[8192,1]{0,1:T(1,128)}, s32[8192,1]{0,1:T(1,128)S(1)}, u32[]{:S(2)}) copy-start(s32[8192,1]{0,1:T(1,128)S(1)} %compare_select_fusion.2) | copy-start | bytes 98308
  94.4 95.4 %all-to-all-start.3 = ((s32[4,6,384]{2,1,0:T(8,128)}), s32[4,6,384]{2,1,0:T(8,128)S(1)}, u32[]{:S(2)}, u32[]{:S(2)}) async-start(s32[4,6,384]{2,1,0:T(8,128)} %reshape.608), calls=%async_computation.3 | async-start | bytes 98304 | tf_op jit(solution)/shard_map/all_to_all | solution.py:264
  101.1 354.0 %copy-start.104 = (f32[1024]{0:T(1024)}, f32[1024]{0:T(1024)S(1)}, u32[]{:S(2)}) copy-start(f32[1024]{0:T(1024)S(1)} %get-tuple-element.139) | copy-start | bytes 12292
  101.1 354.0 %copy-start.106 = (f32[1024]{0:T(1024)}, f32[1024]{0:T(1024)S(1)}, u32[]{:S(2)}) copy-start(f32[1024]{0:T(1024)S(1)} %get-tuple-element.140) | copy-start | bytes 12292
  102.1 353.0 %copy-start.111 = (f32[1024]{0:T(1024)}, f32[1024]{0:T(1024)S(1)}, u32[]{:S(2)}) copy-start(f32[1024]{0:T(1024)S(1)} %add_rsqrt_fusion.3) | copy-start | bytes 12292
  102.4 86.8 %copy-start.17 = (s32[1,1,1,1024,8]{4,3,2,1,0:T(8,128)}, s32[1,1,1,1024,8]{4,3,2,1,0:T(8,128)S(1)}, u32[]{:S(2)}) copy-start(s32[1,1,1,1024,8]{4,3,2,1,0:T(8,128)S(1)} %copy.212) | copy-start | bytes 98308
  103.3 85.9 %copy-start.102 = (s32[8192,1]{0,1:T(1,128)}, s32[8192,1]{0,1:T(1,128)S(1)}, u32[]{:S(2)}) copy-start(s32[8192,1]{0,1:T(1,128)S(1)} %compare_select_fusion.3) | copy-start | bytes 98308
  134.4 320.7 %copy-start.113 = (f32[1024]{0:T(1024)}, f32[1024]{0:T(1024)S(1)}, u32[]{:S(2)}) copy-start(f32[1024]{0:T(1024)S(1)} %add_rsqrt_fusion.1) | copy-start | bytes 12292
  136.2 318.9 %copy-start.115 = (f32[1,512]{1,0:T(1,128)}, f32[1,512]{1,0:T(1,128)S(1)}, u32[]{:S(2)}) copy-start(f32[1,512]{1,0:T(1,128)S(1)} %mul.671) | copy-start | bytes 6148
  189.8 343.4 %copy-start.79 = (s32[4,6,384]{2,1,0:T(8,128)}, s32[4,6,384]{2,1,0:T(8,128)S(1)}, u32[]{:S(2)}) copy-start(s32[4,6,384]{2,1,0:T(8,128)S(1)} %all-to-all-done.3) | copy-start | bytes 110596
  189.8 45.7 %all-to-all-start = ((s32[4,6,384]{2,1,0:T(8,128)}), s32[4,6,384]{2,1,0:T(8,128)S(1)}, u32[]{:S(2)}, u32[]{:S(2)}) async-start(s32[4,6,384]{2,1,0:T(8,128)} %reshape.604), calls=%async_computation | async-start | bytes 98304 | tf_op jit(solution)/shard_map/all_to_all | solution.py:264
  235.5 525.3 %copy-start.81 = (s32[4,6,384]{2,1,0:T(8,128)}, s32[4,6,384]{2,1,0:T(8,128)S(1)}, u32[]{:S(2)}) copy-start(s32[4,6,384]{2,1,0:T(8,128)S(1)} %all-to-all-done) | copy-start | bytes 110596
  235.5 211.7 %all-to-all-start.4 = ((bf16[4,6,384,512]{3,2,1,0:T(8,128)(2,1)}), bf16[4,6,384,512]{3,2,1,0:T(8,128)(2,1)}, u32[]{:S(2)}, u32[]{:S(2)}) async-start(bf16[4,6,384,512]{3,2,1,0:T(8,128)(2,1)} %bitcast.473), calls=%async_computation.4 | async-start | bytes 18874368 | tf_op jit(solution)/shard_map/all_to_all | solution.py:257
  447.3 227.8 %all-to-all-start.1 = ((bf16[4,6,384,512]{3,2,1,0:T(8,128)(2,1)}), bf16[4,6,384,512]{3,2,1,0:T(8,128)(2,1)}, u32[]{:S(2)}, u32[]{:S(2)}) async-start(bf16[4,6,384,512]{3,2,1,0:T(8,128)(2,1)} %bitcast.471), calls=%async_computation.1 | async-start | bytes 18874368 | tf_op jit(solution)/shard_map/all_to_all | solution.py:257
  453.2 80.0 %all-gather.11.cloned.1.call-start = ((), (), s32[]{:S(2)}) async-start(), calls=%async_computation.27 | async-start | bytes 1310720 | tf_op jit(solution)/shard_map/all_gather | solution.py:253
  455.2 225.9 %copy-start.51 = (bf16[1,512,128]{2,1,0:T(8,128)(2,1)}, bf16[1,512,128]{2,1,0:T(8,128)(2,1)S(1)}, u32[]{:S(2)}) copy-start(bf16[1,512,128]{2,1,0:T(8,128)(2,1)S(1)} %all_gather.58) | copy-start | bytes 393220
  456.2 224.9 %copy-start.32 = (bf16[1024,512]{1,0:T(8,128)(2,1)}, bf16[1024,512]{1,0:T(8,128)(2,1)S(1)}, u32[]{:S(2)}) copy-start(bf16[1024,512]{1,0:T(8,128)(2,1)S(1)} %get-tuple-element.101) | copy-start | bytes 3145732
  459.5 73.7 %copy-start.135 = (s32[4]{0:T(128)}, s32[4]{0:T(128)S(1)}, u32[]{:S(2)}) copy-start(s32[4]{0:T(128)S(1)} %gather_fusion.5) | copy-start | bytes 52
  461.8 221.1 %copy-start.47 = (bf16[1,6,512,64]{2,3,1,0:T(8,128)(2,1)}, bf16[1,6,512,64]{2,3,1,0:T(8,128)(2,1)S(1)}, u32[]{:S(2)}) copy-start(bf16[1,6,512,64]{2,3,1,0:T(8,128)(2,1)S(1)} %all_gather.57) | copy-start | bytes 1179652
  464.6 343.6 %copy-start.49 = (bf16[1,6,512,64]{2,3,1,0:T(8,128)(2,1)}, bf16[1,6,512,64]{2,3,1,0:T(8,128)(2,1)S(1)}, u32[]{:S(2)}) copy-start(bf16[1,6,512,64]{2,3,1,0:T(8,128)(2,1)S(1)} %all_gather.60) | copy-start | bytes 1179652
  471.6 78.5 %copy-start.55 = (bf16[4,6,384,64]{2,3,0,1:T(8,128)(2,1)}, bf16[4,6,384,64]{2,3,0,1:T(8,128)(2,1)S(1)}, u32[]{:S(2)}) copy-start(bf16[4,6,384,64]{2,3,0,1:T(8,128)(2,1)S(1)} %fusion.148) | copy-start | bytes 3538948
  675.1 227.7 %all-to-all-start.5 = ((bf16[4,6,384,512]{3,2,1,0:T(8,128)(2,1)}), bf16[4,6,384,512]{3,2,1,0:T(8,128)(2,1)}, u32[]{:S(2)}, u32[]{:S(2)}) async-start(bf16[4,6,384,512]{3,2,1,0:T(8,128)(2,1)} %copy.163), calls=%async_computation.5 | async-start | bytes 18874368 | tf_op jit(solution)/shard_map/all_to_all | solution.py:274
  680.8 80.0 %all-gather.5.cloned.1.call-start = ((), (), s32[]{:S(2)}) async-start(), calls=%async_computation.24 | async-start | bytes 1310720 | tf_op jit(solution)/shard_map/all_gather | solution.py:253
  682.9 78.0 %copy-start.137 = (s32[4]{0:T(128)}, s32[4]{0:T(128)S(1)}, u32[]{:S(2)}) copy-start(s32[4]{0:T(128)S(1)} %gather_fusion.1) | copy-start | bytes 52
  689.5 88.2 %copy-start.57 = (bf16[4,6,384,64]{2,3,0,1:T(8,128)(2,1)}, bf16[4,6,384,64]{2,3,0,1:T(8,128)(2,1)S(1)}, u32[]{:S(2)}) copy-start(bf16[4,6,384,64]{2,3,0,1:T(8,128)(2,1)S(1)} %fusion.151) | copy-start | bytes 3538948
  822.5 87.5 %copy-start.142 = (bf16[1,256]{1,0:T(2,128)(2,1)S(1)}, bf16[1,256]{1,0:T(2,128)(2,1)}, u32[]{:S(2)}) copy-start(bf16[1,256]{1,0:T(2,128)(2,1)} %param.27) | copy-start | bytes 1540
  822.5 89.8 %copy-start.143 = (bf16[1,256]{1,0:T(2,128)(2,1)S(1)}, bf16[1,256]{1,0:T(2,128)(2,1)}, u32[]{:S(2)}) copy-start(bf16[1,256]{1,0:T(2,128)(2,1)} %param.28) | copy-start | bytes 1540
  822.5 92.2 %copy-start.128 = (bf16[1,1024]{1,0:T(2,128)(2,1)S(1)}, bf16[1,1024]{1,0:T(2,128)(2,1)}, u32[]{:S(2)}) copy-start(bf16[1,1024]{1,0:T(2,128)(2,1)} %param.30) | copy-start | bytes 6148
  822.5 94.6 %copy-start.15 = (s32[1,1,1,1024,8]{4,3,2,1,0:T(8,128)S(1)}, s32[1,1,1,1024,8]{4,3,2,1,0:T(8,128)}, u32[]{:S(2)}) copy-start(s32[1,1,1,1024,8]{4,3,2,1,0:T(8,128)} %copy-done.14) | copy-start | bytes 98308
  822.5 95.0 %copy-start.18 = (s32[1,1,1,1024,8]{4,3,2,1,0:T(8,128)S(1)}, s32[1,1,1,1024,8]{4,3,2,1,0:T(8,128)}, u32[]{:S(2)}) copy-start(s32[1,1,1,1024,8]{4,3,2,1,0:T(8,128)} %copy-done.17) | copy-start | bytes 98308
  902.7 211.0 %all-to-all-start.2 = ((bf16[4,6,384,512]{3,2,1,0:T(8,128)(2,1)}), bf16[4,6,384,512]{3,2,1,0:T(8,128)(2,1)}, u32[]{:S(2)}, u32[]{:S(2)}) async-start(bf16[4,6,384,512]{3,2,1,0:T(8,128)(2,1)} %copy.154), calls=%async_computation.2 | async-start | bytes 18874368 | tf_op jit(solution)/shard_map/all_to_all | solution.py:274
  908.7 255.8 %all-gather.7.cloned.1.call-start = ((), (), s32[]{:S(2)}) async-start(), calls=%async_computation.25 | async-start | bytes 3145728 | tf_op jit(solution)/shard_map/all_gather | solution.py:212
  909.3 269.3 %all-gather.9.cloned.1.call-start = ((), (), s32[]{:S(2)}) async-start(), calls=%async_computation.26 | async-start | bytes 3145728 | tf_op jit(solution)/shard_map/all_gather | solution.py:214
  988.4 66.9 %copy-start.24 = (f32[1024,8]{1,0:T(8,128)}, f32[1024,8]{1,0:T(8,128)S(1)}, u32[]{:S(2)}) copy-start(f32[1024,8]{1,0:T(8,128)S(1)} %fusion.223) | copy-start | bytes 98308
  989.7 67.8 %copy-start.19 = (s32[1,1,1,1024,8]{4,3,2,1,0:T(8,128)S(1)}, s32[1,1,1,1024,8]{4,3,2,1,0:T(8,128)}, u32[]{:S(2)}) copy-start(s32[1,1,1,1024,8]{4,3,2,1,0:T(8,128)} %copy-done.17) | copy-start | bytes 98308
  989.7 68.4 %copy-start.101 = (s32[8192,1]{0,1:T(1,128)S(1)}, s32[8192,1]{0,1:T(1,128)}, u32[]{:S(2)}) copy-start(s32[8192,1]{0,1:T(1,128)} %copy-done.100) | copy-start | bytes 98308
  989.7 68.5 %copy-start.103 = (s32[8192,1]{0,1:T(1,128)S(1)}, s32[8192,1]{0,1:T(1,128)}, u32[]{:S(2)}) copy-start(s32[8192,1]{0,1:T(1,128)} %copy-done.102) | copy-start | bytes 98308
  1056.8 152.2 %copy-start.117 = (f32[1024]{0:T(1024)}, f32[1024]{0:T(1024)S(1)}, u32[]{:S(2)}) copy-start(f32[1024]{0:T(1024)S(1)} %fusion.262) | copy-start | bytes 12292
  1057.5 151.5 %copy-start.119 = (f32[1024]{0:T(1024)}, f32[1024]{0:T(1024)S(1)}, u32[]{:S(2)}) copy-start(f32[1024]{0:T(1024)S(1)} %fusion.261) | copy-start | bytes 12292
  1058.5 206.9 %copy-start.27 = (f32[1024,8]{1,0:T(8,128)}, f32[1024,8]{1,0:T(8,128)S(1)}, u32[]{:S(2)}) copy-start(f32[1024,8]{1,0:T(8,128)S(1)} %fusion.221) | copy-start | bytes 98308
  1259.6 210.9 %all-to-all-start.8 = ((bf16[4,6,384,512]{3,2,1,0:T(8,128)(2,1)}), bf16[4,6,384,512]{3,2,1,0:T(8,128)(2,1)}, u32[]{:S(2)}, u32[]{:S(2)}) async-start(bf16[4,6,384,512]{3,2,1,0:T(8,128)(2,1)} %bitcast.474), calls=%async_computation.9 | async-start | bytes 18874368 | tf_op jit(solution)/shard_map/all_to_all | solution.py:395
  1470.5 211.2 %all-to-all-start.6 = ((bf16[4,6,384,512]{3,2,1,0:T(8,128)(2,1)}), bf16[4,6,384,512]{3,2,1,0:T(8,128)(2,1)}, u32[]{:S(2)}, u32[]{:S(2)}) async-start(bf16[4,6,384,512]{3,2,1,0:T(8,128)(2,1)} %bitcast.472), calls=%async_computation.6 | async-start | bytes 18874368 | tf_op jit(solution)/shard_map/all_to_all | solution.py:395
  1569.7 118.3 %copy-start.88 = (f32[4,6,384]{2,1,0:T(8,128)S(1)}, f32[4,6,384]{2,1,0:T(8,128)}, u32[]{:S(2)}) copy-start(f32[4,6,384]{2,1,0:T(8,128)} %copy-done.87) | copy-start | bytes 110596
  1569.7 118.3 %copy-start.90 = (f32[4,6,384]{2,1,0:T(8,128)S(1)}, f32[4,6,384]{2,1,0:T(8,128)}, u32[]{:S(2)}) copy-start(f32[4,6,384]{2,1,0:T(8,128)} %copy-done.89) | copy-start | bytes 110596
  1681.7 211.3 %all-to-all-start.9 = ((bf16[4,6,384,512]{3,2,1,0:T(8,128)(2,1)}), bf16[4,6,384,512]{3,2,1,0:T(8,128)(2,1)}, u32[]{:S(2)}, u32[]{:S(2)}) async-start(bf16[4,6,384,512]{3,2,1,0:T(8,128)(2,1)} %copy.175), calls=%async_computation.10 | async-start | bytes 18874368 | tf_op jit(solution)/shard_map/all_to_all | solution.py:416
  1796.2 102.7 %copy-start.56 = (bf16[4,6,384,64]{2,3,0,1:T(8,128)(2,1)S(1)}, bf16[4,6,384,64]{2,3,0,1:T(8,128)(2,1)}, u32[]{:S(2)}) copy-start(bf16[4,6,384,64]{2,3,0,1:T(8,128)(2,1)} %copy-done.55) | copy-start | bytes 3538948
  1893.0 267.6 %all-to-all-start.7 = ((bf16[4,6,384,512]{3,2,1,0:T(8,128)(2,1)}), bf16[4,6,384,512]{3,2,1,0:T(8,128)(2,1)}, u32[]{:S(2)}, u32[]{:S(2)}) async-start(bf16[4,6,384,512]{3,2,1,0:T(8,128)(2,1)} %copy.167), calls=%async_computation.7 | async-start | bytes 18874368 | tf_op jit(solution)/shard_map/all_to_all | solution.py:416
  1898.8 89.0 %reduce-scatter.33.cloned.1.call-start = ((), (), s32[]{:S(2)}) async-start(), calls=%async_computation.29 | async-start | bytes 1310720 | tf_op jit(solution)/shard_map/reduce_scatter | solution.py:417
  1908.7 200.1 %reduce-scatter.31.cloned.1.call-start = ((), (), s32[]{:S(2)}) async-start(), calls=%async_computation.28 | async-start | bytes 1310720 | tf_op jit(solution)/shard_map/reduce_scatter | solution.py:417
  1933.6 332.0 %reduce-scatter.57.cloned.1.call-start = ((), (), s32[]{:S(2)}) async-start(), calls=%async_computation.41 | async-start | bytes 270336
  1934.5 441.7 %reduce-scatter.53.cloned.1.call-start = ((), (), s32[]{:S(2)}) async-start(), calls=%async_computation.39 | async-start | bytes 270336
  1935.5 573.1 %reduce-scatter.51.cloned.1.call-start = ((), (), s32[]{:S(2)}) async-start(), calls=%async_computation.38 | async-start | bytes 270336
  1936.5 705.6 %reduce-scatter.55.cloned.1.call-start = ((), (), s32[]{:S(2)}) async-start(), calls=%async_computation.40 | async-start | bytes 1081344
  1950.2 725.2 %reduce-scatter.49.cloned.1.call-start = ((), (), s32[]{:S(2)}) async-start(), calls=%async_computation.37 | async-start | bytes 442368
  1974.1 738.0 %reduce-scatter.47.cloned.1.call-start = ((), (), s32[]{:S(2)}) async-start(), calls=%async_computation.36 | async-start | bytes 442368
  1985.1 126.3 %copy-start.74 = (s32[8192]{0:T(1024)S(1)}, s32[8192]{0:T(1024)}, u32[]{:S(2)}) copy-start(s32[8192]{0:T(1024)} %copy-done.73) | copy-start | bytes 98308
  1987.3 860.9 %reduce-scatter.45.cloned.1.call-start = ((), (), s32[]{:S(2)}) async-start(), calls=%async_computation.35 | async-start | bytes 270336
  2220.0 760.3 %reduce-scatter.43.cloned.1.call-start = ((), (), s32[]{:S(2)}) async-start(), calls=%async_computation.34 | async-start | bytes 270336
  2222.7 890.5 %reduce-scatter.37.cloned.1.call-start = ((), (), s32[]{:S(2)}) async-start(), calls=%async_computation.31 | async-start | bytes 270336 | tf_op jit(solution)/shard_map/reduce_scatter | solution.py:462
  2224.2 1030.8 %reduce-scatter.41.cloned.1.call-start = ((), (), s32[]{:S(2)}) async-start(), calls=%async_computation.33 | async-start | bytes 4325376 | tf_op jit(solution)/shard_map/reduce_scatter | solution.py:467
  2236.0 1161.2 %reduce-scatter.39.cloned.1.call-start = ((), (), s32[]{:S(2)}) async-start(), calls=%async_computation.32 | async-start | bytes 4325376 | tf_op jit(solution)/shard_map/reduce_scatter | solution.py:465
  2246.9 1283.4 %reduce-scatter.35.cloned.1.call-start = ((), (), s32[]{:S(2)}) async-start(), calls=%async_computation.30 | async-start | bytes 270336 | tf_op jit(solution)/shard_map/reduce_scatter | solution.py:461
  2263.1 454.2 %copy-start.63 = (bf16[1024,128]{1,0:T(8,128)(2,1)S(1)}, bf16[1024,128]{1,0:T(8,128)(2,1)}, u32[]{:S(2)}) copy-start(bf16[1024,128]{1,0:T(8,128)(2,1)} %reduce-scatter.33.cloned.1.call-done) | copy-start | bytes 786436
  (118 other events, 1335.6 us)
Sparse Core Ops, SparseCore 0:
  458.4 74.7 all-gather.10
  683.3 77.5 all-gather.4
  1908.8 70.4 reduce-scatter.32
  1981.6 127.1 reduce-scatter.30
  2110.9 132.9 reduce-scatter.56
  2246.0 130.1 reduce-scatter.52
  2378.5 130.1 reduce-scatter.50
  2511.0 131.0 reduce-scatter.54
  2645.1 30.2 reduce-scatter.48
  2678.3 33.7 reduce-scatter.46
  2714.4 133.8 reduce-scatter.44
  2850.4 129.7 reduce-scatter.42
  2983.1 130.0 reduce-scatter.36
  3115.9 138.9 reduce-scatter.40
  3257.8 139.3 reduce-scatter.38
  3400.0 130.2 reduce-scatter.34
Sparse Core Ops, SparseCore 1:
  910.8 11.8 all-gather.6
  924.0 11.6 all-gather.8
where the time goes:
time: 3550 us; the launch traced here: 3540 us
  waiting for transfers between devices  2190 us (62%)
  local copies, waits for them, and re-layouts  706 us (20%)
  matrix products  367 us (10%)
  other arithmetic  176 us (5%)
  starting transfers between devices  60.6 us (2%)
    unnamed x26, waiting for transfers between devices  690 us
    all_to_all x2, waiting for transfers between devices, local(): lax.all_to_all(send_grads.reshape(group_size, experts // group_size, CAP,...  269 us
    all_to_all x2, waiting for transfers between devices, local(): lax.all_to_all(send_rows.reshape(group_size, experts // group_size, CAP,...  247 us
    reduce_scatter x1, waiting for transfers between devices, local(): lax.psum_scatter(stacked[6], ('dp', 'expert', 'fsdp'), scatter_dimension=...  142 us
    reduce_scatter x1, waiting for transfers between devices, local(): lax.psum_scatter(stacked[8], ('dp', 'expert', 'fsdp'), scatter_dimension=...  142 us
    reduce_scatter x1, waiting for transfers between devices, local(): lax.psum_scatter(stacked[2], ('dp', 'expert', 'fsdp'), scatter_dimension=...  133 us
    all_gather x2, waiting for transfers between devices, local(): lax.all_gather(kv_local, 'expert', axis=0, tiled=True)  133 us
    gather x6, local copies, waits for them, and re-layouts, local(): gate_probs = jax.nn.softmax(jnp.take_along_axis(logits, route_now, 1), -1)  133 us
  transfers between devices with their start and end apart: 28, of which 21 were waited for; matrix products, arithmetic and copies ran while one was open for 30% of the time, Pallas kernels for 0%

commit v1 on v0

v1 whole, which is shorter than its diff:
```python
import functools

import jax
import jax.numpy as jnp
from jax import lax
from jax.experimental import pallas as pl
from jax.experimental.pallas import tpu as pltpu
from jax.sharding import PartitionSpec as P

EPSILON = 1e-05
NEGATIVE = -1e30
GELU_SCALE = 0.7978845608028654
GELU_CUBIC = 0.044715
BLOCK = 256
AXES = ("dp", "expert", "fsdp")
F32 = jnp.float32
BF16 = jnp.bfloat16
VMEM_BYTES = 60 << 20


def dot_nn(left, right):
    return lax.dot_general(left, right, (((1,), (0,)), ((), ())), preferred_element_type=F32)


def dot_nt(left, right):
    return lax.dot_general(left, right, (((1,), (1,)), ((), ())), preferred_element_type=F32)


def dot_tn(left, right):
    return lax.dot_general(left, right, (((0,), (0,)), ((), ())), preferred_element_type=F32)


def normalize(values):
    center = values - jnp.mean(values, -1, keepdims=True)
    spread = lax.rsqrt(jnp.mean(center * center, -1, keepdims=True) + EPSILON)
    return center * spread, spread


def fold_rows(values, combine):
    rows, columns = values.shape
    return combine(values.reshape(rows // 8, 8, columns), 0)


def pick_slots(table_ref, slot, picks, width, span):
    experts = slot.shape[0]
    picked = []
    for pick in range(picks):
        value = table_ref[pick * width : (pick + 1) * width, :]
        for expert in range(pick + 1, experts - picks + pick + 1):
            hit = jnp.broadcast_to(slot[expert : expert + 1, :], (width, span)) == pick
            value = jnp.where(hit, table_ref[expert * width : (expert + 1) * width, :], value)
        picked.append(value)
    return picked


def spread_slots(read, slot, expert, picks, width, span):
    experts = slot.shape[0]
    row = jnp.broadcast_to(slot[expert : expert + 1, :], (width, span))
    value = jnp.zeros((width, span), F32)
    for pick in range(max(0, expert - experts + picks), min(expert, picks - 1) + 1):
        value = jnp.where(row == pick, read(pick), value)
    return value


def forward_kernel(
    lens,
    x_ref,
    route_ref,
    gain_ref,
    shift_ref,
    w_ref,
    wk_ref,
    wv_ref,
    hid_ref,
    kaug_ref,
    vaug_ref,
    kt_ref,
    q_ref,
    ctx_ref,
    lse_ref,
    gate_ref,
    slot_ref,
    table,
    qaug,
    scores,
    vt,
    acc,
):
    block = pl.program_id(1)
    length = lens[pl.program_id(0)]
    span = x_ref.shape[2]
    experts = slot_ref.shape[2]
    picks = route_ref.shape[2]
    width = kt_ref.shape[3]
    half = w_ref.shape[2]
    rows = picks * span

    normed, _ = normalize(x_ref[0, 0].astype(F32))
    hid = (normed * gain_ref[...] + shift_ref[...]).astype(BF16)
    hid_ref[0, 0] = hid
    table[...] = dot_nt(w_ref[0], hid[:, :half]) + dot_nt(w_ref[1], hid[:, half:])
    head = experts * width
    kt_ref[0, 0, 0] = table[head : head + width, :].astype(BF16)
    vt[block] = table[head + width : head + 2 * width, :].astype(BF16)

    lane = lax.broadcasted_iota(jnp.int32, (span, 2 * width), 1)
    place = block * span + lax.broadcasted_iota(jnp.int32, (span, 2 * width), 0)
    ones = jnp.where(lane < width + 4, 1.0, 0.0)
    cut = jnp.where(place < length, 0.0, NEGATIVE)
    keys = jnp.where(lane < width, dot_nn(hid, wk_ref[...]), jnp.where(lane == width, cut, ones))
    kaug_ref[0, block] = keys.astype(BF16)
    vals = jnp.where(lane < width, dot_nn(hid, wv_ref[...]), ones)
    vaug_ref[0, block] = vals.astype(BF16)

    logits = table[head + 2 * width : head + 2 * width + experts, :]
    expert_id = lax.broadcasted_iota(jnp.int32, (experts, span), 0)
    chosen = jnp.zeros((experts, span), F32)
    for pick in range(picks):
        chosen = jnp.where(expert_id == route_ref[0, 0, pick : pick + 1, :], 1.0, chosen)
    lower = jnp.where(
        lax.broadcasted_iota(jnp.int32, (experts, experts), 1)
        < lax.broadcasted_iota(jnp.int32, (experts, experts), 0),
        1.0,
        0.0,
    )
    slot = jnp.where(chosen > 0.0, dot_nn(lower, chosen), -1.0).astype(jnp.int32)
    slot_ref[0, 0] = slot
    masked = jnp.where(chosen > 0.0, logits, NEGATIVE)
    raised = jnp.where(chosen > 0.0, jnp.exp(masked - jnp.max(masked, 0, keepdims=True)), 0.0)
    gate_ref[0, 0] = raised / jnp.sum(raised, 0, keepdims=True)

    picked = pick_slots(table, slot, picks, width, span)
    for pick in range(picks):
        qaug[0:width, pick * span : (pick + 1) * span] = (
            picked[pick].astype(BF16) * (width**-0.5)
        ).astype(BF16)
    q_ref[0, 0] = qaug[0:width, :]
    side = lax.broadcasted_iota(jnp.int32, (width, rows), 0)
    qaug[width : 2 * width, :] = jnp.where(side == 0, 1.0, 0.0).astype(BF16)

    def score_step(at, top):
        part = dot_nn(kaug_ref[0, at], qaug[...])
        scores[at] = part
        return jnp.maximum(top, fold_rows(part, jnp.max))

    used = jnp.minimum(block, (length + span - 1) // span)
    top = lax.fori_loop(0, used, score_step, jnp.full((8, rows), NEGATIVE, F32))
    causal = lax.broadcasted_iota(jnp.int32, (span, rows), 0) <= (
        lax.broadcasted_iota(jnp.int32, (span, rows), 1) & (span - 1)
    )
    part = jnp.where(causal, dot_nn(kaug_ref[0, block], qaug[...]), NEGATIVE)
    top = jnp.maximum(top, fold_rows(part, jnp.max))
    top = jnp.max(top, 0, keepdims=True)
    raised = jnp.exp(part - top)
    acc[...] = dot_nn(vt[block], raised.astype(BF16))
    total = fold_rows(raised, jnp.sum)

    def value_step(at, total):
        raised = jnp.exp(scores[at] - top)
        acc[...] += dot_nn(vt[at], raised.astype(BF16))
        return total + fold_rows(raised, jnp.sum)

    total = lax.fori_loop(0, used, value_step, total)
    total = jnp.sum(total, 0, keepdims=True)
    ctx_ref[0, 0] = (acc[...] * (1.0 / total)).astype(BF16)
    lse_ref[0, 0] = top + jnp.log(total)


def middle_kernel(
    lens,
    x_ref,
    ctx_ref,
    gate_ref,
    slot_ref,
    cot_ref,
    w_ref,
    gain_ref,
    shift_ref,
    up_ref,
    up_shift_ref,
    down_ref,
    down_shift_ref,
    out_ref,
    mid_ref,
    do_ref,
    delta_ref,
    gl_ref,
    down_grad_ref,
    up_grad_ref,
    wo_grad_ref,
    small_ref,
    up_shift_grad_ref,
    gated,
    cexp,
    table,
    down_acc,
    up_acc,
    wo_acc,
):
    micro = pl.program_id(0)
    block = pl.program_id(1)
    length = lens[micro]
    span = x_ref.shape[2]
    experts = slot_ref.shape[2]
    width = ctx_ref.shape[2]
    picks = ctx_ref.shape[3] // span
    half = w_ref.shape[2]
    first = (micro == 0) & (block == 0)
    last = (micro == pl.num_programs(0) - 1) & (block == pl.num_programs(1) - 1)

    @pl.when(first)
    def _():
        down_acc[...] = jnp.zeros_like(down_acc)
        up_acc[...] = jnp.zeros_like(up_acc)
        wo_acc[...] = jnp.zeros_like(wo_acc)
        small_ref[...] = jnp.zeros_like(small_ref)
        up_shift_grad_ref[...] = jnp.zeros_like(up_shift_grad_ref)

    slot = slot_ref[0, 0]
    gates = gate_ref[0, 0]
    gate = [
        jnp.sum(jnp.where(slot == pick, gates, 0.0), 0, keepdims=True) for pick in range(picks)
    ]
    for pick in range(picks):
        at = slice(pick * span, (pick + 1) * span)
        gated[:, at] = ctx_ref[0, 0, :, at].astype(F32) * gate[pick]
    for expert in range(experts):
        cexp[expert * width : (expert + 1) * width, :] = spread_slots(
            lambda pick: gated[:, pick * span : (pick + 1) * span],
            slot,
            expert,
            picks,
            width,
            span,
        ).astype(BF16)
    mixed = x_ref[0, 0].astype(F32) + jnp.concatenate(
        [dot_tn(cexp[...], w_ref[0]), dot_tn(cexp[...], w_ref[1])], 1
    )
    normed, spread = normalize(mixed)
    hid = (normed * gain_ref[...] + shift_ref[...]).astype(BF16)
    place = block * span + lax.broadcasted_iota(jnp.int32, (span, 1), 0)
    grad = jnp.where(place < length, cot_ref[0, 0], 0.0)
    grad_b = grad.astype(BF16)
    hid_t = hid.T
    out = mixed + down_shift_ref[...]
    back = jnp.zeros_like(mixed)
    hidden_units = up_ref.shape[1]
    step = min(hidden_units, 512)
    for at in range(0, hidden_units, step):
        cut = slice(at, at + step)
        pre = dot_nn(hid, up_ref[:, cut]) + up_shift_ref[:, cut]
        square = pre * pre
        bent = jnp.tanh(pre * (GELU_SCALE + (GELU_SCALE * GELU_CUBIC) * square))
        rise = 0.5 + 0.5 * bent
        active = (pre * rise).astype(BF16)
        slope = rise + (0.5 * pre) * (1.0 - bent * bent) * (
            GELU_SCALE + (3.0 * GELU_SCALE * GELU_CUBIC) * square
        )
        grad_pre = dot_nt(grad_b, down_ref[cut, :]) * slope
        grad_pre_b = grad_pre.astype(BF16)
        out = out + dot_nn(active, down_ref[cut, :])
        back = back + dot_nt(grad_pre_b, up_ref[:, cut])
        down_acc[cut, :] += dot_nn(active.T, grad_b)
        up_acc[:, cut] += dot_nn(hid_t, grad_pre_b)
        up_shift_grad_ref[:, cut] += fold_rows(grad_pre, jnp.sum)
    out_ref[0, 0] = out
    scaled = back * gain_ref[...]
    mid = grad + spread * (
        scaled
        - jnp.mean(scaled, -1, keepdims=True)
        - normed * jnp.mean(scaled * normed, -1, keepdims=True)
    )
    mid_ref[0, 0] = mid
    small_ref[0] += fold_rows(back * normed, jnp.sum)
    small_ref[1] += fold_rows(back, jnp.sum)
    small_ref[2] += fold_rows(grad_b.astype(F32), jnp.sum)

    mid_b = mid.astype(BF16)
    wo_acc[...] += dot_nt(mid_b.T, cexp[...])
    table[...] = dot_nt(w_ref[0], mid_b[:, :half]) + dot_nt(w_ref[1], mid_b[:, half:])
    picked = pick_slots(table, slot, picks, width, span)
    grad_gate = []
    for pick in range(picks):
        at = slice(pick * span, (pick + 1) * span)
        ctx = ctx_ref[0, 0, :, at].astype(F32)
        grad_gate.append(jnp.sum(picked[pick] * ctx, 0, keepdims=True))
        grad_ctx = (picked[pick] * gate[pick]).astype(BF16)
        do_ref[0, 0, :, at] = grad_ctx
        delta_ref[0, 0, :, at] = jnp.sum(grad_ctx.astype(F32) * ctx, 0, keepdims=True)
    average = gate[0] * grad_gate[0]
    for pick in range(1, picks):
        average = average + gate[pick] * grad_gate[pick]
    grad_logits = jnp.zeros((experts, span), F32)
    for pick in range(picks):
        grad_logits = jnp.where(
            slot == pick, gate[pick] * (grad_gate[pick] - average), grad_logits
        )
    gl_ref[0, 0] = grad_logits

    @pl.when(last)
    def _():
        down_grad_ref[...] = down_acc[...].astype(BF16)
        up_grad_ref[...] = up_acc[...].astype(BF16)
        wo_grad_ref[...] = wo_acc[...].astype(BF16)


def split_three(values):
    high = values.astype(BF16).astype(F32)
    rest = values - high
    middle = rest.astype(BF16).astype(F32)
    return high, middle, rest - middle


def backward_kernel(
    lens,
    hid_ref,
    kaug_ref,
    vaug_ref,
    kt_ref,
    q_ref,
    lse_ref,
    do_ref,
    delta_ref,
    slot_ref,
    gl_ref,
    r_ref,
    w_grad_ref,
    qaug,
    daug,
    dq,
    dkt,
    dvt,
    w_acc,
):
    micro = pl.program_id(0)
    step = pl.program_id(1)
    blocks = pl.num_programs(1)
    block = blocks - 1 - step
    length = lens[micro]
    span = hid_ref.shape[2]
    experts = slot_ref.shape[2]
    width = q_ref.shape[2]
    rows = q_ref.shape[3]
    picks = rows // span
    head = experts * width

    @pl.when((micro == 0) & (step == 0))
    def _():
        w_acc[...] = jnp.zeros_like(w_acc)

    @pl.when(step == 0)
    def _():
        dkt[...] = jnp.zeros_like(dkt)
        dvt[...] = jnp.zeros_like(dvt)

    @pl.when(block * span >= length)
    def _():
        r_ref[...] = jnp.zeros_like(r_ref)

    @pl.when(block * span < length)
    def _():
        side = lax.broadcasted_iota(jnp.int32, (width, rows), 0)
        qaug[0:width, :] = q_ref[0, 0]
        high, middle, low = split_three(-lse_ref[0, 0])
        qaug[width : 2 * width, :] = jnp.where(
            side == 0,
            1.0,
            jnp.where(side == 1, high, jnp.where(side == 2, middle, jnp.where(side == 3, low, 0.0))),
        ).astype(BF16)
        daug[0:width, :] = do_ref[0, 0]
        high, middle, low = split_three(-delta_ref[0, 0])
        daug[width : 2 * width, :] = jnp.where(
            side == 0, high, jnp.where(side == 1, middle, jnp.where(side == 2, low, 0.0))
        ).astype(BF16)

        def key_step(at, probs):
            probs_b = probs.astype(BF16)
            slopes = (probs * dot_nn(vaug_ref[0, at], daug[...])).astype(BF16)
            dvt[at] += dot_nt(daug[0:width, :], probs_b)
            dkt[at] += dot_nt(qaug[0:width, :], slopes)
            return dot_nn(kt_ref[0, at], slopes)

        causal = lax.broadcasted_iota(jnp.int32, (span, rows), 0) <= (
            lax.broadcasted_iota(jnp.int32, (span, rows), 1) & (span - 1)
        )
        dq[...] = key_step(
            block, jnp.where(causal, jnp.exp(dot_nn(kaug_ref[0, block], qaug[...])), 0.0)
        )

        def body(at, carry):
            dq[...] += key_step(at, jnp.exp(dot_nn(kaug_ref[0, at], qaug[...])))
            return carry

        lax.fori_loop(0, block, body, 0)
        dq[...] = dq[...] * (width**-0.5)
        slot = slot_ref[0, 0]
        for expert in range(experts):
            r_ref[0, 0, expert * width : (expert + 1) * width, :] = spread_slots(
                lambda pick: dq[:, pick * span : (pick + 1) * span],
                slot,
                expert,
                picks,
                width,
                span,
            ).astype(BF16)
        r_ref[0, 0, head : head + width, :] = dkt[block].astype(BF16)
        r_ref[0, 0, head + width : head + 2 * width, :] = dvt[block].astype(BF16)
        tail = r_ref.shape[2] - head - 2 * width
        r_ref[0, 0, head + 2 * width :, :] = jnp.concatenate(
            [gl_ref[0, 0], jnp.zeros((tail - experts, span), F32)], 0
        ).astype(BF16)
        w_acc[...] += dot_nt(hid_ref[0, 0].T, r_ref[0, 0])

    @pl.when((micro == pl.num_programs(0) - 1) & (step == blocks - 1))
    def _():
        w_grad_ref[...] = w_acc[...].astype(BF16)


def input_kernel(x_ref, mid_ref, r_ref, w_ref, gain_ref, out_ref, small_ref):
    first = (pl.program_id(0) == 0) & (pl.program_id(1) == 0)

    @pl.when(first)
    def _():
        small_ref[...] = jnp.zeros_like(small_ref)

    back = jnp.concatenate(
        [dot_tn(r_ref[0, 0], w_ref[0]), dot_tn(r_ref[0, 0], w_ref[1])], 1
    )
    normed, spread = normalize(x_ref[0, 0].astype(F32))
    scaled = back * gain_ref[...]
    out_ref[0, 0] = mid_ref[0, 0] + spread * (
        scaled
        - jnp.mean(scaled, -1, keepdims=True)
        - normed * jnp.mean(scaled * normed, -1, keepdims=True)
    )
    small_ref[0] += fold_rows(back * normed, jnp.sum)
    small_ref[1] += fold_rows(back, jnp.sum)


def full(shape):
    return pl.BlockSpec(shape, lambda *ids: (0,) * len(shape))


def blocked(shape):
    tail = (0,) * (len(shape) - 2)
    return pl.BlockSpec((1, 1) + tuple(shape[2:]), lambda m, i, *refs: (m, i) + tail)


def reversed_blocks(shape):
    tail = (0,) * (len(shape) - 2)
    last = shape[1] - 1
    return pl.BlockSpec((1, 1) + tuple(shape[2:]), lambda m, i, *refs: (m, last - i) + tail)


def whole(shape):
    tail = (0,) * (len(shape) - 1)
    return pl.BlockSpec((1,) + tuple(shape[1:]), lambda m, i, *refs: (m,) + tail)


def struct(shape, dtype):
    return jax.ShapeDtypeStruct(shape, dtype)


def params():
    return pltpu.CompilerParams(
        dimension_semantics=("arbitrary", "arbitrary"), vmem_limit_bytes=VMEM_BYTES
    )


def cost(flops, transcendentals, moved):
    return pl.CostEstimate(flops=flops, transcendentals=transcendentals, bytes_accessed=moved)


def exchange(value, axis, distance):
    count = lax.axis_size(axis)
    return lax.ppermute(value, axis, [(at, at ^ distance) for at in range(count)])


def permute_groups(value, index):
    groups = value.shape[0]
    bit = 1
    while bit < groups:
        pairs = value.reshape((groups // (2 * bit), 2, bit) + value.shape[1:])
        value = jnp.where((index & bit) != 0, pairs[:, ::-1].reshape(value.shape), value)
        bit *= 2
    return value


def pick_at(value, index, dim):
    return lax.dynamic_index_in_dim(value, index, dim, keepdims=False)


def reduce_axis(value, axis, dim, relative=False, keep=False):
    count = lax.axis_size(axis)
    me = lax.axis_index(axis)
    base = 0 if relative else me
    total = pick_at(value, base, dim).astype(F32)
    for distance in range(1, count):
        sent = pick_at(value, distance if relative else me ^ distance, dim)
        total = total + exchange(sent, axis, distance).astype(F32)
    return total if keep else total.astype(BF16)


def local(
    inputs,
    lengths,
    routes,
    ln1_gain,
    ln1_bias,
    kv_weight,
    router_weight,
    query_weight,
    out_weight,
    ln2_gain,
    ln2_bias,
    up_weight,
    up_bias,
    down_weight,
    down_bias,
    out_cotangent,
):
    micro_count, _, slots, model = inputs.shape
    experts = router_weight.shape[2]
    width = query_weight.shape[3]
    picks = routes.shape[4]
    hidden_units = up_weight.shape[2]
    dp_size, z_size, f_size = (lax.axis_size(axis) for axis in AXES)
    z_at = lax.axis_index("expert")
    seq_index = (lax.axis_index("dp") * z_size + z_at) * f_size + lax.axis_index("fsdp")
    own_experts = experts // z_size
    half = model // f_size
    span = min(BLOCK, slots)
    blocks = slots // span
    rows = picks * span
    head = experts * width
    spare = -(-experts // 16) * 16
    all_rows = head + 2 * width + spare

    def gather(value, dim):
        return lax.all_gather(value, "fsdp", axis=dim, tiled=True)

    lens = lax.dynamic_index_in_dim(lengths, seq_index, 1, keepdims=False)

    def transposed_heads(weight):
        own = jnp.swapaxes(weight[0], 1, 2).reshape(own_experts * width, half)
        return [own] + [exchange(own, "expert", distance) for distance in range(1, z_size)]

    query_parts = transposed_heads(query_weight)
    out_parts = transposed_heads(out_weight)
    router_t = router_weight[0].T.reshape(z_size, own_experts, half)
    router_t = permute_groups(router_t, z_at).reshape(experts, half)
    router_t = jnp.pad(router_t, ((0, spare - experts), (0, 0)))
    proj = lax.all_gather(
        jnp.concatenate(query_parts + [kv_weight[0].T, router_t], 0), "fsdp", axis=0
    )
    out_proj = lax.all_gather(jnp.concatenate(out_parts, 0), "fsdp", axis=0)
    kv_full = gather(kv_weight[0], 0)
    key_weight = jnp.pad(kv_full[:, :width], ((0, 0), (0, width)))
    value_weight = jnp.pad(kv_full[:, width:], ((0, 0), (0, width)))
    gains = gather(jnp.concatenate([ln1_gain, ln1_bias, ln2_gain, ln2_bias, down_bias], 0), 1)
    gains = gains.astype(F32)
    gain1, shift1, gain2, shift2, down_shift = (gains[at : at + 1] for at in range(5))
    up_shift = gather(up_bias, 1).astype(F32)
    up_full = gather(up_weight[0], 0)
    down_full = gather(down_weight[0], 0)

    local_routes = routes[0, :, 0]
    local_routes = ((local_routes // own_experts) ^ z_at) * own_experts + local_routes % own_experts
    route_t = jnp.swapaxes(local_routes.reshape(micro_count, blocks, span, picks), 2, 3)
    states = inputs.reshape(micro_count, blocks, span, model)
    cotangent = out_cotangent.reshape(micro_count, blocks, span, model)

    grid = (micro_count, blocks)
    hid_s = struct((micro_count, blocks, span, model), BF16)
    aug_s = struct((micro_count, blocks, span, 2 * width), BF16)
    kt_s = struct((micro_count, blocks, 1, width, span), BF16)
    q_s = struct((micro_count, blocks, width, rows), BF16)
    row_s = struct((micro_count, blocks, 1, rows), F32)
    gate_s = struct((micro_count, blocks, experts, span), F32)
    slot_s = struct((micro_count, blocks, experts, span), jnp.int32)
    tokens = micro_count * slots
    pair_flops = tokens * picks * slots * width
    hid, kaug, vaug, kt, q, ctx, lse, gates, slot = pl.pallas_call(
        forward_kernel,
        name="forward",
        grid_spec=pltpu.PrefetchScalarGridSpec(
            num_scalar_prefetch=1,
            grid=grid,
            in_specs=[
                blocked(states.shape),
                blocked(route_t.shape),
                full(gain1.shape),
                full(shift1.shape),
                full(proj.shape),
                full(key_weight.shape),
                full(value_weight.shape),
            ],
            out_specs=[
                blocked(hid_s.shape),
                whole(aug_s.shape),
                whole(aug_s.shape),
                blocked(kt_s.shape),
                blocked(q_s.shape),
                blocked(q_s.shape),
                blocked(row_s.shape),
                blocked(gate_s.shape),
                blocked(slot_s.shape),
            ],
            scratch_shapes=[
                pltpu.VMEM((all_rows, span), F32),
                pltpu.VMEM((2 * width, rows), BF16),
                pltpu.VMEM((blocks, span, rows), F32),
                pltpu.VMEM((blocks, width, span), BF16),
                pltpu.VMEM((width, rows), F32),
            ],
        ),
        out_shape=[hid_s, aug_s, aug_s, kt_s, q_s, q_s, row_s, gate_s, slot_s],
        compiler_params=params(),
        cost_estimate=cost(2 * tokens * model * all_rows + 8 * pair_flops, 0, 8 << 20),
    )(lens, states, route_t, gain1, shift1, proj, key_weight, value_weight)

    state_s = struct((micro_count, blocks, span, model), F32)
    outputs, mid, grad_ctx, delta, grad_logits, down_grad, up_grad, wo_grad, small2, up_small = (
        pl.pallas_call(
            middle_kernel,
            name="middle",
            grid_spec=pltpu.PrefetchScalarGridSpec(
                num_scalar_prefetch=1,
                grid=grid,
                in_specs=[
                    blocked(states.shape),
                    blocked(q_s.shape),
                    blocked(gate_s.shape),
                    blocked(slot_s.shape),
                    blocked(cotangent.shape),
                    full(out_proj.shape),
                    full(gain2.shape),
                    full(shift2.shape),
                    full(up_full.shape),
                    full(up_shift.shape),
                    full(down_full.shape),
                    full(down_shift.shape),
                ],
                out_specs=[
                    blocked(state_s.shape),
                    blocked(state_s.shape),
                    blocked(q_s.shape),
                    blocked(row_s.shape),
                    blocked(gate_s.shape),
                    full((hidden_units, model)),
                    full((model, hidden_units)),
                    full((model, head)),
                    full((3, 8, model)),
                    full((8, hidden_units)),
                ],
                scratch_shapes=[
                    pltpu.VMEM((width, rows), F32),
                    pltpu.VMEM((head, span), BF16),
                    pltpu.VMEM((head, span), F32),
                    pltpu.VMEM((hidden_units, model), F32),
                    pltpu.VMEM((model, hidden_units), F32),
                    pltpu.VMEM((model, head), F32),
                ],
            ),
            out_shape=[
                state_s,
                state_s,
                q_s,
                row_s,
                gate_s,
                struct((hidden_units, model), BF16),
                struct((model, hidden_units), BF16),
                struct((model, head), BF16),
                struct((3, 8, model), F32),
                struct((8, hidden_units), F32),
            ],
            compiler_params=params(),
            cost_estimate=cost(
                2 * tokens * model * (6 * hidden_units + 3 * head), 0, 24 << 20
            ),
        )(
            lens,
            states,
            ctx,
            gates,
            slot,
            cotangent,
            out_proj,
            gain2,
            shift2,
            up_full,
            up_shift,
            down_full,
            down_shift,
        )
    )

    r_s = struct((micro_count, blocks, all_rows, span), BF16)
    routed, w_grad = pl.pallas_call(
        backward_kernel,
        name="backward",
        grid_spec=pltpu.PrefetchScalarGridSpec(
            num_scalar_prefetch=1,
            grid=grid,
            in_specs=[
                reversed_blocks(hid_s.shape),
                whole(aug_s.shape),
                whole(aug_s.shape),
                whole((micro_count, blocks, width, span)),
                reversed_blocks(q_s.shape),
                reversed_blocks(row_s.shape),
                reversed_blocks(q_s.shape),
                reversed_blocks(row_s.shape),
                reversed_blocks(slot_s.shape),
                reversed_blocks(gate_s.shape),
            ],
            out_specs=[reversed_blocks(r_s.shape), full((model, all_rows))],
            scratch_shapes=[
                pltpu.VMEM((2 * width, rows), BF16),
                pltpu.VMEM((2 * width, rows), BF16),
                pltpu.VMEM((width, rows), F32),
                pltpu.VMEM((blocks, width, span), F32),
                pltpu.VMEM((blocks, width, span), F32),
                pltpu.VMEM((model, all_rows), F32),
            ],
        ),
        out_shape=[r_s, struct((model, all_rows), BF16)],
        compiler_params=params(),
        cost_estimate=cost(2 * tokens * model * all_rows + 20 * pair_flops, 0, 24 << 20),
    )(
        lens,
        hid,
        kaug,
        vaug,
        kt.reshape(micro_count, blocks, width, span),
        q,
        lse,
        grad_ctx,
        delta,
        slot,
        grad_logits,
    )

    input_grad, small1 = pl.pallas_call(
        input_kernel,
        name="input_back",
        grid_spec=pltpu.PrefetchScalarGridSpec(
            num_scalar_prefetch=0,
            grid=grid,
            in_specs=[
                blocked(states.shape),
                blocked(state_s.shape),
                blocked(r_s.shape),
                full(proj.shape),
                full(gain1.shape),
            ],
            out_specs=[blocked(state_s.shape), full((2, 8, model))],
        ),
        out_shape=[state_s, struct((2, 8, model), F32)],
        compiler_params=params(),
        cost_estimate=cost(2 * tokens * model * all_rows, 0, 20 << 20),
    )(states, mid, routed, proj, gain1)

    def reduce_shared(value, chunk):
        value = value.reshape(dp_size, z_size, f_size, chunk, value.shape[1])
        value = reduce_axis(value, "fsdp", 2)
        value = reduce_axis(value, "dp", 0)
        return reduce_axis(value, "expert", 0, keep=True)

    def reduce_heads(value):
        chunk = model // (dp_size * f_size)
        value = value.reshape(dp_size, f_size, chunk, z_size, own_experts * width)
        value = reduce_axis(value, "fsdp", 1)
        value = reduce_axis(value, "dp", 0)
        value = reduce_axis(value, "expert", 1, relative=True, keep=True)
        return jnp.swapaxes(value.reshape(chunk, own_experts, width), 0, 1)[None]

    devices = dp_size * z_size * f_size
    up_weight_grad = reduce_shared(up_grad, model // devices)
    down_weight_grad = reduce_shared(down_grad, hidden_units // devices)
    out_weight_grad = reduce_heads(wo_grad)
    query_weight_grad = reduce_heads(w_grad[:, :head])

    chunk = model // devices
    router_grad = w_grad[:, head + 2 * width : head + 2 * width + experts].astype(F32)
    router_grad = permute_groups(router_grad.T.reshape(z_size, own_experts, model), z_at)
    router_grad = jnp.pad(router_grad.reshape(experts, model).T, ((0, 0), (0, spare - experts)))
    narrow = jnp.concatenate([w_grad[:, head : head + 2 * width].astype(F32), router_grad], 1)
    narrow = narrow.reshape(devices, chunk * (2 * width + spare))
    vectors = jnp.concatenate([jnp.sum(small1, 1), jnp.sum(small2, 1)], 0)
    vectors = jnp.swapaxes(vectors.reshape(5, devices, chunk), 0, 1).reshape(devices, 5 * chunk)
    up_vector = jnp.sum(up_small, 0).reshape(devices, hidden_units // devices)
    packed = jnp.concatenate([narrow, vectors, up_vector], 1)
    packed = lax.all_to_all(packed, AXES, split_axis=0, concat_axis=0, tiled=True)
    packed = jnp.sum(packed.reshape(devices, -1), 0)
    cut = chunk * (2 * width + spare)
    narrow = packed[:cut].reshape(chunk, 2 * width + spare)
    vectors = packed[cut : cut + 5 * chunk].reshape(5, 1, chunk)
    up_vector = packed[cut + 5 * chunk :][None]
    shape = (micro_count, 1, slots, model)
    return (
        outputs.reshape(shape),
        input_grad.reshape(shape),
        vectors[0],
        vectors[1],
        narrow[None, :, : 2 * width],
        narrow[None, :, 2 * width : 2 * width + experts],
        query_weight_grad,
        out_weight_grad,
        vectors[2],
        vectors[3],
        up_weight_grad[None],
        up_vector,
        down_weight_grad[None],
        vectors[4],
    )


def solution(mesh):
    shards = P(None, AXES, None, None)
    return jax.shard_map(
        local,
        mesh=mesh,
        in_specs=(
            shards,
            P(),
            P(None, None, AXES, None, None),
            P(None, "fsdp"),
            P(None, "fsdp"),
            P(None, "fsdp", None),
            P(None, "fsdp", None),
            P(None, "expert", "fsdp", None),
            P(None, "expert", "fsdp", None),
            P(None, "fsdp"),
            P(None, "fsdp"),
            P(None, "fsdp", None),
            P(None, "fsdp"),
            P(None, "fsdp", None),
            P(None, "fsdp"),
            shards,
        ),
        out_specs=(
            shards,
            shards,
            P(None, AXES),
            P(None, AXES),
            P(None, AXES, None),
            P(None, AXES, None),
            P(None, "expert", ("dp", "fsdp"), None),
            P(None, "expert", ("dp", "fsdp"), None),
            P(None, AXES),
            P(None, AXES),
            P(None, AXES, None),
            P(None, AXES),
            P(None, AXES, None),
            P(None, AXES),
        ),
        check_vma=False,
    )
```

time: 3550 us -> 317 us (0.09)
  waiting for transfers between devices: 2190 us -> 59.3 us
  local copies, waits for them, and re-layouts: 706 us -> 22.8 us
  matrix products: 367 us -> 0 us
  other arithmetic: 176 us -> 15.4 us
  Pallas kernels: 0 us -> 146 us
    all_to_all x10 -> x1, waiting for transfers between devices: 700 us -> 1.8 us  [local(): lax.all_to_all(packed, AXES, split_axis=0, concat_axis=0, tiled=True)]
    unnamed x26 -> x4, waiting for transfers between devices: 690 us -> 1.24 us
    reduce_scatter x6 -> x0, waiting for transfers between devices: 667 us -> none  [the longest x1 142 us: local(): lax.psum_scatter(stacked[6], ('dp', 'expert', 'fsdp'), scatter_dimension=...]
    gather x18 -> x0, local copies, waits for them, and re-layouts: 553 us -> none  [the longest x6 133 us: local(): gate_probs = jax.nn.softmax(jnp.take_along_axis(logits, route_now, 1), -1)]
    dot_general x50 -> x0, matrix products: 367 us -> none  [the longest x2 61.2 us: expert_backward(): jnp.einsum('sich,sjh->sicj', grad_context, value_part, preferred_element_...]
    pallas_call x0 -> x4, Pallas kernels: none -> 146 us  [the longest x1 62.3 us: local(): pl.pallas_call(middle_kernel, name='middle', grid_spec=pltpu.PrefetchScal...]
    all_gather x4, waiting for transfers between devices: 133 us -> 0.06 us  [the longest x2 0.03 us: gather(): return lax.all_gather(value, 'fsdp', axis=dim, tiled=True)]
    reduce_sum x23 -> x4, other arithmetic: 88.6 us -> 2.02 us  [the longest x1 1.2 us: local(): packed = jnp.sum(packed.reshape(devices, -1), 0)]
  transfers between devices with their start and end apart: 28 -> 39, of which waited for: 21 -> 19; matrix products, arithmetic and copies ran while one was open for 30% -> 9% of each run, Pallas kernels for 0% -> 11%
where the time goes in v1:
time: 317 us; the launch traced here: 316 us
  Pallas kernels  146 us (46%)
  waiting for transfers between devices  59.3 us (19%)
  starting transfers between devices  52 us (16%)
  local copies, waits for them, and re-layouts  22.8 us (7%)
  other arithmetic  15.4 us (5%)
  between operations  14.6 us (5%)
  blocking collectives  5.48 us (2%)
    pallas_call x1, Pallas kernels, local(): pl.pallas_call(middle_kernel, name='middle', grid_spec=pltpu.PrefetchScal...  62.3 us
    ppermute x34, waiting for transfers between devices, exchange(): lax.ppermute(value, axis, [(at, at ^ distance) for at in range(count)])  56.2 us
    ppermute x34, starting transfers between devices, exchange(): lax.ppermute(value, axis, [(at, at ^ distance) for at in range(count)])  40.3 us
    pallas_call x1, Pallas kernels, local(): pl.pallas_call(backward_kernel, name='backward', grid_spec=pltpu.Prefetch...  37.5 us
    pallas_call x1, Pallas kernels, local(): pl.pallas_call(forward_kernel, name='forward', grid_spec=pltpu.PrefetchSc...  34 us
    pallas_call x1, Pallas kernels, local(): pl.pallas_call(input_kernel, name='input_back', grid_spec=pltpu.PrefetchS...  12.6 us
    all_to_all x1, starting transfers between devices, local(): lax.all_to_all(packed, AXES, split_axis=0, concat_axis=0, tiled=True)  11.5 us
    convert_element_type x8, other arithmetic, reduce_axis(): return total if keep else total.astype(BF16)  6.37 us
  transfers between devices with their start and end apart: 39, of which 19 were waited for; matrix products, arithmetic and copies ran while one was open for 9% of the time, Pallas kernels for 11%

profile of v1, /device:TPU:0, one launch (start us, length us, event | category | flops | bytes accessed | tf_op | source)
XLA Modules:
  0.0 315.9 jit_solution(17356687114213263727)
XLA Ops:
  7.3 3.1 collective-permute-start
  10.3 2.6 collective-permute-start.1
  13.7 0.7 reshape.195
  14.5 0.7 select_select_fusion
  15.2 0.9 copy.58
  16.1 0.9 constant_dynamic-update-slice_fusion.4
  17.1 1.8 collective-permute-done
  18.9 8.8 %collective-permute-done.1 = bf16[384,256]{1,0:T(8,128)(2,1)S(1)} collective-permute-done((bf16[384,256]{1,0:T(8,128)(2,1)}, bf16[384,256]{1,0:T(8,128)(2,1)S(1)}, u32[]{:S(2)}, u32[]{:S(2)}) %collective-permute-start.1) | collective-permute-done | bytes 196640 | tf_op jit(solution)/shard_map/ppermute | solution.py:476
  27.8 0.9 copy-done.9
  28.8 3.4 %collective-permute-start.3 = (bf16[384,256]{1,0:T(8,128)(2,1)S(1)}, bf16[384,256]{1,0:T(8,128)(2,1)S(1)}, u32[]{:S(2)}, u32[]{:S(2)}) collective-permute-start(bf16[384,256]{1,0:T(8,128)(2,1)S(1)} %bitcast.208), channel_id=1, source_target_pairs={{0,2},{2,0},{4,6},{6,4},{1,3},{3,1},{5,7},{7,5},{8,10},{10,8},{12,... | collective-permute-start | bytes 589832 | tf_op jit(solution)/shard_map/ppermute | solution.py:476
  32.2 1.1 collective-permute-start.4
  33.3 1.4 collective-permute-start.5
  34.6 3.8 %collective-permute-done.3 = bf16[384,256]{1,0:T(8,128)(2,1)S(1)} collective-permute-done((bf16[384,256]{1,0:T(8,128)(2,1)S(1)}, bf16[384,256]{1,0:T(8,128)(2,1)S(1)}, u32[]{:S(2)}, u32[]{:S(2)}) %collective-permute-start.3) | collective-permute-done | bytes 196640 | tf_op jit(solution)/shard_map/ppermute | solution.py:476
  38.5 10.4 %collective-permute-done.4 = bf16[384,256]{1,0:T(8,128)(2,1)S(1)} collective-permute-done((bf16[384,256]{1,0:T(8,128)(2,1)S(1)}, bf16[384,256]{1,0:T(8,128)(2,1)S(1)}, u32[]{:S(2)}, u32[]{:S(2)}) %collective-permute-start.4) | collective-permute-done | bytes 196640 | tf_op jit(solution)/shard_map/ppermute | solution.py:476
  48.9 0.9 pad_maximum_fusion
  51.3 1.8 all_gather.27
  53.7 1.9 all-gather.1
  55.7 1.8 all_gather.34
  60.9 34.0 %forward.1 = (bf16[2,4,256,512]{3,2,1,0:T(8,128)(2,1)}, bf16[2,4,256,128]{3,2,1,0:T(8,128)(2,1)}, bf16[2,4,256,128]{3,2,1,0:T(8,128)(2,1)}, bf16[2,4,1,64,256]{4...) custom-call(s32[2]{0:T(128)} %fusion.30.lens, ...), custom_call_target="tpu_custom_call" | custom-call | flops 12146704384 | bytes 8388608 | tf_op jit(solution)/shard_map/forward/pallas_call | solution.py:583
  95.0 62.3 %middle.1 = (f32[2,4,256,512]{3,2,1,0:T(8,128)}, f32[2,4,256,512]{3,2,1,0:T(8,128)}, bf16[2,4,64,2048]{3,2,1,0:T(8,128)(2,1)}, f32[2,4,1,2048]{3,2,1,0:T(1,128)}...) custom-call(s32[2]{0:T(128)} %fusion.30.lens, ...), custom_call_target="tpu_custom_call" | custom-call | flops 35433480192 | bytes 25165824 | tf_op jit(solution)/shard_map/middle/pallas_call | solution.py:624
  157.3 37.5 %backward.1 = (bf16[2,4,1696,256]{3,2,1,0:T(8,128)(2,1)}, bf16[512,1696]{1,0:T(8,128)(2,1)}) custom-call(s32[2]{0:T(128)} %fusion.30.lens, bf16[2,4,256,512]{3,2,1,0:T(8,128)(2,1)} %get-tuple-element.42.hid_ref, bf16[2,4,256,128]{3,2,1,0:T(8,128)(2,1)} %get-tuple-element.43.kaug_ref, bf16[2,4,256,128]{3,2,1,0:T(8,128)(2,1)} %get-tuple-element.44.vaug_ref, ...), custom_call_target="tpu_custom_call" | custom-call | flops 25031606272 | bytes 25165824 | tf_op jit(solution)/shard_map/backward/pallas_call | solution.py:699
  194.8 0.9 convert_bitcast_fusion
  195.9 0.9 slice_convert_fusion
  196.8 12.6 %input_back.1 = (f32[2,4,256,512]{3,2,1,0:T(8,128)}, f32[2,8,512]{2,1,0:T(8,128)}) custom-call(bf16[2,4,256,512]{3,2,1,0:T(8,128)(2,1)} %bitcast.195, f32[2,4,256,512]{3,2,1,0:T(8,128)} %get-tuple-element.41.mid_ref, bf16[2,4,1696,256]{3,2,1,0:T(8,128)(2,1)} %get-tuple-element.51.r_ref, bf16[2,1696,256]{2,1,0:T(8,128)(2,1)} %bitcast.197, ...), custom_call_target="tpu_custom_call" | custom-call | flops 3556769792 | bytes 20971520 | tf_op jit(solution)/shard_map/input_back/pallas_call | solution.py:744
  209.4 0.8 reduce_sum.36
  211.5 1.1 copy.65
  212.6 11.5 %all-to-all-start = ((f32[32,1,2704]{2,1,0:T(1,128)}), f32[32,1,2704]{2,1,0:T(1,128)}, u32[]{:S(2)}, u32[]{:S(2)}) async-start(f32[32,1,2704]{2,1,0:T(1,128)} %copy.65), calls=%async_computation | async-start | bytes 720896 | tf_op jit(solution)/shard_map/all_to_all | solution.py:794
  224.4 1.5 copy-done.7
  225.8 1.0 dynamic-slice_bitcast_fusion
  226.9 1.1 dynamic-slice_bitcast_fusion.1
  228.8 3.0 reshape.214
  231.8 2.3 constant_dynamic-slice_fusion.1
  235.0 1.8 all-to-all-done
  236.8 1.2 reduce_sum.39
  240.5 1.3 fusion.2
  242.0 1.2 collective-permute-start.15
  243.1 2.3 collective-permute-start.16
  245.4 1.3 fusion.3
  246.9 2.9 collective-permute-done.14
  249.7 3.7 %collective-permute-done.15 = bf16[64,4,384]{2,0,1:T(8,128)(2,1)S(1)} collective-permute-done((bf16[64,4,384]{2,0,1:T(8,128)(2,1)S(1)}, bf16[64,4,384]{2,0,1:T(8,128)(2,1)S(1)}, u32[]{:S(2)}, u32[]{:S(2)}) %collective-permute-start.15) | collective-permute-done | bytes 196640 | tf_op jit(solution)/shard_map/ppermute | solution.py:476
  253.9 3.3 %collective-permute-start.9 = (bf16[64,4,384]{2,0,1:T(8,128)(2,1)S(1)}, bf16[64,4,384]{2,0,1:T(8,128)(2,1)S(1)}, u32[]{:S(2)}, u32[]{:S(2)}) collective-permute-start(bf16[64,4,384]{2,0,1:T(8,128)(2,1)S(1)} %get-tuple-element.116), channel_id=1, source_target_pairs={{0,24},{8,16},{16,8},{24,0},{1,25},{9,17},{17,9},{25,1},{2,26},{10... | collective-permute-start | bytes 589832 | tf_op jit(solution)/shard_map/ppermute | solution.py:476
  257.3 0.8 collective-permute-done.7
  258.1 5.2 %collective-permute-done.8 = bf16[64,4,384]{2,0,1:T(8,128)(2,1)S(1)} collective-permute-done((bf16[64,4,384]{2,0,1:T(8,128)(2,1)S(1)}, bf16[64,4,384]{2,0,1:T(8,128)(2,1)S(1)}, u32[]{:S(2)}, u32[]{:S(2)}) %collective-permute-start.8) | collective-permute-done | bytes 196640 | tf_op jit(solution)/shard_map/ppermute | solution.py:476
  263.3 1.6 collective-permute-start.18
  264.9 1.4 collective-permute-start.19
  267.0 1.9 collective-permute-done.18
  268.9 0.9 collective-permute-start.11
  269.9 1.2 collective-permute-done.19
  271.0 1.4 collective-permute-start.12
  273.9 3.0 collective-permute-done.12
  277.8 1.7 fusion
  280.0 1.1 collective-permute-start.29
  281.1 2.0 collective-permute-start.30
  283.2 1.5 fusion.1
  285.2 1.1 collective-permute-start.22
  286.3 2.6 collective-permute-done.28
  288.9 0.9 collective-permute-start.23
  289.8 4.1 %collective-permute-done.30 = bf16[4,64,512]{2,1,0:T(8,128)(2,1)S(1)} collective-permute-done((bf16[4,64,512]{2,1,0:T(8,128)(2,1)S(1)}, bf16[4,64,512]{2,1,0:T(8,128)(2,1)S(1)}, u32[]{:S(2)}, u32[]{:S(2)}) %collective-permute-start.30) | collective-permute-done | bytes 262176 | tf_op jit(solution)/shard_map/ppermute | solution.py:476
  294.1 2.7 collective-permute-start.32
  296.8 1.7 collective-permute-start.33
  298.5 0.9 collective-permute-done.23
  299.7 2.9 collective-permute-start.25
  302.6 1.4 collective-permute-start.26
  304.9 3.8 %collective-permute-done.26 = bf16[16,2048]{1,0:T(8,128)(2,1)S(1)} collective-permute-done((bf16[16,2048]{1,0:T(8,128)(2,1)S(1)}, bf16[16,2048]{1,0:T(8,128)(2,1)S(1)}, u32[]{:S(2)}, u32[]{:S(2)}) %collective-permute-start.26) | collective-permute-done | bytes 65568 | tf_op jit(solution)/shard_map/ppermute | solution.py:476
  (158 shorter events, 19.0 us)
Async XLA Ops:
  7.2 51.0 %copy-start = (s32[2,32]{1,0:T(2,128)S(1)}, s32[2,32]{1,0:T(2,128)}, u32[]{:S(2)}) copy-start(s32[2,32]{1,0:T(2,128)} %param.17) | copy-start | bytes 772
  7.2 21.6 %copy-start.12 = (bf16[1,6,256,64]{2,3,1,0:T(8,128)(2,1)S(1)}, bf16[1,6,256,64]{2,3,1,0:T(8,128)(2,1)}, u32[]{:S(2)}) copy-start(bf16[1,6,256,64]{2,3,1,0:T(8,128)(2,1)} %param.24) | copy-start | bytes 589828
  7.2 53.7 %all-gather.10.cloned.1.call-start = ((), (), s32[]{:S(2)}) async-start(), calls=%async_computation.1 | async-start | bytes 2605056 | tf_op jit(solution)/shard_map/all_gather | solution.py:553
  7.3 11.6 %collective-permute-start = (bf16[384,256]{1,0:T(8,128)(2,1)}, bf16[384,256]{1,0:T(8,128)(2,1)S(1)}, u32[]{:S(2)}, u32[]{:S(2)}) collective-permute-start(bf16[384,256]{1,0:T(8,128)(2,1)} %bitcast.212), channel_id=1, source_target_pairs={{0,2},{2,0},{4,6},{6,4},{1,3},{3,1},{5,7},{7,5},{8,10},{10,8},{12,... | collective-permute-start | bytes 589832 | tf_op jit(solution)/shard_map/ppermute | solution.py:476
  10.3 17.4 %collective-permute-start.1 = (bf16[384,256]{1,0:T(8,128)(2,1)}, bf16[384,256]{1,0:T(8,128)(2,1)S(1)}, u32[]{:S(2)}, u32[]{:S(2)}) collective-permute-start(bf16[384,256]{1,0:T(8,128)(2,1)} %bitcast.213), channel_id=1, source_target_pairs={{0,4},{2,6},{4,0},{6,2},{1,5},{3,7},{5,1},{7,3},{8,12},{10,14},{12... | collective-permute-start | bytes 589832 | tf_op jit(solution)/shard_map/ppermute | solution.py:476
  12.9 14.8 %collective-permute-start.2 = (bf16[384,256]{1,0:T(8,128)(2,1)}, bf16[384,256]{1,0:T(8,128)(2,1)S(1)}, u32[]{:S(2)}, u32[]{:S(2)}) collective-permute-start(bf16[384,256]{1,0:T(8,128)(2,1)} %bitcast.214), channel_id=1, source_target_pairs={{0,6},{2,4},{4,2},{6,0},{1,7},{3,5},{5,3},{7,1},{8,14},{10,12},{12... | collective-permute-start | bytes 589832 | tf_op jit(solution)/shard_map/ppermute | solution.py:476
  27.8 0.9 copy-start.9
  28.7 66.2 %all-gather.12.cloned.1.call-start = ((), (), s32[]{:S(2)}) async-start(), calls=%async_computation.2 | async-start | bytes 2359296 | tf_op jit(solution)/shard_map/all_gather | solution.py:556
  28.8 9.7 %collective-permute-start.3 = (bf16[384,256]{1,0:T(8,128)(2,1)S(1)}, bf16[384,256]{1,0:T(8,128)(2,1)S(1)}, u32[]{:S(2)}, u32[]{:S(2)}) collective-permute-start(bf16[384,256]{1,0:T(8,128)(2,1)S(1)} %bitcast.208), channel_id=1, source_target_pairs={{0,2},{2,0},{4,6},{6,4},{1,3},{3,1},{5,7},{7,5},{8,10},{10,8},{12,... | collective-permute-start | bytes 589832 | tf_op jit(solution)/shard_map/ppermute | solution.py:476
  32.2 16.7 %collective-permute-start.4 = (bf16[384,256]{1,0:T(8,128)(2,1)S(1)}, bf16[384,256]{1,0:T(8,128)(2,1)S(1)}, u32[]{:S(2)}, u32[]{:S(2)}) collective-permute-start(bf16[384,256]{1,0:T(8,128)(2,1)S(1)} %bitcast.209), channel_id=1, source_target_pairs={{0,4},{2,6},{4,0},{6,2},{1,5},{3,7},{5,1},{7,3},{8,12},{10,14},{12... | collective-permute-start | bytes 589832 | tf_op jit(solution)/shard_map/ppermute | solution.py:476
  33.3 15.6 %collective-permute-start.5 = (bf16[384,256]{1,0:T(8,128)(2,1)S(1)}, bf16[384,256]{1,0:T(8,128)(2,1)S(1)}, u32[]{:S(2)}, u32[]{:S(2)}) collective-permute-start(bf16[384,256]{1,0:T(8,128)(2,1)S(1)} %bitcast.210), channel_id=1, source_target_pairs={{0,6},{2,4},{4,2},{6,0},{1,7},{3,5},{5,3},{7,1},{8,14},{10,12},{12... | collective-permute-start | bytes 589832 | tf_op jit(solution)/shard_map/ppermute | solution.py:476
  49.8 1.4 copy-start.16
  49.8 1.4 copy-start.17
  49.8 1.4 copy-start.18
  49.8 1.4 copy-start.19
  49.8 1.4 copy-start.20
  49.9 3.9 %copy-start.11 = (bf16[1,256,128]{2,1,0:T(8,128)(2,1)S(1)}, bf16[1,256,128]{2,1,0:T(8,128)(2,1)}, u32[]{:S(2)}) copy-start(bf16[1,256,128]{2,1,0:T(8,128)(2,1)} %param.21) | copy-start | bytes 196612
  49.9 5.9 %copy-start.15 = (bf16[1,1024]{1,0:T(2,128)(2,1)S(1)}, bf16[1,1024]{1,0:T(2,128)(2,1)}, u32[]{:S(2)}) copy-start(bf16[1,1024]{1,0:T(2,128)(2,1)} %param.28) | copy-start | bytes 6148
  49.9 9.7 %copy-start.10 = (s32[1,2,1,1024,8]{3,4,2,1,0:T(8,128)S(1)}, s32[1,2,1,1024,8]{3,4,2,1,0:T(8,128)}, u32[]{:S(2)}) copy-start(s32[1,2,1,1024,8]{3,4,2,1,0:T(8,128)} %param.18) | copy-start | bytes 196612
  49.9 10.3 %copy-start.21 = (pred[128]{0:T(512)(128)(4,1)S(1)}, pred[128]{0:T(512)(128)(4,1)}, u32[]{:S(2)}) copy-start(pred[128]{0:T(512)(128)(4,1)} %constant.151.clone.1) | copy-start | bytes 388
  49.9 45.1 %all-gather.14.cloned.1.call-start = ((), (), s32[]{:S(2)}) async-start(), calls=%async_computation.3 | async-start | bytes 3145728 | tf_op jit(solution)/shard_map/all_gather | solution.py:540
  50.7 44.3 %all-gather.16.cloned.1.call-start = ((), (), s32[]{:S(2)}) async-start(), calls=%async_computation.4 | async-start | bytes 3145728 | tf_op jit(solution)/shard_map/all_gather | solution.py:540
  196.8 13.4 %copy-start.14 = (f32[3,8,512]{2,1,0:T(8,128)S(1)}, f32[3,8,512]{2,1,0:T(8,128)}, u32[]{:S(2)}) copy-start(f32[3,8,512]{2,1,0:T(8,128)} %get-tuple-element.55) | copy-start | bytes 147460
  196.8 14.0 %copy-start.4 = (bf16[512,1696]{1,0:T(8,128)(2,1)S(1)}, bf16[512,1696]{1,0:T(8,128)(2,1)}, u32[]{:S(2)}) copy-start(bf16[512,1696]{1,0:T(8,128)(2,1)} %get-tuple-element.53) | copy-start | bytes 5210116
  210.5 0.8 copy-start.13
  212.6 24.2 %all-to-all-start = ((f32[32,1,2704]{2,1,0:T(1,128)}), f32[32,1,2704]{2,1,0:T(1,128)}, u32[]{:S(2)}, u32[]{:S(2)}) async-start(f32[32,1,2704]{2,1,0:T(1,128)} %copy.65), calls=%async_computation | async-start | bytes 720896 | tf_op jit(solution)/shard_map/all_to_all | solution.py:794
  224.2 1.6 copy-start.7
  224.4 2.5 copy-start.5
  226.9 50.9 %collective-permute-start.27 = (bf16[4,4,64,512]{3,2,1,0:T(8,128)(2,1)}, bf16[4,4,64,512]{3,2,1,0:T(8,128)(2,1)}, u32[]{:S(2)}, u32[]{:S(2)}) collective-permute-start(bf16[4,4,64,512]{3,2,1,0:T(8,128)(2,1)} %dynamic-slice_bitcast_fusion), channel_id=1, source_target_pairs={{0,1},{1,0},{2,3},{3,2},{4,5},{5,4},{6,7},{7,6},{8,9},{9,8},{10,11... | collective-permute-start | bytes 3145736 | tf_op jit(solution)/shard_map/ppermute | solution.py:476
  228.0 55.2 %collective-permute-start.20 = (bf16[4,4,16,2048]{3,2,1,0:T(8,128)(2,1)}, bf16[4,4,16,2048]{3,2,1,0:T(8,128)(2,1)}, u32[]{:S(2)}, u32[]{:S(2)}) collective-permute-start(bf16[4,4,16,2048]{3,2,1,0:T(8,128)(2,1)} %dynamic-slice_bitcast_fusion.1), channel_id=1, source_target_pairs={{0,1},{1,0},{2,3},{3,2},{4,5},{5,4},{6,7},{7,6},{8,9},{9,8},{10,11... | collective-permute-start | bytes 3145736 | tf_op jit(solution)/shard_map/ppermute | solution.py:476
  234.1 6.4 %copy-start.3 = (bf16[4,1,64,4,384]{4,3,2,1,0:T(4,128)(2,1)S(1)}, bf16[4,1,64,4,384]{4,3,2,1,0:T(4,128)(2,1)}, u32[]{:S(2)}) copy-start(bf16[4,1,64,4,384]{4,3,2,1,0:T(4,128)(2,1)} %get-tuple-element.102) | copy-start | bytes 2359300
  234.2 6.2 %collective-permute-start.13 = (bf16[4,64,4,384]{3,1,2,0:T(8,128)(2,1)S(1)}, bf16[4,64,4,384]{3,1,2,0:T(8,128)(2,1)}, u32[]{:S(2)}, u32[]{:S(2)}) collective-permute-start(bf16[4,64,4,384]{3,1,2,0:T(8,128)(2,1)S(1)} %bitcast.203), channel_id=1, source_target_pairs={{0,1},{1,0},{2,3},{3,2},{4,5},{5,4},{6,7},{7,6},{8,9},{9,8},{10,11... | collective-permute-start | bytes 2359304 | tf_op jit(solution)/shard_map/ppermute | solution.py:476
  234.4 8.7 %collective-permute-start.6 = (bf16[4,64,4,384]{3,1,2,0:T(8,128)(2,1)S(1)}, bf16[4,64,4,384]{3,1,2,0:T(8,128)(2,1)}, u32[]{:S(2)}, u32[]{:S(2)}) collective-permute-start(bf16[4,64,4,384]{3,1,2,0:T(8,128)(2,1)S(1)} %bitcast.202), channel_id=1, source_target_pairs={{0,1},{1,0},{2,3},{3,2},{4,5},{5,4},{6,7},{7,6},{8,9},{9,8},{10,11... | collective-permute-start | bytes 2359304 | tf_op jit(solution)/shard_map/ppermute | solution.py:476
  238.0 7.4 %copy-start.2 = (bf16[4,1,64,4,384]{4,3,2,1,0:T(4,128)(2,1)S(1)}, bf16[4,1,64,4,384]{4,3,2,1,0:T(4,128)(2,1)}, u32[]{:S(2)}) copy-start(bf16[4,1,64,4,384]{4,3,2,1,0:T(4,128)(2,1)} %get-tuple-element.143) | copy-start | bytes 2359300
  241.9 7.8 %collective-permute-start.14 = (bf16[64,4,384]{2,0,1:T(8,128)(2,1)S(1)}, bf16[64,4,384]{2,0,1:T(8,128)(2,1)S(1)}, u32[]{:S(2)}, u32[]{:S(2)}) collective-permute-start(bf16[64,4,384]{2,0,1:T(8,128)(2,1)S(1)} %get-tuple-element.112), channel_id=1, source_target_pairs={{0,8},{8,0},{16,24},{24,16},{1,9},{9,1},{17,25},{25,17},{2,10},{10... | collective-permute-start | bytes 589832 | tf_op jit(solution)/shard_map/ppermute | solution.py:476
  242.0 11.5 %collective-permute-start.15 = (bf16[64,4,384]{2,0,1:T(8,128)(2,1)S(1)}, bf16[64,4,384]{2,0,1:T(8,128)(2,1)S(1)}, u32[]{:S(2)}, u32[]{:S(2)}) collective-permute-start(bf16[64,4,384]{2,0,1:T(8,128)(2,1)S(1)} %get-tuple-element.114), channel_id=1, source_target_pairs={{0,16},{8,24},{16,0},{24,8},{1,17},{9,25},{17,1},{25,9},{2,18},{10... | collective-permute-start | bytes 589832 | tf_op jit(solution)/shard_map/ppermute | solution.py:476
  243.1 10.8 %collective-permute-start.16 = (bf16[64,4,384]{2,0,1:T(8,128)(2,1)S(1)}, bf16[64,4,384]{2,0,1:T(8,128)(2,1)S(1)}, u32[]{:S(2)}, u32[]{:S(2)}) collective-permute-start(bf16[64,4,384]{2,0,1:T(8,128)(2,1)S(1)} %get-tuple-element.113), channel_id=1, source_target_pairs={{0,24},{8,16},{16,8},{24,0},{1,25},{9,17},{17,9},{25,1},{2,26},{10... | collective-permute-start | bytes 589832 | tf_op jit(solution)/shard_map/ppermute | solution.py:476
  249.7 8.4 %collective-permute-start.7 = (bf16[64,4,384]{2,0,1:T(8,128)(2,1)S(1)}, bf16[64,4,384]{2,0,1:T(8,128)(2,1)S(1)}, u32[]{:S(2)}, u32[]{:S(2)}) collective-permute-start(bf16[64,4,384]{2,0,1:T(8,128)(2,1)S(1)} %get-tuple-element.115), channel_id=1, source_target_pairs={{0,8},{8,0},{16,24},{24,16},{1,9},{9,1},{17,25},{25,17},{2,10},{10... | collective-permute-start | bytes 589832 | tf_op jit(solution)/shard_map/ppermute | solution.py:476
  253.4 9.9 %collective-permute-start.8 = (bf16[64,4,384]{2,0,1:T(8,128)(2,1)S(1)}, bf16[64,4,384]{2,0,1:T(8,128)(2,1)S(1)}, u32[]{:S(2)}, u32[]{:S(2)}) collective-permute-start(bf16[64,4,384]{2,0,1:T(8,128)(2,1)S(1)} %get-tuple-element.117), channel_id=1, source_target_pairs={{0,16},{8,24},{16,0},{24,8},{1,17},{9,25},{17,1},{25,9},{2,18},{10... | collective-permute-start | bytes 589832 | tf_op jit(solution)/shard_map/ppermute | solution.py:476
  253.9 11.0 %collective-permute-start.9 = (bf16[64,4,384]{2,0,1:T(8,128)(2,1)S(1)}, bf16[64,4,384]{2,0,1:T(8,128)(2,1)S(1)}, u32[]{:S(2)}, u32[]{:S(2)}) collective-permute-start(bf16[64,4,384]{2,0,1:T(8,128)(2,1)S(1)} %get-tuple-element.116), channel_id=1, source_target_pairs={{0,24},{8,16},{16,8},{24,0},{1,25},{9,17},{17,9},{25,1},{2,26},{10... | collective-permute-start | bytes 589832 | tf_op jit(solution)/shard_map/ppermute | solution.py:476
  257.3 20.5 %copy-start.8 = (bf16[2048,512]{1,0:T(8,128)(2,1)S(1)}, bf16[2048,512]{1,0:T(8,128)(2,1)}, u32[]{:S(2)}) copy-start(bf16[2048,512]{1,0:T(8,128)(2,1)} %get-tuple-element.59) | copy-start | bytes 6291460
  258.1 8.3 %collective-permute-start.17 = (bf16[64,384]{1,0:T(8,128)(2,1)S(1)}, bf16[64,384]{1,0:T(8,128)(2,1)S(1)}, u32[]{:S(2)}, u32[]{:S(2)}) collective-permute-start(bf16[64,384]{1,0:T(8,128)(2,1)S(1)} %get-tuple-element.124), channel_id=1, source_target_pairs={{0,2},{2,0},{4,6},{6,4},{1,3},{3,1},{5,7},{7,5},{8,10},{10,8},{12,... | collective-permute-start | bytes 147464 | tf_op jit(solution)/shard_map/ppermute | solution.py:476
  263.3 5.6 %collective-permute-start.18 = (bf16[64,384]{1,0:T(8,128)(2,1)S(1)}, bf16[64,384]{1,0:T(8,128)(2,1)S(1)}, u32[]{:S(2)}, u32[]{:S(2)}) collective-permute-start(bf16[64,384]{1,0:T(8,128)(2,1)S(1)} %get-tuple-element.126), channel_id=1, source_target_pairs={{0,4},{2,6},{4,0},{6,2},{1,5},{3,7},{5,1},{7,3},{8,12},{10,14},{12... | collective-permute-start | bytes 147464 | tf_op jit(solution)/shard_map/ppermute | solution.py:476
  264.9 6.2 %collective-permute-start.19 = (bf16[64,384]{1,0:T(8,128)(2,1)S(1)}, bf16[64,384]{1,0:T(8,128)(2,1)S(1)}, u32[]{:S(2)}, u32[]{:S(2)}) collective-permute-start(bf16[64,384]{1,0:T(8,128)(2,1)S(1)} %get-tuple-element.125), channel_id=1, source_target_pairs={{0,6},{2,4},{4,2},{6,0},{1,7},{3,5},{5,3},{7,1},{8,14},{10,12},{12... | collective-permute-start | bytes 147464 | tf_op jit(solution)/shard_map/ppermute | solution.py:476
  266.4 6.9 %collective-permute-start.10 = (bf16[64,384]{1,0:T(8,128)(2,1)S(1)}, bf16[64,384]{1,0:T(8,128)(2,1)S(1)}, u32[]{:S(2)}, u32[]{:S(2)}) collective-permute-start(bf16[64,384]{1,0:T(8,128)(2,1)S(1)} %get-tuple-element.127), channel_id=1, source_target_pairs={{0,2},{2,0},{4,6},{6,4},{1,3},{3,1},{5,7},{7,5},{8,10},{10,8},{12,... | collective-permute-start | bytes 147464 | tf_op jit(solution)/shard_map/ppermute | solution.py:476
  268.9 5.0 %collective-permute-start.11 = (bf16[64,384]{1,0:T(8,128)(2,1)S(1)}, bf16[64,384]{1,0:T(8,128)(2,1)S(1)}, u32[]{:S(2)}, u32[]{:S(2)}) collective-permute-start(bf16[64,384]{1,0:T(8,128)(2,1)S(1)} %get-tuple-element.129), channel_id=1, source_target_pairs={{0,4},{2,6},{4,0},{6,2},{1,5},{3,7},{5,1},{7,3},{8,12},{10,14},{12... | collective-permute-start | bytes 147464 | tf_op jit(solution)/shard_map/ppermute | solution.py:476
  271.0 5.9 %collective-permute-start.12 = (bf16[64,384]{1,0:T(8,128)(2,1)S(1)}, bf16[64,384]{1,0:T(8,128)(2,1)S(1)}, u32[]{:S(2)}, u32[]{:S(2)}) collective-permute-start(bf16[64,384]{1,0:T(8,128)(2,1)S(1)} %get-tuple-element.128), channel_id=1, source_target_pairs={{0,6},{2,4},{4,2},{6,0},{1,7},{3,5},{5,3},{7,1},{8,14},{10,12},{12... | collective-permute-start | bytes 147464 | tf_op jit(solution)/shard_map/ppermute | solution.py:476
  277.8 5.4 %copy-start.6 = (bf16[512,2048]{1,0:T(8,128)(2,1)S(1)}, bf16[512,2048]{1,0:T(8,128)(2,1)}, u32[]{:S(2)}) copy-start(bf16[512,2048]{1,0:T(8,128)(2,1)} %get-tuple-element.58) | copy-start | bytes 6291460
  279.6 9.3 %collective-permute-start.28 = (bf16[4,64,512]{2,1,0:T(8,128)(2,1)S(1)}, bf16[4,64,512]{2,1,0:T(8,128)(2,1)S(1)}, u32[]{:S(2)}, u32[]{:S(2)}) collective-permute-start(bf16[4,64,512]{2,1,0:T(8,128)(2,1)S(1)} %get-tuple-element.106), channel_id=1, source_target_pairs={{0,8},{8,0},{16,24},{24,16},{1,9},{9,1},{17,25},{25,17},{2,10},{10... | collective-permute-start | bytes 786440 | tf_op jit(solution)/shard_map/ppermute | solution.py:476
  280.0 9.8 %collective-permute-start.29 = (bf16[4,64,512]{2,1,0:T(8,128)(2,1)S(1)}, bf16[4,64,512]{2,1,0:T(8,128)(2,1)S(1)}, u32[]{:S(2)}, u32[]{:S(2)}) collective-permute-start(bf16[4,64,512]{2,1,0:T(8,128)(2,1)S(1)} %get-tuple-element.108), channel_id=1, source_target_pairs={{0,16},{8,24},{16,0},{24,8},{1,17},{9,25},{17,1},{25,9},{2,18},{10... | collective-permute-start | bytes 786440 | tf_op jit(solution)/shard_map/ppermute | solution.py:476
  281.1 12.7 %collective-permute-start.30 = (bf16[4,64,512]{2,1,0:T(8,128)(2,1)S(1)}, bf16[4,64,512]{2,1,0:T(8,128)(2,1)S(1)}, u32[]{:S(2)}, u32[]{:S(2)}) collective-permute-start(bf16[4,64,512]{2,1,0:T(8,128)(2,1)S(1)} %get-tuple-element.107), channel_id=1, source_target_pairs={{0,24},{8,16},{16,8},{24,0},{1,25},{9,17},{17,9},{25,1},{2,26},{10... | collective-permute-start | bytes 786440 | tf_op jit(solution)/shard_map/ppermute | solution.py:476
  284.7 12.1 %collective-permute-start.21 = (bf16[4,16,2048]{2,1,0:T(8,128)(2,1)S(1)}, bf16[4,16,2048]{2,1,0:T(8,128)(2,1)S(1)}, u32[]{:S(2)}, u32[]{:S(2)}) collective-permute-start(bf16[4,16,2048]{2,1,0:T(8,128)(2,1)S(1)} %get-tuple-element.109), channel_id=1, source_target_pairs={{0,8},{8,0},{16,24},{24,16},{1,9},{9,1},{17,25},{25,17},{2,10},{10... | collective-permute-start | bytes 786440 | tf_op jit(solution)/shard_map/ppermute | solution.py:476
  285.2 13.3 %collective-permute-start.22 = (bf16[4,16,2048]{2,1,0:T(8,128)(2,1)S(1)}, bf16[4,16,2048]{2,1,0:T(8,128)(2,1)S(1)}, u32[]{:S(2)}, u32[]{:S(2)}) collective-permute-start(bf16[4,16,2048]{2,1,0:T(8,128)(2,1)S(1)} %get-tuple-element.111), channel_id=1, source_target_pairs={{0,16},{8,24},{16,0},{24,8},{1,17},{9,25},{17,1},{25,9},{2,18},{10... | collective-permute-start | bytes 786440 | tf_op jit(solution)/shard_map/ppermute | solution.py:476
  288.9 20.5 %copy-start.1 = (s32[2,32]{1,0:T(2,128)S(1)}, s32[2,32]{1,0:T(2,128)}, u32[]{:S(2)}) copy-start(s32[2,32]{1,0:T(2,128)} %param.17) | copy-start | bytes 772
  288.9 10.5 %collective-permute-start.23 = (bf16[4,16,2048]{2,1,0:T(8,128)(2,1)S(1)}, bf16[4,16,2048]{2,1,0:T(8,128)(2,1)S(1)}, u32[]{:S(2)}, u32[]{:S(2)}) collective-permute-start(bf16[4,16,2048]{2,1,0:T(8,128)(2,1)S(1)} %get-tuple-element.110), channel_id=1, source_target_pairs={{0,24},{8,16},{16,8},{24,0},{1,25},{9,17},{17,9},{25,1},{2,26},{10... | collective-permute-start | bytes 786440 | tf_op jit(solution)/shard_map/ppermute | solution.py:476
  294.1 8.6 %collective-permute-start.31 = (bf16[64,512]{1,0:T(8,128)(2,1)S(1)}, bf16[64,512]{1,0:T(8,128)(2,1)S(1)}, u32[]{:S(2)}, u32[]{:S(2)}) collective-permute-start(bf16[64,512]{1,0:T(8,128)(2,1)S(1)} %get-tuple-element.118), channel_id=1, source_target_pairs={{0,2},{2,0},{4,6},{6,4},{1,3},{3,1},{5,7},{7,5},{8,10},{10,8},{12,... | collective-permute-start | bytes 196616 | tf_op jit(solution)/shard_map/ppermute | solution.py:476
  294.1 9.9 %collective-permute-start.32 = (bf16[64,512]{1,0:T(8,128)(2,1)S(1)}, bf16[64,512]{1,0:T(8,128)(2,1)S(1)}, u32[]{:S(2)}, u32[]{:S(2)}) collective-permute-start(bf16[64,512]{1,0:T(8,128)(2,1)S(1)} %get-tuple-element.120), channel_id=1, source_target_pairs={{0,4},{2,6},{4,0},{6,2},{1,5},{3,7},{5,1},{7,3},{8,12},{10,14},{12... | collective-permute-start | bytes 196616 | tf_op jit(solution)/shard_map/ppermute | solution.py:476
  296.8 7.3 %collective-permute-start.33 = (bf16[64,512]{1,0:T(8,128)(2,1)S(1)}, bf16[64,512]{1,0:T(8,128)(2,1)S(1)}, u32[]{:S(2)}, u32[]{:S(2)}) collective-permute-start(bf16[64,512]{1,0:T(8,128)(2,1)S(1)} %get-tuple-element.119), channel_id=1, source_target_pairs={{0,6},{2,4},{4,2},{6,0},{1,7},{3,5},{5,3},{7,1},{8,14},{10,12},{12... | collective-permute-start | bytes 196616 | tf_op jit(solution)/shard_map/ppermute | solution.py:476
  299.6 5.2 %collective-permute-start.24 = (bf16[16,2048]{1,0:T(8,128)(2,1)S(1)}, bf16[16,2048]{1,0:T(8,128)(2,1)S(1)}, u32[]{:S(2)}, u32[]{:S(2)}) collective-permute-start(bf16[16,2048]{1,0:T(8,128)(2,1)S(1)} %get-tuple-element.121), channel_id=1, source_target_pairs={{0,2},{2,0},{4,6},{6,4},{1,3},{3,1},{5,7},{7,5},{8,10},{10,8},{12,... | collective-permute-start | bytes 196616 | tf_op jit(solution)/shard_map/ppermute | solution.py:476
  299.7 5.2 %collective-permute-start.25 = (bf16[16,2048]{1,0:T(8,128)(2,1)S(1)}, bf16[16,2048]{1,0:T(8,128)(2,1)S(1)}, u32[]{:S(2)}, u32[]{:S(2)}) collective-permute-start(bf16[16,2048]{1,0:T(8,128)(2,1)S(1)} %get-tuple-element.123), channel_id=1, source_target_pairs={{0,4},{2,6},{4,0},{6,2},{1,5},{3,7},{5,1},{7,3},{8,12},{10,14},{12... | collective-permute-start | bytes 196616 | tf_op jit(solution)/shard_map/ppermute | solution.py:476
  302.6 6.1 %collective-permute-start.26 = (bf16[16,2048]{1,0:T(8,128)(2,1)S(1)}, bf16[16,2048]{1,0:T(8,128)(2,1)S(1)}, u32[]{:S(2)}, u32[]{:S(2)}) collective-permute-start(bf16[16,2048]{1,0:T(8,128)(2,1)S(1)} %get-tuple-element.122), channel_id=1, source_target_pairs={{0,6},{2,4},{4,2},{6,0},{1,7},{3,5},{5,3},{7,1},{8,14},{10,12},{12... | collective-permute-start | bytes 196616 | tf_op jit(solution)/shard_map/ppermute | solution.py:476
Sparse Core Ops, SparseCore 0:
  28.8 12.0 all-gather.9
  50.0 11.0 all-gather.11
  62.7 11.7 all-gather.13
  75.9 11.7 all-gather.15

commit v2 on v1

--- a/solution.py
+++ b/solution.py
@@ -66,11 +66,8 @@
     lens,
     x_ref,
     route_ref,
-    gain_ref,
-    shift_ref,
+    vec_ref,
     w_ref,
-    wk_ref,
-    wv_ref,
     hid_ref,
     kaug_ref,
     vaug_ref,
@@ -96,7 +93,7 @@
     rows = picks * span
 
     normed, _ = normalize(x_ref[0, 0].astype(F32))
-    hid = (normed * gain_ref[...] + shift_ref[...]).astype(BF16)
+    hid = (normed * vec_ref[0:1, :] + vec_ref[1:2, :]).astype(BF16)
     hid_ref[0, 0] = hid
     table[...] = dot_nt(w_ref[0], hid[:, :half]) + dot_nt(w_ref[1], hid[:, half:])
     head = experts * width
@@ -107,9 +104,11 @@
     place = block * span + lax.broadcasted_iota(jnp.int32, (span, 2 * width), 0)
     ones = jnp.where(lane < width + 4, 1.0, 0.0)
     cut = jnp.where(place < length, 0.0, NEGATIVE)
-    keys = jnp.where(lane < width, dot_nn(hid, wk_ref[...]), jnp.where(lane == width, cut, ones))
+    both = dot_nt(hid[:, :half], w_ref[0, head : head + 2 * width, :])
+    both = both + dot_nt(hid[:, half:], w_ref[1, head : head + 2 * width, :])
+    keys = jnp.where(lane < width, both, jnp.where(lane == width, cut, ones))
     kaug_ref[0, block] = keys.astype(BF16)
-    vals = jnp.where(lane < width, dot_nn(hid, wv_ref[...]), ones)
+    vals = jnp.where(lane < width, pltpu.roll(both, width, 1), ones)
     vaug_ref[0, block] = vals.astype(BF16)
 
     logits = table[head + 2 * width : head + 2 * width + experts, :]
@@ -168,35 +167,27 @@
 
 def middle_kernel(
     lens,
+    ids,
     x_ref,
     ctx_ref,
     gate_ref,
     slot_ref,
     cot_ref,
     w_ref,
-    gain_ref,
-    shift_ref,
+    vec_ref,
     up_ref,
     up_shift_ref,
     down_ref,
-    down_shift_ref,
     out_ref,
     mid_ref,
     do_ref,
     delta_ref,
     gl_ref,
-    down_grad_ref,
-    up_grad_ref,
-    wo_grad_ref,
     small_ref,
     up_shift_grad_ref,
-    gated,
-    cexp,
-    table,
-    down_acc,
-    up_acc,
-    wo_acc,
+    *rest,
 ):
+    *grad_refs, gated, cexp, table, down_acc, up_acc, wo_acc = rest
     micro = pl.program_id(0)
     block = pl.program_id(1)
     length = lens[micro]
@@ -204,6 +195,7 @@
     experts = slot_ref.shape[2]
     width = ctx_ref.shape[2]
     picks = ctx_ref.shape[3] // span
+    head = experts * width
     half = w_ref.shape[2]
     first = (micro == 0) & (block == 0)
     last = (micro == pl.num_programs(0) - 1) & (block == pl.num_programs(1) - 1)
@@ -237,12 +229,12 @@
         [dot_tn(cexp[...], w_ref[0]), dot_tn(cexp[...], w_ref[1])], 1
     )
     normed, spread = normalize(mixed)
-    hid = (normed * gain_ref[...] + shift_ref[...]).astype(BF16)
+    hid = (normed * vec_ref[2:3, :] + vec_ref[3:4, :]).astype(BF16)
     place = block * span + lax.broadcasted_iota(jnp.int32, (span, 1), 0)
     grad = jnp.where(place < length, cot_ref[0, 0], 0.0)
     grad_b = grad.astype(BF16)
     hid_t = hid.T
-    out = mixed + down_shift_ref[...]
+    out = mixed + vec_ref[4:5, :]
     back = jnp.zeros_like(mixed)
     hidden_units = up_ref.shape[1]
     step = min(hidden_units, 512)
@@ -264,7 +256,7 @@
         up_acc[:, cut] += dot_nn(hid_t, grad_pre_b)
         up_shift_grad_ref[:, cut] += fold_rows(grad_pre, jnp.sum)
     out_ref[0, 0] = out
-    scaled = back * gain_ref[...]
+    scaled = back * vec_ref[2:3, :]
     mid = grad + spread * (
         scaled
         - jnp.mean(scaled, -1, keepdims=True)
@@ -299,9 +291,47 @@
 
     @pl.when(last)
     def _():
-        down_grad_ref[...] = down_acc[...].astype(BF16)
-        up_grad_ref[...] = up_acc[...].astype(BF16)
-        wo_grad_ref[...] = wo_acc[...].astype(BF16)
+        if len(grad_refs) == 3:
+            for ref, total in zip(grad_refs, (down_acc, up_acc, wo_acc)):
+                ref[...] = total[...].astype(BF16)
+            return
+        targets = grad_refs[0].shape[0] * grad_refs[0].shape[1]
+        up_rows = up_acc.shape[0] // (2 * targets)
+        down_rows = down_acc.shape[0] // (2 * targets)
+
+        def pack(ref, to, fro, shared, heads):
+            at = pack_tiles(ref, to, 0, up_acc, shared * up_rows, up_rows, 0, up_acc.shape[1])
+            at = pack_tiles(ref, to, at, down_acc, shared * down_rows, down_rows, 0, down_acc.shape[1])
+            rows, columns = heads_chunk(wo_acc.shape[0], head, ref)
+            pack_tiles(ref, to, at, wo_acc, heads * rows, rows, fro * columns, columns)
+
+        for_targets(ids, grad_refs, pack)
+
+
+def pack_tiles(ref, to, at, total, row, rows, column, columns):
+    row = pl.multiple_of(row, rows)
+    for lane in range(0, columns, 128):
+        tile = total[pl.ds(row, rows), column + lane : column + lane + 128]
+        ref[to[0], to[1], at : at + rows, :] = tile.astype(BF16)
+        at += rows
+    return at
+
+
+def heads_chunk(model, head, ref):
+    return model // (2 * ref.shape[0]), head // ref.shape[1]
+
+
+def for_targets(ids, refs, pack):
+    def body(dp_far, carry):
+        dp = dp_far ^ ids[0]
+        for z_far in range(refs[0].shape[1]):
+            for f_far in range(2):
+                f = ids[2] ^ f_far
+                shared = (dp * refs[0].shape[1] + (z_far ^ ids[1])) * 2 + f
+                pack(refs[f_far], (dp_far, z_far), z_far, shared, dp * 2 + f)
+        return carry
+
+    lax.fori_loop(0, refs[0].shape[0], body, 0)
 
 
 def split_three(values):
@@ -313,6 +343,7 @@
 
 def backward_kernel(
     lens,
+    ids,
     hid_ref,
     kaug_ref,
     vaug_ref,
@@ -323,15 +354,11 @@
     delta_ref,
     slot_ref,
     gl_ref,
+    order_ref,
     r_ref,
-    w_grad_ref,
-    qaug,
-    daug,
-    dq,
-    dkt,
-    dvt,
-    w_acc,
+    *rest,
 ):
+    *grad_refs, qaug, daug, dq, dkt, dvt, w_acc = rest
     micro = pl.program_id(0)
     step = pl.program_id(1)
     blocks = pl.num_programs(1)
@@ -409,14 +436,30 @@
         r_ref[0, 0, head + 2 * width :, :] = jnp.concatenate(
             [gl_ref[0, 0], jnp.zeros((tail - experts, span), F32)], 0
         ).astype(BF16)
-        w_acc[...] += dot_nt(hid_ref[0, 0].T, r_ref[0, 0])
+        w_acc[:, : r_ref.shape[2]] += dot_nt(hid_ref[0, 0].T, r_ref[0, 0])
 
     @pl.when((micro == pl.num_programs(0) - 1) & (step == blocks - 1))
     def _():
-        w_grad_ref[...] = w_acc[...].astype(BF16)
-
-
-def input_kernel(x_ref, mid_ref, r_ref, w_ref, gain_ref, out_ref, small_ref):
+        if len(grad_refs) == 1:
+            grad_refs[0][...] = w_acc[:, : r_ref.shape[2]].astype(BF16)
+            return
+        routed = head + 2 * width
+        spare = order_ref.shape[0]
+        w_acc[:, routed:] = dot_nn(
+            w_acc[:, routed : routed + spare].astype(BF16), order_ref[...]
+        )
+        targets = grad_refs[0].shape[0] * grad_refs[0].shape[1]
+        shared_rows = w_acc.shape[0] // (2 * targets)
+
+        def pack(ref, to, fro, shared, heads):
+            rows, columns = heads_chunk(w_acc.shape[0], head, ref)
+            at = pack_tiles(ref, to, 0, w_acc, heads * rows, rows, fro * columns, columns)
+            pack_tiles(ref, to, at, w_acc, shared * shared_rows, shared_rows, head, w_acc.shape[1] - head)
+
+        for_targets(ids, grad_refs, pack)
+
+
+def input_kernel(x_ref, mid_ref, r_ref, w_ref, vec_ref, out_ref, small_ref):
     first = (pl.program_id(0) == 0) & (pl.program_id(1) == 0)
 
     @pl.when(first)
@@ -427,7 +470,7 @@
         [dot_tn(r_ref[0, 0], w_ref[0]), dot_tn(r_ref[0, 0], w_ref[1])], 1
     )
     normed, spread = normalize(x_ref[0, 0].astype(F32))
-    scaled = back * gain_ref[...]
+    scaled = back * vec_ref[0:1, :]
     out_ref[0, 0] = mid_ref[0, 0] + spread * (
         scaled
         - jnp.mean(scaled, -1, keepdims=True)
@@ -499,6 +542,48 @@
         sent = pick_at(value, distance if relative else me ^ distance, dim)
         total = total + exchange(sent, axis, distance).astype(F32)
     return total if keep else total.astype(BF16)
+
+
+def core_stage(grads):
+    keep, send = grads
+    other = exchange(send, "fsdp", 1)
+    return [(keep[at].astype(F32) + other[at].astype(F32)).astype(BF16) for at in range(keep.shape[0])]
+
+
+def split_targets(value, axis):
+    return [value[at] for at in range(lax.axis_size(axis))]
+
+
+def send_stage(parts, axis):
+    return [exchange(parts[distance], axis, distance) for distance in range(1, len(parts))]
+
+
+def total_up(own, received):
+    total = own.astype(F32)
+    for part in received:
+        total = total + part.astype(F32)
+    return total
+
+
+def add_up(own, received):
+    return total_up(own, received).astype(BF16)
+
+
+def open_tiles(value, at, rows, columns):
+    count = columns // 128
+    tiles = value[at : at + count * rows].reshape(count, rows, 128)
+    return jnp.swapaxes(tiles, 0, 1).reshape(rows, columns), at + count * rows
+
+
+def sum_packed(parts, devices):
+    packed = jnp.concatenate(parts, 1)
+    packed = lax.all_to_all(packed, AXES, split_axis=0, concat_axis=0, tiled=True)
+    packed = jnp.sum(packed.reshape(devices, -1), 0)
+    result, at = [], 0
+    for part in parts:
+        result.append(packed[at : at + part.shape[1]])
+        at += part.shape[1]
+    return result
 
 
 def local(
@@ -525,8 +610,10 @@
     picks = routes.shape[4]
     hidden_units = up_weight.shape[2]
     dp_size, z_size, f_size = (lax.axis_size(axis) for axis in AXES)
-    z_at = lax.axis_index("expert")
-    seq_index = (lax.axis_index("dp") * z_size + z_at) * f_size + lax.axis_index("fsdp")
+    dp_at, z_at, f_at = (lax.axis_index(axis) for axis in AXES)
+    ids = jnp.stack([dp_at, z_at, f_at]).astype(jnp.int32)
+    seq_index = (dp_at * z_size + z_at) * f_size + f_at
+    devices = dp_size * z_size * f_size
     own_experts = experts // z_size
     half = model // f_size
     span = min(BLOCK, slots)
@@ -535,34 +622,37 @@
     head = experts * width
     spare = -(-experts // 16) * 16
     all_rows = head + 2 * width + spare
-
-    def gather(value, dim):
-        return lax.all_gather(value, "fsdp", axis=dim, tiled=True)
-
+    chunk = model // devices
+    aligned = chunk % 16 == 0 and (head // z_size) % 128 == 0
     lens = lax.dynamic_index_in_dim(lengths, seq_index, 1, keepdims=False)
 
-    def transposed_heads(weight):
-        own = jnp.swapaxes(weight[0], 1, 2).reshape(own_experts * width, half)
+    def both_halves(own, other, dim):
+        near = jnp.concatenate([own, other], dim)
+        return jnp.where(f_at == 0, near, jnp.concatenate([other, own], dim))
+
+    def head_parts(own):
         return [own] + [exchange(own, "expert", distance) for distance in range(1, z_size)]
 
-    query_parts = transposed_heads(query_weight)
-    out_parts = transposed_heads(out_weight)
+    def transposed(weight):
+        return jnp.swapaxes(weight[0], 1, 2).reshape(own_experts * width, half)
+
+    query_parts = head_parts(transposed(query_weight))
     router_t = router_weight[0].T.reshape(z_size, own_experts, half)
     router_t = permute_groups(router_t, z_at).reshape(experts, half)
     router_t = jnp.pad(router_t, ((0, spare - experts), (0, 0)))
-    proj = lax.all_gather(
-        jnp.concatenate(query_parts + [kv_weight[0].T, router_t], 0), "fsdp", axis=0
-    )
-    out_proj = lax.all_gather(jnp.concatenate(out_parts, 0), "fsdp", axis=0)
-    kv_full = gather(kv_weight[0], 0)
-    key_weight = jnp.pad(kv_full[:, :width], ((0, 0), (0, width)))
-    value_weight = jnp.pad(kv_full[:, width:], ((0, 0), (0, width)))
-    gains = gather(jnp.concatenate([ln1_gain, ln1_bias, ln2_gain, ln2_bias, down_bias], 0), 1)
-    gains = gains.astype(F32)
-    gain1, shift1, gain2, shift2, down_shift = (gains[at : at + 1] for at in range(5))
-    up_shift = gather(up_bias, 1).astype(F32)
-    up_full = gather(up_weight[0], 0)
-    down_full = gather(down_weight[0], 0)
+    proj = jnp.concatenate(query_parts + [kv_weight[0].T, router_t], 0)
+    proj_other = exchange(proj, "fsdp", 1)
+    proj = both_halves(proj[None], proj_other[None], 0)
+    vectors = jnp.concatenate([ln1_gain, ln1_bias, ln2_gain, ln2_bias, down_bias], 0)
+    small = jnp.concatenate([vectors, up_bias.reshape(-1, half)], 0)
+    small_other = exchange(small, "fsdp", 1)
+    vectors = both_halves(vectors, small_other[:5], 1).astype(F32)
+    up_shift = both_halves(up_bias, small_other[5:].reshape(1, -1), 1).astype(F32)
+
+    own_out, proj = lax.optimization_barrier((transposed(out_weight), proj))
+    out_parts = head_parts(own_out)
+    up_full = lax.all_gather(up_weight[0], "fsdp", axis=0, tiled=True)
+    down_full = lax.all_gather(down_weight[0], "fsdp", axis=0, tiled=True)
 
     local_routes = routes[0, :, 0]
     local_routes = ((local_routes // own_experts) ^ z_at) * own_experts + local_routes % own_experts
@@ -589,11 +679,8 @@
             in_specs=[
                 blocked(states.shape),
                 blocked(route_t.shape),
-                full(gain1.shape),
-                full(shift1.shape),
+                full(vectors.shape),
                 full(proj.shape),
-                full(key_weight.shape),
-                full(value_weight.shape),
             ],
             out_specs=[
                 blocked(hid_s.shape),
@@ -616,91 +703,107 @@
         ),
         out_shape=[hid_s, aug_s, aug_s, kt_s, q_s, q_s, row_s, gate_s, slot_s],
         compiler_params=params(),
-        cost_estimate=cost(2 * tokens * model * all_rows + 8 * pair_flops, 0, 8 << 20),
-    )(lens, states, route_t, gain1, shift1, proj, key_weight, value_weight)
-
+        cost_estimate=cost(2 * tokens * model * all_rows + 16 * pair_flops, 0, 64 << 20),
+    )(lens, states, route_t, vectors, proj)
+
+    ctx, up_full, down_full, *out_parts = lax.optimization_barrier(
+        (ctx, up_full, down_full, *out_parts)
+    )
+    out_proj = jnp.concatenate(out_parts, 0)[None]
+    out_proj = both_halves(out_proj, exchange(out_proj, "fsdp", 1), 0)
     state_s = struct((micro_count, blocks, span, model), F32)
-    outputs, mid, grad_ctx, delta, grad_logits, down_grad, up_grad, wo_grad, small2, up_small = (
-        pl.pallas_call(
-            middle_kernel,
-            name="middle",
-            grid_spec=pltpu.PrefetchScalarGridSpec(
-                num_scalar_prefetch=1,
-                grid=grid,
-                in_specs=[
-                    blocked(states.shape),
-                    blocked(q_s.shape),
-                    blocked(gate_s.shape),
-                    blocked(slot_s.shape),
-                    blocked(cotangent.shape),
-                    full(out_proj.shape),
-                    full(gain2.shape),
-                    full(shift2.shape),
-                    full(up_full.shape),
-                    full(up_shift.shape),
-                    full(down_full.shape),
-                    full(down_shift.shape),
-                ],
-                out_specs=[
-                    blocked(state_s.shape),
-                    blocked(state_s.shape),
-                    blocked(q_s.shape),
-                    blocked(row_s.shape),
-                    blocked(gate_s.shape),
-                    full((hidden_units, model)),
-                    full((model, hidden_units)),
-                    full((model, head)),
-                    full((3, 8, model)),
-                    full((8, hidden_units)),
-                ],
-                scratch_shapes=[
-                    pltpu.VMEM((width, rows), F32),
-                    pltpu.VMEM((head, span), BF16),
-                    pltpu.VMEM((head, span), F32),
-                    pltpu.VMEM((hidden_units, model), F32),
-                    pltpu.VMEM((model, hidden_units), F32),
-                    pltpu.VMEM((model, head), F32),
-                ],
-            ),
-            out_shape=[
-                state_s,
-                state_s,
-                q_s,
-                row_s,
-                gate_s,
-                struct((hidden_units, model), BF16),
-                struct((model, hidden_units), BF16),
-                struct((model, head), BF16),
-                struct((3, 8, model), F32),
-                struct((8, hidden_units), F32),
+    mid_rows = chunk * hidden_units * 2 // 128 + head // z_size * (chunk * z_size) // 128
+    late_rows = head // z_size * (chunk * z_size) // 128 + 2 * chunk
+    if aligned:
+        mid_grads = [struct((dp_size, z_size, mid_rows, 128), BF16)] * 2
+        late_grads = [struct((dp_size, z_size, late_rows, 128), BF16)] * 2
+    else:
+        mid_grads = [
+            struct((hidden_units, model), BF16),
+            struct((model, hidden_units), BF16),
+            struct((model, head), BF16),
+        ]
+        late_grads = [struct((model, all_rows), BF16)]
+    outputs, mid, grad_ctx, delta, grad_logits, small2, up_small, *mid_grads = pl.pallas_call(
+        middle_kernel,
+        name="middle",
+        grid_spec=pltpu.PrefetchScalarGridSpec(
+            num_scalar_prefetch=2,
+            grid=grid,
+            in_specs=[
+                blocked(states.shape),
+                blocked(q_s.shape),
+                blocked(gate_s.shape),
+                blocked(slot_s.shape),
+                blocked(cotangent.shape),
+                full(out_proj.shape),
+                full(vectors.shape),
+                full(up_full.shape),
+                full(up_shift.shape),
+                full(down_full.shape),
             ],
-            compiler_params=params(),
-            cost_estimate=cost(
-                2 * tokens * model * (6 * hidden_units + 3 * head), 0, 24 << 20
-            ),
-        )(
-            lens,
-            states,
-            ctx,
-            gates,
-            slot,
-            cotangent,
-            out_proj,
-            gain2,
-            shift2,
-            up_full,
-            up_shift,
-            down_full,
-            down_shift,
-        )
-    )
-
+            out_specs=[
+                blocked(state_s.shape),
+                blocked(state_s.shape),
+                blocked(q_s.shape),
+                blocked(row_s.shape),
+                blocked(gate_s.shape),
+                full((3, 8, model)),
+                full((8, hidden_units)),
+            ]
+            + [full(leaf.shape) for leaf in mid_grads],
+            scratch_shapes=[
+                pltpu.VMEM((width, rows), F32),
+                pltpu.VMEM((head, span), BF16),
+                pltpu.VMEM((head, span), F32),
+                pltpu.VMEM((hidden_units, model), F32),
+                pltpu.VMEM((model, hidden_units), F32),
+                pltpu.VMEM((model, head), F32),
+            ],
+        ),
+        out_shape=[
+            state_s,
+            state_s,
+            q_s,
+            row_s,
+            gate_s,
+            struct((3, 8, model), F32),
+            struct((8, hidden_units), F32),
+        ]
+        + mid_grads,
+        compiler_params=params(),
+        cost_estimate=cost(2 * tokens * model * (6 * hidden_units + 3 * head), 0, 200 << 20),
+    )(
+        lens,
+        ids,
+        states,
+        ctx,
+        gates,
+        slot,
+        cotangent,
+        out_proj,
+        vectors,
+        up_full,
+        up_shift,
+        down_full,
+    )
+
+    if aligned:
+        mid_sums = core_stage(mid_grads)
+        grad_ctx, *mid_sums = lax.optimization_barrier((grad_ctx, *mid_sums))
+        mid_received = send_stage(mid_sums, "dp")
+
+    expert_id = jnp.arange(experts)
+    moved = ((expert_id // own_experts) ^ z_at) * own_experts + expert_id % own_experts
+    order = jnp.pad(
+        (jnp.arange(spare)[:, None] == moved[None, :]).astype(BF16), ((0, 0), (0, 128 - experts))
+    )
     r_s = struct((micro_count, blocks, all_rows, span), BF16)
-    routed, w_grad = pl.pallas_call(
+    routed, *late_grads = pl.pallas_call(
         backward_kernel,
         name="backward",
         grid_spec=pltpu.PrefetchScalarGridSpec(
-            num_scalar_prefetch=1,
+            num_scalar_prefetch=2,
             grid=grid,
             in_specs=[
                 reversed_blocks(hid_s.shape),
@@ -713,22 +816,24 @@
                 reversed_blocks(row_s.shape),
                 reversed_blocks(slot_s.shape),
                 reversed_blocks(gate_s.shape),
+                full(order.shape),
             ],
-            out_specs=[reversed_blocks(r_s.shape), full((model, all_rows))],
+            out_specs=[reversed_blocks(r_s.shape)] + [full(leaf.shape) for leaf in late_grads],
             scratch_shapes=[
                 pltpu.VMEM((2 * width, rows), BF16),
                 pltpu.VMEM((2 * width, rows), BF16),
                 pltpu.VMEM((width, rows), F32),
                 pltpu.VMEM((blocks, width, span), F32),
                 pltpu.VMEM((blocks, width, span), F32),
-                pltpu.VMEM((model, all_rows), F32),
+                pltpu.VMEM((model, head + 2 * width + 128), F32),
             ],
         ),
-        out_shape=[r_s, struct((model, all_rows), BF16)],
+        out_shape=[r_s] + late_grads,
         compiler_params=params(),
-        cost_estimate=cost(2 * tokens * model * all_rows + 20 * pair_flops, 0, 24 << 20),
+        cost_estimate=cost(2 * tokens * model * all_rows + 40 * pair_flops, 0, 100 << 20),
     )(
         lens,
+        ids,
         hid,
         kaug,
         vaug,
@@ -739,7 +844,18 @@
         delta,
         slot,
         grad_logits,
-    )
+        order,
+    )
+
+    if aligned:
+        *mid_received, late_grads[0], late_grads[1] = lax.optimization_barrier(
+            (*mid_received, *late_grads)
+        )
+        late_sums = core_stage(late_grads)
+        mid_sums = split_targets(add_up(mid_sums[0], mid_received), "expert")
+        routed, *late_sums = lax.optimization_barrier((routed, *late_sums))
+        late_received = send_stage(late_sums, "dp")
+        mid_received = send_stage(mid_sums, "expert")
 
     input_grad, small1 = pl.pallas_call(
         input_kernel,
@@ -752,67 +868,85 @@
                 blocked(state_s.shape),
                 blocked(r_s.shape),
                 full(proj.shape),
-                full(gain1.shape),
+                full(vectors.shape),
             ],
             out_specs=[blocked(state_s.shape), full((2, 8, model))],
         ),
         out_shape=[state_s, struct((2, 8, model), F32)],
         compiler_params=params(),
-        cost_estimate=cost(2 * tokens * model * all_rows, 0, 20 << 20),
-    )(states, mid, routed, proj, gain1)
-
-    def reduce_shared(value, chunk):
-        value = value.reshape(dp_size, z_size, f_size, chunk, value.shape[1])
-        value = reduce_axis(value, "fsdp", 2)
-        value = reduce_axis(value, "dp", 0)
-        return reduce_axis(value, "expert", 0, keep=True)
-
-    def reduce_heads(value):
-        chunk = model // (dp_size * f_size)
-        value = value.reshape(dp_size, f_size, chunk, z_size, own_experts * width)
-        value = reduce_axis(value, "fsdp", 1)
-        value = reduce_axis(value, "dp", 0)
-        value = reduce_axis(value, "expert", 1, relative=True, keep=True)
-        return jnp.swapaxes(value.reshape(chunk, own_experts, width), 0, 1)[None]
-
-    devices = dp_size * z_size * f_size
-    up_weight_grad = reduce_shared(up_grad, model // devices)
-    down_weight_grad = reduce_shared(down_grad, hidden_units // devices)
-    out_weight_grad = reduce_heads(wo_grad)
-    query_weight_grad = reduce_heads(w_grad[:, :head])
-
-    chunk = model // devices
-    router_grad = w_grad[:, head + 2 * width : head + 2 * width + experts].astype(F32)
-    router_grad = permute_groups(router_grad.T.reshape(z_size, own_experts, model), z_at)
-    router_grad = jnp.pad(router_grad.reshape(experts, model).T, ((0, 0), (0, spare - experts)))
-    narrow = jnp.concatenate([w_grad[:, head : head + 2 * width].astype(F32), router_grad], 1)
-    narrow = narrow.reshape(devices, chunk * (2 * width + spare))
-    vectors = jnp.concatenate([jnp.sum(small1, 1), jnp.sum(small2, 1)], 0)
-    vectors = jnp.swapaxes(vectors.reshape(5, devices, chunk), 0, 1).reshape(devices, 5 * chunk)
-    up_vector = jnp.sum(up_small, 0).reshape(devices, hidden_units // devices)
-    packed = jnp.concatenate([narrow, vectors, up_vector], 1)
-    packed = lax.all_to_all(packed, AXES, split_axis=0, concat_axis=0, tiled=True)
-    packed = jnp.sum(packed.reshape(devices, -1), 0)
-    cut = chunk * (2 * width + spare)
-    narrow = packed[:cut].reshape(chunk, 2 * width + spare)
-    vectors = packed[cut : cut + 5 * chunk].reshape(5, 1, chunk)
-    up_vector = packed[cut + 5 * chunk :][None]
+        cost_estimate=cost(2 * tokens * model * all_rows, 0, 40 << 20),
+    )(states, mid, routed, proj, vectors)
+
+    if aligned:
+        small1, *received = lax.optimization_barrier((small1, *late_received, *mid_received))
+        late_received = received[: dp_size - 1]
+        mid_received = received[dp_size - 1 :]
+    small = jnp.concatenate([jnp.sum(small1, 1), jnp.sum(small2, 1)], 0)
+    small = jnp.swapaxes(small.reshape(5, devices, chunk), 0, 1).reshape(devices, 5 * chunk)
+    up_small = jnp.sum(up_small, 0).reshape(devices, hidden_units // devices)
+    packed = [small, up_small]
+
+    def open_heads(value):
+        return jnp.swapaxes(value.reshape(-1, own_experts, width), 0, 1)[None]
+
+    if aligned:
+        late_sums = split_targets(add_up(late_sums[0], late_received), "expert")
+        late_received = send_stage(late_sums, "expert")
+        mid_total = total_up(mid_sums[0], mid_received)
+        up_weight_grad, at = open_tiles(mid_total, 0, chunk, hidden_units)
+        down_weight_grad, at = open_tiles(mid_total, at, hidden_units // devices, model)
+        out_weight_grad, at = open_tiles(mid_total, at, chunk * z_size, head // z_size)
+        packed = sum_packed(packed, devices)
+        late_total = total_up(late_sums[0], late_received)
+        query_weight_grad, at = open_tiles(late_total, 0, chunk * z_size, head // z_size)
+        kv_grad = late_total[at : at + chunk]
+        router_grad = late_total[at + chunk : at + 2 * chunk, :experts]
+        query_weight_grad, out_weight_grad = map(open_heads, (query_weight_grad, out_weight_grad))
+    else:
+        down_grad, up_grad, wo_grad = mid_grads
+        w_grad = late_grads[0]
+
+        def reduce_shared(value, part):
+            value = value.reshape(dp_size, z_size, f_size, part, value.shape[1])
+            value = reduce_axis(value, "fsdp", 2)
+            value = reduce_axis(value, "dp", 0)
+            return reduce_axis(value, "expert", 0, keep=True)
+
+        def reduce_heads(value):
+            value = value.reshape(dp_size, f_size, chunk * z_size, z_size, own_experts * width)
+            value = reduce_axis(value, "fsdp", 1)
+            value = reduce_axis(value, "dp", 0)
+            return open_heads(reduce_axis(value, "expert", 1, relative=True, keep=True))
+
+        up_weight_grad = reduce_shared(up_grad, chunk)
+        down_weight_grad = reduce_shared(down_grad, hidden_units // devices)
+        out_weight_grad = reduce_heads(wo_grad)
+        query_weight_grad = reduce_heads(w_grad[:, :head])
+        router_grad = w_grad[:, head + 2 * width : head + 2 * width + experts].astype(F32)
+        router_grad = permute_groups(router_grad.T.reshape(z_size, own_experts, model), z_at)
+        router_grad = router_grad.reshape(experts, model).T
+        kv_grad = w_grad[:, head : head + 2 * width].astype(F32)
+        packed += [kv_grad.reshape(devices, -1), router_grad.reshape(devices, -1)]
+        packed = sum_packed(packed, devices)
+        kv_grad = packed[2].reshape(chunk, 2 * width)
+        router_grad = packed[3].reshape(chunk, experts)
+    small = packed[0].reshape(5, 1, chunk)
     shape = (micro_count, 1, slots, model)
     return (
         outputs.reshape(shape),
         input_grad.reshape(shape),
-        vectors[0],
-        vectors[1],
-        narrow[None, :, : 2 * width],
-        narrow[None, :, 2 * width : 2 * width + experts],
+        small[0],
+        small[1],
+        kv_grad[None],
+        router_grad[None],
         query_weight_grad,
         out_weight_grad,
-        vectors[2],
-        vectors[3],
+        small[2],
+        small[3],
         up_weight_grad[None],
-        up_vector,
+        packed[1][None],
         down_weight_grad[None],
-        vectors[4],
+        small[4],
     )
 
 

time: 317 us -> 246 us (0.78)
  waiting for transfers between devices: 59.3 us -> 22.7 us
  starting transfers between devices: 52 us -> 36.5 us
  local copies, waits for them, and re-layouts: 22.8 us -> 10.8 us
  blocking collectives: 5.48 us -> 0 us
    ppermute x34 -> x23, waiting for transfers between devices: 56.2 us -> 21.8 us  [exchange(): lax.ppermute(value, axis, [(at, at ^ distance) for at in range(count)])]
    all_to_all x1, starting transfers between devices: 11.5 us -> 3.23 us  [sum_packed(): lax.all_to_all(packed, AXES, split_axis=0, concat_axis=0, tiled=True)]
    ppermute x34 -> x23, starting transfers between devices: 40.3 us -> 33.2 us  [exchange(): lax.ppermute(value, axis, [(at, at ^ distance) for at in range(count)])]
    all_gather x3 -> x0, blocking collectives: 5.48 us -> none  [gather(): return lax.all_gather(value, 'fsdp', axis=dim, tiled=True)]
    reshape x10 -> x6, local copies, waits for them, and re-layouts: 4.12 us -> 0.49 us  [the longest x2 0.25 us: open_tiles(): tiles = value[at:at + count * rows].reshape(count, rows, 128)]
    convert_element_type x10 -> x6, other arithmetic: 7.9 us -> 6.59 us  [the longest x2 3.67 us: core_stage(): (keep[at].astype(F32) + other[at].astype(F32)).astype(BF16)]
  transfers between devices with their start and end apart: 39 -> 26, of which waited for: 19 -> 8; matrix products, arithmetic and copies ran while one was open for 9% -> 6% of each run, Pallas kernels for 11% -> 34%
where the time goes in v2:
time: 246 us; the launch traced here: 243 us
  Pallas kernels  146 us (59%)
  starting transfers between devices  36.5 us (15%)
  waiting for transfers between devices  22.7 us (9%)
  between operations  14.7 us (6%)
  other arithmetic  12.6 us (5%)
  local copies, waits for them, and re-layouts  10.8 us (4%)
    pallas_call x1, Pallas kernels, local(): pl.pallas_call(middle_kernel, name='middle', grid_spec=pltpu.PrefetchScal...  62.1 us
    pallas_call x1, Pallas kernels, local(): pl.pallas_call(backward_kernel, name='backward', grid_spec=pltpu.Prefetch...  37.6 us
    pallas_call x1, Pallas kernels, local(): pl.pallas_call(forward_kernel, name='forward', grid_spec=pltpu.PrefetchSc...  33.5 us
    ppermute x23, starting transfers between devices, exchange(): lax.ppermute(value, axis, [(at, at ^ distance) for at in range(count)])  33.2 us
    ppermute x23, waiting for transfers between devices, exchange(): lax.ppermute(value, axis, [(at, at ^ distance) for at in range(count)])  21.8 us
    pallas_call x1, Pallas kernels, local(): pl.pallas_call(input_kernel, name='input_back', grid_spec=pltpu.PrefetchS...  12.4 us
  transfers between devices with their start and end apart: 26, of which 8 were waited for; matrix products, arithmetic and copies ran while one was open for 6% of the time, Pallas kernels for 34%

profile of v2, /device:TPU:0, one launch (start us, length us, event | category | flops | bytes accessed | tf_op | source)
XLA Modules:
  0.0 242.8 jit_solution(5714250317524598320)
XLA Ops:
  7.3 0.7 all-gather.5.cloned.1.call-update
  8.0 3.1 %collective-permute-start.1 = (bf16[384,256]{1,0:T(8,128)(2,1)}, bf16[384,256]{1,0:T(8,128)(2,1)S(1)}, u32[]{:S(2)}, u32[]{:S(2)}) collective-permute-start(bf16[384,256]{1,0:T(8,128)(2,1)} %bitcast.145), channel_id=1, source_target_pairs={{0,2},{2,0},{4,6},{6,4},{1,3},{3,1},{5,7},{7,5},{8,10},{10,8},{12,... | collective-permute-start | bytes 589832 | tf_op jit(solution)/shard_map/ppermute | solution.py:519
  11.1 2.6 %collective-permute-start.2 = (bf16[384,256]{1,0:T(8,128)(2,1)}, bf16[384,256]{1,0:T(8,128)(2,1)S(1)}, u32[]{:S(2)}, u32[]{:S(2)}) collective-permute-start(bf16[384,256]{1,0:T(8,128)(2,1)} %bitcast.146), channel_id=1, source_target_pairs={{0,4},{2,6},{4,0},{6,2},{1,5},{3,7},{5,1},{7,3},{8,12},{10,14},{12... | collective-permute-start | bytes 589832 | tf_op jit(solution)/shard_map/ppermute | solution.py:519
  13.7 0.7 reshape_reshape.9
  14.5 0.7 reshape.253
  15.3 0.7 select_select_fusion
  16.0 0.9 copy.56
  17.0 2.7 %collective-permute-done.1 = bf16[384,256]{1,0:T(8,128)(2,1)S(1)} collective-permute-done((bf16[384,256]{1,0:T(8,128)(2,1)}, bf16[384,256]{1,0:T(8,128)(2,1)S(1)}, u32[]{:S(2)}, u32[]{:S(2)}) %collective-permute-start.1) | collective-permute-done | bytes 196640 | tf_op jit(solution)/shard_map/ppermute | solution.py:519
  19.7 8.8 %collective-permute-done.2 = bf16[384,256]{1,0:T(8,128)(2,1)S(1)} collective-permute-done((bf16[384,256]{1,0:T(8,128)(2,1)}, bf16[384,256]{1,0:T(8,128)(2,1)S(1)}, u32[]{:S(2)}, u32[]{:S(2)}) %collective-permute-start.2) | collective-permute-done | bytes 196640 | tf_op jit(solution)/shard_map/ppermute | solution.py:519
  28.8 0.1 concatenate.62
  28.9 0.5 collective-permute-start
  29.5 0.7 fusion.15.route_ref
  30.3 0.7 dynamic-slice_reduce_fusion.lens
  31.0 0.1 collective-permute-done
  31.1 0.6 fusion.17.vec_ref
  31.7 1.5 maximum_select_fusion.w_ref
  33.2 3.3 %collective-permute-start.5 = (bf16[384,256]{1,0:T(8,128)(2,1)S(1)}, bf16[384,256]{1,0:T(8,128)(2,1)S(1)}, u32[]{:S(2)}, u32[]{:S(2)}) collective-permute-start(bf16[384,256]{1,0:T(8,128)(2,1)S(1)} %bitcast.141), channel_id=1, source_target_pairs={{0,2},{2,0},{4,6},{6,4},{1,3},{3,1},{5,7},{7,5},{8,10},{10,8},{12,... | collective-permute-start | bytes 589832 | tf_op jit(solution)/shard_map/ppermute | solution.py:519
  36.5 1.0 collective-permute-start.6
  37.5 1.5 collective-permute-start.7
  39.0 33.5 %forward.1 = (bf16[2,4,256,512]{3,2,1,0:T(8,128)(2,1)}, bf16[2,4,256,128]{3,2,1,0:T(8,128)(2,1)}, bf16[2,4,256,128]{3,2,1,0:T(8,128)(2,1)}, bf16[2,4,1,64,256]{4...) custom-call(s32[2]{0:T(128)} %dynamic-slice_reduce_fusion.lens, ...), custom_call_target="tpu_custom_call" | custom-call | flops 20736638976 | bytes 67108864 | tf_op jit(solution)/shard_map/forward/pallas_call | solution.py:673
  72.7 0.6 pad_add_fusion.ids
  73.3 0.6 fusion.16.up_shift_ref
  73.9 1.1 collective-permute-done.8
  75.0 1.4 maximum_select_fusion.1.w_ref
  76.4 62.1 %middle.1 = (f32[2,4,256,512]{3,2,1,0:T(8,128)}, f32[2,4,256,512]{3,2,1,0:T(8,128)}, bf16[2,4,64,2048]{3,2,1,0:T(8,128)(2,1)}, f32[2,4,1,2048]{3,2,1,0:T(1,128)}...) custom-call(s32[2]{0:T(128)} %dynamic-slice_reduce_fusion.lens, ...), custom_call_target="tpu_custom_call" | custom-call | flops 35433480192 | bytes 209715200 | tf_op jit(solution)/shard_map/middle/pallas_call | solution.py:727
  138.5 0.2 collective-permute-start.9
  138.7 0.6 pad_convert_fusion.order_ref
  139.3 4.8 %collective-permute-done.9 = bf16[4,4,704,128]{3,2,1,0:T(8,128)(2,1)S(1)} collective-permute-done((bf16[4,4,704,128]{3,2,1,0:T(8,128)(2,1)}, bf16[4,4,704,128]{3,2,1,0:T(8,128)(2,1)S(1)}, u32[]{:S(2)}, u32[]{:S(2)}) %collective-permute-start.9) | collective-permute-done | bytes 2883616 | tf_op jit(solution)/shard_map/ppermute | solution.py:519
  144.1 3.4 %fusion.3 = (bf16[4,704,128]{2,1,0:T(8,128)(2,1)S(1)}, bf16[4,704,128]{2,1,0:T(8,128)(2,1)S(1)}, bf16[4,704,128]{2,1,0:T(8,128)(2,1)}, bf16[4,704,128]{2,1,0:T(8,128)(2,1)S(1)}) fusion(bf16[4,4,704,128]{3,2,1,0:T(8,128)(2,1)S(1)} %collective-permute-done.9, bf16[4,4,704,128]{3,2,1,0:T(8,128)(2,1)} %get-tuple-element.89), kind=kLoop, calls=%fused_computation.11 | loop fusion | flops 5767168 | bytes 8650752 | tf_op jit(solution)/shard_map/convert_element_type | solution.py:550
  147.5 1.5 collective-permute-start.10
  149.0 0.6 collective-permute-start.11
  149.7 1.4 collective-permute-start.12
  151.0 37.6 %backward.1 = (bf16[2,4,1696,256]{3,2,1,0:T(8,128)(2,1)}, bf16[4,4,224,128]{3,2,1,0:T(8,128)(2,1)}, bf16[4,4,224,128]{3,2,1,0:T(8,128)(2,1)}) custom-call(s32[2]{0:T(128)} %dynamic-slice_reduce_fusion.lens, s32[3]{0:T(128)} %pad_add_fusion.ids, bf16[2,4,256,512]{3,2,1,0:T(8,128)(2,1)} %get-tuple-element.82.hid_ref, ...), custom_call_target="tpu_custom_call" | custom-call | flops 46506442752 | bytes 104857600 | tf_op jit(solution)/shard_map/backward/pallas_call | solution.py:802
  188.8 1.6 add_convert_fusion
  190.5 0.9 collective-permute-start.17
  191.4 3.5 %collective-permute-start.19 = (bf16[704,128]{1,0:T(8,128)(2,1)S(1)}, bf16[704,128]{1,0:T(8,128)(2,1)S(1)}, u32[]{:S(2)}, u32[]{:S(2)}) collective-permute-start(bf16[704,128]{1,0:T(8,128)(2,1)S(1)} %get-tuple-element.186), channel_id=1, source_target_pairs={{0,6},{2,4},{4,2},{6,0},{1,7},{3,5},{5,3},{7,1},{8,14},{10,12},{12... | collective-permute-start | bytes 540680 | tf_op jit(solution)/shard_map/ppermute | solution.py:519
  194.9 0.2 fusion.9
  195.2 6.9 %collective-permute-start.14 = (bf16[4,224,128]{2,1,0:T(8,128)(2,1)S(1)}, bf16[4,224,128]{2,1,0:T(8,128)(2,1)S(1)}, u32[]{:S(2)}, u32[]{:S(2)}) collective-permute-start(bf16[4,224,128]{2,1,0:T(8,128)(2,1)S(1)} %get-tuple-element.105), channel_id=1, source_target_pairs={{0,8},{8,0},{16,24},{24,16},{1,9},{9,1},{17,25},{25,17},{2,10},{10... | collective-permute-start | bytes 688136 | tf_op jit(solution)/shard_map/ppermute | solution.py:519
  202.1 1.5 collective-permute-start.16
  203.6 12.4 %input_back.1 = (f32[2,4,256,512]{3,2,1,0:T(8,128)}, f32[2,8,512]{2,1,0:T(8,128)}) custom-call(bf16[2,4,256,512]{3,2,1,0:T(8,128)(2,1)} %bitcast.129, f32[2,4,256,512]{3,2,1,0:T(8,128)} %get-tuple-element.81.mid_ref, bf16[2,4,1696,256]{3,2,1,0:T(8,128)(2,1)} %get-tuple-element.102.r_ref, bf16[2,1696,256]{2,1,0:T(8,128)(2,1)} %maximum_select_fusion.w_ref, ...), custom_call_target="tpu_custom_call" | custom-call | flops 3556769792 | bytes 41943040 | tf_op jit(solution)/shard_map/input_back/pallas_call | solution.py:860
  216.1 0.1 fusion.5
  216.2 0.6 copy-done.8
  216.8 0.1 reshape.260
  217.0 0.1 pad_maximum_fusion
  217.1 0.6 all_to_all.6
  217.8 3.2 %all-to-all-start = ((f32[32,1,144]{2,1,0:T(1,128)}), f32[32,1,144]{2,1,0:T(1,128)S(1)}, u32[]{:S(2)}, u32[]{:S(2)}) async-start(f32[32,1,144]{2,1,0:T(1,128)} %all_to_all.6), calls=%async_computation | async-start | bytes 65536 | tf_op jit(solution)/shard_map/all_to_all | solution.py:580
  221.0 0.1 add_convert_fusion.5
  221.3 0.7 broadcast_in_dim_reshape.6
  221.9 0.1 copy.62
  222.0 0.7 broadcast_in_dim_reshape.7
  222.7 0.1 copy.60
  222.9 0.8 copy.66
  223.7 1.8 collective-permute-start.20
  225.4 2.4 collective-permute-start.21
  227.8 0.2 collective-permute-start.22
  228.1 0.2 all-to-all-done
  228.3 0.6 slice_bitcast_fusion.11
  228.9 0.6 slice_bitcast_fusion.12
  229.5 2.4 collective-permute-done.21
  231.9 2.0 collective-permute-done.22
  233.9 0.6 slice_bitcast_fusion.8
  234.5 0.6 slice_bitcast_fusion.9
  235.1 0.1 copy.59
  235.2 0.8 copy.65
  (93 shorter events, 1.3 us)
Async XLA Ops:
  7.2 23.1 %copy-start = (s32[2,32]{1,0:T(2,128)S(1)}, s32[2,32]{1,0:T(2,128)}, u32[]{:S(2)}) copy-start(s32[2,32]{1,0:T(2,128)} %param.17) | copy-start | bytes 772
  7.2 9.7 %copy-start.5 = (bf16[1,6,256,64]{2,3,1,0:T(8,128)(2,1)S(1)}, bf16[1,6,256,64]{2,3,1,0:T(8,128)(2,1)}, u32[]{:S(2)}) copy-start(bf16[1,6,256,64]{2,3,1,0:T(8,128)(2,1)} %param.23) | copy-start | bytes 589828
  7.2 21.5 %copy-start.9 = (bf16[1,1024]{1,0:T(2,128)(2,1)S(1)}, bf16[1,1024]{1,0:T(2,128)(2,1)}, u32[]{:S(2)}) copy-start(bf16[1,1024]{1,0:T(2,128)(2,1)} %param.28) | copy-start | bytes 6148
  7.2 21.5 %copy-start.10 = (bf16[1,256]{1,0:T(2,128)(2,1)S(1)}, bf16[1,256]{1,0:T(2,128)(2,1)}, u32[]{:S(2)}) copy-start(bf16[1,256]{1,0:T(2,128)(2,1)} %param.19) | copy-start | bytes 1540
  7.2 21.5 %copy-start.11 = (bf16[1,256]{1,0:T(2,128)(2,1)S(1)}, bf16[1,256]{1,0:T(2,128)(2,1)}, u32[]{:S(2)}) copy-start(bf16[1,256]{1,0:T(2,128)(2,1)} %param.20) | copy-start | bytes 1540
  7.2 21.5 %copy-start.12 = (bf16[1,256]{1,0:T(2,128)(2,1)S(1)}, bf16[1,256]{1,0:T(2,128)(2,1)}, u32[]{:S(2)}) copy-start(bf16[1,256]{1,0:T(2,128)(2,1)} %param.25) | copy-start | bytes 1540
  7.2 21.5 %copy-start.13 = (bf16[1,256]{1,0:T(2,128)(2,1)S(1)}, bf16[1,256]{1,0:T(2,128)(2,1)}, u32[]{:S(2)}) copy-start(bf16[1,256]{1,0:T(2,128)(2,1)} %param.26) | copy-start | bytes 1540
  7.3 21.5 %copy-start.14 = (bf16[1,256]{1,0:T(2,128)(2,1)S(1)}, bf16[1,256]{1,0:T(2,128)(2,1)}, u32[]{:S(2)}) copy-start(bf16[1,256]{1,0:T(2,128)(2,1)} %param.30) | copy-start | bytes 1540
  7.3 65.3 %all-gather.5.cloned.1.call-start = ((), (), s32[]{:S(2)}) async-start(), calls=%async_computation.1 | async-start | bytes 3145728 | tf_op jit(solution)/shard_map/all_gather | solution.py:654
  8.0 64.6 %all-gather.7.cloned.1.call-start = ((), (), s32[]{:S(2)}) async-start(), calls=%async_computation.2 | async-start | bytes 3145728 | tf_op jit(solution)/shard_map/all_gather | solution.py:655
  8.0 11.6 %collective-permute-start.1 = (bf16[384,256]{1,0:T(8,128)(2,1)}, bf16[384,256]{1,0:T(8,128)(2,1)S(1)}, u32[]{:S(2)}, u32[]{:S(2)}) collective-permute-start(bf16[384,256]{1,0:T(8,128)(2,1)} %bitcast.145), channel_id=1, source_target_pairs={{0,2},{2,0},{4,6},{6,4},{1,3},{3,1},{5,7},{7,5},{8,10},{10,8},{12,... | collective-permute-start | bytes 589832 | tf_op jit(solution)/shard_map/ppermute | solution.py:519
  11.1 17.4 %collective-permute-start.2 = (bf16[384,256]{1,0:T(8,128)(2,1)}, bf16[384,256]{1,0:T(8,128)(2,1)S(1)}, u32[]{:S(2)}, u32[]{:S(2)}) collective-permute-start(bf16[384,256]{1,0:T(8,128)(2,1)} %bitcast.146), channel_id=1, source_target_pairs={{0,4},{2,6},{4,0},{6,2},{1,5},{3,7},{5,1},{7,3},{8,12},{10,14},{12... | collective-permute-start | bytes 589832 | tf_op jit(solution)/shard_map/ppermute | solution.py:519
  13.7 14.8 %collective-permute-start.3 = (bf16[384,256]{1,0:T(8,128)(2,1)}, bf16[384,256]{1,0:T(8,128)(2,1)S(1)}, u32[]{:S(2)}, u32[]{:S(2)}) collective-permute-start(bf16[384,256]{1,0:T(8,128)(2,1)} %bitcast.147), channel_id=1, source_target_pairs={{0,6},{2,4},{4,2},{6,0},{1,7},{3,5},{5,3},{7,1},{8,14},{10,12},{12... | collective-permute-start | bytes 589832 | tf_op jit(solution)/shard_map/ppermute | solution.py:519
  15.2 14.3 %copy-start.3 = (s32[1,2,1,1024,8]{3,4,2,1,0:T(8,128)S(1)}, s32[1,2,1,1024,8]{3,4,2,1,0:T(8,128)}, u32[]{:S(2)}) copy-start(s32[1,2,1,1024,8]{3,4,2,1,0:T(8,128)} %param.18) | copy-start | bytes 196612
  28.6 3.1 %collective-permute-start.4 = (bf16[1696,256]{1,0:T(8,128)(2,1)S(1)}, bf16[1696,256]{1,0:T(8,128)(2,1)S(1)}, u32[]{:S(2)}, u32[]{:S(2)}) collective-permute-start(bf16[1696,256]{1,0:T(8,128)(2,1)S(1)} %pad_dynamic-update-slice_fusion), channel_id=1, source_target_pairs={{0,1},{1,0},{2,3},{3,2},{4,5},{5,4},{6,7},{7,6},{8,9},{9,8},{10,11... | collective-permute-start | bytes 2605064 | tf_op jit(solution)/shard_map/ppermute | solution.py:519
  28.9 2.2 collective-permute-start
  31.7 1.5 copy-start.4
  33.2 39.3 %collective-permute-start.5 = (bf16[384,256]{1,0:T(8,128)(2,1)S(1)}, bf16[384,256]{1,0:T(8,128)(2,1)S(1)}, u32[]{:S(2)}, u32[]{:S(2)}) collective-permute-start(bf16[384,256]{1,0:T(8,128)(2,1)S(1)} %bitcast.141), channel_id=1, source_target_pairs={{0,2},{2,0},{4,6},{6,4},{1,3},{3,1},{5,7},{7,5},{8,10},{10,8},{12,... | collective-permute-start | bytes 589832 | tf_op jit(solution)/shard_map/ppermute | solution.py:519
  36.5 36.0 %collective-permute-start.6 = (bf16[384,256]{1,0:T(8,128)(2,1)S(1)}, bf16[384,256]{1,0:T(8,128)(2,1)S(1)}, u32[]{:S(2)}, u32[]{:S(2)}) collective-permute-start(bf16[384,256]{1,0:T(8,128)(2,1)S(1)} %bitcast.142), channel_id=1, source_target_pairs={{0,4},{2,6},{4,0},{6,2},{1,5},{3,7},{5,1},{7,3},{8,12},{10,14},{12... | collective-permute-start | bytes 589832 | tf_op jit(solution)/shard_map/ppermute | solution.py:519
  37.5 35.0 %collective-permute-start.7 = (bf16[384,256]{1,0:T(8,128)(2,1)S(1)}, bf16[384,256]{1,0:T(8,128)(2,1)S(1)}, u32[]{:S(2)}, u32[]{:S(2)}) collective-permute-start(bf16[384,256]{1,0:T(8,128)(2,1)S(1)} %bitcast.143), channel_id=1, source_target_pairs={{0,6},{2,4},{4,2},{6,0},{1,7},{3,5},{5,3},{7,1},{8,14},{10,12},{12... | collective-permute-start | bytes 589832 | tf_op jit(solution)/shard_map/ppermute | solution.py:519
  72.6 2.4 collective-permute-start.8
  138.5 5.6 %collective-permute-start.9 = (bf16[4,4,704,128]{3,2,1,0:T(8,128)(2,1)}, bf16[4,4,704,128]{3,2,1,0:T(8,128)(2,1)S(1)}, u32[]{:S(2)}, u32[]{:S(2)}) collective-permute-start(bf16[4,4,704,128]{3,2,1,0:T(8,128)(2,1)} %get-tuple-element.90), channel_id=1, source_target_pairs={{0,1},{1,0},{2,3},{3,2},{4,5},{5,4},{6,7},{7,6},{8,9},{9,8},{10,11... | collective-permute-start | bytes 8650760 | tf_op jit(solution)/shard_map/ppermute | solution.py:519
  147.5 41.1 %collective-permute-start.10 = (bf16[4,704,128]{2,1,0:T(8,128)(2,1)}, bf16[4,704,128]{2,1,0:T(8,128)(2,1)S(1)}, u32[]{:S(2)}, u32[]{:S(2)}) collective-permute-start(bf16[4,704,128]{2,1,0:T(8,128)(2,1)} %get-tuple-element.95), channel_id=1, source_target_pairs={{0,8},{8,0},{16,24},{24,16},{1,9},{9,1},{17,25},{25,17},{2,10},{10... | collective-permute-start | bytes 2162696 | tf_op jit(solution)/shard_map/ppermute | solution.py:519
  149.0 39.6 %collective-permute-start.11 = (bf16[4,704,128]{2,1,0:T(8,128)(2,1)S(1)}, bf16[4,704,128]{2,1,0:T(8,128)(2,1)S(1)}, u32[]{:S(2)}, u32[]{:S(2)}) collective-permute-start(bf16[4,704,128]{2,1,0:T(8,128)(2,1)S(1)} %get-tuple-element.96), channel_id=1, source_target_pairs={{0,16},{8,24},{16,0},{24,8},{1,17},{9,25},{17,1},{25,9},{2,18},{10... | collective-permute-start | bytes 2162696 | tf_op jit(solution)/shard_map/ppermute | solution.py:519
  149.7 39.0 %collective-permute-start.12 = (bf16[4,704,128]{2,1,0:T(8,128)(2,1)S(1)}, bf16[4,704,128]{2,1,0:T(8,128)(2,1)}, u32[]{:S(2)}, u32[]{:S(2)}) collective-permute-start(bf16[4,704,128]{2,1,0:T(8,128)(2,1)S(1)} %get-tuple-element.97), channel_id=1, source_target_pairs={{0,24},{8,16},{16,8},{24,0},{1,25},{9,17},{17,9},{25,1},{2,26},{10... | collective-permute-start | bytes 2162696 | tf_op jit(solution)/shard_map/ppermute | solution.py:519
  151.0 37.7 %copy-start.7 = (f32[3,8,512]{2,1,0:T(8,128)S(1)}, f32[3,8,512]{2,1,0:T(8,128)}, u32[]{:S(2)}) copy-start(f32[3,8,512]{2,1,0:T(8,128)} %get-tuple-element.113) | copy-start | bytes 147460
  151.0 37.7 %copy-start.6 = (f32[8,2048]{1,0:T(8,128)S(1)}, f32[8,2048]{1,0:T(8,128)}, u32[]{:S(2)}) copy-start(f32[8,2048]{1,0:T(8,128)} %get-tuple-element.114) | copy-start | bytes 196612
  188.6 6.3 %collective-permute-start.13 = (bf16[4,4,224,128]{3,2,1,0:T(8,128)(2,1)}, bf16[4,4,224,128]{3,2,1,0:T(8,128)(2,1)S(1)}, u32[]{:S(2)}, u32[]{:S(2)}) collective-permute-start(bf16[4,4,224,128]{3,2,1,0:T(8,128)(2,1)} %get-tuple-element.101), channel_id=1, source_target_pairs={{0,1},{1,0},{2,3},{3,2},{4,5},{5,4},{6,7},{7,6},{8,9},{9,8},{10,11... | collective-permute-start | bytes 2752520 | tf_op jit(solution)/shard_map/ppermute | solution.py:519
  188.8 6.1 %copy-start.2 = (bf16[4,4,224,128]{3,2,1,0:T(8,128)(2,1)S(1)}, bf16[4,4,224,128]{3,2,1,0:T(8,128)(2,1)}, u32[]{:S(2)}) copy-start(bf16[4,4,224,128]{3,2,1,0:T(8,128)(2,1)} %get-tuple-element.100) | copy-start | bytes 2752516
  190.5 11.6 %collective-permute-start.17 = (bf16[704,128]{1,0:T(8,128)(2,1)S(1)}, bf16[704,128]{1,0:T(8,128)(2,1)S(1)}, u32[]{:S(2)}, u32[]{:S(2)}) collective-permute-start(bf16[704,128]{1,0:T(8,128)(2,1)S(1)} %get-tuple-element.188), channel_id=1, source_target_pairs={{0,2},{2,0},{4,6},{6,4},{1,3},{3,1},{5,7},{7,5},{8,10},{10,8},{12,... | collective-permute-start | bytes 540680 | tf_op jit(solution)/shard_map/ppermute | solution.py:519
  191.4 24.6 %collective-permute-start.18 = (bf16[704,128]{1,0:T(8,128)(2,1)S(1)}, bf16[704,128]{1,0:T(8,128)(2,1)S(1)}, u32[]{:S(2)}, u32[]{:S(2)}) collective-permute-start(bf16[704,128]{1,0:T(8,128)(2,1)S(1)} %get-tuple-element.187), channel_id=1, source_target_pairs={{0,4},{2,6},{4,0},{6,2},{1,5},{3,7},{5,1},{7,3},{8,12},{10,14},{12... | collective-permute-start | bytes 540680 | tf_op jit(solution)/shard_map/ppermute | solution.py:519
  191.4 24.6 %collective-permute-start.19 = (bf16[704,128]{1,0:T(8,128)(2,1)S(1)}, bf16[704,128]{1,0:T(8,128)(2,1)S(1)}, u32[]{:S(2)}, u32[]{:S(2)}) collective-permute-start(bf16[704,128]{1,0:T(8,128)(2,1)S(1)} %get-tuple-element.186), channel_id=1, source_target_pairs={{0,6},{2,4},{4,2},{6,0},{1,7},{3,5},{5,3},{7,1},{8,14},{10,12},{12... | collective-permute-start | bytes 540680 | tf_op jit(solution)/shard_map/ppermute | solution.py:519
  195.2 20.9 %collective-permute-start.14 = (bf16[4,224,128]{2,1,0:T(8,128)(2,1)S(1)}, bf16[4,224,128]{2,1,0:T(8,128)(2,1)S(1)}, u32[]{:S(2)}, u32[]{:S(2)}) collective-permute-start(bf16[4,224,128]{2,1,0:T(8,128)(2,1)S(1)} %get-tuple-element.105), channel_id=1, source_target_pairs={{0,8},{8,0},{16,24},{24,16},{1,9},{9,1},{17,25},{25,17},{2,10},{10... | collective-permute-start | bytes 688136 | tf_op jit(solution)/shard_map/ppermute | solution.py:519
  202.1 14.0 %collective-permute-start.15 = (bf16[4,224,128]{2,1,0:T(8,128)(2,1)S(1)}, bf16[4,224,128]{2,1,0:T(8,128)(2,1)S(1)}, u32[]{:S(2)}, u32[]{:S(2)}) collective-permute-start(bf16[4,224,128]{2,1,0:T(8,128)(2,1)S(1)} %get-tuple-element.106), channel_id=1, source_target_pairs={{0,16},{8,24},{16,0},{24,8},{1,17},{9,25},{17,1},{25,9},{2,18},{10... | collective-permute-start | bytes 688136 | tf_op jit(solution)/shard_map/ppermute | solution.py:519
  202.1 14.0 %collective-permute-start.16 = (bf16[4,224,128]{2,1,0:T(8,128)(2,1)S(1)}, bf16[4,224,128]{2,1,0:T(8,128)(2,1)S(1)}, u32[]{:S(2)}, u32[]{:S(2)}) collective-permute-start(bf16[4,224,128]{2,1,0:T(8,128)(2,1)S(1)} %get-tuple-element.107), channel_id=1, source_target_pairs={{0,24},{8,16},{16,8},{24,0},{1,25},{9,17},{17,9},{25,1},{2,26},{10... | collective-permute-start | bytes 688136 | tf_op jit(solution)/shard_map/ppermute | solution.py:519
  216.0 0.8 copy-start.8
  217.8 10.5 %all-to-all-start = ((f32[32,1,144]{2,1,0:T(1,128)}), f32[32,1,144]{2,1,0:T(1,128)S(1)}, u32[]{:S(2)}, u32[]{:S(2)}) async-start(f32[32,1,144]{2,1,0:T(1,128)} %all_to_all.6), calls=%async_computation | async-start | bytes 65536 | tf_op jit(solution)/shard_map/all_to_all | solution.py:580
  221.2 14.8 %copy-start.1 = (s32[2,32]{1,0:T(2,128)S(1)}, s32[2,32]{1,0:T(2,128)}, u32[]{:S(2)}) copy-start(s32[2,32]{1,0:T(2,128)} %param.17) | copy-start | bytes 772
  223.7 5.8 %collective-permute-start.20 = (bf16[224,128]{1,0:T(8,128)(2,1)S(1)}, bf16[224,128]{1,0:T(8,128)(2,1)S(1)}, u32[]{:S(2)}, u32[]{:S(2)}) collective-permute-start(bf16[224,128]{1,0:T(8,128)(2,1)S(1)} %get-tuple-element.191), channel_id=1, source_target_pairs={{0,2},{2,0},{4,6},{6,4},{1,3},{3,1},{5,7},{7,5},{8,10},{10,8},{12,... | collective-permute-start | bytes 172040 | tf_op jit(solution)/shard_map/ppermute | solution.py:519
  225.4 6.4 %collective-permute-start.21 = (bf16[224,128]{1,0:T(8,128)(2,1)S(1)}, bf16[224,128]{1,0:T(8,128)(2,1)S(1)}, u32[]{:S(2)}, u32[]{:S(2)}) collective-permute-start(bf16[224,128]{1,0:T(8,128)(2,1)S(1)} %get-tuple-element.193), channel_id=1, source_target_pairs={{0,4},{2,6},{4,0},{6,2},{1,5},{3,7},{5,1},{7,3},{8,12},{10,14},{12... | collective-permute-start | bytes 172040 | tf_op jit(solution)/shard_map/ppermute | solution.py:519
  227.8 6.0 %collective-permute-start.22 = (bf16[224,128]{1,0:T(8,128)(2,1)S(1)}, bf16[224,128]{1,0:T(8,128)(2,1)S(1)}, u32[]{:S(2)}, u32[]{:S(2)}) collective-permute-start(bf16[224,128]{1,0:T(8,128)(2,1)S(1)} %get-tuple-element.192), channel_id=1, source_target_pairs={{0,6},{2,4},{4,2},{6,0},{1,7},{3,5},{5,3},{7,1},{8,14},{10,12},{12... | collective-permute-start | bytes 172040 | tf_op jit(solution)/shard_map/ppermute | solution.py:519
Sparse Core Ops, SparseCore 0:
  9.6 13.2 all-gather.4
  29.6 12.5 all-gather.6

commit v3 on v2

--- a/solution.py
+++ b/solution.py
@@ -36,19 +36,25 @@
     return center * spread, spread
 
 
+def halves(ref):
+    rows = ref.shape[0] // 2
+    return ref.at[pl.ds(0, rows)], ref.at[pl.ds(rows, rows)]
+
+
 def fold_rows(values, combine):
     rows, columns = values.shape
     return combine(values.reshape(rows // 8, 8, columns), 0)
 
 
-def pick_slots(table_ref, slot, picks, width, span):
-    experts = slot.shape[0]
+def pick_slots(table_ref, slot, picks, width, start=0):
+    experts, span = slot.shape
+    lanes = slice(start, start + span)
     picked = []
     for pick in range(picks):
-        value = table_ref[pick * width : (pick + 1) * width, :]
+        value = table_ref[pick * width : (pick + 1) * width, lanes]
         for expert in range(pick + 1, experts - picks + pick + 1):
             hit = jnp.broadcast_to(slot[expert : expert + 1, :], (width, span)) == pick
-            value = jnp.where(hit, table_ref[expert * width : (expert + 1) * width, :], value)
+            value = jnp.where(hit, table_ref[expert * width : (expert + 1) * width, lanes], value)
         picked.append(value)
     return picked
 
@@ -64,10 +70,12 @@
 
 def forward_kernel(
     lens,
+    ids,
     x_ref,
     route_ref,
     vec_ref,
-    w_ref,
+    own_ref,
+    other_ref,
     hid_ref,
     kaug_ref,
     vaug_ref,
@@ -82,20 +90,25 @@
     scores,
     vt,
     acc,
+    w_ref,
+    sems,
 ):
     block = pl.program_id(1)
     length = lens[pl.program_id(0)]
+    first = (pl.program_id(0) == 0) & (block == 0)
+    load_halves(first, ids[2], sems, [(own_ref, other_ref, w_ref)])
     span = x_ref.shape[2]
     experts = slot_ref.shape[2]
     picks = route_ref.shape[2]
     width = kt_ref.shape[3]
-    half = w_ref.shape[2]
+    half = w_ref.shape[1]
+    low, high = halves(w_ref)
     rows = picks * span
 
     normed, _ = normalize(x_ref[0, 0].astype(F32))
     hid = (normed * vec_ref[0:1, :] + vec_ref[1:2, :]).astype(BF16)
     hid_ref[0, 0] = hid
-    table[...] = dot_nt(w_ref[0], hid[:, :half]) + dot_nt(w_ref[1], hid[:, half:])
+    table[...] = dot_nt(low[...], hid[:, :half]) + dot_nt(high[...], hid[:, half:])
     head = experts * width
     kt_ref[0, 0, 0] = table[head : head + width, :].astype(BF16)
     vt[block] = table[head + width : head + 2 * width, :].astype(BF16)
@@ -104,8 +117,8 @@
     place = block * span + lax.broadcasted_iota(jnp.int32, (span, 2 * width), 0)
     ones = jnp.where(lane < width + 4, 1.0, 0.0)
     cut = jnp.where(place < length, 0.0, NEGATIVE)
-    both = dot_nt(hid[:, :half], w_ref[0, head : head + 2 * width, :])
-    both = both + dot_nt(hid[:, half:], w_ref[1, head : head + 2 * width, :])
+    both = dot_nt(hid[:, :half], low[head : head + 2 * width, :])
+    both = both + dot_nt(hid[:, half:], high[head : head + 2 * width, :])
     keys = jnp.where(lane < width, both, jnp.where(lane == width, cut, ones))
     kaug_ref[0, block] = keys.astype(BF16)
     vals = jnp.where(lane < width, pltpu.roll(both, width, 1), ones)
@@ -128,7 +141,7 @@
     raised = jnp.where(chosen > 0.0, jnp.exp(masked - jnp.max(masked, 0, keepdims=True)), 0.0)
     gate_ref[0, 0] = raised / jnp.sum(raised, 0, keepdims=True)
 
-    picked = pick_slots(table, slot, picks, width, span)
+    picked = pick_slots(table, slot, picks, width)
     for pick in range(picks):
         qaug[0:width, pick * span : (pick + 1) * span] = (
             picked[pick].astype(BF16) * (width**-0.5)
@@ -173,11 +186,14 @@
     gate_ref,
     slot_ref,
     cot_ref,
-    w_ref,
+    own_ref,
+    other_ref,
     vec_ref,
-    up_ref,
+    own_up_ref,
+    other_up_ref,
     up_shift_ref,
-    down_ref,
+    own_down_ref,
+    other_down_ref,
     out_ref,
     mid_ref,
     do_ref,
@@ -187,107 +203,139 @@
     up_shift_grad_ref,
     *rest,
 ):
-    *grad_refs, gated, cexp, table, down_acc, up_acc, wo_acc = rest
+    *grad_refs, gated, cexp, table, down_acc, up_acc, wo_acc, w_ref, up_ref, down_ref, sems = rest
     micro = pl.program_id(0)
     block = pl.program_id(1)
     length = lens[micro]
-    span = x_ref.shape[2]
+    subs, span, model = x_ref.shape[1:]
+    tokens = subs * span
     experts = slot_ref.shape[2]
     width = ctx_ref.shape[2]
     picks = ctx_ref.shape[3] // span
     head = experts * width
-    half = w_ref.shape[2]
+    half = w_ref.shape[1]
+    low, high = halves(w_ref)
     first = (micro == 0) & (block == 0)
     last = (micro == pl.num_programs(0) - 1) & (block == pl.num_programs(1) - 1)
 
-    @pl.when(first)
-    def _():
+    def clear():
         down_acc[...] = jnp.zeros_like(down_acc)
         up_acc[...] = jnp.zeros_like(up_acc)
         wo_acc[...] = jnp.zeros_like(wo_acc)
         small_ref[...] = jnp.zeros_like(small_ref)
         up_shift_grad_ref[...] = jnp.zeros_like(up_shift_grad_ref)
 
-    slot = slot_ref[0, 0]
-    gates = gate_ref[0, 0]
-    gate = [
-        jnp.sum(jnp.where(slot == pick, gates, 0.0), 0, keepdims=True) for pick in range(picks)
-    ]
-    for pick in range(picks):
-        at = slice(pick * span, (pick + 1) * span)
-        gated[:, at] = ctx_ref[0, 0, :, at].astype(F32) * gate[pick]
-    for expert in range(experts):
-        cexp[expert * width : (expert + 1) * width, :] = spread_slots(
-            lambda pick: gated[:, pick * span : (pick + 1) * span],
-            slot,
-            expert,
-            picks,
-            width,
-            span,
-        ).astype(BF16)
-    mixed = x_ref[0, 0].astype(F32) + jnp.concatenate(
-        [dot_tn(cexp[...], w_ref[0]), dot_tn(cexp[...], w_ref[1])], 1
+    load_halves(
+        first,
+        ids[2],
+        sems,
+        [
+            (own_ref, other_ref, w_ref),
+            (own_up_ref, other_up_ref, up_ref),
+            (own_down_ref, other_down_ref, down_ref),
+        ],
+        clear,
+    )
+    slots = [slot_ref[0, sub] for sub in range(subs)]
+    gate = []
+    for sub in range(subs):
+        gates = gate_ref[0, sub]
+        gate.append(
+            [
+                jnp.sum(jnp.where(slots[sub] == pick, gates, 0.0), 0, keepdims=True)
+                for pick in range(picks)
+            ]
+        )
+        for pick in range(picks):
+            at = slice(pick * span, (pick + 1) * span)
+            gated[sub, :, at] = ctx_ref[0, sub, :, at].astype(F32) * gate[sub][pick]
+        for expert in range(experts):
+            cexp[expert * width : (expert + 1) * width, sub * span : (sub + 1) * span] = spread_slots(
+                lambda pick: gated[sub, :, pick * span : (pick + 1) * span],
+                slots[sub],
+                expert,
+                picks,
+                width,
+                span,
+            ).astype(BF16)
+    mixed = x_ref[0].reshape(tokens, model).astype(F32) + jnp.concatenate(
+        [dot_tn(cexp[...], low[...]), dot_tn(cexp[...], high[...])], 1
     )
     normed, spread = normalize(mixed)
     hid = (normed * vec_ref[2:3, :] + vec_ref[3:4, :]).astype(BF16)
-    place = block * span + lax.broadcasted_iota(jnp.int32, (span, 1), 0)
-    grad = jnp.where(place < length, cot_ref[0, 0], 0.0)
+    place = block * tokens + lax.broadcasted_iota(jnp.int32, (tokens, 1), 0)
+    grad = jnp.where(place < length, cot_ref[0].reshape(tokens, model), 0.0)
     grad_b = grad.astype(BF16)
     hid_t = hid.T
     out = mixed + vec_ref[4:5, :]
     back = jnp.zeros_like(mixed)
     hidden_units = up_ref.shape[1]
-    step = min(hidden_units, 512)
-    for at in range(0, hidden_units, step):
-        cut = slice(at, at + step)
-        pre = dot_nn(hid, up_ref[:, cut]) + up_shift_ref[:, cut]
-        square = pre * pre
-        bent = jnp.tanh(pre * (GELU_SCALE + (GELU_SCALE * GELU_CUBIC) * square))
-        rise = 0.5 + 0.5 * bent
-        active = (pre * rise).astype(BF16)
-        slope = rise + (0.5 * pre) * (1.0 - bent * bent) * (
-            GELU_SCALE + (3.0 * GELU_SCALE * GELU_CUBIC) * square
-        )
-        grad_pre = dot_nt(grad_b, down_ref[cut, :]) * slope
-        grad_pre_b = grad_pre.astype(BF16)
-        out = out + dot_nn(active, down_ref[cut, :])
-        back = back + dot_nt(grad_pre_b, up_ref[:, cut])
-        down_acc[cut, :] += dot_nn(active.T, grad_b)
-        up_acc[:, cut] += dot_nn(hid_t, grad_pre_b)
-        up_shift_grad_ref[:, cut] += fold_rows(grad_pre, jnp.sum)
-    out_ref[0, 0] = out
+    step = min(hidden_units, 256)
+    cuts = [slice(at, at + step) for at in range(0, hidden_units, step)]
+
+    def ahead(cut):
+        return dot_nn(hid, up_ref[:, cut]), dot_nt(grad_b, down_ref[cut, :])
+
+    held = ahead(cuts[0])
+    ready = None
+    for n in range(len(cuts) + 1):
+        pre, grad_act = held if held is not None else (None, None)
+        held = ahead(cuts[n + 1]) if n + 1 < len(cuts) else None
+        fresh = None
+        if n < len(cuts):
+            cut = cuts[n]
+            pre = pre + up_shift_ref[:, cut]
+            square = pre * pre
+            bent = jnp.tanh(pre * (GELU_SCALE + (GELU_SCALE * GELU_CUBIC) * square))
+            rise = 0.5 + 0.5 * bent
+            slope = rise + (0.5 * pre) * (1.0 - bent * bent) * (
+                GELU_SCALE + (3.0 * GELU_SCALE * GELU_CUBIC) * square
+            )
+            grad_pre = grad_act * slope
+            up_shift_grad_ref[:, cut] += fold_rows(grad_pre, jnp.sum)
+            fresh = (cut, (pre * rise).astype(BF16), grad_pre.astype(BF16))
+        if ready is not None:
+            cut, active, grad_pre_b = ready
+            out = out + dot_nn(active, down_ref[cut, :])
+            back = back + dot_nt(grad_pre_b, up_ref[:, cut])
+            down_acc[cut, :] += dot_nn(active.T, grad_b)
+            up_acc[:, cut] += dot_nn(hid_t, grad_pre_b)
+        ready = fresh
+    out_ref[0] = out.reshape(subs, span, model)
     scaled = back * vec_ref[2:3, :]
     mid = grad + spread * (
         scaled
         - jnp.mean(scaled, -1, keepdims=True)
         - normed * jnp.mean(scaled * normed, -1, keepdims=True)
     )
-    mid_ref[0, 0] = mid
+    mid_ref[0] = mid.reshape(subs, span, model)
     small_ref[0] += fold_rows(back * normed, jnp.sum)
     small_ref[1] += fold_rows(back, jnp.sum)
     small_ref[2] += fold_rows(grad_b.astype(F32), jnp.sum)
 
     mid_b = mid.astype(BF16)
     wo_acc[...] += dot_nt(mid_b.T, cexp[...])
-    table[...] = dot_nt(w_ref[0], mid_b[:, :half]) + dot_nt(w_ref[1], mid_b[:, half:])
-    picked = pick_slots(table, slot, picks, width, span)
-    grad_gate = []
-    for pick in range(picks):
-        at = slice(pick * span, (pick + 1) * span)
-        ctx = ctx_ref[0, 0, :, at].astype(F32)
-        grad_gate.append(jnp.sum(picked[pick] * ctx, 0, keepdims=True))
-        grad_ctx = (picked[pick] * gate[pick]).astype(BF16)
-        do_ref[0, 0, :, at] = grad_ctx
-        delta_ref[0, 0, :, at] = jnp.sum(grad_ctx.astype(F32) * ctx, 0, keepdims=True)
-    average = gate[0] * grad_gate[0]
-    for pick in range(1, picks):
-        average = average + gate[pick] * grad_gate[pick]
-    grad_logits = jnp.zeros((experts, span), F32)
-    for pick in range(picks):
-        grad_logits = jnp.where(
-            slot == pick, gate[pick] * (grad_gate[pick] - average), grad_logits
-        )
-    gl_ref[0, 0] = grad_logits
+    table[...] = dot_nt(low[...], mid_b[:, :half]) + dot_nt(high[...], mid_b[:, half:])
+    for sub in range(subs):
+        slot = slots[sub]
+        picked = pick_slots(table, slot, picks, width, sub * span)
+        grad_gate = []
+        for pick in range(picks):
+            at = slice(pick * span, (pick + 1) * span)
+            ctx = ctx_ref[0, sub, :, at].astype(F32)
+            grad_gate.append(jnp.sum(picked[pick] * ctx, 0, keepdims=True))
+            grad_ctx = (picked[pick] * gate[sub][pick]).astype(BF16)
+            do_ref[0, sub, :, at] = grad_ctx
+            delta_ref[0, sub, :, at] = jnp.sum(grad_ctx.astype(F32) * ctx, 0, keepdims=True)
+        average = gate[sub][0] * grad_gate[0]
+        for pick in range(1, picks):
+            average = average + gate[sub][pick] * grad_gate[pick]
+        grad_logits = jnp.zeros((experts, span), F32)
+        for pick in range(picks):
+            grad_logits = jnp.where(
+                slot == pick, gate[sub][pick] * (grad_gate[pick] - average), grad_logits
+            )
+        gl_ref[0, sub] = grad_logits
 
     @pl.when(last)
     def _():
@@ -308,10 +356,29 @@
         for_targets(ids, grad_refs, pack)
 
 
+def load_halves(first, core, sems, moves, meanwhile=lambda: None):
+    @pl.when(first)
+    def _():
+        copies = []
+        for own, other, target in moves:
+            half = target.shape[0] // 2
+            for source, at in ((own, core), (other, 1 - core)):
+                place = target.at[pl.ds(pl.multiple_of(at * half, half), half)]
+                copies.append(pltpu.make_async_copy(source, place, sems.at[len(copies)]))
+        for copy in copies:
+            copy.start()
+        meanwhile()
+        for copy in copies:
+            copy.wait()
+
+
 def pack_tiles(ref, to, at, total, row, rows, column, columns):
     row = pl.multiple_of(row, rows)
     for lane in range(0, columns, 128):
-        tile = total[pl.ds(row, rows), column + lane : column + lane + 128]
+        start = column + lane
+        if not isinstance(start, int):
+            start = pl.multiple_of(start, 128)
+        tile = total[pl.ds(row, rows), pl.ds(start, 128)]
         ref[to[0], to[1], at : at + rows, :] = tile.astype(BF16)
         at += rows
     return at
@@ -400,22 +467,45 @@
             side == 0, high, jnp.where(side == 1, middle, jnp.where(side == 2, low, 0.0))
         ).astype(BF16)
 
-        def key_step(at, probs):
-            probs_b = probs.astype(BF16)
-            slopes = (probs * dot_nn(vaug_ref[0, at], daug[...])).astype(BF16)
-            dvt[at] += dot_nt(daug[0:width, :], probs_b)
-            dkt[at] += dot_nt(qaug[0:width, :], slopes)
-            return dot_nn(kt_ref[0, at], slopes)
-
-        causal = lax.broadcasted_iota(jnp.int32, (span, rows), 0) <= (
-            lax.broadcasted_iota(jnp.int32, (span, rows), 1) & (span - 1)
+        lanes = 256
+        causal = lax.broadcasted_iota(jnp.int32, (span, lanes), 0) <= (
+            lax.broadcasted_iota(jnp.int32, (span, lanes), 1) & (span - 1)
         )
-        dq[...] = key_step(
-            block, jnp.where(causal, jnp.exp(dot_nn(kaug_ref[0, block], qaug[...])), 0.0)
-        )
+
+        def key_step(at, diagonal):
+            dv = dvt[at]
+            dk = dkt[at]
+            cuts = [slice(start, start + lanes) for start in range(0, rows, lanes)]
+
+            def ahead(cut):
+                return dot_nn(kaug_ref[0, at], qaug[:, cut]), dot_nn(vaug_ref[0, at], daug[:, cut])
+
+            held = ahead(cuts[0])
+            back = None
+            for n in range(len(cuts) + 1):
+                scores, dprobs = held if held is not None else (None, None)
+                held = ahead(cuts[n + 1]) if n + 1 < len(cuts) else None
+                fresh = None
+                if n < len(cuts):
+                    probs = jnp.exp(scores)
+                    if diagonal:
+                        probs = jnp.where(causal, probs, 0.0)
+                    slopes = (probs * dprobs).astype(BF16)
+                    fresh = (cuts[n], probs.astype(BF16), slopes)
+                if back is not None:
+                    cut, probs_b, slopes = back
+                    dv = dv + dot_nt(daug[0:width, cut], probs_b)
+                    dk = dk + dot_nt(qaug[0:width, cut], slopes)
+                    part = dot_nn(kt_ref[0, at], slopes)
+                    dq[:, cut] = part if diagonal else dq[:, cut] + part
+                back = fresh
+            dvt[at] = dv
+            dkt[at] = dk
+
+        key_step(block, True)
 
         def body(at, carry):
-            dq[...] += key_step(at, jnp.exp(dot_nn(kaug_ref[0, at], qaug[...])))
+            key_step(at, False)
             return carry
 
         lax.fori_loop(0, block, body, 0)
@@ -459,16 +549,19 @@
         for_targets(ids, grad_refs, pack)
 
 
-def input_kernel(x_ref, mid_ref, r_ref, w_ref, vec_ref, out_ref, small_ref):
+def input_kernel(
+    ids, x_ref, mid_ref, r_ref, own_ref, other_ref, vec_ref, out_ref, small_ref, w_ref, sems
+):
     first = (pl.program_id(0) == 0) & (pl.program_id(1) == 0)
+    load_halves(first, ids[0], sems, [(own_ref, other_ref, w_ref)])
 
     @pl.when(first)
     def _():
         small_ref[...] = jnp.zeros_like(small_ref)
 
-    back = jnp.concatenate(
-        [dot_tn(r_ref[0, 0], w_ref[0]), dot_tn(r_ref[0, 0], w_ref[1])], 1
-    )
+    low, high = halves(w_ref)
+    routed = r_ref[0, 0]
+    back = jnp.concatenate([dot_tn(routed, low[...]), dot_tn(routed, high[...])], 1)
     normed, spread = normalize(x_ref[0, 0].astype(F32))
     scaled = back * vec_ref[0:1, :]
     out_ref[0, 0] = mid_ref[0, 0] + spread * (
@@ -487,6 +580,15 @@
 def blocked(shape):
     tail = (0,) * (len(shape) - 2)
     return pl.BlockSpec((1, 1) + tuple(shape[2:]), lambda m, i, *refs: (m, i) + tail)
+
+
+def grouped(shape, group):
+    tail = (0,) * (len(shape) - 2)
+    return pl.BlockSpec((1, group) + tuple(shape[2:]), lambda m, i, *refs: (m, i) + tail)
+
+
+def in_place():
+    return pl.BlockSpec(memory_space=pl.ANY)
 
 
 def reversed_blocks(shape):
@@ -619,6 +721,7 @@
     span = min(BLOCK, slots)
     blocks = slots // span
     rows = picks * span
+    group = 2 if blocks % 2 == 0 else 1
     head = experts * width
     spare = -(-experts // 16) * 16
     all_rows = head + 2 * width + spare
@@ -636,27 +739,33 @@
     def transposed(weight):
         return jnp.swapaxes(weight[0], 1, 2).reshape(own_experts * width, half)
 
+    def start_of(routes):
+        local_routes = routes[0, :, 0]
+        group = (local_routes // own_experts) ^ z_at
+        local_routes = group * own_experts + local_routes % own_experts
+        return jnp.swapaxes(local_routes.reshape(micro_count, blocks, span, picks), 2, 3)
+
     query_parts = head_parts(transposed(query_weight))
     router_t = router_weight[0].T.reshape(z_size, own_experts, half)
     router_t = permute_groups(router_t, z_at).reshape(experts, half)
     router_t = jnp.pad(router_t, ((0, spare - experts), (0, 0)))
-    proj = jnp.concatenate(query_parts + [kv_weight[0].T, router_t], 0)
-    proj_other = exchange(proj, "fsdp", 1)
-    proj = both_halves(proj[None], proj_other[None], 0)
     vectors = jnp.concatenate([ln1_gain, ln1_bias, ln2_gain, ln2_bias, down_bias], 0)
     small = jnp.concatenate([vectors, up_bias.reshape(-1, half)], 0)
     small_other = exchange(small, "fsdp", 1)
     vectors = both_halves(vectors, small_other[:5], 1).astype(F32)
     up_shift = both_halves(up_bias, small_other[5:].reshape(1, -1), 1).astype(F32)
 
-    own_out, proj = lax.optimization_barrier((transposed(out_weight), proj))
+    up_other = exchange(up_weight[0], "fsdp", 1)
+    down_other = exchange(down_weight[0], "fsdp", 1)
+    route_t = start_of(routes)
+    lens, ids, route_t, vectors, up_shift, router_t, *query_parts = lax.optimization_barrier(
+        (lens, ids, route_t, vectors, up_shift, router_t, *query_parts)
+    )
+    proj = jnp.concatenate(query_parts + [kv_weight[0].T, router_t], 0)
+    proj_other = exchange(proj, "fsdp", 1)
+    own_out, proj_other = lax.optimization_barrier((transposed(out_weight), proj_other))
     out_parts = head_parts(own_out)
-    up_full = lax.all_gather(up_weight[0], "fsdp", axis=0, tiled=True)
-    down_full = lax.all_gather(down_weight[0], "fsdp", axis=0, tiled=True)
-
-    local_routes = routes[0, :, 0]
-    local_routes = ((local_routes // own_experts) ^ z_at) * own_experts + local_routes % own_experts
-    route_t = jnp.swapaxes(local_routes.reshape(micro_count, blocks, span, picks), 2, 3)
+
     states = inputs.reshape(micro_count, blocks, span, model)
     cotangent = out_cotangent.reshape(micro_count, blocks, span, model)
 
@@ -674,13 +783,14 @@
         forward_kernel,
         name="forward",
         grid_spec=pltpu.PrefetchScalarGridSpec(
-            num_scalar_prefetch=1,
+            num_scalar_prefetch=2,
             grid=grid,
             in_specs=[
                 blocked(states.shape),
                 blocked(route_t.shape),
                 full(vectors.shape),
-                full(proj.shape),
+                in_place(),
+                in_place(),
             ],
             out_specs=[
                 blocked(hid_s.shape),
@@ -699,18 +809,18 @@
                 pltpu.VMEM((blocks, span, rows), F32),
                 pltpu.VMEM((blocks, width, span), BF16),
                 pltpu.VMEM((width, rows), F32),
+                pltpu.VMEM((2 * all_rows, half), BF16),
+                pltpu.SemaphoreType.DMA((2,)),
             ],
         ),
         out_shape=[hid_s, aug_s, aug_s, kt_s, q_s, q_s, row_s, gate_s, slot_s],
         compiler_params=params(),
         cost_estimate=cost(2 * tokens * model * all_rows + 16 * pair_flops, 0, 64 << 20),
-    )(lens, states, route_t, vectors, proj)
-
-    ctx, up_full, down_full, *out_parts = lax.optimization_barrier(
-        (ctx, up_full, down_full, *out_parts)
-    )
-    out_proj = jnp.concatenate(out_parts, 0)[None]
-    out_proj = both_halves(out_proj, exchange(out_proj, "fsdp", 1), 0)
+    )(lens, ids, states, route_t, vectors, proj, proj_other)
+
+    ctx, *out_parts = lax.optimization_barrier((ctx, *out_parts))
+    out_proj = jnp.concatenate(out_parts, 0)
+    out_other = exchange(out_proj, "fsdp", 1)
     state_s = struct((micro_count, blocks, span, model), F32)
     mid_rows = chunk * hidden_units * 2 // 128 + head // z_size * (chunk * z_size) // 128
     late_rows = head // z_size * (chunk * z_size) // 128 + 2 * chunk
@@ -729,36 +839,43 @@
         name="middle",
         grid_spec=pltpu.PrefetchScalarGridSpec(
             num_scalar_prefetch=2,
-            grid=grid,
+            grid=(micro_count, blocks // group),
             in_specs=[
-                blocked(states.shape),
-                blocked(q_s.shape),
-                blocked(gate_s.shape),
-                blocked(slot_s.shape),
-                blocked(cotangent.shape),
-                full(out_proj.shape),
+                grouped(states.shape, group),
+                grouped(q_s.shape, group),
+                grouped(gate_s.shape, group),
+                grouped(slot_s.shape, group),
+                grouped(cotangent.shape, group),
+                in_place(),
+                in_place(),
                 full(vectors.shape),
-                full(up_full.shape),
+                in_place(),
+                in_place(),
                 full(up_shift.shape),
-                full(down_full.shape),
+                in_place(),
+                in_place(),
             ],
             out_specs=[
-                blocked(state_s.shape),
-                blocked(state_s.shape),
-                blocked(q_s.shape),
-                blocked(row_s.shape),
-                blocked(gate_s.shape),
+                grouped(state_s.shape, group),
+                grouped(state_s.shape, group),
+                grouped(q_s.shape, group),
+                grouped(row_s.shape, group),
+                grouped(gate_s.shape, group),
                 full((3, 8, model)),
                 full((8, hidden_units)),
             ]
             + [full(leaf.shape) for leaf in mid_grads],
             scratch_shapes=[
-                pltpu.VMEM((width, rows), F32),
-                pltpu.VMEM((head, span), BF16),
-                pltpu.VMEM((head, span), F32),
+                pltpu.VMEM((group, width, rows), F32),
+                pltpu.VMEM((head, group * span), BF16),
+                pltpu.VMEM((head, group * span), F32),
                 pltpu.VMEM((hidden_units, model), F32),
                 pltpu.VMEM((model, hidden_units), F32),
                 pltpu.VMEM((model, head), F32),
+                pltpu.VMEM((2 * head, half), BF16),
+                pltpu.VMEM((model, hidden_units), BF16),
+                pltpu.VMEM((hidden_units, model), BF16),
+                pltpu.SemaphoreType.DMA((6,)),
             ],
         ),
         out_shape=[
@@ -782,10 +899,13 @@
         slot,
         cotangent,
         out_proj,
+        out_other,
         vectors,
-        up_full,
+        up_weight[0],
+        up_other,
         up_shift,
-        down_full,
+        down_weight[0],
+        down_other,
     )
 
     if aligned:
@@ -851,31 +971,41 @@
         *mid_received, late_grads[0], late_grads[1] = lax.optimization_barrier(
             (*mid_received, *late_grads)
         )
+        *mid_received, late_grads[0], late_grads[1] = lax.optimization_barrier(
+            (*mid_received, *late_grads)
+        )
         late_sums = core_stage(late_grads)
+        *mid_received, late_sums[0] = lax.optimization_barrier((*mid_received, late_sums[0]))
         mid_sums = split_targets(add_up(mid_sums[0], mid_received), "expert")
-        routed, *late_sums = lax.optimization_barrier((routed, *late_sums))
+        routed, *sums = lax.optimization_barrier((routed, *mid_sums, *late_sums))
+        mid_sums, late_sums = sums[:z_size], sums[z_size:]
+        mid_received = send_stage(mid_sums, "expert")
         late_received = send_stage(late_sums, "dp")
-        mid_received = send_stage(mid_sums, "expert")
 
     input_grad, small1 = pl.pallas_call(
         input_kernel,
         name="input_back",
         grid_spec=pltpu.PrefetchScalarGridSpec(
-            num_scalar_prefetch=0,
+            num_scalar_prefetch=1,
             grid=grid,
             in_specs=[
                 blocked(states.shape),
                 blocked(state_s.shape),
                 blocked(r_s.shape),
-                full(proj.shape),
+                in_place(),
+                in_place(),
                 full(vectors.shape),
             ],
             out_specs=[blocked(state_s.shape), full((2, 8, model))],
+            scratch_shapes=[
+                pltpu.VMEM((2 * all_rows, half), BF16),
+                pltpu.SemaphoreType.DMA((2,)),
+            ],
         ),
         out_shape=[state_s, struct((2, 8, model), F32)],
         compiler_params=params(),
         cost_estimate=cost(2 * tokens * model * all_rows, 0, 40 << 20),
-    )(states, mid, routed, proj, vectors)
+    )(ids[2:], states, mid, routed, proj, proj_other, vectors)
 
     if aligned:
         small1, *received = lax.optimization_barrier((small1, *late_received, *mid_received))
@@ -891,12 +1021,13 @@
 
     if aligned:
         late_sums = split_targets(add_up(late_sums[0], late_received), "expert")
-        late_received = send_stage(late_sums, "expert")
+        packed[0], *late_sums = lax.optimization_barrier((packed[0], *late_sums))
+        packed = sum_packed(packed, devices)
         mid_total = total_up(mid_sums[0], mid_received)
         up_weight_grad, at = open_tiles(mid_total, 0, chunk, hidden_units)
         down_weight_grad, at = open_tiles(mid_total, at, hidden_units // devices, model)
         out_weight_grad, at = open_tiles(mid_total, at, chunk * z_size, head // z_size)
-        packed = sum_packed(packed, devices)
+        late_received = send_stage(late_sums, "expert")
         late_total = total_up(late_sums[0], late_received)
         query_weight_grad, at = open_tiles(late_total, 0, chunk * z_size, head // z_size)
         kv_grad = late_total[at : at + chunk]

time: 246 us -> 223 us (0.907)
  between operations: 14.7 us -> 1.23 us
  starting transfers between devices: 36.5 us -> 31 us
  Pallas kernels: 146 us -> 141 us
  local copies, waits for them, and re-layouts: 10.8 us -> 15.2 us
  waiting for transfers between devices: 22.7 us -> 19.9 us
    pallas_call x1, Pallas kernels: 62.1 us -> 57.3 us  [local(): pl.pallas_call(middle_kernel, name='middle', grid_spec=pltpu.PrefetchScal...]
    ppermute x23 -> x25, starting transfers between devices: 33.2 us -> 28.3 us  [exchange(): lax.ppermute(value, axis, [(at, at ^ distance) for at in range(count)])]
    select_n x2 -> x0, other arithmetic: 2.91 us -> none  [both_halves(): return jnp.where(f_at == 0, near, jnp.concatenate([other, own], dim))]
    unnamed x40 -> x37, local copies, waits for them, and re-layouts: 3.27 us -> 5.6 us
    ppermute x23 -> x25, waiting for transfers between devices: 21.8 us -> 19.6 us  [exchange(): lax.ppermute(value, axis, [(at, at ^ distance) for at in range(count)])]
  transfers between devices with their start and end apart: 26 -> 26, of which waited for: 8 -> 8; matrix products, arithmetic and copies ran while one was open for 6% -> 7% of each run, Pallas kernels for 34% -> 38%
where the time goes in v3:
time: 223 us; the launch traced here: 222 us
  Pallas kernels  141 us (63%)
  starting transfers between devices  31 us (14%)
  waiting for transfers between devices  19.9 us (9%)
  local copies, waits for them, and re-layouts  15.2 us (7%)
  other arithmetic  13.1 us (6%)
    pallas_call x1, Pallas kernels, local(): pl.pallas_call(middle_kernel, name='middle', grid_spec=pltpu.PrefetchScal...  57.3 us
    pallas_call x1, Pallas kernels, local(): pl.pallas_call(backward_kernel, name='backward', grid_spec=pltpu.Prefetch...  36.3 us
    pallas_call x1, Pallas kernels, local(): pl.pallas_call(forward_kernel, name='forward', grid_spec=pltpu.PrefetchSc...  34 us
    ppermute x25, starting transfers between devices, exchange(): lax.ppermute(value, axis, [(at, at ^ distance) for at in range(count)])  28.3 us
    ppermute x25, waiting for transfers between devices, exchange(): lax.ppermute(value, axis, [(at, at ^ distance) for at in range(count)])  19.6 us
    pallas_call x1, Pallas kernels, local(): pl.pallas_call(input_kernel, name='input_back', grid_spec=pltpu.PrefetchS...  13.9 us
    unnamed x37, local copies, waits for them, and re-layouts  5.6 us
    convert_element_type x2, other arithmetic, core_stage(): (keep[at].astype(F32) + other[at].astype(F32)).astype(BF16)  5.25 us
  transfers between devices with their start and end apart: 26, of which 8 were waited for; matrix products, arithmetic and copies ran while one was open for 7% of the time, Pallas kernels for 38%

profile of v3, /device:TPU:0, one launch (start us, length us, event | category | flops | bytes accessed | tf_op | source)
XLA Modules:
  0.0 221.9 jit_solution(12520468940318136694)
XLA Ops:
  0.7 3.1 %collective-permute-start.1 = (bf16[384,256]{1,0:T(8,128)(2,1)}, bf16[384,256]{1,0:T(8,128)(2,1)S(1)}, u32[]{:S(2)}, u32[]{:S(2)}) collective-permute-start(bf16[384,256]{1,0:T(8,128)(2,1)} %bitcast.129), channel_id=1, source_target_pairs={{0,2},{2,0},{4,6},{6,4},{1,3},{3,1},{5,7},{7,5},{8,10},{10,8},{12,... | collective-permute-start | bytes 589832 | tf_op jit(solution)/shard_map/ppermute | solution.py:621
  3.8 2.6 %collective-permute-start.2 = (bf16[384,256]{1,0:T(8,128)(2,1)}, bf16[384,256]{1,0:T(8,128)(2,1)S(1)}, u32[]{:S(2)}, u32[]{:S(2)}) collective-permute-start(bf16[384,256]{1,0:T(8,128)(2,1)} %bitcast.130), channel_id=1, source_target_pairs={{0,4},{2,6},{4,0},{6,2},{1,5},{3,7},{5,1},{7,3},{8,12},{10,14},{12... | collective-permute-start | bytes 589832 | tf_op jit(solution)/shard_map/ppermute | solution.py:621
  6.4 0.7 reduce.2
  7.1 0.9 concatenate.50
  8.0 0.7 reshape_reshape.9
  8.8 0.7 reshape.246
  9.5 0.9 broadcast_remainder_fusion
  10.4 0.9 sign_compare_fusion
  11.3 0.7 select_select_fusion
  12.0 0.7 fusion.11.route_ref
  12.7 0.6 pad_add_fusion.ids
  13.3 0.8 concatenate.49
  14.1 0.9 copy.56
  15.0 0.7 dynamic-slice_reduce_fusion.lens
  15.7 0.6 fusion.13.vec_ref
  16.4 1.4 fusion.12.up_shift_ref
  17.7 3.4 %collective-permute-done.2 = bf16[384,256]{1,0:T(8,128)(2,1)S(1)} collective-permute-done((bf16[384,256]{1,0:T(8,128)(2,1)}, bf16[384,256]{1,0:T(8,128)(2,1)S(1)}, u32[]{:S(2)}, u32[]{:S(2)}) %collective-permute-start.2) | collective-permute-done | bytes 196640 | tf_op jit(solution)/shard_map/ppermute | solution.py:621
  21.1 0.9 constant_dynamic-update-slice_fusion.4
  22.3 0.5 collective-permute-start.10
  22.8 2.3 %collective-permute-done.4.other_ref = bf16[1696,256]{1,0:T(8,128)(2,1)S(1)} collective-permute-done((bf16[1696,256]{1,0:T(8,128)(2,1)S(1)}, bf16[1696,256]{1,0:T(8,128)(2,1)S(1)}, u32[]{:S(2)}, u32[]{:S(2)}) %collective-permute-start.4) | collective-permute-done | bytes 868384 | tf_op jit(solution)/shard_map/ppermute | solution.py:621
  25.1 3.4 %collective-permute-start.5 = (bf16[384,256]{1,0:T(8,128)(2,1)S(1)}, bf16[384,256]{1,0:T(8,128)(2,1)S(1)}, u32[]{:S(2)}, u32[]{:S(2)}) collective-permute-start(bf16[384,256]{1,0:T(8,128)(2,1)S(1)} %bitcast.133), channel_id=1, source_target_pairs={{0,2},{2,0},{4,6},{6,4},{1,3},{3,1},{5,7},{7,5},{8,10},{10,8},{12,... | collective-permute-start | bytes 589832 | tf_op jit(solution)/shard_map/ppermute | solution.py:621
  28.5 1.1 collective-permute-start.6
  29.5 1.4 collective-permute-start.7
  30.9 34.0 %forward.1 = (bf16[2,4,256,512]{3,2,1,0:T(8,128)(2,1)}, bf16[2,4,256,128]{3,2,1,0:T(8,128)(2,1)}, bf16[2,4,256,128]{3,2,1,0:T(8,128)(2,1)}, bf16[2,4,1,64,256]{4...) custom-call(s32[2]{0:T(128)} %dynamic-slice_reduce_fusion.lens, ...), custom_call_target="tpu_custom_call" | custom-call | flops 20736638976 | bytes 67108864 | tf_op jit(solution)/shard_map/forward/pallas_call | solution.py:782
  65.2 2.3 %collective-permute-done.8.other_ref = bf16[1536,256]{1,0:T(8,128)(2,1)S(1)} collective-permute-done((bf16[1536,256]{1,0:T(8,128)(2,1)S(1)}, bf16[1536,256]{1,0:T(8,128)(2,1)S(1)}, u32[]{:S(2)}, u32[]{:S(2)}) %collective-permute-start.8) | collective-permute-done | bytes 786464 | tf_op jit(solution)/shard_map/ppermute | solution.py:621
  67.5 0.9 copy-done.11
  68.4 57.3 %middle.1 = (f32[2,4,256,512]{3,2,1,0:T(8,128)}, f32[2,4,256,512]{3,2,1,0:T(8,128)}, bf16[2,4,64,2048]{3,2,1,0:T(8,128)(2,1)}, f32[2,4,1,2048]{3,2,1,0:T(1,128)}...) custom-call(s32[2]{0:T(128)} %dynamic-slice_reduce_fusion.lens, ...), custom_call_target="tpu_custom_call" | custom-call | flops 35433480192 | bytes 209715200 | tf_op jit(solution)/shard_map/middle/pallas_call | solution.py:837
  125.7 0.2 collective-permute-start.11
  125.9 0.6 pad_convert_fusion.order_ref
  126.5 4.7 %collective-permute-done.11 = bf16[4,4,704,128]{3,2,1,0:T(8,128)(2,1)S(1)} collective-permute-done((bf16[4,4,704,128]{3,2,1,0:T(8,128)(2,1)}, bf16[4,4,704,128]{3,2,1,0:T(8,128)(2,1)S(1)}, u32[]{:S(2)}, u32[]{:S(2)}) %collective-permute-start.11) | collective-permute-done | bytes 2883616 | tf_op jit(solution)/shard_map/ppermute | solution.py:621
  131.2 3.7 %fusion.3 = (bf16[4,704,128]{2,1,0:T(8,128)(2,1)S(1)}, bf16[4,704,128]{2,1,0:T(8,128)(2,1)}, bf16[4,704,128]{2,1,0:T(8,128)(2,1)}, bf16[4,704,128]{2,1,0:T(8,128)(2,1)S(1)}) fusion(bf16[4,4,704,128]{3,2,1,0:T(8,128)(2,1)S(1)} %collective-permute-done.11, bf16[4,4,704,128]{3,2,1,0:T(8,128)(2,1)} %get-tuple-element.118), kind=kLoop, calls=%fused_computation.8 | loop fusion | flops 5767168 | bytes 8650752 | tf_op jit(solution)/shard_map/convert_element_type | solution.py:652
  135.0 1.5 collective-permute-start.12
  136.5 1.5 collective-permute-start.13
  138.0 0.5 collective-permute-start.14
  138.5 36.3 %backward.1 = (bf16[2,4,1696,256]{3,2,1,0:T(8,128)(2,1)}, bf16[4,4,224,128]{3,2,1,0:T(8,128)(2,1)}, bf16[4,4,224,128]{3,2,1,0:T(8,128)(2,1)}) custom-call(s32[2]{0:T(128)} %dynamic-slice_reduce_fusion.lens, s32[3]{0:T(128)} %pad_add_fusion.ids, bf16[2,4,256,512]{3,2,1,0:T(8,128)(2,1)} %get-tuple-element.111.hid_ref, ...), custom_call_target="tpu_custom_call" | custom-call | flops 46506442752 | bytes 104857600 | tf_op jit(solution)/shard_map/backward/pallas_call | solution.py:922
  174.9 2.7 %collective-permute-done.15 = bf16[4,4,224,128]{3,2,1,0:T(8,128)(2,1)S(1)} collective-permute-done((bf16[4,4,224,128]{3,2,1,0:T(8,128)(2,1)}, bf16[4,4,224,128]{3,2,1,0:T(8,128)(2,1)S(1)}, u32[]{:S(2)}, u32[]{:S(2)}) %collective-permute-start.15) | collective-permute-done | bytes 917536 | tf_op jit(solution)/shard_map/ppermute | solution.py:621
  177.6 1.5 fusion.7
  179.1 0.4 add_convert_fusion
  179.6 0.5 copy-done.9
  180.1 0.6 slice.130.ids
  180.8 1.5 collective-permute-start.16
  182.4 2.0 collective-permute-start.18
  184.3 2.5 %collective-permute-start.20 = (bf16[704,128]{1,0:T(8,128)(2,1)S(1)}, bf16[704,128]{1,0:T(8,128)(2,1)S(1)}, u32[]{:S(2)}, u32[]{:S(2)}) collective-permute-start(bf16[704,128]{1,0:T(8,128)(2,1)S(1)} %get-tuple-element.146), channel_id=1, source_target_pairs={{0,4},{2,6},{4,0},{6,2},{1,5},{3,7},{5,1},{7,3},{8,12},{10,14},{12... | collective-permute-start | bytes 540680 | tf_op jit(solution)/shard_map/ppermute | solution.py:621
  186.8 1.8 collective-permute-start.21
  188.7 13.9 %input_back.1 = (f32[2,4,256,512]{3,2,1,0:T(8,128)}, f32[2,8,512]{2,1,0:T(8,128)}) custom-call(s32[1]{0:T(128)} %slice.130.ids, bf16[2,4,256,512]{3,2,1,0:T(8,128)(2,1)} %bitcast.119, f32[2,4,256,512]{3,2,1,0:T(8,128)} %get-tuple-element.110.mid_ref, bf16[2,4,1696,256]{3,2,1,0:T(8,128)(2,1)} %get-tuple-element.139.r_ref, bf16[1696,256]{1,0:T(8,128)(2,1)} %copy-done.2, ...), custom_call_target="tpu_custom_call" | custom-call | flops 3556769792 | bytes 41943040 | tf_op jit(solution)/shard_map/input_back/pallas_call | solution.py:985
  202.7 0.5 copy-done.8
  203.6 0.6 all_to_all.6
  204.3 2.7 %all-to-all-start = ((f32[32,1,144]{2,1,0:T(1,128)}), f32[32,1,144]{2,1,0:T(1,128)S(1)}, u32[]{:S(2)}, u32[]{:S(2)}) async-start(f32[32,1,144]{2,1,0:T(1,128)} %all_to_all.6), calls=%async_computation | async-start | bytes 65536 | tf_op jit(solution)/shard_map/all_to_all | solution.py:682
  207.2 0.7 broadcast_in_dim_reshape.6
  208.0 0.7 broadcast_in_dim_reshape.7
  208.7 0.1 copy.60
  208.8 0.8 copy.66
  209.6 1.8 collective-permute-start.22
  211.4 2.4 %collective-permute-start.23 = (bf16[224,128]{1,0:T(8,128)(2,1)S(1)}, bf16[224,128]{1,0:T(8,128)(2,1)S(1)}, u32[]{:S(2)}, u32[]{:S(2)}) collective-permute-start(bf16[224,128]{1,0:T(8,128)(2,1)S(1)} %get-tuple-element.158), channel_id=1, source_target_pairs={{0,4},{2,6},{4,0},{6,2},{1,5},{3,7},{5,1},{7,3},{8,12},{10,14},{12... | collective-permute-start | bytes 172040 | tf_op jit(solution)/shard_map/ppermute | solution.py:621
  213.8 0.2 collective-permute-start.24
  214.0 0.2 all-to-all-done
  214.3 0.6 slice_bitcast_fusion.11
  214.9 0.6 slice_bitcast_fusion.12
  215.5 2.3 %collective-permute-done.23 = bf16[224,128]{1,0:T(8,128)(2,1)S(1)} collective-permute-done((bf16[224,128]{1,0:T(8,128)(2,1)S(1)}, bf16[224,128]{1,0:T(8,128)(2,1)S(1)}, u32[]{:S(2)}, u32[]{:S(2)}) %collective-permute-start.23) | collective-permute-done | bytes 57376 | tf_op jit(solution)/shard_map/ppermute | solution.py:621
  217.8 2.0 collective-permute-done.24
  219.8 0.6 slice_bitcast_fusion.8
  220.4 0.6 slice_bitcast_fusion.9
  221.0 0.1 copy.59
  221.1 0.8 copy.65
  (88 shorter events, 1.8 us)
Async XLA Ops:
  0.6 14.4 %copy-start = (s32[2,32]{1,0:T(2,128)S(1)}, s32[2,32]{1,0:T(2,128)}, u32[]{:S(2)}) copy-start(s32[2,32]{1,0:T(2,128)} %param.17) | copy-start | bytes 772
  0.7 22.1 %copy-start.10 = (bf16[1,256,2048]{2,1,0:T(8,128)(2,1)S(1)}, bf16[1,256,2048]{2,1,0:T(8,128)(2,1)}, u32[]{:S(2)}) copy-start(bf16[1,256,2048]{2,1,0:T(8,128)(2,1)} %param.27) | copy-start | bytes 3145732
  0.7 24.4 %copy-start.4 = (bf16[1,6,256,64]{2,3,1,0:T(8,128)(2,1)S(1)}, bf16[1,6,256,64]{2,3,1,0:T(8,128)(2,1)}, u32[]{:S(2)}) copy-start(bf16[1,6,256,64]{2,3,1,0:T(8,128)(2,1)} %param.24) | copy-start | bytes 589828
  0.7 17.1 %collective-permute-start.1 = (bf16[384,256]{1,0:T(8,128)(2,1)}, bf16[384,256]{1,0:T(8,128)(2,1)S(1)}, u32[]{:S(2)}, u32[]{:S(2)}) collective-permute-start(bf16[384,256]{1,0:T(8,128)(2,1)} %bitcast.129), channel_id=1, source_target_pairs={{0,2},{2,0},{4,6},{6,4},{1,3},{3,1},{5,7},{7,5},{8,10},{10,8},{12,... | collective-permute-start | bytes 589832 | tf_op jit(solution)/shard_map/ppermute | solution.py:621
  3.8 17.4 %collective-permute-start.2 = (bf16[384,256]{1,0:T(8,128)(2,1)}, bf16[384,256]{1,0:T(8,128)(2,1)S(1)}, u32[]{:S(2)}, u32[]{:S(2)}) collective-permute-start(bf16[384,256]{1,0:T(8,128)(2,1)} %bitcast.130), channel_id=1, source_target_pairs={{0,4},{2,6},{4,0},{6,2},{1,5},{3,7},{5,1},{7,3},{8,12},{10,14},{12... | collective-permute-start | bytes 589832 | tf_op jit(solution)/shard_map/ppermute | solution.py:621
  6.4 14.8 %collective-permute-start.3 = (bf16[384,256]{1,0:T(8,128)(2,1)}, bf16[384,256]{1,0:T(8,128)(2,1)S(1)}, u32[]{:S(2)}, u32[]{:S(2)}) collective-permute-start(bf16[384,256]{1,0:T(8,128)(2,1)} %bitcast.131), channel_id=1, source_target_pairs={{0,6},{2,4},{4,2},{6,0},{1,7},{3,5},{5,3},{7,1},{8,14},{10,12},{12... | collective-permute-start | bytes 589832 | tf_op jit(solution)/shard_map/ppermute | solution.py:621
  7.9 7.8 %collective-permute-start = (bf16[9,256]{1,0:T(8,128)(2,1)S(1)}, bf16[9,256]{1,0:T(8,128)(2,1)S(1)}, u32[]{:S(2)}, u32[]{:S(2)}) collective-permute-start(bf16[9,256]{1,0:T(8,128)(2,1)S(1)} %concatenate.50), channel_id=1, source_target_pairs={{0,1},{1,0},{2,3},{3,2},{4,5},{5,4},{6,7},{7,6},{8,9},{9,8},{10,11... | collective-permute-start | bytes 13832 | tf_op jit(solution)/shard_map/ppermute | solution.py:621
  22.2 8.8 %copy-start.2 = (bf16[1696,256]{1,0:T(8,128)(2,1)}, bf16[1696,256]{1,0:T(8,128)(2,1)S(1)}, u32[]{:S(2)}) copy-start(bf16[1696,256]{1,0:T(8,128)(2,1)S(1)} %constant_dynamic-update-slice_fusion.own_ref) | copy-start | bytes 2605060
  22.2 2.9 %collective-permute-start.4 = (bf16[1696,256]{1,0:T(8,128)(2,1)S(1)}, bf16[1696,256]{1,0:T(8,128)(2,1)S(1)}, u32[]{:S(2)}, u32[]{:S(2)}) collective-permute-start(bf16[1696,256]{1,0:T(8,128)(2,1)S(1)} %constant_dynamic-update-slice_fusion.own_ref), channel_id=1, source_target_pairs={{0,1},{1,0},{2,3},{3,2},{4,5},{5,4},{6,7},{7,6},{8,9},{9,8},{10,11... | collective-permute-start | bytes 2605064 | tf_op jit(solution)/shard_map/ppermute | solution.py:621
  22.3 42.9 %collective-permute-start.10 = (bf16[1024,512]{1,0:T(8,128)(2,1)}, bf16[1024,512]{1,0:T(8,128)(2,1)}, u32[]{:S(2)}, u32[]{:S(2)}) collective-permute-start(bf16[1024,512]{1,0:T(8,128)(2,1)} %bitcast.24.own_down_ref), channel_id=1, source_target_pairs={{0,1},{1,0},{2,3},{3,2},{4,5},{5,4},{6,7},{7,6},{8,9},{9,8},{10,11... | collective-permute-start | bytes 3145736 | tf_op jit(solution)/shard_map/ppermute | solution.py:621
  22.8 42.5 %collective-permute-start.9 = (bf16[256,2048]{1,0:T(8,128)(2,1)S(1)}, bf16[256,2048]{1,0:T(8,128)(2,1)}, u32[]{:S(2)}, u32[]{:S(2)}) collective-permute-start(bf16[256,2048]{1,0:T(8,128)(2,1)S(1)} %bitcast.145), channel_id=1, source_target_pairs={{0,1},{1,0},{2,3},{3,2},{4,5},{5,4},{6,7},{7,6},{8,9},{9,8},{10,11... | collective-permute-start | bytes 3145736 | tf_op jit(solution)/shard_map/ppermute | solution.py:621
  25.1 5.8 %copy-start.3 = (bf16[1696,256]{1,0:T(8,128)(2,1)}, bf16[1696,256]{1,0:T(8,128)(2,1)S(1)}, u32[]{:S(2)}) copy-start(bf16[1696,256]{1,0:T(8,128)(2,1)S(1)} %collective-permute-done.4.other_ref) | copy-start | bytes 2605060
  25.1 39.9 %collective-permute-start.5 = (bf16[384,256]{1,0:T(8,128)(2,1)S(1)}, bf16[384,256]{1,0:T(8,128)(2,1)S(1)}, u32[]{:S(2)}, u32[]{:S(2)}) collective-permute-start(bf16[384,256]{1,0:T(8,128)(2,1)S(1)} %bitcast.133), channel_id=1, source_target_pairs={{0,2},{2,0},{4,6},{6,4},{1,3},{3,1},{5,7},{7,5},{8,10},{10,8},{12,... | collective-permute-start | bytes 589832 | tf_op jit(solution)/shard_map/ppermute | solution.py:621
  28.5 36.5 %collective-permute-start.6 = (bf16[384,256]{1,0:T(8,128)(2,1)S(1)}, bf16[384,256]{1,0:T(8,128)(2,1)S(1)}, u32[]{:S(2)}, u32[]{:S(2)}) collective-permute-start(bf16[384,256]{1,0:T(8,128)(2,1)S(1)} %bitcast.134), channel_id=1, source_target_pairs={{0,4},{2,6},{4,0},{6,2},{1,5},{3,7},{5,1},{7,3},{8,12},{10,14},{12... | collective-permute-start | bytes 589832 | tf_op jit(solution)/shard_map/ppermute | solution.py:621
  29.5 35.5 %collective-permute-start.7 = (bf16[384,256]{1,0:T(8,128)(2,1)S(1)}, bf16[384,256]{1,0:T(8,128)(2,1)S(1)}, u32[]{:S(2)}, u32[]{:S(2)}) collective-permute-start(bf16[384,256]{1,0:T(8,128)(2,1)S(1)} %bitcast.135), channel_id=1, source_target_pairs={{0,6},{2,4},{4,2},{6,0},{1,7},{3,5},{5,3},{7,1},{8,14},{10,12},{12... | collective-permute-start | bytes 589832 | tf_op jit(solution)/shard_map/ppermute | solution.py:621
  65.1 2.4 %copy-start.6 = (bf16[1536,256]{1,0:T(8,128)(2,1)}, bf16[1536,256]{1,0:T(8,128)(2,1)S(1)}, u32[]{:S(2)}) copy-start(bf16[1536,256]{1,0:T(8,128)(2,1)S(1)} %constant_dynamic-update-slice_fusion.5.own_ref) | copy-start | bytes 2359300
  65.1 2.4 %collective-permute-start.8 = (bf16[1536,256]{1,0:T(8,128)(2,1)S(1)}, bf16[1536,256]{1,0:T(8,128)(2,1)S(1)}, u32[]{:S(2)}, u32[]{:S(2)}) collective-permute-start(bf16[1536,256]{1,0:T(8,128)(2,1)S(1)} %constant_dynamic-update-slice_fusion.5.own_ref), channel_id=1, source_target_pairs={{0,1},{1,0},{2,3},{3,2},{4,5},{5,4},{6,7},{7,6},{8,9},{9,8},{10,11... | collective-permute-start | bytes 2359304 | tf_op jit(solution)/shard_map/ppermute | solution.py:621
  67.5 0.9 copy-start.11
  125.7 5.6 %collective-permute-start.11 = (bf16[4,4,704,128]{3,2,1,0:T(8,128)(2,1)}, bf16[4,4,704,128]{3,2,1,0:T(8,128)(2,1)S(1)}, u32[]{:S(2)}, u32[]{:S(2)}) collective-permute-start(bf16[4,4,704,128]{3,2,1,0:T(8,128)(2,1)} %get-tuple-element.119), channel_id=1, source_target_pairs={{0,1},{1,0},{2,3},{3,2},{4,5},{5,4},{6,7},{7,6},{8,9},{9,8},{10,11... | collective-permute-start | bytes 8650760 | tf_op jit(solution)/shard_map/ppermute | solution.py:621
  135.0 39.8 %collective-permute-start.12 = (bf16[4,704,128]{2,1,0:T(8,128)(2,1)}, bf16[4,704,128]{2,1,0:T(8,128)(2,1)S(1)}, u32[]{:S(2)}, u32[]{:S(2)}) collective-permute-start(bf16[4,704,128]{2,1,0:T(8,128)(2,1)} %get-tuple-element.125), channel_id=1, source_target_pairs={{0,8},{8,0},{16,24},{24,16},{1,9},{9,1},{17,25},{25,17},{2,10},{10... | collective-permute-start | bytes 2162696 | tf_op jit(solution)/shard_map/ppermute | solution.py:621
  136.5 38.3 %collective-permute-start.13 = (bf16[4,704,128]{2,1,0:T(8,128)(2,1)}, bf16[4,704,128]{2,1,0:T(8,128)(2,1)S(1)}, u32[]{:S(2)}, u32[]{:S(2)}) collective-permute-start(bf16[4,704,128]{2,1,0:T(8,128)(2,1)} %get-tuple-element.126), channel_id=1, source_target_pairs={{0,16},{8,24},{16,0},{24,8},{1,17},{9,25},{17,1},{25,9},{2,18},{10... | collective-permute-start | bytes 2162696 | tf_op jit(solution)/shard_map/ppermute | solution.py:621
  138.0 36.8 %collective-permute-start.14 = (bf16[4,704,128]{2,1,0:T(8,128)(2,1)S(1)}, bf16[4,704,128]{2,1,0:T(8,128)(2,1)S(1)}, u32[]{:S(2)}, u32[]{:S(2)}) collective-permute-start(bf16[4,704,128]{2,1,0:T(8,128)(2,1)S(1)} %get-tuple-element.127), channel_id=1, source_target_pairs={{0,24},{8,16},{16,8},{24,0},{1,25},{9,17},{17,9},{25,1},{2,26},{10... | collective-permute-start | bytes 2162696 | tf_op jit(solution)/shard_map/ppermute | solution.py:621
  174.8 2.7 %collective-permute-start.15 = (bf16[4,4,224,128]{3,2,1,0:T(8,128)(2,1)}, bf16[4,4,224,128]{3,2,1,0:T(8,128)(2,1)S(1)}, u32[]{:S(2)}, u32[]{:S(2)}) collective-permute-start(bf16[4,4,224,128]{3,2,1,0:T(8,128)(2,1)} %get-tuple-element.134), channel_id=1, source_target_pairs={{0,1},{1,0},{2,3},{3,2},{4,5},{5,4},{6,7},{7,6},{8,9},{9,8},{10,11... | collective-permute-start | bytes 2752520 | tf_op jit(solution)/shard_map/ppermute | solution.py:621
  179.5 0.7 copy-start.9
  179.5 1.2 copy-start.7
  179.5 1.2 copy-start.5
  179.6 7.3 %collective-permute-start.19 = (bf16[704,128]{1,0:T(8,128)(2,1)S(1)}, bf16[704,128]{1,0:T(8,128)(2,1)S(1)}, u32[]{:S(2)}, u32[]{:S(2)}) collective-permute-start(bf16[704,128]{1,0:T(8,128)(2,1)S(1)} %get-tuple-element.145), channel_id=1, source_target_pairs={{0,2},{2,0},{4,6},{6,4},{1,3},{3,1},{5,7},{7,5},{8,10},{10,8},{12,... | collective-permute-start | bytes 540680 | tf_op jit(solution)/shard_map/ppermute | solution.py:621
  180.8 21.7 %collective-permute-start.16 = (bf16[4,224,128]{2,1,0:T(8,128)(2,1)S(1)}, bf16[4,224,128]{2,1,0:T(8,128)(2,1)S(1)}, u32[]{:S(2)}, u32[]{:S(2)}) collective-permute-start(bf16[4,224,128]{2,1,0:T(8,128)(2,1)S(1)} %get-tuple-element.142), channel_id=1, source_target_pairs={{0,8},{8,0},{16,24},{24,16},{1,9},{9,1},{17,25},{25,17},{2,10},{10... | collective-permute-start | bytes 688136 | tf_op jit(solution)/shard_map/ppermute | solution.py:621
  182.4 20.2 %collective-permute-start.17 = (bf16[4,224,128]{2,1,0:T(8,128)(2,1)S(1)}, bf16[4,224,128]{2,1,0:T(8,128)(2,1)S(1)}, u32[]{:S(2)}, u32[]{:S(2)}) collective-permute-start(bf16[4,224,128]{2,1,0:T(8,128)(2,1)S(1)} %get-tuple-element.143), channel_id=1, source_target_pairs={{0,16},{8,24},{16,0},{24,8},{1,17},{9,25},{17,1},{25,9},{2,18},{10... | collective-permute-start | bytes 688136 | tf_op jit(solution)/shard_map/ppermute | solution.py:621
  182.4 20.2 %collective-permute-start.18 = (bf16[4,224,128]{2,1,0:T(8,128)(2,1)S(1)}, bf16[4,224,128]{2,1,0:T(8,128)(2,1)S(1)}, u32[]{:S(2)}, u32[]{:S(2)}) collective-permute-start(bf16[4,224,128]{2,1,0:T(8,128)(2,1)S(1)} %get-tuple-element.144), channel_id=1, source_target_pairs={{0,24},{8,16},{16,8},{24,0},{1,25},{9,17},{17,9},{25,1},{2,26},{10... | collective-permute-start | bytes 688136 | tf_op jit(solution)/shard_map/ppermute | solution.py:621
  184.3 18.2 %collective-permute-start.20 = (bf16[704,128]{1,0:T(8,128)(2,1)S(1)}, bf16[704,128]{1,0:T(8,128)(2,1)S(1)}, u32[]{:S(2)}, u32[]{:S(2)}) collective-permute-start(bf16[704,128]{1,0:T(8,128)(2,1)S(1)} %get-tuple-element.146), channel_id=1, source_target_pairs={{0,4},{2,6},{4,0},{6,2},{1,5},{3,7},{5,1},{7,3},{8,12},{10,14},{12... | collective-permute-start | bytes 540680 | tf_op jit(solution)/shard_map/ppermute | solution.py:621
  186.8 15.7 %collective-permute-start.21 = (bf16[704,128]{1,0:T(8,128)(2,1)S(1)}, bf16[704,128]{1,0:T(8,128)(2,1)S(1)}, u32[]{:S(2)}, u32[]{:S(2)}) collective-permute-start(bf16[704,128]{1,0:T(8,128)(2,1)S(1)} %get-tuple-element.147), channel_id=1, source_target_pairs={{0,6},{2,4},{4,2},{6,0},{1,7},{3,5},{5,3},{7,1},{8,14},{10,12},{12... | collective-permute-start | bytes 540680 | tf_op jit(solution)/shard_map/ppermute | solution.py:621
  202.5 0.8 copy-start.8
  204.3 9.9 %all-to-all-start = ((f32[32,1,144]{2,1,0:T(1,128)}), f32[32,1,144]{2,1,0:T(1,128)S(1)}, u32[]{:S(2)}, u32[]{:S(2)}) async-start(f32[32,1,144]{2,1,0:T(1,128)} %all_to_all.6), calls=%async_computation | async-start | bytes 65536 | tf_op jit(solution)/shard_map/all_to_all | solution.py:682
  207.1 14.8 %copy-start.1 = (s32[2,32]{1,0:T(2,128)S(1)}, s32[2,32]{1,0:T(2,128)}, u32[]{:S(2)}) copy-start(s32[2,32]{1,0:T(2,128)} %param.17) | copy-start | bytes 772
  209.6 5.9 %collective-permute-start.22 = (bf16[224,128]{1,0:T(8,128)(2,1)S(1)}, bf16[224,128]{1,0:T(8,128)(2,1)S(1)}, u32[]{:S(2)}, u32[]{:S(2)}) collective-permute-start(bf16[224,128]{1,0:T(8,128)(2,1)S(1)} %get-tuple-element.157), channel_id=1, source_target_pairs={{0,2},{2,0},{4,6},{6,4},{1,3},{3,1},{5,7},{7,5},{8,10},{10,8},{12,... | collective-permute-start | bytes 172040 | tf_op jit(solution)/shard_map/ppermute | solution.py:621
  211.4 6.4 %collective-permute-start.23 = (bf16[224,128]{1,0:T(8,128)(2,1)S(1)}, bf16[224,128]{1,0:T(8,128)(2,1)S(1)}, u32[]{:S(2)}, u32[]{:S(2)}) collective-permute-start(bf16[224,128]{1,0:T(8,128)(2,1)S(1)} %get-tuple-element.158), channel_id=1, source_target_pairs={{0,4},{2,6},{4,0},{6,2},{1,5},{3,7},{5,1},{7,3},{8,12},{10,14},{12... | collective-permute-start | bytes 172040 | tf_op jit(solution)/shard_map/ppermute | solution.py:621
  213.8 6.0 %collective-permute-start.24 = (bf16[224,128]{1,0:T(8,128)(2,1)S(1)}, bf16[224,128]{1,0:T(8,128)(2,1)S(1)}, u32[]{:S(2)}, u32[]{:S(2)}) collective-permute-start(bf16[224,128]{1,0:T(8,128)(2,1)S(1)} %get-tuple-element.159), channel_id=1, source_target_pairs={{0,6},{2,4},{4,2},{6,0},{1,7},{3,5},{5,3},{7,1},{8,14},{10,12},{12... | collective-permute-start | bytes 172040 | tf_op jit(solution)/shard_map/ppermute | solution.py:621

commit v4 on v3

--- a/solution.py
+++ b/solution.py
@@ -96,7 +96,9 @@
     block = pl.program_id(1)
     length = lens[pl.program_id(0)]
     first = (pl.program_id(0) == 0) & (block == 0)
-    load_halves(first, ids[2], sems, [(own_ref, other_ref, w_ref)])
+    copies = half_copies(ids[2], sems, [(own_ref, other_ref, w_ref)])
+    start_all(first, copies)
+    wait_all(first, copies)
     span = x_ref.shape[2]
     experts = slot_ref.shape[2]
     picks = route_ref.shape[2]
@@ -225,8 +227,7 @@
         small_ref[...] = jnp.zeros_like(small_ref)
         up_shift_grad_ref[...] = jnp.zeros_like(up_shift_grad_ref)
 
-    load_halves(
-        first,
+    copies = half_copies(
         ids[2],
         sems,
         [
@@ -234,8 +235,9 @@
             (own_up_ref, other_up_ref, up_ref),
             (own_down_ref, other_down_ref, down_ref),
         ],
-        clear,
-    )
+    )
+    start_all(first, copies, clear)
+    wait_all(first, copies)
     slots = [slot_ref[0, sub] for sub in range(subs)]
     gate = []
     for sub in range(subs):
@@ -356,18 +358,27 @@
         for_targets(ids, grad_refs, pack)
 
 
-def load_halves(first, core, sems, moves, meanwhile=lambda: None):
+def half_copies(core, sems, moves):
+    copies = []
+    for own, other, target in moves:
+        half = target.shape[0] // 2
+        for source, at in ((own, core), (other, 1 - core)):
+            place = target.at[pl.ds(pl.multiple_of(at * half, half), half)]
+            copies.append(pltpu.make_async_copy(source, place, sems.at[len(copies)]))
+    return copies
+
+
+def start_all(first, copies, meanwhile=lambda: None):
     @pl.when(first)
     def _():
-        copies = []
-        for own, other, target in moves:
-            half = target.shape[0] // 2
-            for source, at in ((own, core), (other, 1 - core)):
-                place = target.at[pl.ds(pl.multiple_of(at * half, half), half)]
-                copies.append(pltpu.make_async_copy(source, place, sems.at[len(copies)]))
         for copy in copies:
             copy.start()
         meanwhile()
+
+
+def wait_all(first, copies):
+    @pl.when(first)
+    def _():
         for copy in copies:
             copy.wait()
 
@@ -422,10 +433,13 @@
     slot_ref,
     gl_ref,
     order_ref,
+    columns_ref,
+    own_ref,
+    other_ref,
     r_ref,
     *rest,
 ):
-    *grad_refs, qaug, daug, dq, dkt, dvt, w_acc = rest
+    *grad_refs, qaug, daug, dq, dkt, dvt, w_acc, w_ref, sems = rest
     micro = pl.program_id(0)
     step = pl.program_id(1)
     blocks = pl.num_programs(1)
@@ -438,9 +452,11 @@
     picks = rows // span
     head = experts * width
 
-    @pl.when((micro == 0) & (step == 0))
-    def _():
+    def clear():
         w_acc[...] = jnp.zeros_like(w_acc)
+
+    copies = half_copies(ids[2], sems, [(own_ref, other_ref, w_ref)])
+    start_all((micro == 0) & (step == 0), copies, clear)
 
     @pl.when(step == 0)
     def _():
@@ -526,23 +542,43 @@
         r_ref[0, 0, head + 2 * width :, :] = jnp.concatenate(
             [gl_ref[0, 0], jnp.zeros((tail - experts, span), F32)], 0
         ).astype(BF16)
-        w_acc[:, : r_ref.shape[2]] += dot_nt(hid_ref[0, 0].T, r_ref[0, 0])
+        summing = jnp.concatenate([hid_ref[0, 0].T, jnp.ones((16, span), BF16)], 0)
+        w_acc[:, : r_ref.shape[2]] += dot_nt(summing, r_ref[0, 0])
 
     @pl.when((micro == pl.num_programs(0) - 1) & (step == blocks - 1))
     def _():
-        if len(grad_refs) == 1:
-            grad_refs[0][...] = w_acc[:, : r_ref.shape[2]].astype(BF16)
-            return
+        for copy in copies:
+            copy.wait()
+        model = hid_ref.shape[3]
+        used = r_ref.shape[2]
+        low, high = halves(w_ref)
+        token_sum = w_acc[model : model + 1, :used]
+        gain_sum, shift_sum = [], []
+        for at, part in ((0, low), (model // 2, high)):
+            weight = part[...].T.astype(F32)
+            total = w_acc[at : at + model // 2, :used]
+            gain_sum.append(jnp.sum(weight * total, 1, keepdims=True))
+            shift_sum.append(jnp.sum(weight * token_sum, 1, keepdims=True))
+        gain_sum, shift_sum = jnp.concatenate(gain_sum, 0), jnp.concatenate(shift_sum, 0)
+        columns = columns_ref[...]
+        gain, shift = columns[:, experts : experts + 1], columns[:, experts + 1 : experts + 2]
+        gain_sum = (gain_sum - shift * shift_sum) / gain
+        lane = lax.broadcasted_iota(jnp.int32, columns.shape, 1)
+        columns = jnp.where(
+            lane == experts, gain_sum, jnp.where(lane == experts + 1, shift_sum, columns)
+        )
         routed = head + 2 * width
         spare = order_ref.shape[0]
-        w_acc[:, routed:] = dot_nn(
-            w_acc[:, routed : routed + spare].astype(BF16), order_ref[...]
-        )
+        router = w_acc[:model, routed : routed + spare].astype(BF16)
+        w_acc[:model, routed:] = columns + dot_nn(router, order_ref[...])
+        if len(grad_refs) == 1:
+            grad_refs[0][...] = w_acc[:model, :].astype(BF16)
+            return
         targets = grad_refs[0].shape[0] * grad_refs[0].shape[1]
-        shared_rows = w_acc.shape[0] // (2 * targets)
+        shared_rows = model // (2 * targets)
 
         def pack(ref, to, fro, shared, heads):
-            rows, columns = heads_chunk(w_acc.shape[0], head, ref)
+            rows, columns = heads_chunk(model, head, ref)
             at = pack_tiles(ref, to, 0, w_acc, heads * rows, rows, fro * columns, columns)
             pack_tiles(ref, to, at, w_acc, shared * shared_rows, shared_rows, head, w_acc.shape[1] - head)
 
@@ -550,27 +586,49 @@
 
 
 def input_kernel(
-    ids, x_ref, mid_ref, r_ref, own_ref, other_ref, vec_ref, out_ref, small_ref, w_ref, sems
+    ids, x_ref, mid_ref, r_ref, own_ref, other_ref, vec_ref, out_ref, w_ref, sems
 ):
     first = (pl.program_id(0) == 0) & (pl.program_id(1) == 0)
-    load_halves(first, ids[0], sems, [(own_ref, other_ref, w_ref)])
-
-    @pl.when(first)
-    def _():
-        small_ref[...] = jnp.zeros_like(small_ref)
-
+    copies = half_copies(ids[0], sems, [(own_ref, other_ref, w_ref)])
+    start_all(first, copies)
+
+    wait_all(first, copies)
+    subs, span, model = x_ref.shape[1:]
+    normed, spread = normalize(x_ref[0].reshape(subs * span, model).astype(F32))
     low, high = halves(w_ref)
     routed = r_ref[0, 0]
     back = jnp.concatenate([dot_tn(routed, low[...]), dot_tn(routed, high[...])], 1)
-    normed, spread = normalize(x_ref[0, 0].astype(F32))
     scaled = back * vec_ref[0:1, :]
-    out_ref[0, 0] = mid_ref[0, 0] + spread * (
+    total = mid_ref[0].reshape(subs * span, model) + spread * (
         scaled
         - jnp.mean(scaled, -1, keepdims=True)
         - normed * jnp.mean(scaled * normed, -1, keepdims=True)
     )
-    small_ref[0] += fold_rows(back * normed, jnp.sum)
-    small_ref[1] += fold_rows(back, jnp.sum)
+    out_ref[0] = total.reshape(subs, span, model)
+
+
+def finish_kernel(experts, deep, *refs):
+    parts, (heads_ref, kv_ref, router_ref, up_shift_ref, *vector_refs) = refs[:-9], refs[-9:]
+    total = parts[0][...].astype(F32)
+    for part in parts[1:]:
+        total = total + part[...].astype(F32)
+    _, own_experts, rows, width = heads_ref.shape
+    per_tile = 128 // width
+    for expert in range(own_experts):
+        at = expert // per_tile * rows
+        lane = expert % per_tile * width
+        heads_ref[0, expert] = total[at : at + rows, lane : lane + width]
+    at = own_experts // per_tile * rows
+    chunk = kv_ref.shape[1]
+    kv_ref[0] = total[at : at + chunk]
+    tile = total[at + chunk : at + 2 * chunk]
+    router_ref[0] = tile[:, :experts]
+    turned = tile.T
+    for ref, row in zip(vector_refs, range(experts, experts + 5)):
+        ref[...] = turned[row : row + 1]
+    up_shift_ref[...] = jnp.concatenate(
+        [turned[row : row + 1] for row in range(experts + 5, experts + 5 + deep)], 1
+    )
 
 
 def full(shape):
@@ -675,17 +733,6 @@
     count = columns // 128
     tiles = value[at : at + count * rows].reshape(count, rows, 128)
     return jnp.swapaxes(tiles, 0, 1).reshape(rows, columns), at + count * rows
-
-
-def sum_packed(parts, devices):
-    packed = jnp.concatenate(parts, 1)
-    packed = lax.all_to_all(packed, AXES, split_axis=0, concat_axis=0, tiled=True)
-    packed = jnp.sum(packed.reshape(devices, -1), 0)
-    result, at = [], 0
-    for part in parts:
-        result.append(packed[at : at + part.shape[1]])
-        at += part.shape[1]
-    return result
 
 
 def local(
@@ -833,7 +880,7 @@
             struct((model, hidden_units), BF16),
             struct((model, head), BF16),
         ]
-        late_grads = [struct((model, all_rows), BF16)]
+        late_grads = [struct((model, head + 2 * width + 128), BF16)]
     outputs, mid, grad_ctx, delta, grad_logits, small2, up_small, *mid_grads = pl.pallas_call(
         middle_kernel,
         name="middle",
@@ -918,7 +965,22 @@
     order = jnp.pad(
         (jnp.arange(spare)[:, None] == moved[None, :]).astype(BF16), ((0, 0), (0, 128 - experts))
     )
-    r_s = struct((micro_count, blocks, all_rows, span), BF16)
+    deep = hidden_units // model
+    columns = jnp.concatenate(
+        [
+            vectors[:2].T,
+            jnp.sum(small2, 1).T,
+            jnp.swapaxes(jnp.sum(up_small, 0).reshape(devices, deep, chunk), 1, 2).reshape(model, deep),
+        ],
+        1,
+    )
+    columns = jnp.pad(columns, ((0, 0), (experts, 128 - experts - 5 - deep)))
+    r_s = struct((micro_count, blocks // group, all_rows, group * span), BF16)
+
+    def routed_block(m, i, *refs):
+        block = blocks - 1 - i
+        return m, block // group, 0, block % group
+
     routed, *late_grads = pl.pallas_call(
         backward_kernel,
         name="backward",
@@ -937,15 +999,21 @@
                 reversed_blocks(slot_s.shape),
                 reversed_blocks(gate_s.shape),
                 full(order.shape),
+                full(columns.shape),
+                in_place(),
+                in_place(),
             ],
-            out_specs=[reversed_blocks(r_s.shape)] + [full(leaf.shape) for leaf in late_grads],
+            out_specs=[pl.BlockSpec((1, 1, all_rows, span), routed_block)]
+            + [full(leaf.shape) for leaf in late_grads],
             scratch_shapes=[
                 pltpu.VMEM((2 * width, rows), BF16),
                 pltpu.VMEM((2 * width, rows), BF16),
                 pltpu.VMEM((width, rows), F32),
                 pltpu.VMEM((blocks, width, span), F32),
                 pltpu.VMEM((blocks, width, span), F32),
-                pltpu.VMEM((model, head + 2 * width + 128), F32),
+                pltpu.VMEM((model + 16, head + 2 * width + 128), F32),
+                pltpu.VMEM((2 * all_rows, half), BF16),
+                pltpu.SemaphoreType.DMA((2,)),
             ],
         ),
         out_shape=[r_s] + late_grads,
@@ -965,6 +1033,9 @@
         slot,
         grad_logits,
         order,
+        columns,
+        proj,
+        proj_other,
     )
 
     if aligned:
@@ -982,57 +1053,58 @@
         mid_received = send_stage(mid_sums, "expert")
         late_received = send_stage(late_sums, "dp")
 
-    input_grad, small1 = pl.pallas_call(
+    input_grad = pl.pallas_call(
         input_kernel,
         name="input_back",
         grid_spec=pltpu.PrefetchScalarGridSpec(
             num_scalar_prefetch=1,
-            grid=grid,
+            grid=(micro_count, blocks // group),
             in_specs=[
-                blocked(states.shape),
-                blocked(state_s.shape),
+                grouped(states.shape, group),
+                grouped(state_s.shape, group),
                 blocked(r_s.shape),
                 in_place(),
                 in_place(),
                 full(vectors.shape),
             ],
-            out_specs=[blocked(state_s.shape), full((2, 8, model))],
+            out_specs=grouped(state_s.shape, group),
             scratch_shapes=[
                 pltpu.VMEM((2 * all_rows, half), BF16),
                 pltpu.SemaphoreType.DMA((2,)),
             ],
         ),
-        out_shape=[state_s, struct((2, 8, model), F32)],
+        out_shape=state_s,
         compiler_params=params(),
         cost_estimate=cost(2 * tokens * model * all_rows, 0, 40 << 20),
     )(ids[2:], states, mid, routed, proj, proj_other, vectors)
 
+    def open_heads(value):
+        return jnp.swapaxes(value.reshape(-1, own_experts, width), 0, 1)[None]
+
     if aligned:
-        small1, *received = lax.optimization_barrier((small1, *late_received, *mid_received))
+        input_grad, *received = lax.optimization_barrier(
+            (input_grad, *late_received, *mid_received)
+        )
         late_received = received[: dp_size - 1]
         mid_received = received[dp_size - 1 :]
-    small = jnp.concatenate([jnp.sum(small1, 1), jnp.sum(small2, 1)], 0)
-    small = jnp.swapaxes(small.reshape(5, devices, chunk), 0, 1).reshape(devices, 5 * chunk)
-    up_small = jnp.sum(up_small, 0).reshape(devices, hidden_units // devices)
-    packed = [small, up_small]
-
-    def open_heads(value):
-        return jnp.swapaxes(value.reshape(-1, own_experts, width), 0, 1)[None]
-
-    if aligned:
         late_sums = split_targets(add_up(late_sums[0], late_received), "expert")
-        packed[0], *late_sums = lax.optimization_barrier((packed[0], *late_sums))
-        packed = sum_packed(packed, devices)
+        late_received = send_stage(late_sums, "expert")
         mid_total = total_up(mid_sums[0], mid_received)
         up_weight_grad, at = open_tiles(mid_total, 0, chunk, hidden_units)
         down_weight_grad, at = open_tiles(mid_total, at, hidden_units // devices, model)
         out_weight_grad, at = open_tiles(mid_total, at, chunk * z_size, head // z_size)
-        late_received = send_stage(late_sums, "expert")
-        late_total = total_up(late_sums[0], late_received)
-        query_weight_grad, at = open_tiles(late_total, 0, chunk * z_size, head // z_size)
-        kv_grad = late_total[at : at + chunk]
-        router_grad = late_total[at + chunk : at + 2 * chunk, :experts]
-        query_weight_grad, out_weight_grad = map(open_heads, (query_weight_grad, out_weight_grad))
+        out_weight_grad = open_heads(out_weight_grad)
+        query_weight_grad, kv_grad, router_grad, up_bias_grad, *small = pl.pallas_call(
+            functools.partial(finish_kernel, experts, deep),
+            name="finish",
+            out_shape=[
+                struct((1, own_experts, chunk * z_size, width), F32),
+                struct((1, chunk, 2 * width), F32),
+                struct((1, chunk, experts), F32),
+                struct((1, deep * chunk), F32),
+            ]
+            + [struct((1, chunk), F32)] * 5,
+        )(late_sums[0], *late_received)
     else:
         down_grad, up_grad, wo_grad = mid_grads
         w_grad = late_grads[0]
@@ -1053,29 +1125,25 @@
         down_weight_grad = reduce_shared(down_grad, hidden_units // devices)
         out_weight_grad = reduce_heads(wo_grad)
         query_weight_grad = reduce_heads(w_grad[:, :head])
-        router_grad = w_grad[:, head + 2 * width : head + 2 * width + experts].astype(F32)
-        router_grad = permute_groups(router_grad.T.reshape(z_size, own_experts, model), z_at)
-        router_grad = router_grad.reshape(experts, model).T
-        kv_grad = w_grad[:, head : head + 2 * width].astype(F32)
-        packed += [kv_grad.reshape(devices, -1), router_grad.reshape(devices, -1)]
-        packed = sum_packed(packed, devices)
-        kv_grad = packed[2].reshape(chunk, 2 * width)
-        router_grad = packed[3].reshape(chunk, experts)
-    small = packed[0].reshape(5, 1, chunk)
+        narrow = reduce_shared(w_grad[:, head:], chunk)
+        kv_grad, router_grad = narrow[None, :, : 2 * width], narrow[None, :, 2 * width :]
+        small = [router_grad[:, :, experts + at] for at in range(5)]
+        up_bias_grad = router_grad[0, :, experts + 5 : experts + 5 + deep].T.reshape(1, -1)
+        router_grad = router_grad[:, :, :experts]
     shape = (micro_count, 1, slots, model)
     return (
         outputs.reshape(shape),
         input_grad.reshape(shape),
         small[0],
         small[1],
-        kv_grad[None],
-        router_grad[None],
+        kv_grad,
+        router_grad,
         query_weight_grad,
         out_weight_grad,
         small[2],
         small[3],
         up_weight_grad[None],
-        packed[1][None],
+        up_bias_grad,
         down_weight_grad[None],
         small[4],
     )

time: 223 us -> 217 us (0.973)
  waiting for transfers between devices: 19.9 us -> 13.7 us
  starting transfers between devices: 31 us -> 34.3 us
  Pallas kernels: 141 us -> 138 us
    ppermute x25, starting transfers between devices: 28.3 us -> 34.3 us  [exchange(): lax.ppermute(value, axis, [(at, at ^ distance) for at in range(count)])]
    ppermute x25, waiting for transfers between devices: 19.6 us -> 13.7 us  [exchange(): lax.ppermute(value, axis, [(at, at ^ distance) for at in range(count)])]
    pallas_call x1, Pallas kernels: 36.3 us -> 32.8 us  [local(): pl.pallas_call(backward_kernel, name='backward', grid_spec=pltpu.Prefetch...]
    all_to_all x1 -> x0, starting transfers between devices: 2.69 us -> none  [sum_packed(): lax.all_to_all(packed, AXES, split_axis=0, concat_axis=0, tiled=True)]
    unnamed x37 -> x36, local copies, waits for them, and re-layouts: 5.6 us -> 4.86 us
  transfers between devices with their start and end apart: 26 -> 25, of which waited for: 8 -> 7; matrix products, arithmetic and copies ran while one was open for 7% -> 9% of each run, Pallas kernels for 38% -> 37%
where the time goes in v4:
time: 217 us; the launch traced here: 216 us
  Pallas kernels  138 us (64%)
  starting transfers between devices  34.3 us (16%)
  other arithmetic  15 us (7%)
  waiting for transfers between devices  13.7 us (6%)
  local copies, waits for them, and re-layouts  13.5 us (6%)
    pallas_call x1, Pallas kernels, local(): pl.pallas_call(middle_kernel, name='middle', grid_spec=pltpu.PrefetchScal...  57.3 us
    ppermute x25, starting transfers between devices, exchange(): lax.ppermute(value, axis, [(at, at ^ distance) for at in range(count)])  34.3 us
    pallas_call x1, Pallas kernels, local(): pl.pallas_call(forward_kernel, name='forward', grid_spec=pltpu.PrefetchSc...  34.1 us
    pallas_call x1, Pallas kernels, local(): pl.pallas_call(backward_kernel, name='backward', grid_spec=pltpu.Prefetch...  32.8 us
    ppermute x25, waiting for transfers between devices, exchange(): lax.ppermute(value, axis, [(at, at ^ distance) for at in range(count)])  13.7 us
    pallas_call x1, Pallas kernels, local(): pl.pallas_call(input_kernel, name='input_back', grid_spec=pltpu.PrefetchS...  12.2 us
    convert_element_type x2, other arithmetic, core_stage(): (keep[at].astype(F32) + other[at].astype(F32)).astype(BF16)  5.69 us
    unnamed x36, local copies, waits for them, and re-layouts  4.86 us
  transfers between devices with their start and end apart: 25, of which 7 were waited for; matrix products, arithmetic and copies ran while one was open for 9% of the time, Pallas kernels for 37%

profile of v4, /device:TPU:0, one launch (start us, length us, event | category | flops | bytes accessed | tf_op | source)
XLA Modules:
  0.0 216.0 jit_solution(9856336135016866365)
XLA Ops:
  0.7 3.1 %collective-permute-start.1 = (bf16[384,256]{1,0:T(8,128)(2,1)}, bf16[384,256]{1,0:T(8,128)(2,1)S(1)}, u32[]{:S(2)}, u32[]{:S(2)}) collective-permute-start(bf16[384,256]{1,0:T(8,128)(2,1)} %bitcast.108), channel_id=1, source_target_pairs={{0,2},{2,0},{4,6},{6,4},{1,3},{3,1},{5,7},{7,5},{8,10},{10,8},{12,... | collective-permute-start | bytes 589832 | tf_op jit(solution)/shard_map/ppermute | solution.py:679
  3.8 2.6 %collective-permute-start.2 = (bf16[384,256]{1,0:T(8,128)(2,1)}, bf16[384,256]{1,0:T(8,128)(2,1)S(1)}, u32[]{:S(2)}, u32[]{:S(2)}) collective-permute-start(bf16[384,256]{1,0:T(8,128)(2,1)} %bitcast.109), channel_id=1, source_target_pairs={{0,4},{2,6},{4,0},{6,2},{1,5},{3,7},{5,1},{7,3},{8,12},{10,14},{12... | collective-permute-start | bytes 589832 | tf_op jit(solution)/shard_map/ppermute | solution.py:679
  6.4 0.7 reduce.1
  7.1 0.9 concatenate.47
  8.0 0.7 reshape_reshape.6
  8.7 0.7 reshape.227
  9.5 0.9 broadcast_remainder_fusion
  10.3 0.9 sign_compare_fusion
  11.3 0.7 select_select_fusion
  12.0 0.7 fusion.11.route_ref
  12.7 0.6 pad_add_fusion.ids
  13.3 0.8 concatenate.46
  14.0 0.9 copy.53
  15.0 0.7 dynamic-slice_reduce_fusion.lens
  15.7 0.6 fusion.13.vec_ref
  16.3 1.4 fusion.12.up_shift_ref
  17.7 3.4 %collective-permute-done.2 = bf16[384,256]{1,0:T(8,128)(2,1)S(1)} collective-permute-done((bf16[384,256]{1,0:T(8,128)(2,1)}, bf16[384,256]{1,0:T(8,128)(2,1)S(1)}, u32[]{:S(2)}, u32[]{:S(2)}) %collective-permute-start.2) | collective-permute-done | bytes 196640 | tf_op jit(solution)/shard_map/ppermute | solution.py:679
  21.1 0.9 constant_dynamic-update-slice_fusion.4
  22.3 0.5 collective-permute-start.10
  22.8 2.3 %collective-permute-done.4.other_ref = bf16[1696,256]{1,0:T(8,128)(2,1)S(1)} collective-permute-done((bf16[1696,256]{1,0:T(8,128)(2,1)S(1)}, bf16[1696,256]{1,0:T(8,128)(2,1)S(1)}, u32[]{:S(2)}, u32[]{:S(2)}) %collective-permute-start.4) | collective-permute-done | bytes 868384 | tf_op jit(solution)/shard_map/ppermute | solution.py:679
  25.1 3.4 %collective-permute-start.5 = (bf16[384,256]{1,0:T(8,128)(2,1)S(1)}, bf16[384,256]{1,0:T(8,128)(2,1)S(1)}, u32[]{:S(2)}, u32[]{:S(2)}) collective-permute-start(bf16[384,256]{1,0:T(8,128)(2,1)S(1)} %bitcast.112), channel_id=1, source_target_pairs={{0,2},{2,0},{4,6},{6,4},{1,3},{3,1},{5,7},{7,5},{8,10},{10,8},{12,... | collective-permute-start | bytes 589832 | tf_op jit(solution)/shard_map/ppermute | solution.py:679
  28.5 1.1 collective-permute-start.6
  29.5 1.4 collective-permute-start.7
  30.9 34.1 %forward.1 = (bf16[2,4,256,512]{3,2,1,0:T(8,128)(2,1)}, bf16[2,4,256,128]{3,2,1,0:T(8,128)(2,1)}, bf16[2,4,256,128]{3,2,1,0:T(8,128)(2,1)}, bf16[2,4,1,64,256]{4...) custom-call(s32[2]{0:T(128)} %dynamic-slice_reduce_fusion.lens, ...), custom_call_target="tpu_custom_call" | custom-call | flops 20736638976 | bytes 67108864 | tf_op jit(solution)/shard_map/forward/pallas_call | solution.py:829
  65.3 2.3 %collective-permute-done.8.other_ref = bf16[1536,256]{1,0:T(8,128)(2,1)S(1)} collective-permute-done((bf16[1536,256]{1,0:T(8,128)(2,1)S(1)}, bf16[1536,256]{1,0:T(8,128)(2,1)S(1)}, u32[]{:S(2)}, u32[]{:S(2)}) %collective-permute-start.8) | collective-permute-done | bytes 786464 | tf_op jit(solution)/shard_map/ppermute | solution.py:679
  67.5 0.9 copy-done.11
  68.4 57.3 %middle.1 = (f32[2,4,256,512]{3,2,1,0:T(8,128)}, f32[2,4,256,512]{3,2,1,0:T(8,128)}, bf16[2,4,64,2048]{3,2,1,0:T(8,128)(2,1)}, f32[2,4,1,2048]{3,2,1,0:T(1,128)}...) custom-call(s32[2]{0:T(128)} %dynamic-slice_reduce_fusion.lens, ...), custom_call_target="tpu_custom_call" | custom-call | flops 35433480192 | bytes 209715200 | tf_op jit(solution)/shard_map/middle/pallas_call | solution.py:884
  125.7 0.2 collective-permute-start.11
  125.9 0.6 pad_convert_fusion.order_ref
  126.5 0.7 slice_bitcast_fusion.8
  127.3 0.9 reduce_sum.19
  128.1 0.1 reshape.236
  128.3 0.8 reduce_sum.18
  129.2 0.1 copy.55
  129.3 0.9 pad.17.columns_ref
  130.2 1.1 collective-permute-done.11
  131.3 4.1 %fusion.3 = (bf16[4,704,128]{2,1,0:T(8,128)(2,1)}, bf16[4,704,128]{2,1,0:T(8,128)(2,1)}, bf16[4,704,128]{2,1,0:T(8,128)(2,1)}, bf16[4,704,128]{2,1,0:T(8,128)(2,1)}) fusion(bf16[4,4,704,128]{3,2,1,0:T(8,128)(2,1)S(1)} %collective-permute-done.11, bf16[4,4,704,128]{3,2,1,0:T(8,128)(2,1)} %get-tuple-element.120), kind=kLoop, calls=%fused_computation.8 | loop fusion | flops 5767168 | bytes 8650752 | tf_op jit(solution)/shard_map/convert_element_type | solution.py:710
  135.4 0.6 collective-permute-start.12
  135.9 1.6 collective-permute-start.13
  137.6 1.3 collective-permute-start.14
  138.8 32.8 %backward.1 = (bf16[2,2,1696,512]{3,2,1,0:T(8,128)(2,1)}, bf16[4,4,224,128]{3,2,1,0:T(8,128)(2,1)}, bf16[4,4,224,128]{3,2,1,0:T(8,128)(2,1)}) custom-call(s32[2]{0:T(128)} %dynamic-slice_reduce_fusion.lens, s32[3]{0:T(128)} %pad_add_fusion.ids, bf16[2,4,256,512]{3,2,1,0:T(8,128)(2,1)} %get-tuple-element.113.hid_ref, ...), custom_call_target="tpu_custom_call" | custom-call | flops 46506442752 | bytes 104857600 | tf_op jit(solution)/shard_map/backward/pallas_call | solution.py:984
  171.7 2.7 %collective-permute-done.15 = bf16[4,4,224,128]{3,2,1,0:T(8,128)(2,1)S(1)} collective-permute-done((bf16[4,4,224,128]{3,2,1,0:T(8,128)(2,1)}, bf16[4,4,224,128]{3,2,1,0:T(8,128)(2,1)S(1)}, u32[]{:S(2)}, u32[]{:S(2)}) %collective-permute-start.15) | collective-permute-done | bytes 917536 | tf_op jit(solution)/shard_map/ppermute | solution.py:679
  174.4 1.6 fusion.7
  176.0 0.4 add_convert_fusion
  176.6 0.5 copy-done.10
  177.1 0.6 slice.95.ids
  177.7 3.4 %collective-permute-start.16 = (bf16[4,224,128]{2,1,0:T(8,128)(2,1)S(1)}, bf16[4,224,128]{2,1,0:T(8,128)(2,1)S(1)}, u32[]{:S(2)}, u32[]{:S(2)}) collective-permute-start(bf16[4,224,128]{2,1,0:T(8,128)(2,1)S(1)} %get-tuple-element.144), channel_id=1, source_target_pairs={{0,8},{8,0},{16,24},{24,16},{1,9},{9,1},{17,25},{25,17},{2,10},{10... | collective-permute-start | bytes 688136 | tf_op jit(solution)/shard_map/ppermute | solution.py:679
  181.1 1.5 collective-permute-start.18
  182.6 6.2 %collective-permute-start.20 = (bf16[704,128]{1,0:T(8,128)(2,1)S(1)}, bf16[704,128]{1,0:T(8,128)(2,1)S(1)}, u32[]{:S(2)}, u32[]{:S(2)}) collective-permute-start(bf16[704,128]{1,0:T(8,128)(2,1)S(1)} %get-tuple-element.148), channel_id=1, source_target_pairs={{0,4},{2,6},{4,0},{6,2},{1,5},{3,7},{5,1},{7,3},{8,12},{10,14},{12... | collective-permute-start | bytes 540680 | tf_op jit(solution)/shard_map/ppermute | solution.py:679
  188.8 0.5 collective-permute-start.21
  189.3 12.2 %input_back.1 = f32[2,4,256,512]{3,2,1,0:T(8,128)} custom-call(s32[1]{0:T(128)} %slice.95.ids, bf16[2,4,256,512]{3,2,1,0:T(8,128)(2,1)} %bitcast.100, f32[2,4,256,512]{3,2,1,0:T(8,128)} %get-tuple-element.112.mid_ref, bf16[2,2,1696,512]{3,2,1,0:T(8,128)(2,1)} %get-tuple-element.143.r_ref, bf16[1696,256]{1,0:T(8,128)(2,1)} %copy-done.3, ...), custom_call_target="tpu_custom_call" | custom-call | flops 3556769792 | bytes 41943040 | tf_op jit(solution)/shard_map/input_back/pallas_call | solution.py:1056
  201.5 0.1 add_convert_fusion.5
  201.7 0.6 slice_bitcast_fusion.4
  202.3 3.5 %collective-permute-start.22 = (bf16[224,128]{1,0:T(8,128)(2,1)S(1)}, bf16[224,128]{1,0:T(8,128)(2,1)S(1)}, u32[]{:S(2)}, u32[]{:S(2)}) collective-permute-start(bf16[224,128]{1,0:T(8,128)(2,1)S(1)} %get-tuple-element.240), channel_id=1, source_target_pairs={{0,2},{2,0},{4,6},{6,4},{1,3},{3,1},{5,7},{7,5},{8,10},{10,8},{12,... | collective-permute-start | bytes 172040 | tf_op jit(solution)/shard_map/ppermute | solution.py:679
  205.8 1.6 collective-permute-start.23
  207.4 1.5 collective-permute-start.24
  209.1 0.7 broadcast_in_dim_reshape.6
  209.8 0.7 broadcast_in_dim_reshape.7
  210.5 0.1 copy.56
  210.7 0.8 copy.61
  211.5 1.0 collective-permute-done.23.refs_2_
  212.5 0.9 collective-permute-done.24.refs_3_
  213.4 0.6 copy-done.8
  214.1 1.8 finish.1
  (77 shorter events, 1.2 us)
Async XLA Ops:
  0.6 14.3 %copy-start = (s32[2,32]{1,0:T(2,128)S(1)}, s32[2,32]{1,0:T(2,128)}, u32[]{:S(2)}) copy-start(s32[2,32]{1,0:T(2,128)} %param.17) | copy-start | bytes 772
  0.7 24.4 %copy-start.5 = (bf16[1,6,256,64]{2,3,1,0:T(8,128)(2,1)S(1)}, bf16[1,6,256,64]{2,3,1,0:T(8,128)(2,1)}, u32[]{:S(2)}) copy-start(bf16[1,6,256,64]{2,3,1,0:T(8,128)(2,1)} %param.24) | copy-start | bytes 589828
  0.7 17.0 %collective-permute-start.1 = (bf16[384,256]{1,0:T(8,128)(2,1)}, bf16[384,256]{1,0:T(8,128)(2,1)S(1)}, u32[]{:S(2)}, u32[]{:S(2)}) collective-permute-start(bf16[384,256]{1,0:T(8,128)(2,1)} %bitcast.108), channel_id=1, source_target_pairs={{0,2},{2,0},{4,6},{6,4},{1,3},{3,1},{5,7},{7,5},{8,10},{10,8},{12,... | collective-permute-start | bytes 589832 | tf_op jit(solution)/shard_map/ppermute | solution.py:679
  3.8 17.4 %collective-permute-start.2 = (bf16[384,256]{1,0:T(8,128)(2,1)}, bf16[384,256]{1,0:T(8,128)(2,1)S(1)}, u32[]{:S(2)}, u32[]{:S(2)}) collective-permute-start(bf16[384,256]{1,0:T(8,128)(2,1)} %bitcast.109), channel_id=1, source_target_pairs={{0,4},{2,6},{4,0},{6,2},{1,5},{3,7},{5,1},{7,3},{8,12},{10,14},{12... | collective-permute-start | bytes 589832 | tf_op jit(solution)/shard_map/ppermute | solution.py:679
  6.3 14.8 %collective-permute-start.3 = (bf16[384,256]{1,0:T(8,128)(2,1)}, bf16[384,256]{1,0:T(8,128)(2,1)S(1)}, u32[]{:S(2)}, u32[]{:S(2)}) collective-permute-start(bf16[384,256]{1,0:T(8,128)(2,1)} %bitcast.110), channel_id=1, source_target_pairs={{0,6},{2,4},{4,2},{6,0},{1,7},{3,5},{5,3},{7,1},{8,14},{10,12},{12... | collective-permute-start | bytes 589832 | tf_op jit(solution)/shard_map/ppermute | solution.py:679
  7.9 7.8 %collective-permute-start = (bf16[9,256]{1,0:T(8,128)(2,1)S(1)}, bf16[9,256]{1,0:T(8,128)(2,1)S(1)}, u32[]{:S(2)}, u32[]{:S(2)}) collective-permute-start(bf16[9,256]{1,0:T(8,128)(2,1)S(1)} %concatenate.47), channel_id=1, source_target_pairs={{0,1},{1,0},{2,3},{3,2},{4,5},{5,4},{6,7},{7,6},{8,9},{9,8},{10,11... | collective-permute-start | bytes 13832 | tf_op jit(solution)/shard_map/ppermute | solution.py:679
  22.2 8.8 %copy-start.3 = (bf16[1696,256]{1,0:T(8,128)(2,1)}, bf16[1696,256]{1,0:T(8,128)(2,1)S(1)}, u32[]{:S(2)}) copy-start(bf16[1696,256]{1,0:T(8,128)(2,1)S(1)} %constant_dynamic-update-slice_fusion.own_ref) | copy-start | bytes 2605060
  22.2 2.9 %collective-permute-start.4 = (bf16[1696,256]{1,0:T(8,128)(2,1)S(1)}, bf16[1696,256]{1,0:T(8,128)(2,1)S(1)}, u32[]{:S(2)}, u32[]{:S(2)}) collective-permute-start(bf16[1696,256]{1,0:T(8,128)(2,1)S(1)} %constant_dynamic-update-slice_fusion.own_ref), channel_id=1, source_target_pairs={{0,1},{1,0},{2,3},{3,2},{4,5},{5,4},{6,7},{7,6},{8,9},{9,8},{10,11... | collective-permute-start | bytes 2605064 | tf_op jit(solution)/shard_map/ppermute | solution.py:679
  22.3 43.0 %collective-permute-start.10 = (bf16[1024,512]{1,0:T(8,128)(2,1)}, bf16[1024,512]{1,0:T(8,128)(2,1)}, u32[]{:S(2)}, u32[]{:S(2)}) collective-permute-start(bf16[1024,512]{1,0:T(8,128)(2,1)} %bitcast.24.own_down_ref), channel_id=1, source_target_pairs={{0,1},{1,0},{2,3},{3,2},{4,5},{5,4},{6,7},{7,6},{8,9},{9,8},{10,11... | collective-permute-start | bytes 3145736 | tf_op jit(solution)/shard_map/ppermute | solution.py:679
  22.8 42.5 %collective-permute-start.9 = (bf16[256,2048]{1,0:T(8,128)(2,1)}, bf16[256,2048]{1,0:T(8,128)(2,1)}, u32[]{:S(2)}, u32[]{:S(2)}) collective-permute-start(bf16[256,2048]{1,0:T(8,128)(2,1)} %bitcast.23.own_up_ref), channel_id=1, source_target_pairs={{0,1},{1,0},{2,3},{3,2},{4,5},{5,4},{6,7},{7,6},{8,9},{9,8},{10,11... | collective-permute-start | bytes 3145736 | tf_op jit(solution)/shard_map/ppermute | solution.py:679
  25.1 5.8 %copy-start.4 = (bf16[1696,256]{1,0:T(8,128)(2,1)}, bf16[1696,256]{1,0:T(8,128)(2,1)S(1)}, u32[]{:S(2)}) copy-start(bf16[1696,256]{1,0:T(8,128)(2,1)S(1)} %collective-permute-done.4.other_ref) | copy-start | bytes 2605060
  25.1 39.9 %collective-permute-start.5 = (bf16[384,256]{1,0:T(8,128)(2,1)S(1)}, bf16[384,256]{1,0:T(8,128)(2,1)S(1)}, u32[]{:S(2)}, u32[]{:S(2)}) collective-permute-start(bf16[384,256]{1,0:T(8,128)(2,1)S(1)} %bitcast.112), channel_id=1, source_target_pairs={{0,2},{2,0},{4,6},{6,4},{1,3},{3,1},{5,7},{7,5},{8,10},{10,8},{12,... | collective-permute-start | bytes 589832 | tf_op jit(solution)/shard_map/ppermute | solution.py:679
  28.5 36.6 %collective-permute-start.6 = (bf16[384,256]{1,0:T(8,128)(2,1)S(1)}, bf16[384,256]{1,0:T(8,128)(2,1)S(1)}, u32[]{:S(2)}, u32[]{:S(2)}) collective-permute-start(bf16[384,256]{1,0:T(8,128)(2,1)S(1)} %bitcast.113), channel_id=1, source_target_pairs={{0,4},{2,6},{4,0},{6,2},{1,5},{3,7},{5,1},{7,3},{8,12},{10,14},{12... | collective-permute-start | bytes 589832 | tf_op jit(solution)/shard_map/ppermute | solution.py:679
  29.5 35.5 %collective-permute-start.7 = (bf16[384,256]{1,0:T(8,128)(2,1)S(1)}, bf16[384,256]{1,0:T(8,128)(2,1)S(1)}, u32[]{:S(2)}, u32[]{:S(2)}) collective-permute-start(bf16[384,256]{1,0:T(8,128)(2,1)S(1)} %bitcast.114), channel_id=1, source_target_pairs={{0,6},{2,4},{4,2},{6,0},{1,7},{3,5},{5,3},{7,1},{8,14},{10,12},{12... | collective-permute-start | bytes 589832 | tf_op jit(solution)/shard_map/ppermute | solution.py:679
  65.2 2.4 %copy-start.9 = (bf16[1536,256]{1,0:T(8,128)(2,1)}, bf16[1536,256]{1,0:T(8,128)(2,1)S(1)}, u32[]{:S(2)}) copy-start(bf16[1536,256]{1,0:T(8,128)(2,1)S(1)} %constant_dynamic-update-slice_fusion.5.own_ref) | copy-start | bytes 2359300
  65.2 2.4 %collective-permute-start.8 = (bf16[1536,256]{1,0:T(8,128)(2,1)S(1)}, bf16[1536,256]{1,0:T(8,128)(2,1)S(1)}, u32[]{:S(2)}, u32[]{:S(2)}) collective-permute-start(bf16[1536,256]{1,0:T(8,128)(2,1)S(1)} %constant_dynamic-update-slice_fusion.5.own_ref), channel_id=1, source_target_pairs={{0,1},{1,0},{2,3},{3,2},{4,5},{5,4},{6,7},{7,6},{8,9},{9,8},{10,11... | collective-permute-start | bytes 2359304 | tf_op jit(solution)/shard_map/ppermute | solution.py:679
  67.5 0.9 copy-start.11
  125.7 5.6 %collective-permute-start.11 = (bf16[4,4,704,128]{3,2,1,0:T(8,128)(2,1)}, bf16[4,4,704,128]{3,2,1,0:T(8,128)(2,1)S(1)}, u32[]{:S(2)}, u32[]{:S(2)}) collective-permute-start(bf16[4,4,704,128]{3,2,1,0:T(8,128)(2,1)} %get-tuple-element.121), channel_id=1, source_target_pairs={{0,1},{1,0},{2,3},{3,2},{4,5},{5,4},{6,7},{7,6},{8,9},{9,8},{10,11... | collective-permute-start | bytes 8650760 | tf_op jit(solution)/shard_map/ppermute | solution.py:679
  135.4 36.3 %collective-permute-start.12 = (bf16[4,704,128]{2,1,0:T(8,128)(2,1)}, bf16[4,704,128]{2,1,0:T(8,128)(2,1)S(1)}, u32[]{:S(2)}, u32[]{:S(2)}) collective-permute-start(bf16[4,704,128]{2,1,0:T(8,128)(2,1)} %get-tuple-element.129), channel_id=1, source_target_pairs={{0,8},{8,0},{16,24},{24,16},{1,9},{9,1},{17,25},{25,17},{2,10},{10... | collective-permute-start | bytes 2162696 | tf_op jit(solution)/shard_map/ppermute | solution.py:679
  135.9 35.7 %collective-permute-start.13 = (bf16[4,704,128]{2,1,0:T(8,128)(2,1)}, bf16[4,704,128]{2,1,0:T(8,128)(2,1)S(1)}, u32[]{:S(2)}, u32[]{:S(2)}) collective-permute-start(bf16[4,704,128]{2,1,0:T(8,128)(2,1)} %get-tuple-element.130), channel_id=1, source_target_pairs={{0,16},{8,24},{16,0},{24,8},{1,17},{9,25},{17,1},{25,9},{2,18},{10... | collective-permute-start | bytes 2162696 | tf_op jit(solution)/shard_map/ppermute | solution.py:679
  137.6 34.1 %collective-permute-start.14 = (bf16[4,704,128]{2,1,0:T(8,128)(2,1)}, bf16[4,704,128]{2,1,0:T(8,128)(2,1)S(1)}, u32[]{:S(2)}, u32[]{:S(2)}) collective-permute-start(bf16[4,704,128]{2,1,0:T(8,128)(2,1)} %get-tuple-element.131), channel_id=1, source_target_pairs={{0,24},{8,16},{16,8},{24,0},{1,25},{9,17},{17,9},{25,1},{2,26},{10... | collective-permute-start | bytes 2162696 | tf_op jit(solution)/shard_map/ppermute | solution.py:679
  171.6 4.4 %copy-start.2 = (bf16[4,704,128]{2,1,0:T(8,128)(2,1)S(1)}, bf16[4,704,128]{2,1,0:T(8,128)(2,1)}, u32[]{:S(2)}) copy-start(bf16[4,704,128]{2,1,0:T(8,128)(2,1)} %get-tuple-element.128) | copy-start | bytes 2162692
  171.7 2.7 %collective-permute-start.15 = (bf16[4,4,224,128]{3,2,1,0:T(8,128)(2,1)}, bf16[4,4,224,128]{3,2,1,0:T(8,128)(2,1)S(1)}, u32[]{:S(2)}, u32[]{:S(2)}) collective-permute-start(bf16[4,4,224,128]{3,2,1,0:T(8,128)(2,1)} %get-tuple-element.138), channel_id=1, source_target_pairs={{0,1},{1,0},{2,3},{3,2},{4,5},{5,4},{6,7},{7,6},{8,9},{9,8},{10,11... | collective-permute-start | bytes 2752520 | tf_op jit(solution)/shard_map/ppermute | solution.py:679
  176.4 0.7 copy-start.10
  176.5 12.3 %collective-permute-start.19 = (bf16[704,128]{1,0:T(8,128)(2,1)S(1)}, bf16[704,128]{1,0:T(8,128)(2,1)S(1)}, u32[]{:S(2)}, u32[]{:S(2)}) collective-permute-start(bf16[704,128]{1,0:T(8,128)(2,1)S(1)} %get-tuple-element.147), channel_id=1, source_target_pairs={{0,2},{2,0},{4,6},{6,4},{1,3},{3,1},{5,7},{7,5},{8,10},{10,8},{12,... | collective-permute-start | bytes 540680 | tf_op jit(solution)/shard_map/ppermute | solution.py:679
  177.7 23.9 %collective-permute-start.16 = (bf16[4,224,128]{2,1,0:T(8,128)(2,1)S(1)}, bf16[4,224,128]{2,1,0:T(8,128)(2,1)S(1)}, u32[]{:S(2)}, u32[]{:S(2)}) collective-permute-start(bf16[4,224,128]{2,1,0:T(8,128)(2,1)S(1)} %get-tuple-element.144), channel_id=1, source_target_pairs={{0,8},{8,0},{16,24},{24,16},{1,9},{9,1},{17,25},{25,17},{2,10},{10... | collective-permute-start | bytes 688136 | tf_op jit(solution)/shard_map/ppermute | solution.py:679
  181.1 20.4 %collective-permute-start.17 = (bf16[4,224,128]{2,1,0:T(8,128)(2,1)S(1)}, bf16[4,224,128]{2,1,0:T(8,128)(2,1)S(1)}, u32[]{:S(2)}, u32[]{:S(2)}) collective-permute-start(bf16[4,224,128]{2,1,0:T(8,128)(2,1)S(1)} %get-tuple-element.145), channel_id=1, source_target_pairs={{0,16},{8,24},{16,0},{24,8},{1,17},{9,25},{17,1},{25,9},{2,18},{10... | collective-permute-start | bytes 688136 | tf_op jit(solution)/shard_map/ppermute | solution.py:679
  181.1 20.4 %collective-permute-start.18 = (bf16[4,224,128]{2,1,0:T(8,128)(2,1)S(1)}, bf16[4,224,128]{2,1,0:T(8,128)(2,1)S(1)}, u32[]{:S(2)}, u32[]{:S(2)}) collective-permute-start(bf16[4,224,128]{2,1,0:T(8,128)(2,1)S(1)} %get-tuple-element.146), channel_id=1, source_target_pairs={{0,24},{8,16},{16,8},{24,0},{1,25},{9,17},{17,9},{25,1},{2,26},{10... | collective-permute-start | bytes 688136 | tf_op jit(solution)/shard_map/ppermute | solution.py:679
  182.6 18.9 %collective-permute-start.20 = (bf16[704,128]{1,0:T(8,128)(2,1)S(1)}, bf16[704,128]{1,0:T(8,128)(2,1)S(1)}, u32[]{:S(2)}, u32[]{:S(2)}) collective-permute-start(bf16[704,128]{1,0:T(8,128)(2,1)S(1)} %get-tuple-element.148), channel_id=1, source_target_pairs={{0,4},{2,6},{4,0},{6,2},{1,5},{3,7},{5,1},{7,3},{8,12},{10,14},{12... | collective-permute-start | bytes 540680 | tf_op jit(solution)/shard_map/ppermute | solution.py:679
  188.8 12.7 %collective-permute-start.21 = (bf16[704,128]{1,0:T(8,128)(2,1)S(1)}, bf16[704,128]{1,0:T(8,128)(2,1)S(1)}, u32[]{:S(2)}, u32[]{:S(2)}) collective-permute-start(bf16[704,128]{1,0:T(8,128)(2,1)S(1)} %get-tuple-element.149), channel_id=1, source_target_pairs={{0,6},{2,4},{4,2},{6,0},{1,7},{3,5},{5,3},{7,1},{8,14},{10,12},{12... | collective-permute-start | bytes 540680 | tf_op jit(solution)/shard_map/ppermute | solution.py:679
  202.3 9.2 %collective-permute-start.22 = (bf16[224,128]{1,0:T(8,128)(2,1)S(1)}, bf16[224,128]{1,0:T(8,128)(2,1)S(1)}, u32[]{:S(2)}, u32[]{:S(2)}) collective-permute-start(bf16[224,128]{1,0:T(8,128)(2,1)S(1)} %get-tuple-element.240), channel_id=1, source_target_pairs={{0,2},{2,0},{4,6},{6,4},{1,3},{3,1},{5,7},{7,5},{8,10},{10,8},{12,... | collective-permute-start | bytes 172040 | tf_op jit(solution)/shard_map/ppermute | solution.py:679
  205.8 6.7 %collective-permute-start.23 = (bf16[224,128]{1,0:T(8,128)(2,1)S(1)}, bf16[224,128]{1,0:T(8,128)(2,1)S(1)}, u32[]{:S(2)}, u32[]{:S(2)}) collective-permute-start(bf16[224,128]{1,0:T(8,128)(2,1)S(1)} %get-tuple-element.239), channel_id=1, source_target_pairs={{0,4},{2,6},{4,0},{6,2},{1,5},{3,7},{5,1},{7,3},{8,12},{10,14},{12... | collective-permute-start | bytes 172040 | tf_op jit(solution)/shard_map/ppermute | solution.py:679
  207.4 6.0 %collective-permute-start.24 = (bf16[224,128]{1,0:T(8,128)(2,1)S(1)}, bf16[224,128]{1,0:T(8,128)(2,1)S(1)}, u32[]{:S(2)}, u32[]{:S(2)}) collective-permute-start(bf16[224,128]{1,0:T(8,128)(2,1)S(1)} %get-tuple-element.238), channel_id=1, source_target_pairs={{0,6},{2,4},{4,2},{6,0},{1,7},{3,5},{5,3},{7,1},{8,14},{10,12},{12... | collective-permute-start | bytes 172040 | tf_op jit(solution)/shard_map/ppermute | solution.py:679
  208.9 7.0 %copy-start.1 = (s32[2,32]{1,0:T(2,128)S(1)}, s32[2,32]{1,0:T(2,128)}, u32[]{:S(2)}) copy-start(s32[2,32]{1,0:T(2,128)} %param.17) | copy-start | bytes 772
  211.5 2.0 copy-start.6
  212.5 1.0 copy-start.7
  213.4 0.6 copy-start.8

commit v5 on v4

--- a/solution.py
+++ b/solution.py
@@ -49,6 +49,7 @@
 def pick_slots(table_ref, slot, picks, width, start=0):
     experts, span = slot.shape
     lanes = slice(start, start + span)
+    slot = slot.astype(table_ref.dtype)
     picked = []
     for pick in range(picks):
         value = table_ref[pick * width : (pick + 1) * width, lanes]
@@ -62,7 +63,7 @@
 def spread_slots(read, slot, expert, picks, width, span):
     experts = slot.shape[0]
     row = jnp.broadcast_to(slot[expert : expert + 1, :], (width, span))
-    value = jnp.zeros((width, span), F32)
+    value = jnp.zeros((width, span), slot.dtype)
     for pick in range(max(0, expert - experts + picks), min(expert, picks - 1) + 1):
         value = jnp.where(row == pick, read(pick), value)
     return value
@@ -110,10 +111,11 @@
     normed, _ = normalize(x_ref[0, 0].astype(F32))
     hid = (normed * vec_ref[0:1, :] + vec_ref[1:2, :]).astype(BF16)
     hid_ref[0, 0] = hid
-    table[...] = dot_nt(low[...], hid[:, :half]) + dot_nt(high[...], hid[:, half:])
     head = experts * width
-    kt_ref[0, 0, 0] = table[head : head + width, :].astype(BF16)
-    vt[block] = table[head + width : head + 2 * width, :].astype(BF16)
+    products = dot_nt(low[...], hid[:, :half]) + dot_nt(high[...], hid[:, half:])
+    table[...] = products[:head].astype(BF16)
+    kt_ref[0, 0, 0] = products[head : head + width, :].astype(BF16)
+    vt[block] = products[head + width : head + 2 * width, :].astype(BF16)
 
     lane = lax.broadcasted_iota(jnp.int32, (span, 2 * width), 1)
     place = block * span + lax.broadcasted_iota(jnp.int32, (span, 2 * width), 0)
@@ -126,7 +128,7 @@
     vals = jnp.where(lane < width, pltpu.roll(both, width, 1), ones)
     vaug_ref[0, block] = vals.astype(BF16)
 
-    logits = table[head + 2 * width : head + 2 * width + experts, :]
+    logits = products[head + 2 * width : head + 2 * width + experts, :]
     expert_id = lax.broadcasted_iota(jnp.int32, (experts, span), 0)
     chosen = jnp.zeros((experts, span), F32)
     for pick in range(picks):
@@ -146,7 +148,7 @@
     picked = pick_slots(table, slot, picks, width)
     for pick in range(picks):
         qaug[0:width, pick * span : (pick + 1) * span] = (
-            picked[pick].astype(BF16) * (width**-0.5)
+            picked[pick] * (width**-0.5)
         ).astype(BF16)
     q_ref[0, 0] = qaug[0:width, :]
     side = lax.broadcasted_iota(jnp.int32, (width, rows), 0)
@@ -250,16 +252,16 @@
         )
         for pick in range(picks):
             at = slice(pick * span, (pick + 1) * span)
-            gated[sub, :, at] = ctx_ref[0, sub, :, at].astype(F32) * gate[sub][pick]
+            gated[sub, :, at] = (ctx_ref[0, sub, :, at].astype(F32) * gate[sub][pick]).astype(BF16)
         for expert in range(experts):
             cexp[expert * width : (expert + 1) * width, sub * span : (sub + 1) * span] = spread_slots(
                 lambda pick: gated[sub, :, pick * span : (pick + 1) * span],
-                slots[sub],
+                slots[sub].astype(BF16),
                 expert,
                 picks,
                 width,
                 span,
-            ).astype(BF16)
+            )
     mixed = x_ref[0].reshape(tokens, model).astype(F32) + jnp.concatenate(
         [dot_tn(cexp[...], low[...]), dot_tn(cexp[...], high[...])], 1
     )
@@ -317,7 +319,8 @@
 
     mid_b = mid.astype(BF16)
     wo_acc[...] += dot_nt(mid_b.T, cexp[...])
-    table[...] = dot_nt(low[...], mid_b[:, :half]) + dot_nt(high[...], mid_b[:, half:])
+    products = dot_nt(low[...], mid_b[:, :half]) + dot_nt(high[...], mid_b[:, half:])
+    table[...] = products.astype(BF16)
     for sub in range(subs):
         slot = slots[sub]
         picked = pick_slots(table, slot, picks, width, sub * span)
@@ -325,8 +328,9 @@
         for pick in range(picks):
             at = slice(pick * span, (pick + 1) * span)
             ctx = ctx_ref[0, sub, :, at].astype(F32)
-            grad_gate.append(jnp.sum(picked[pick] * ctx, 0, keepdims=True))
-            grad_ctx = (picked[pick] * gate[sub][pick]).astype(BF16)
+            found = picked[pick].astype(F32)
+            grad_gate.append(jnp.sum(found * ctx, 0, keepdims=True))
+            grad_ctx = (found * gate[sub][pick]).astype(BF16)
             do_ref[0, sub, :, at] = grad_ctx
             delta_ref[0, sub, :, at] = jnp.sum(grad_ctx.astype(F32) * ctx, 0, keepdims=True)
         average = gate[sub][0] * grad_gate[0]
@@ -525,17 +529,17 @@
             return carry
 
         lax.fori_loop(0, block, body, 0)
-        dq[...] = dq[...] * (width**-0.5)
-        slot = slot_ref[0, 0]
+        scaled = (dq[...] * (width**-0.5)).astype(BF16)
+        slot = slot_ref[0, 0].astype(BF16)
         for expert in range(experts):
             r_ref[0, 0, expert * width : (expert + 1) * width, :] = spread_slots(
-                lambda pick: dq[:, pick * span : (pick + 1) * span],
+                lambda pick: scaled[:, pick * span : (pick + 1) * span],
                 slot,
                 expert,
                 picks,
                 width,
                 span,
-            ).astype(BF16)
+            )
         r_ref[0, 0, head : head + width, :] = dkt[block].astype(BF16)
         r_ref[0, 0, head + width : head + 2 * width, :] = dvt[block].astype(BF16)
         tail = r_ref.shape[2] - head - 2 * width
@@ -851,7 +855,7 @@
                 blocked(slot_s.shape),
             ],
             scratch_shapes=[
-                pltpu.VMEM((all_rows, span), F32),
+                pltpu.VMEM((head, span), BF16),
                 pltpu.VMEM((2 * width, rows), BF16),
                 pltpu.VMEM((blocks, span, rows), F32),
                 pltpu.VMEM((blocks, width, span), BF16),
@@ -913,9 +917,9 @@
             ]
             + [full(leaf.shape) for leaf in mid_grads],
             scratch_shapes=[
-                pltpu.VMEM((group, width, rows), F32),
+                pltpu.VMEM((group, width, rows), BF16),
                 pltpu.VMEM((head, group * span), BF16),
-                pltpu.VMEM((head, group * span), F32),
+                pltpu.VMEM((head, group * span), BF16),
                 pltpu.VMEM((hidden_units, model), F32),
                 pltpu.VMEM((model, hidden_units), F32),
                 pltpu.VMEM((model, head), F32),

time: 217 us -> 211 us (0.972)
  Pallas kernels: 138 us -> 128 us
  waiting for transfers between devices: 13.7 us -> 17.9 us
    pallas_call x1, Pallas kernels: 32.8 us -> 27.1 us  [local(): pl.pallas_call(backward_kernel, name='backward', grid_spec=pltpu.Prefetch...]
    ppermute x25, waiting for transfers between devices: 13.7 us -> 17.9 us  [exchange(): lax.ppermute(value, axis, [(at, at ^ distance) for at in range(count)])]
    pallas_call x1, Pallas kernels: 57.3 us -> 55 us  [local(): pl.pallas_call(middle_kernel, name='middle', grid_spec=pltpu.PrefetchScal...]
  transfers between devices with their start and end apart: 25 -> 25, of which waited for: 7 -> 7; matrix products, arithmetic and copies ran while one was open for 9% -> 9% of each run, Pallas kernels for 37% -> 34%
where the time goes in v5:
time: 211 us; the launch traced here: 209 us
  Pallas kernels  128 us (61%)
  starting transfers between devices  33.2 us (16%)
  waiting for transfers between devices  17.9 us (8%)
  other arithmetic  15 us (7%)
  local copies, waits for them, and re-layouts  13 us (6%)
    pallas_call x1, Pallas kernels, local(): pl.pallas_call(middle_kernel, name='middle', grid_spec=pltpu.PrefetchScal...  55 us
    ppermute x25, starting transfers between devices, exchange(): lax.ppermute(value, axis, [(at, at ^ distance) for at in range(count)])  33.2 us
    pallas_call x1, Pallas kernels, local(): pl.pallas_call(forward_kernel, name='forward', grid_spec=pltpu.PrefetchSc...  32.4 us
    pallas_call x1, Pallas kernels, local(): pl.pallas_call(backward_kernel, name='backward', grid_spec=pltpu.Prefetch...  27.1 us
    ppermute x25, waiting for transfers between devices, exchange(): lax.ppermute(value, axis, [(at, at ^ distance) for at in range(count)])  17.9 us
    pallas_call x1, Pallas kernels, local(): pl.pallas_call(input_kernel, name='input_back', grid_spec=pltpu.PrefetchS...  12.2 us
    convert_element_type x2, other arithmetic, core_stage(): (keep[at].astype(F32) + other[at].astype(F32)).astype(BF16)  5.69 us
    unnamed x36, local copies, waits for them, and re-layouts  4.38 us
  transfers between devices with their start and end apart: 25, of which 7 were waited for; matrix products, arithmetic and copies ran while one was open for 9% of the time, Pallas kernels for 34%

profile of v5, /device:TPU:0, one launch (start us, length us, event | category | flops | bytes accessed | tf_op | source)
XLA Modules:
  0.0 208.9 jit_solution(13743669372943521683)
XLA Ops:
  0.7 3.1 %collective-permute-start.1 = (bf16[384,256]{1,0:T(8,128)(2,1)}, bf16[384,256]{1,0:T(8,128)(2,1)S(1)}, u32[]{:S(2)}, u32[]{:S(2)}) collective-permute-start(bf16[384,256]{1,0:T(8,128)(2,1)} %bitcast.108), channel_id=1, source_target_pairs={{0,2},{2,0},{4,6},{6,4},{1,3},{3,1},{5,7},{7,5},{8,10},{10,8},{12,... | collective-permute-start | bytes 589832 | tf_op jit(solution)/shard_map/ppermute | solution.py:683
  3.8 2.6 %collective-permute-start.2 = (bf16[384,256]{1,0:T(8,128)(2,1)}, bf16[384,256]{1,0:T(8,128)(2,1)S(1)}, u32[]{:S(2)}, u32[]{:S(2)}) collective-permute-start(bf16[384,256]{1,0:T(8,128)(2,1)} %bitcast.109), channel_id=1, source_target_pairs={{0,4},{2,6},{4,0},{6,2},{1,5},{3,7},{5,1},{7,3},{8,12},{10,14},{12... | collective-permute-start | bytes 589832 | tf_op jit(solution)/shard_map/ppermute | solution.py:683
  6.4 0.7 reduce.1
  7.1 0.9 concatenate.47
  8.0 0.7 reshape_reshape.6
  8.7 0.7 reshape.227
  9.5 0.9 broadcast_remainder_fusion
  10.3 0.9 sign_compare_fusion
  11.3 0.7 select_select_fusion
  12.0 0.7 fusion.11.route_ref
  12.7 0.6 pad_add_fusion.ids
  13.3 0.8 concatenate.46
  14.0 0.9 copy.53
  15.0 0.7 dynamic-slice_reduce_fusion.lens
  15.7 0.6 fusion.13.vec_ref
  16.3 1.4 fusion.12.up_shift_ref
  17.7 3.4 %collective-permute-done.2 = bf16[384,256]{1,0:T(8,128)(2,1)S(1)} collective-permute-done((bf16[384,256]{1,0:T(8,128)(2,1)}, bf16[384,256]{1,0:T(8,128)(2,1)S(1)}, u32[]{:S(2)}, u32[]{:S(2)}) %collective-permute-start.2) | collective-permute-done | bytes 196640 | tf_op jit(solution)/shard_map/ppermute | solution.py:683
  21.1 0.9 constant_dynamic-update-slice_fusion.4
  22.3 0.5 collective-permute-start.10
  22.8 2.3 %collective-permute-done.4.other_ref = bf16[1696,256]{1,0:T(8,128)(2,1)S(1)} collective-permute-done((bf16[1696,256]{1,0:T(8,128)(2,1)S(1)}, bf16[1696,256]{1,0:T(8,128)(2,1)S(1)}, u32[]{:S(2)}, u32[]{:S(2)}) %collective-permute-start.4) | collective-permute-done | bytes 868384 | tf_op jit(solution)/shard_map/ppermute | solution.py:683
  25.1 3.4 %collective-permute-start.5 = (bf16[384,256]{1,0:T(8,128)(2,1)S(1)}, bf16[384,256]{1,0:T(8,128)(2,1)S(1)}, u32[]{:S(2)}, u32[]{:S(2)}) collective-permute-start(bf16[384,256]{1,0:T(8,128)(2,1)S(1)} %bitcast.112), channel_id=1, source_target_pairs={{0,2},{2,0},{4,6},{6,4},{1,3},{3,1},{5,7},{7,5},{8,10},{10,8},{12,... | collective-permute-start | bytes 589832 | tf_op jit(solution)/shard_map/ppermute | solution.py:683
  28.5 1.1 collective-permute-start.6
  29.5 1.4 collective-permute-start.7
  30.9 32.4 %forward.1 = (bf16[2,4,256,512]{3,2,1,0:T(8,128)(2,1)}, bf16[2,4,256,128]{3,2,1,0:T(8,128)(2,1)}, bf16[2,4,256,128]{3,2,1,0:T(8,128)(2,1)}, bf16[2,4,1,64,256]{4...) custom-call(s32[2]{0:T(128)} %dynamic-slice_reduce_fusion.lens, ...), custom_call_target="tpu_custom_call" | custom-call | flops 20736638976 | bytes 67108864 | tf_op jit(solution)/shard_map/forward/pallas_call | solution.py:833
  63.6 2.3 %collective-permute-done.8.other_ref = bf16[1536,256]{1,0:T(8,128)(2,1)S(1)} collective-permute-done((bf16[1536,256]{1,0:T(8,128)(2,1)S(1)}, bf16[1536,256]{1,0:T(8,128)(2,1)S(1)}, u32[]{:S(2)}, u32[]{:S(2)}) %collective-permute-start.8) | collective-permute-done | bytes 786464 | tf_op jit(solution)/shard_map/ppermute | solution.py:683
  65.8 0.9 copy-done.11
  66.7 55.0 %middle.1 = (f32[2,4,256,512]{3,2,1,0:T(8,128)}, f32[2,4,256,512]{3,2,1,0:T(8,128)}, bf16[2,4,64,2048]{3,2,1,0:T(8,128)(2,1)}, f32[2,4,1,2048]{3,2,1,0:T(1,128)}...) custom-call(s32[2]{0:T(128)} %dynamic-slice_reduce_fusion.lens, ...), custom_call_target="tpu_custom_call" | custom-call | flops 35433480192 | bytes 209715200 | tf_op jit(solution)/shard_map/middle/pallas_call | solution.py:888
  121.8 0.2 collective-permute-start.11
  122.0 0.6 pad_convert_fusion.order_ref
  122.6 0.7 slice_bitcast_fusion.8
  123.3 0.9 reduce_sum.19
  124.2 0.1 reshape.236
  124.4 0.8 reduce_sum.18
  125.2 0.1 copy.55
  125.4 0.9 pad.17.columns_ref
  126.2 1.1 collective-permute-done.11
  127.3 4.1 %fusion.3 = (bf16[4,704,128]{2,1,0:T(8,128)(2,1)}, bf16[4,704,128]{2,1,0:T(8,128)(2,1)}, bf16[4,704,128]{2,1,0:T(8,128)(2,1)}, bf16[4,704,128]{2,1,0:T(8,128)(2,1)}) fusion(bf16[4,4,704,128]{3,2,1,0:T(8,128)(2,1)S(1)} %collective-permute-done.11, bf16[4,4,704,128]{3,2,1,0:T(8,128)(2,1)} %get-tuple-element.120), kind=kLoop, calls=%fused_computation.8 | loop fusion | flops 5767168 | bytes 8650752 | tf_op jit(solution)/shard_map/convert_element_type | solution.py:714
  131.4 0.7 collective-permute-start.12
  132.1 2.3 %collective-permute-start.13 = (bf16[4,704,128]{2,1,0:T(8,128)(2,1)}, bf16[4,704,128]{2,1,0:T(8,128)(2,1)S(1)}, u32[]{:S(2)}, u32[]{:S(2)}) collective-permute-start(bf16[4,704,128]{2,1,0:T(8,128)(2,1)} %get-tuple-element.130), channel_id=1, source_target_pairs={{0,16},{8,24},{16,0},{24,8},{1,17},{9,25},{17,1},{25,9},{2,18},{10... | collective-permute-start | bytes 2162696 | tf_op jit(solution)/shard_map/ppermute | solution.py:683
  134.4 0.5 collective-permute-start.14
  134.9 27.1 %backward.1 = (bf16[2,2,1696,512]{3,2,1,0:T(8,128)(2,1)}, bf16[4,4,224,128]{3,2,1,0:T(8,128)(2,1)}, bf16[4,4,224,128]{3,2,1,0:T(8,128)(2,1)}) custom-call(s32[2]{0:T(128)} %dynamic-slice_reduce_fusion.lens, s32[3]{0:T(128)} %pad_add_fusion.ids, bf16[2,4,256,512]{3,2,1,0:T(8,128)(2,1)} %get-tuple-element.113.hid_ref, ...), custom_call_target="tpu_custom_call" | custom-call | flops 46506442752 | bytes 104857600 | tf_op jit(solution)/shard_map/backward/pallas_call | solution.py:988
  162.0 4.2 %collective-permute-done.13 = bf16[4,704,128]{2,1,0:T(8,128)(2,1)S(1)} collective-permute-done((bf16[4,704,128]{2,1,0:T(8,128)(2,1)}, bf16[4,704,128]{2,1,0:T(8,128)(2,1)S(1)}, u32[]{:S(2)}, u32[]{:S(2)}) %collective-permute-start.13) | collective-permute-done | bytes 720928 | tf_op jit(solution)/shard_map/ppermute | solution.py:683
  166.2 2.7 %collective-permute-done.15 = bf16[4,4,224,128]{3,2,1,0:T(8,128)(2,1)S(1)} collective-permute-done((bf16[4,4,224,128]{3,2,1,0:T(8,128)(2,1)}, bf16[4,4,224,128]{3,2,1,0:T(8,128)(2,1)S(1)}, u32[]{:S(2)}, u32[]{:S(2)}) %collective-permute-start.15) | collective-permute-done | bytes 917536 | tf_op jit(solution)/shard_map/ppermute | solution.py:683
  168.9 1.6 fusion.7
  170.6 0.4 add_convert_fusion
  171.0 1.1 collective-permute-start.19
  172.1 0.6 slice.95.ids
  172.7 1.5 collective-permute-start.16
  174.1 5.2 %collective-permute-start.17 = (bf16[4,224,128]{2,1,0:T(8,128)(2,1)S(1)}, bf16[4,224,128]{2,1,0:T(8,128)(2,1)S(1)}, u32[]{:S(2)}, u32[]{:S(2)}) collective-permute-start(bf16[4,224,128]{2,1,0:T(8,128)(2,1)S(1)} %get-tuple-element.145), channel_id=1, source_target_pairs={{0,16},{8,24},{16,0},{24,8},{1,17},{9,25},{17,1},{25,9},{2,18},{10... | collective-permute-start | bytes 688136 | tf_op jit(solution)/shard_map/ppermute | solution.py:683
  179.4 1.2 collective-permute-start.20
  180.6 2.7 %collective-permute-start.21 = (bf16[704,128]{1,0:T(8,128)(2,1)S(1)}, bf16[704,128]{1,0:T(8,128)(2,1)S(1)}, u32[]{:S(2)}, u32[]{:S(2)}) collective-permute-start(bf16[704,128]{1,0:T(8,128)(2,1)S(1)} %get-tuple-element.149), channel_id=1, source_target_pairs={{0,6},{2,4},{4,2},{6,0},{1,7},{3,5},{5,3},{7,1},{8,14},{10,12},{12... | collective-permute-start | bytes 540680 | tf_op jit(solution)/shard_map/ppermute | solution.py:683
  183.3 12.2 %input_back.1 = f32[2,4,256,512]{3,2,1,0:T(8,128)} custom-call(s32[1]{0:T(128)} %slice.95.ids, bf16[2,4,256,512]{3,2,1,0:T(8,128)(2,1)} %bitcast.100, f32[2,4,256,512]{3,2,1,0:T(8,128)} %get-tuple-element.112.mid_ref, bf16[2,2,1696,512]{3,2,1,0:T(8,128)(2,1)} %get-tuple-element.143.r_ref, bf16[1696,256]{1,0:T(8,128)(2,1)} %copy-done.3, ...), custom_call_target="tpu_custom_call" | custom-call | flops 3556769792 | bytes 41943040 | tf_op jit(solution)/shard_map/input_back/pallas_call | solution.py:1060
  195.5 0.1 add_convert_fusion.5
  195.6 0.6 slice_bitcast_fusion.4
  196.3 3.2 %collective-permute-start.22 = (bf16[224,128]{1,0:T(8,128)(2,1)S(1)}, bf16[224,128]{1,0:T(8,128)(2,1)S(1)}, u32[]{:S(2)}, u32[]{:S(2)}) collective-permute-start(bf16[224,128]{1,0:T(8,128)(2,1)S(1)} %get-tuple-element.240), channel_id=1, source_target_pairs={{0,2},{2,0},{4,6},{6,4},{1,3},{3,1},{5,7},{7,5},{8,10},{10,8},{12,... | collective-permute-start | bytes 172040 | tf_op jit(solution)/shard_map/ppermute | solution.py:683
  199.5 0.4 collective-permute-start.23
  199.8 2.0 collective-permute-start.24
  202.0 0.7 broadcast_in_dim_reshape.6
  202.8 0.7 broadcast_in_dim_reshape.7
  203.5 0.1 copy.56
  203.6 0.8 copy.61
  204.4 1.9 collective-permute-done.23.refs_2_
  206.3 0.6 copy-done.7
  207.0 1.8 finish.1
  (77 shorter events, 1.0 us)
Async XLA Ops:
  0.6 14.3 %copy-start = (s32[2,32]{1,0:T(2,128)S(1)}, s32[2,32]{1,0:T(2,128)}, u32[]{:S(2)}) copy-start(s32[2,32]{1,0:T(2,128)} %param.17) | copy-start | bytes 772
  0.7 24.4 %copy-start.5 = (bf16[1,6,256,64]{2,3,1,0:T(8,128)(2,1)S(1)}, bf16[1,6,256,64]{2,3,1,0:T(8,128)(2,1)}, u32[]{:S(2)}) copy-start(bf16[1,6,256,64]{2,3,1,0:T(8,128)(2,1)} %param.24) | copy-start | bytes 589828
  0.7 17.0 %collective-permute-start.1 = (bf16[384,256]{1,0:T(8,128)(2,1)}, bf16[384,256]{1,0:T(8,128)(2,1)S(1)}, u32[]{:S(2)}, u32[]{:S(2)}) collective-permute-start(bf16[384,256]{1,0:T(8,128)(2,1)} %bitcast.108), channel_id=1, source_target_pairs={{0,2},{2,0},{4,6},{6,4},{1,3},{3,1},{5,7},{7,5},{8,10},{10,8},{12,... | collective-permute-start | bytes 589832 | tf_op jit(solution)/shard_map/ppermute | solution.py:683
  3.8 17.4 %collective-permute-start.2 = (bf16[384,256]{1,0:T(8,128)(2,1)}, bf16[384,256]{1,0:T(8,128)(2,1)S(1)}, u32[]{:S(2)}, u32[]{:S(2)}) collective-permute-start(bf16[384,256]{1,0:T(8,128)(2,1)} %bitcast.109), channel_id=1, source_target_pairs={{0,4},{2,6},{4,0},{6,2},{1,5},{3,7},{5,1},{7,3},{8,12},{10,14},{12... | collective-permute-start | bytes 589832 | tf_op jit(solution)/shard_map/ppermute | solution.py:683
  6.3 14.8 %collective-permute-start.3 = (bf16[384,256]{1,0:T(8,128)(2,1)}, bf16[384,256]{1,0:T(8,128)(2,1)S(1)}, u32[]{:S(2)}, u32[]{:S(2)}) collective-permute-start(bf16[384,256]{1,0:T(8,128)(2,1)} %bitcast.110), channel_id=1, source_target_pairs={{0,6},{2,4},{4,2},{6,0},{1,7},{3,5},{5,3},{7,1},{8,14},{10,12},{12... | collective-permute-start | bytes 589832 | tf_op jit(solution)/shard_map/ppermute | solution.py:683
  7.9 7.8 %collective-permute-start = (bf16[9,256]{1,0:T(8,128)(2,1)S(1)}, bf16[9,256]{1,0:T(8,128)(2,1)S(1)}, u32[]{:S(2)}, u32[]{:S(2)}) collective-permute-start(bf16[9,256]{1,0:T(8,128)(2,1)S(1)} %concatenate.47), channel_id=1, source_target_pairs={{0,1},{1,0},{2,3},{3,2},{4,5},{5,4},{6,7},{7,6},{8,9},{9,8},{10,11... | collective-permute-start | bytes 13832 | tf_op jit(solution)/shard_map/ppermute | solution.py:683
  22.2 8.8 %copy-start.3 = (bf16[1696,256]{1,0:T(8,128)(2,1)}, bf16[1696,256]{1,0:T(8,128)(2,1)S(1)}, u32[]{:S(2)}) copy-start(bf16[1696,256]{1,0:T(8,128)(2,1)S(1)} %constant_dynamic-update-slice_fusion.own_ref) | copy-start | bytes 2605060
  22.2 2.9 %collective-permute-start.4 = (bf16[1696,256]{1,0:T(8,128)(2,1)S(1)}, bf16[1696,256]{1,0:T(8,128)(2,1)S(1)}, u32[]{:S(2)}, u32[]{:S(2)}) collective-permute-start(bf16[1696,256]{1,0:T(8,128)(2,1)S(1)} %constant_dynamic-update-slice_fusion.own_ref), channel_id=1, source_target_pairs={{0,1},{1,0},{2,3},{3,2},{4,5},{5,4},{6,7},{7,6},{8,9},{9,8},{10,11... | collective-permute-start | bytes 2605064 | tf_op jit(solution)/shard_map/ppermute | solution.py:683
  22.3 41.3 %collective-permute-start.10 = (bf16[1024,512]{1,0:T(8,128)(2,1)}, bf16[1024,512]{1,0:T(8,128)(2,1)}, u32[]{:S(2)}, u32[]{:S(2)}) collective-permute-start(bf16[1024,512]{1,0:T(8,128)(2,1)} %bitcast.24.own_down_ref), channel_id=1, source_target_pairs={{0,1},{1,0},{2,3},{3,2},{4,5},{5,4},{6,7},{7,6},{8,9},{9,8},{10,11... | collective-permute-start | bytes 3145736 | tf_op jit(solution)/shard_map/ppermute | solution.py:683
  22.8 40.8 %collective-permute-start.9 = (bf16[256,2048]{1,0:T(8,128)(2,1)}, bf16[256,2048]{1,0:T(8,128)(2,1)}, u32[]{:S(2)}, u32[]{:S(2)}) collective-permute-start(bf16[256,2048]{1,0:T(8,128)(2,1)} %bitcast.23.own_up_ref), channel_id=1, source_target_pairs={{0,1},{1,0},{2,3},{3,2},{4,5},{5,4},{6,7},{7,6},{8,9},{9,8},{10,11... | collective-permute-start | bytes 3145736 | tf_op jit(solution)/shard_map/ppermute | solution.py:683
  25.1 5.8 %copy-start.4 = (bf16[1696,256]{1,0:T(8,128)(2,1)}, bf16[1696,256]{1,0:T(8,128)(2,1)S(1)}, u32[]{:S(2)}) copy-start(bf16[1696,256]{1,0:T(8,128)(2,1)S(1)} %collective-permute-done.4.other_ref) | copy-start | bytes 2605060
  25.1 38.2 %collective-permute-start.5 = (bf16[384,256]{1,0:T(8,128)(2,1)S(1)}, bf16[384,256]{1,0:T(8,128)(2,1)S(1)}, u32[]{:S(2)}, u32[]{:S(2)}) collective-permute-start(bf16[384,256]{1,0:T(8,128)(2,1)S(1)} %bitcast.112), channel_id=1, source_target_pairs={{0,2},{2,0},{4,6},{6,4},{1,3},{3,1},{5,7},{7,5},{8,10},{10,8},{12,... | collective-permute-start | bytes 589832 | tf_op jit(solution)/shard_map/ppermute | solution.py:683
  28.5 34.9 %collective-permute-start.6 = (bf16[384,256]{1,0:T(8,128)(2,1)S(1)}, bf16[384,256]{1,0:T(8,128)(2,1)S(1)}, u32[]{:S(2)}, u32[]{:S(2)}) collective-permute-start(bf16[384,256]{1,0:T(8,128)(2,1)S(1)} %bitcast.113), channel_id=1, source_target_pairs={{0,4},{2,6},{4,0},{6,2},{1,5},{3,7},{5,1},{7,3},{8,12},{10,14},{12... | collective-permute-start | bytes 589832 | tf_op jit(solution)/shard_map/ppermute | solution.py:683
  29.5 33.8 %collective-permute-start.7 = (bf16[384,256]{1,0:T(8,128)(2,1)S(1)}, bf16[384,256]{1,0:T(8,128)(2,1)S(1)}, u32[]{:S(2)}, u32[]{:S(2)}) collective-permute-start(bf16[384,256]{1,0:T(8,128)(2,1)S(1)} %bitcast.114), channel_id=1, source_target_pairs={{0,6},{2,4},{4,2},{6,0},{1,7},{3,5},{5,3},{7,1},{8,14},{10,12},{12... | collective-permute-start | bytes 589832 | tf_op jit(solution)/shard_map/ppermute | solution.py:683
  63.5 2.4 %copy-start.9 = (bf16[1536,256]{1,0:T(8,128)(2,1)}, bf16[1536,256]{1,0:T(8,128)(2,1)S(1)}, u32[]{:S(2)}) copy-start(bf16[1536,256]{1,0:T(8,128)(2,1)S(1)} %constant_dynamic-update-slice_fusion.5.own_ref) | copy-start | bytes 2359300
  63.5 2.4 %collective-permute-start.8 = (bf16[1536,256]{1,0:T(8,128)(2,1)S(1)}, bf16[1536,256]{1,0:T(8,128)(2,1)S(1)}, u32[]{:S(2)}, u32[]{:S(2)}) collective-permute-start(bf16[1536,256]{1,0:T(8,128)(2,1)S(1)} %constant_dynamic-update-slice_fusion.5.own_ref), channel_id=1, source_target_pairs={{0,1},{1,0},{2,3},{3,2},{4,5},{5,4},{6,7},{7,6},{8,9},{9,8},{10,11... | collective-permute-start | bytes 2359304 | tf_op jit(solution)/shard_map/ppermute | solution.py:683
  65.8 0.9 copy-start.11
  121.8 5.6 %collective-permute-start.11 = (bf16[4,4,704,128]{3,2,1,0:T(8,128)(2,1)}, bf16[4,4,704,128]{3,2,1,0:T(8,128)(2,1)S(1)}, u32[]{:S(2)}, u32[]{:S(2)}) collective-permute-start(bf16[4,4,704,128]{3,2,1,0:T(8,128)(2,1)} %get-tuple-element.121), channel_id=1, source_target_pairs={{0,1},{1,0},{2,3},{3,2},{4,5},{5,4},{6,7},{7,6},{8,9},{9,8},{10,11... | collective-permute-start | bytes 8650760 | tf_op jit(solution)/shard_map/ppermute | solution.py:683
  131.4 30.6 %collective-permute-start.12 = (bf16[4,704,128]{2,1,0:T(8,128)(2,1)}, bf16[4,704,128]{2,1,0:T(8,128)(2,1)S(1)}, u32[]{:S(2)}, u32[]{:S(2)}) collective-permute-start(bf16[4,704,128]{2,1,0:T(8,128)(2,1)} %get-tuple-element.129), channel_id=1, source_target_pairs={{0,8},{8,0},{16,24},{24,16},{1,9},{9,1},{17,25},{25,17},{2,10},{10... | collective-permute-start | bytes 2162696 | tf_op jit(solution)/shard_map/ppermute | solution.py:683
  132.1 34.1 %collective-permute-start.13 = (bf16[4,704,128]{2,1,0:T(8,128)(2,1)}, bf16[4,704,128]{2,1,0:T(8,128)(2,1)S(1)}, u32[]{:S(2)}, u32[]{:S(2)}) collective-permute-start(bf16[4,704,128]{2,1,0:T(8,128)(2,1)} %get-tuple-element.130), channel_id=1, source_target_pairs={{0,16},{8,24},{16,0},{24,8},{1,17},{9,25},{17,1},{25,9},{2,18},{10... | collective-permute-start | bytes 2162696 | tf_op jit(solution)/shard_map/ppermute | solution.py:683
  134.4 31.8 %collective-permute-start.14 = (bf16[4,704,128]{2,1,0:T(8,128)(2,1)}, bf16[4,704,128]{2,1,0:T(8,128)(2,1)S(1)}, u32[]{:S(2)}, u32[]{:S(2)}) collective-permute-start(bf16[4,704,128]{2,1,0:T(8,128)(2,1)} %get-tuple-element.131), channel_id=1, source_target_pairs={{0,24},{8,16},{16,8},{24,0},{1,25},{9,17},{17,9},{25,1},{2,26},{10... | collective-permute-start | bytes 2162696 | tf_op jit(solution)/shard_map/ppermute | solution.py:683
  162.0 8.6 %copy-start.2 = (bf16[4,704,128]{2,1,0:T(8,128)(2,1)S(1)}, bf16[4,704,128]{2,1,0:T(8,128)(2,1)}, u32[]{:S(2)}) copy-start(bf16[4,704,128]{2,1,0:T(8,128)(2,1)} %get-tuple-element.128) | copy-start | bytes 2162692
  166.2 2.7 %collective-permute-start.15 = (bf16[4,4,224,128]{3,2,1,0:T(8,128)(2,1)}, bf16[4,4,224,128]{3,2,1,0:T(8,128)(2,1)S(1)}, u32[]{:S(2)}, u32[]{:S(2)}) collective-permute-start(bf16[4,4,224,128]{3,2,1,0:T(8,128)(2,1)} %get-tuple-element.138), channel_id=1, source_target_pairs={{0,1},{1,0},{2,3},{3,2},{4,5},{5,4},{6,7},{7,6},{8,9},{9,8},{10,11... | collective-permute-start | bytes 2752520 | tf_op jit(solution)/shard_map/ppermute | solution.py:683
  170.9 1.2 copy-start.10
  171.0 9.6 %collective-permute-start.19 = (bf16[704,128]{1,0:T(8,128)(2,1)S(1)}, bf16[704,128]{1,0:T(8,128)(2,1)S(1)}, u32[]{:S(2)}, u32[]{:S(2)}) collective-permute-start(bf16[704,128]{1,0:T(8,128)(2,1)S(1)} %get-tuple-element.147), channel_id=1, source_target_pairs={{0,2},{2,0},{4,6},{6,4},{1,3},{3,1},{5,7},{7,5},{8,10},{10,8},{12,... | collective-permute-start | bytes 540680 | tf_op jit(solution)/shard_map/ppermute | solution.py:683
  172.7 22.8 %collective-permute-start.16 = (bf16[4,224,128]{2,1,0:T(8,128)(2,1)S(1)}, bf16[4,224,128]{2,1,0:T(8,128)(2,1)S(1)}, u32[]{:S(2)}, u32[]{:S(2)}) collective-permute-start(bf16[4,224,128]{2,1,0:T(8,128)(2,1)S(1)} %get-tuple-element.144), channel_id=1, source_target_pairs={{0,8},{8,0},{16,24},{24,16},{1,9},{9,1},{17,25},{25,17},{2,10},{10... | collective-permute-start | bytes 688136 | tf_op jit(solution)/shard_map/ppermute | solution.py:683
  174.1 21.3 %collective-permute-start.17 = (bf16[4,224,128]{2,1,0:T(8,128)(2,1)S(1)}, bf16[4,224,128]{2,1,0:T(8,128)(2,1)S(1)}, u32[]{:S(2)}, u32[]{:S(2)}) collective-permute-start(bf16[4,224,128]{2,1,0:T(8,128)(2,1)S(1)} %get-tuple-element.145), channel_id=1, source_target_pairs={{0,16},{8,24},{16,0},{24,8},{1,17},{9,25},{17,1},{25,9},{2,18},{10... | collective-permute-start | bytes 688136 | tf_op jit(solution)/shard_map/ppermute | solution.py:683
  179.4 16.1 %collective-permute-start.18 = (bf16[4,224,128]{2,1,0:T(8,128)(2,1)S(1)}, bf16[4,224,128]{2,1,0:T(8,128)(2,1)S(1)}, u32[]{:S(2)}, u32[]{:S(2)}) collective-permute-start(bf16[4,224,128]{2,1,0:T(8,128)(2,1)S(1)} %get-tuple-element.146), channel_id=1, source_target_pairs={{0,24},{8,16},{16,8},{24,0},{1,25},{9,17},{17,9},{25,1},{2,26},{10... | collective-permute-start | bytes 688136 | tf_op jit(solution)/shard_map/ppermute | solution.py:683
  179.4 16.1 %collective-permute-start.20 = (bf16[704,128]{1,0:T(8,128)(2,1)S(1)}, bf16[704,128]{1,0:T(8,128)(2,1)S(1)}, u32[]{:S(2)}, u32[]{:S(2)}) collective-permute-start(bf16[704,128]{1,0:T(8,128)(2,1)S(1)} %get-tuple-element.148), channel_id=1, source_target_pairs={{0,4},{2,6},{4,0},{6,2},{1,5},{3,7},{5,1},{7,3},{8,12},{10,14},{12... | collective-permute-start | bytes 540680 | tf_op jit(solution)/shard_map/ppermute | solution.py:683
  180.6 14.9 %collective-permute-start.21 = (bf16[704,128]{1,0:T(8,128)(2,1)S(1)}, bf16[704,128]{1,0:T(8,128)(2,1)S(1)}, u32[]{:S(2)}, u32[]{:S(2)}) collective-permute-start(bf16[704,128]{1,0:T(8,128)(2,1)S(1)} %get-tuple-element.149), channel_id=1, source_target_pairs={{0,6},{2,4},{4,2},{6,0},{1,7},{3,5},{5,3},{7,1},{8,14},{10,12},{12... | collective-permute-start | bytes 540680 | tf_op jit(solution)/shard_map/ppermute | solution.py:683
  196.3 8.2 %collective-permute-start.22 = (bf16[224,128]{1,0:T(8,128)(2,1)S(1)}, bf16[224,128]{1,0:T(8,128)(2,1)S(1)}, u32[]{:S(2)}, u32[]{:S(2)}) collective-permute-start(bf16[224,128]{1,0:T(8,128)(2,1)S(1)} %get-tuple-element.240), channel_id=1, source_target_pairs={{0,2},{2,0},{4,6},{6,4},{1,3},{3,1},{5,7},{7,5},{8,10},{10,8},{12,... | collective-permute-start | bytes 172040 | tf_op jit(solution)/shard_map/ppermute | solution.py:683
  199.5 6.8 %collective-permute-start.23 = (bf16[224,128]{1,0:T(8,128)(2,1)S(1)}, bf16[224,128]{1,0:T(8,128)(2,1)S(1)}, u32[]{:S(2)}, u32[]{:S(2)}) collective-permute-start(bf16[224,128]{1,0:T(8,128)(2,1)S(1)} %get-tuple-element.239), channel_id=1, source_target_pairs={{0,4},{2,6},{4,0},{6,2},{1,5},{3,7},{5,1},{7,3},{8,12},{10,14},{12... | collective-permute-start | bytes 172040 | tf_op jit(solution)/shard_map/ppermute | solution.py:683
  199.8 6.5 %collective-permute-start.24 = (bf16[224,128]{1,0:T(8,128)(2,1)S(1)}, bf16[224,128]{1,0:T(8,128)(2,1)S(1)}, u32[]{:S(2)}, u32[]{:S(2)}) collective-permute-start(bf16[224,128]{1,0:T(8,128)(2,1)S(1)} %get-tuple-element.238), channel_id=1, source_target_pairs={{0,6},{2,4},{4,2},{6,0},{1,7},{3,5},{5,3},{7,1},{8,14},{10,12},{12... | collective-permute-start | bytes 172040 | tf_op jit(solution)/shard_map/ppermute | solution.py:683
  201.8 6.9 %copy-start.1 = (s32[2,32]{1,0:T(2,128)S(1)}, s32[2,32]{1,0:T(2,128)}, u32[]{:S(2)}) copy-start(s32[2,32]{1,0:T(2,128)} %param.17) | copy-start | bytes 772
  204.4 1.9 copy-start.6
  206.3 0.6 copy-start.7
  206.3 0.6 copy-start.8

commit v6 on v5

--- a/solution.py
+++ b/solution.py
@@ -312,12 +312,12 @@
         - jnp.mean(scaled, -1, keepdims=True)
         - normed * jnp.mean(scaled * normed, -1, keepdims=True)
     )
-    mid_ref[0] = mid.reshape(subs, span, model)
     small_ref[0] += fold_rows(back * normed, jnp.sum)
     small_ref[1] += fold_rows(back, jnp.sum)
     small_ref[2] += fold_rows(grad_b.astype(F32), jnp.sum)
 
     mid_b = mid.astype(BF16)
+    mid_ref[0] = mid_b.reshape(subs, span, model)
     wo_acc[...] += dot_nt(mid_b.T, cexp[...])
     products = dot_nt(low[...], mid_b[:, :half]) + dot_nt(high[...], mid_b[:, half:])
     table[...] = products.astype(BF16)
@@ -603,7 +603,7 @@
     routed = r_ref[0, 0]
     back = jnp.concatenate([dot_tn(routed, low[...]), dot_tn(routed, high[...])], 1)
     scaled = back * vec_ref[0:1, :]
-    total = mid_ref[0].reshape(subs * span, model) + spread * (
+    total = mid_ref[0].reshape(subs * span, model).astype(F32) + spread * (
         scaled
         - jnp.mean(scaled, -1, keepdims=True)
         - normed * jnp.mean(scaled * normed, -1, keepdims=True)
@@ -809,12 +809,14 @@
     up_other = exchange(up_weight[0], "fsdp", 1)
     down_other = exchange(down_weight[0], "fsdp", 1)
     route_t = start_of(routes)
-    lens, ids, route_t, vectors, up_shift, router_t, *query_parts = lax.optimization_barrier(
-        (lens, ids, route_t, vectors, up_shift, router_t, *query_parts)
+    own_out = transposed(out_weight)
+    lens, ids, route_t, vectors, up_shift, router_t, own_out, *query_parts = (
+        lax.optimization_barrier(
+            (lens, ids, route_t, vectors, up_shift, router_t, own_out, *query_parts)
+        )
     )
     proj = jnp.concatenate(query_parts + [kv_weight[0].T, router_t], 0)
     proj_other = exchange(proj, "fsdp", 1)
-    own_out, proj_other = lax.optimization_barrier((transposed(out_weight), proj_other))
     out_parts = head_parts(own_out)
 
     states = inputs.reshape(micro_count, blocks, span, model)
@@ -931,7 +933,7 @@
         ),
         out_shape=[
             state_s,
-            state_s,
+            hid_s,
             q_s,
             row_s,
             gate_s,

time: 211 us -> 208 us (0.986)
  Pallas kernels: 128 us -> 137 us
  starting transfers between devices: 33.2 us -> 26.9 us
  waiting for transfers between devices: 17.9 us -> 13 us
    pallas_call x1, Pallas kernels: 27.1 us -> 36.5 us  [local(): pl.pallas_call(backward_kernel, name='backward', grid_spec=pltpu.Prefetch...]
    ppermute x25, starting transfers between devices: 33.2 us -> 26.9 us  [exchange(): lax.ppermute(value, axis, [(at, at ^ distance) for at in range(count)])]
    ppermute x25, waiting for transfers between devices: 17.9 us -> 13 us  [exchange(): lax.ppermute(value, axis, [(at, at ^ distance) for at in range(count)])]
  transfers between devices with their start and end apart: 25 -> 25, of which waited for: 7 -> 6; matrix products, arithmetic and copies ran while one was open for 9% -> 9% of each run, Pallas kernels for 34% -> 39%
where the time goes in v6:
time: 208 us; the launch traced here: 207 us
  Pallas kernels  137 us (66%)
  starting transfers between devices  26.9 us (13%)
  other arithmetic  15 us (7%)
  local copies, waits for them, and re-layouts  13.5 us (6%)
  waiting for transfers between devices  13 us (6%)
    pallas_call x1, Pallas kernels, local(): pl.pallas_call(middle_kernel, name='middle', grid_spec=pltpu.PrefetchScal...  54.9 us
    pallas_call x1, Pallas kernels, local(): pl.pallas_call(backward_kernel, name='backward', grid_spec=pltpu.Prefetch...  36.5 us
    pallas_call x1, Pallas kernels, local(): pl.pallas_call(forward_kernel, name='forward', grid_spec=pltpu.PrefetchSc...  32.4 us
    ppermute x25, starting transfers between devices, exchange(): lax.ppermute(value, axis, [(at, at ^ distance) for at in range(count)])  26.9 us
    ppermute x25, waiting for transfers between devices, exchange(): lax.ppermute(value, axis, [(at, at ^ distance) for at in range(count)])  13 us
    pallas_call x1, Pallas kernels, local(): pl.pallas_call(input_kernel, name='input_back', grid_spec=pltpu.PrefetchS...  11.9 us
    convert_element_type x2, other arithmetic, core_stage(): (keep[at].astype(F32) + other[at].astype(F32)).astype(BF16)  5.71 us
    unnamed x36, local copies, waits for them, and re-layouts  4.87 us
  transfers between devices with their start and end apart: 25, of which 6 were waited for; matrix products, arithmetic and copies ran while one was open for 9% of the time, Pallas kernels for 39%

profile of v6, /device:TPU:0, one launch (start us, length us, event | category | flops | bytes accessed | tf_op | source)
XLA Modules:
  0.0 207.3 jit_solution(17624678086187777902)
XLA Ops:
  0.7 3.1 %collective-permute-start.1 = (bf16[384,256]{1,0:T(8,128)(2,1)}, bf16[384,256]{1,0:T(8,128)(2,1)S(1)}, u32[]{:S(2)}, u32[]{:S(2)}) collective-permute-start(bf16[384,256]{1,0:T(8,128)(2,1)} %bitcast.108), channel_id=1, source_target_pairs={{0,2},{2,0},{4,6},{6,4},{1,3},{3,1},{5,7},{7,5},{8,10},{10,8},{12,... | collective-permute-start | bytes 589832 | tf_op jit(solution)/shard_map/ppermute | solution.py:683
  3.8 2.6 %collective-permute-start.2 = (bf16[384,256]{1,0:T(8,128)(2,1)}, bf16[384,256]{1,0:T(8,128)(2,1)S(1)}, u32[]{:S(2)}, u32[]{:S(2)}) collective-permute-start(bf16[384,256]{1,0:T(8,128)(2,1)} %bitcast.109), channel_id=1, source_target_pairs={{0,4},{2,6},{4,0},{6,2},{1,5},{3,7},{5,1},{7,3},{8,12},{10,14},{12... | collective-permute-start | bytes 589832 | tf_op jit(solution)/shard_map/ppermute | solution.py:683
  6.4 0.7 reduce.1
  7.1 0.9 concatenate.47
  8.0 0.7 reshape_reshape.6
  8.7 0.7 reshape.227
  9.5 0.9 broadcast_remainder_fusion
  10.3 0.9 sign_compare_fusion
  11.3 0.7 select_select_fusion
  12.0 0.7 fusion.11.route_ref
  12.7 0.6 pad_add_fusion.ids
  13.3 0.8 concatenate.46
  14.0 0.9 copy.53
  15.0 0.7 dynamic-slice_reduce_fusion.lens
  15.7 0.6 fusion.13.vec_ref
  16.3 1.4 fusion.12.up_shift_ref
  17.7 3.4 %collective-permute-done.2 = bf16[384,256]{1,0:T(8,128)(2,1)S(1)} collective-permute-done((bf16[384,256]{1,0:T(8,128)(2,1)}, bf16[384,256]{1,0:T(8,128)(2,1)S(1)}, u32[]{:S(2)}, u32[]{:S(2)}) %collective-permute-start.2) | collective-permute-done | bytes 196640 | tf_op jit(solution)/shard_map/ppermute | solution.py:683
  21.1 0.9 constant_dynamic-update-slice_fusion.4
  22.3 0.5 collective-permute-start.10
  22.8 3.4 %collective-permute-start.5 = (bf16[384,256]{1,0:T(8,128)(2,1)S(1)}, bf16[384,256]{1,0:T(8,128)(2,1)S(1)}, u32[]{:S(2)}, u32[]{:S(2)}) collective-permute-start(bf16[384,256]{1,0:T(8,128)(2,1)S(1)} %bitcast.112), channel_id=1, source_target_pairs={{0,2},{2,0},{4,6},{6,4},{1,3},{3,1},{5,7},{7,5},{8,10},{10,8},{12,... | collective-permute-start | bytes 589832 | tf_op jit(solution)/shard_map/ppermute | solution.py:683
  26.2 1.0 collective-permute-start.6
  27.2 1.5 collective-permute-start.7
  28.7 32.4 %forward.1 = (bf16[2,4,256,512]{3,2,1,0:T(8,128)(2,1)}, bf16[2,4,256,128]{3,2,1,0:T(8,128)(2,1)}, bf16[2,4,256,128]{3,2,1,0:T(8,128)(2,1)}, bf16[2,4,1,64,256]{4...) custom-call(s32[2]{0:T(128)} %dynamic-slice_reduce_fusion.lens, ...), custom_call_target="tpu_custom_call" | custom-call | flops 20736638976 | bytes 67108864 | tf_op jit(solution)/shard_map/forward/pallas_call | solution.py:835
  61.4 2.3 %collective-permute-done.8.other_ref = bf16[1536,256]{1,0:T(8,128)(2,1)S(1)} collective-permute-done((bf16[1536,256]{1,0:T(8,128)(2,1)S(1)}, bf16[1536,256]{1,0:T(8,128)(2,1)S(1)}, u32[]{:S(2)}, u32[]{:S(2)}) %collective-permute-start.8) | collective-permute-done | bytes 786464 | tf_op jit(solution)/shard_map/ppermute | solution.py:683
  63.6 0.9 copy-done.11
  64.5 54.9 %middle.1 = (f32[2,4,256,512]{3,2,1,0:T(8,128)}, bf16[2,4,256,512]{3,2,1,0:T(8,128)(2,1)}, bf16[2,4,64,2048]{3,2,1,0:T(8,128)(2,1)}, f32[2,4,1,2048]{3,2,1,0:T(1...) custom-call(s32[2]{0:T(128)} %dynamic-slice_reduce_fusion.lens, ...), custom_call_target="tpu_custom_call" | custom-call | flops 35433480192 | bytes 209715200 | tf_op jit(solution)/shard_map/middle/pallas_call | solution.py:890
  119.4 0.2 collective-permute-start.11
  119.7 0.6 pad_convert_fusion.order_ref
  120.3 0.7 slice_bitcast_fusion.8
  121.0 0.9 reduce_sum.19
  121.9 0.1 reshape.236
  122.0 0.1 reshape.237
  122.1 0.8 reduce_sum.18
  122.9 0.1 copy.55
  123.1 0.9 pad.17.columns_ref
  123.9 1.1 collective-permute-done.11
  125.0 4.1 %fusion.3 = (bf16[4,704,128]{2,1,0:T(8,128)(2,1)}, bf16[4,704,128]{2,1,0:T(8,128)(2,1)}, bf16[4,704,128]{2,1,0:T(8,128)(2,1)}, bf16[4,704,128]{2,1,0:T(8,128)(2,1)}) fusion(bf16[4,4,704,128]{3,2,1,0:T(8,128)(2,1)S(1)} %collective-permute-done.11, bf16[4,4,704,128]{3,2,1,0:T(8,128)(2,1)} %get-tuple-element.118), kind=kLoop, calls=%fused_computation.8 | loop fusion | flops 5767168 | bytes 8650752 | tf_op jit(solution)/shard_map/convert_element_type | solution.py:714
  129.1 0.6 collective-permute-start.12
  129.7 2.4 %collective-permute-start.13 = (bf16[4,704,128]{2,1,0:T(8,128)(2,1)}, bf16[4,704,128]{2,1,0:T(8,128)(2,1)S(1)}, u32[]{:S(2)}, u32[]{:S(2)}) collective-permute-start(bf16[4,704,128]{2,1,0:T(8,128)(2,1)} %get-tuple-element.128), channel_id=1, source_target_pairs={{0,16},{8,24},{16,0},{24,8},{1,17},{9,25},{17,1},{25,9},{2,18},{10... | collective-permute-start | bytes 2162696 | tf_op jit(solution)/shard_map/ppermute | solution.py:683
  132.1 0.5 collective-permute-start.14
  132.6 36.5 %backward.1 = (bf16[2,2,1696,512]{3,2,1,0:T(8,128)(2,1)}, bf16[4,4,224,128]{3,2,1,0:T(8,128)(2,1)}, bf16[4,4,224,128]{3,2,1,0:T(8,128)(2,1)}) custom-call(s32[2]{0:T(128)} %dynamic-slice_reduce_fusion.lens, s32[3]{0:T(128)} %pad_add_fusion.ids, bf16[2,4,256,512]{3,2,1,0:T(8,128)(2,1)} %get-tuple-element.111.hid_ref, ...), custom_call_target="tpu_custom_call" | custom-call | flops 46506442752 | bytes 104857600 | tf_op jit(solution)/shard_map/backward/pallas_call | solution.py:990
  169.2 2.7 %collective-permute-done.15 = bf16[4,4,224,128]{3,2,1,0:T(8,128)(2,1)S(1)} collective-permute-done((bf16[4,4,224,128]{3,2,1,0:T(8,128)(2,1)}, bf16[4,4,224,128]{3,2,1,0:T(8,128)(2,1)S(1)}, u32[]{:S(2)}, u32[]{:S(2)}) %collective-permute-start.15) | collective-permute-done | bytes 917536 | tf_op jit(solution)/shard_map/ppermute | solution.py:683
  171.9 1.6 fusion.7
  173.5 0.4 add_convert_fusion
  174.0 0.5 copy-done.10
  174.5 0.6 slice.95.ids
  175.1 3.0 %collective-permute-start.17 = (bf16[4,224,128]{2,1,0:T(8,128)(2,1)S(1)}, bf16[4,224,128]{2,1,0:T(8,128)(2,1)S(1)}, u32[]{:S(2)}, u32[]{:S(2)}) collective-permute-start(bf16[4,224,128]{2,1,0:T(8,128)(2,1)S(1)} %get-tuple-element.143), channel_id=1, source_target_pairs={{0,16},{8,24},{16,0},{24,8},{1,17},{9,25},{17,1},{25,9},{2,18},{10... | collective-permute-start | bytes 688136 | tf_op jit(solution)/shard_map/ppermute | solution.py:683
  178.1 0.5 collective-permute-start.18
  178.6 2.0 collective-permute-done.19
  180.6 1.9 collective-permute-start.21
  182.5 11.9 %input_back.1 = f32[2,4,256,512]{3,2,1,0:T(8,128)} custom-call(s32[1]{0:T(128)} %slice.95.ids, bf16[2,4,256,512]{3,2,1,0:T(8,128)(2,1)} %bitcast.100, bf16[2,4,256,512]{3,2,1,0:T(8,128)(2,1)} %get-tuple-element.110.mid_ref, bf16[2,2,1696,512]{3,2,1,0:T(8,128)(2,1)} %get-tuple-element.141.r_ref, bf16[1696,256]{1,0:T(8,128)(2,1)} %copy-done.3, ...), custom_call_target="tpu_custom_call" | custom-call | flops 3556769792 | bytes 41943040 | tf_op jit(solution)/shard_map/input_back/pallas_call | solution.py:1062
  194.4 0.1 add_convert_fusion.5
  194.6 0.6 slice_bitcast_fusion.4
  195.2 3.0 %collective-permute-start.22 = (bf16[224,128]{1,0:T(8,128)(2,1)S(1)}, bf16[224,128]{1,0:T(8,128)(2,1)S(1)}, u32[]{:S(2)}, u32[]{:S(2)}) collective-permute-start(bf16[224,128]{1,0:T(8,128)(2,1)S(1)} %get-tuple-element.238), channel_id=1, source_target_pairs={{0,2},{2,0},{4,6},{6,4},{1,3},{3,1},{5,7},{7,5},{8,10},{10,8},{12,... | collective-permute-start | bytes 172040 | tf_op jit(solution)/shard_map/ppermute | solution.py:683
  198.2 2.4 %collective-permute-start.24 = (bf16[224,128]{1,0:T(8,128)(2,1)S(1)}, bf16[224,128]{1,0:T(8,128)(2,1)S(1)}, u32[]{:S(2)}, u32[]{:S(2)}) collective-permute-start(bf16[224,128]{1,0:T(8,128)(2,1)S(1)} %get-tuple-element.236), channel_id=1, source_target_pairs={{0,6},{2,4},{4,2},{6,0},{1,7},{3,5},{5,3},{7,1},{8,14},{10,12},{12... | collective-permute-start | bytes 172040 | tf_op jit(solution)/shard_map/ppermute | solution.py:683
  200.5 0.1 convert_add_fusion
  200.7 0.7 broadcast_in_dim_reshape.6
  201.4 0.1 copy.58
  201.5 0.7 broadcast_in_dim_reshape.7
  202.2 0.1 copy.56
  202.3 0.8 copy.61
  203.1 1.6 collective-permute-done.23.refs_2_
  204.7 0.6 copy-done.7
  205.4 1.8 finish.1
  (77 shorter events, 0.9 us)
Async XLA Ops:
  0.6 14.3 %copy-start = (s32[2,32]{1,0:T(2,128)S(1)}, s32[2,32]{1,0:T(2,128)}, u32[]{:S(2)}) copy-start(s32[2,32]{1,0:T(2,128)} %param.17) | copy-start | bytes 772
  0.7 22.2 %copy-start.5 = (bf16[1,6,256,64]{2,3,1,0:T(8,128)(2,1)S(1)}, bf16[1,6,256,64]{2,3,1,0:T(8,128)(2,1)}, u32[]{:S(2)}) copy-start(bf16[1,6,256,64]{2,3,1,0:T(8,128)(2,1)} %param.24) | copy-start | bytes 589828
  0.7 17.0 %collective-permute-start.1 = (bf16[384,256]{1,0:T(8,128)(2,1)}, bf16[384,256]{1,0:T(8,128)(2,1)S(1)}, u32[]{:S(2)}, u32[]{:S(2)}) collective-permute-start(bf16[384,256]{1,0:T(8,128)(2,1)} %bitcast.108), channel_id=1, source_target_pairs={{0,2},{2,0},{4,6},{6,4},{1,3},{3,1},{5,7},{7,5},{8,10},{10,8},{12,... | collective-permute-start | bytes 589832 | tf_op jit(solution)/shard_map/ppermute | solution.py:683
  3.8 17.4 %collective-permute-start.2 = (bf16[384,256]{1,0:T(8,128)(2,1)}, bf16[384,256]{1,0:T(8,128)(2,1)S(1)}, u32[]{:S(2)}, u32[]{:S(2)}) collective-permute-start(bf16[384,256]{1,0:T(8,128)(2,1)} %bitcast.109), channel_id=1, source_target_pairs={{0,4},{2,6},{4,0},{6,2},{1,5},{3,7},{5,1},{7,3},{8,12},{10,14},{12... | collective-permute-start | bytes 589832 | tf_op jit(solution)/shard_map/ppermute | solution.py:683
  6.3 14.8 %collective-permute-start.3 = (bf16[384,256]{1,0:T(8,128)(2,1)}, bf16[384,256]{1,0:T(8,128)(2,1)S(1)}, u32[]{:S(2)}, u32[]{:S(2)}) collective-permute-start(bf16[384,256]{1,0:T(8,128)(2,1)} %bitcast.110), channel_id=1, source_target_pairs={{0,6},{2,4},{4,2},{6,0},{1,7},{3,5},{5,3},{7,1},{8,14},{10,12},{12... | collective-permute-start | bytes 589832 | tf_op jit(solution)/shard_map/ppermute | solution.py:683
  7.9 7.8 %collective-permute-start = (bf16[9,256]{1,0:T(8,128)(2,1)S(1)}, bf16[9,256]{1,0:T(8,128)(2,1)S(1)}, u32[]{:S(2)}, u32[]{:S(2)}) collective-permute-start(bf16[9,256]{1,0:T(8,128)(2,1)S(1)} %concatenate.47), channel_id=1, source_target_pairs={{0,1},{1,0},{2,3},{3,2},{4,5},{5,4},{6,7},{7,6},{8,9},{9,8},{10,11... | collective-permute-start | bytes 13832 | tf_op jit(solution)/shard_map/ppermute | solution.py:683
  22.2 6.6 %copy-start.3 = (bf16[1696,256]{1,0:T(8,128)(2,1)}, bf16[1696,256]{1,0:T(8,128)(2,1)S(1)}, u32[]{:S(2)}) copy-start(bf16[1696,256]{1,0:T(8,128)(2,1)S(1)} %constant_dynamic-update-slice_fusion.own_ref) | copy-start | bytes 2605060
  22.2 5.0 %collective-permute-start.4 = (bf16[1696,256]{1,0:T(8,128)(2,1)S(1)}, bf16[1696,256]{1,0:T(8,128)(2,1)S(1)}, u32[]{:S(2)}, u32[]{:S(2)}) collective-permute-start(bf16[1696,256]{1,0:T(8,128)(2,1)S(1)} %constant_dynamic-update-slice_fusion.own_ref), channel_id=1, source_target_pairs={{0,1},{1,0},{2,3},{3,2},{4,5},{5,4},{6,7},{7,6},{8,9},{9,8},{10,11... | collective-permute-start | bytes 2605064 | tf_op jit(solution)/shard_map/ppermute | solution.py:683
  22.3 39.1 %collective-permute-start.10 = (bf16[1024,512]{1,0:T(8,128)(2,1)}, bf16[1024,512]{1,0:T(8,128)(2,1)}, u32[]{:S(2)}, u32[]{:S(2)}) collective-permute-start(bf16[1024,512]{1,0:T(8,128)(2,1)} %bitcast.24.own_down_ref), channel_id=1, source_target_pairs={{0,1},{1,0},{2,3},{3,2},{4,5},{5,4},{6,7},{7,6},{8,9},{9,8},{10,11... | collective-permute-start | bytes 3145736 | tf_op jit(solution)/shard_map/ppermute | solution.py:683
  22.8 38.6 %collective-permute-start.9 = (bf16[256,2048]{1,0:T(8,128)(2,1)}, bf16[256,2048]{1,0:T(8,128)(2,1)}, u32[]{:S(2)}, u32[]{:S(2)}) collective-permute-start(bf16[256,2048]{1,0:T(8,128)(2,1)} %bitcast.23.own_up_ref), channel_id=1, source_target_pairs={{0,1},{1,0},{2,3},{3,2},{4,5},{5,4},{6,7},{7,6},{8,9},{9,8},{10,11... | collective-permute-start | bytes 3145736 | tf_op jit(solution)/shard_map/ppermute | solution.py:683
  22.8 38.3 %collective-permute-start.5 = (bf16[384,256]{1,0:T(8,128)(2,1)S(1)}, bf16[384,256]{1,0:T(8,128)(2,1)S(1)}, u32[]{:S(2)}, u32[]{:S(2)}) collective-permute-start(bf16[384,256]{1,0:T(8,128)(2,1)S(1)} %bitcast.112), channel_id=1, source_target_pairs={{0,2},{2,0},{4,6},{6,4},{1,3},{3,1},{5,7},{7,5},{8,10},{10,8},{12,... | collective-permute-start | bytes 589832 | tf_op jit(solution)/shard_map/ppermute | solution.py:683
  26.2 34.9 %collective-permute-start.6 = (bf16[384,256]{1,0:T(8,128)(2,1)S(1)}, bf16[384,256]{1,0:T(8,128)(2,1)S(1)}, u32[]{:S(2)}, u32[]{:S(2)}) collective-permute-start(bf16[384,256]{1,0:T(8,128)(2,1)S(1)} %bitcast.113), channel_id=1, source_target_pairs={{0,4},{2,6},{4,0},{6,2},{1,5},{3,7},{5,1},{7,3},{8,12},{10,14},{12... | collective-permute-start | bytes 589832 | tf_op jit(solution)/shard_map/ppermute | solution.py:683
  27.2 1.5 copy-start.4
  27.2 34.0 %collective-permute-start.7 = (bf16[384,256]{1,0:T(8,128)(2,1)S(1)}, bf16[384,256]{1,0:T(8,128)(2,1)S(1)}, u32[]{:S(2)}, u32[]{:S(2)}) collective-permute-start(bf16[384,256]{1,0:T(8,128)(2,1)S(1)} %bitcast.114), channel_id=1, source_target_pairs={{0,6},{2,4},{4,2},{6,0},{1,7},{3,5},{5,3},{7,1},{8,14},{10,12},{12... | collective-permute-start | bytes 589832 | tf_op jit(solution)/shard_map/ppermute | solution.py:683
  61.3 2.4 %copy-start.9 = (bf16[1536,256]{1,0:T(8,128)(2,1)}, bf16[1536,256]{1,0:T(8,128)(2,1)S(1)}, u32[]{:S(2)}) copy-start(bf16[1536,256]{1,0:T(8,128)(2,1)S(1)} %constant_dynamic-update-slice_fusion.5.own_ref) | copy-start | bytes 2359300
  61.3 2.4 %collective-permute-start.8 = (bf16[1536,256]{1,0:T(8,128)(2,1)S(1)}, bf16[1536,256]{1,0:T(8,128)(2,1)S(1)}, u32[]{:S(2)}, u32[]{:S(2)}) collective-permute-start(bf16[1536,256]{1,0:T(8,128)(2,1)S(1)} %constant_dynamic-update-slice_fusion.5.own_ref), channel_id=1, source_target_pairs={{0,1},{1,0},{2,3},{3,2},{4,5},{5,4},{6,7},{7,6},{8,9},{9,8},{10,11... | collective-permute-start | bytes 2359304 | tf_op jit(solution)/shard_map/ppermute | solution.py:683
  63.6 0.9 copy-start.11
  119.4 5.6 %collective-permute-start.11 = (bf16[4,4,704,128]{3,2,1,0:T(8,128)(2,1)}, bf16[4,4,704,128]{3,2,1,0:T(8,128)(2,1)S(1)}, u32[]{:S(2)}, u32[]{:S(2)}) collective-permute-start(bf16[4,4,704,128]{3,2,1,0:T(8,128)(2,1)} %get-tuple-element.119), channel_id=1, source_target_pairs={{0,1},{1,0},{2,3},{3,2},{4,5},{5,4},{6,7},{7,6},{8,9},{9,8},{10,11... | collective-permute-start | bytes 8650760 | tf_op jit(solution)/shard_map/ppermute | solution.py:683
  129.1 40.0 %collective-permute-start.12 = (bf16[4,704,128]{2,1,0:T(8,128)(2,1)}, bf16[4,704,128]{2,1,0:T(8,128)(2,1)S(1)}, u32[]{:S(2)}, u32[]{:S(2)}) collective-permute-start(bf16[4,704,128]{2,1,0:T(8,128)(2,1)} %get-tuple-element.127), channel_id=1, source_target_pairs={{0,8},{8,0},{16,24},{24,16},{1,9},{9,1},{17,25},{25,17},{2,10},{10... | collective-permute-start | bytes 2162696 | tf_op jit(solution)/shard_map/ppermute | solution.py:683
  129.7 39.4 %collective-permute-start.13 = (bf16[4,704,128]{2,1,0:T(8,128)(2,1)}, bf16[4,704,128]{2,1,0:T(8,128)(2,1)S(1)}, u32[]{:S(2)}, u32[]{:S(2)}) collective-permute-start(bf16[4,704,128]{2,1,0:T(8,128)(2,1)} %get-tuple-element.128), channel_id=1, source_target_pairs={{0,16},{8,24},{16,0},{24,8},{1,17},{9,25},{17,1},{25,9},{2,18},{10... | collective-permute-start | bytes 2162696 | tf_op jit(solution)/shard_map/ppermute | solution.py:683
  132.1 37.0 %collective-permute-start.14 = (bf16[4,704,128]{2,1,0:T(8,128)(2,1)}, bf16[4,704,128]{2,1,0:T(8,128)(2,1)S(1)}, u32[]{:S(2)}, u32[]{:S(2)}) collective-permute-start(bf16[4,704,128]{2,1,0:T(8,128)(2,1)} %get-tuple-element.129), channel_id=1, source_target_pairs={{0,24},{8,16},{16,8},{24,0},{1,25},{9,17},{17,9},{25,1},{2,26},{10... | collective-permute-start | bytes 2162696 | tf_op jit(solution)/shard_map/ppermute | solution.py:683
  169.1 4.4 %copy-start.2 = (bf16[4,704,128]{2,1,0:T(8,128)(2,1)S(1)}, bf16[4,704,128]{2,1,0:T(8,128)(2,1)}, u32[]{:S(2)}) copy-start(bf16[4,704,128]{2,1,0:T(8,128)(2,1)} %get-tuple-element.126) | copy-start | bytes 2162692
  169.1 2.7 %collective-permute-start.15 = (bf16[4,4,224,128]{3,2,1,0:T(8,128)(2,1)}, bf16[4,4,224,128]{3,2,1,0:T(8,128)(2,1)S(1)}, u32[]{:S(2)}, u32[]{:S(2)}) collective-permute-start(bf16[4,4,224,128]{3,2,1,0:T(8,128)(2,1)} %get-tuple-element.136), channel_id=1, source_target_pairs={{0,1},{1,0},{2,3},{3,2},{4,5},{5,4},{6,7},{7,6},{8,9},{9,8},{10,11... | collective-permute-start | bytes 2752520 | tf_op jit(solution)/shard_map/ppermute | solution.py:683
  173.9 0.7 copy-start.10
  173.9 6.7 %collective-permute-start.19 = (bf16[704,128]{1,0:T(8,128)(2,1)S(1)}, bf16[704,128]{1,0:T(8,128)(2,1)S(1)}, u32[]{:S(2)}, u32[]{:S(2)}) collective-permute-start(bf16[704,128]{1,0:T(8,128)(2,1)S(1)} %get-tuple-element.145), channel_id=1, source_target_pairs={{0,2},{2,0},{4,6},{6,4},{1,3},{3,1},{5,7},{7,5},{8,10},{10,8},{12,... | collective-permute-start | bytes 540680 | tf_op jit(solution)/shard_map/ppermute | solution.py:683
  175.1 19.3 %collective-permute-start.16 = (bf16[4,224,128]{2,1,0:T(8,128)(2,1)S(1)}, bf16[4,224,128]{2,1,0:T(8,128)(2,1)S(1)}, u32[]{:S(2)}, u32[]{:S(2)}) collective-permute-start(bf16[4,224,128]{2,1,0:T(8,128)(2,1)S(1)} %get-tuple-element.142), channel_id=1, source_target_pairs={{0,8},{8,0},{16,24},{24,16},{1,9},{9,1},{17,25},{25,17},{2,10},{10... | collective-permute-start | bytes 688136 | tf_op jit(solution)/shard_map/ppermute | solution.py:683
  175.1 19.3 %collective-permute-start.17 = (bf16[4,224,128]{2,1,0:T(8,128)(2,1)S(1)}, bf16[4,224,128]{2,1,0:T(8,128)(2,1)S(1)}, u32[]{:S(2)}, u32[]{:S(2)}) collective-permute-start(bf16[4,224,128]{2,1,0:T(8,128)(2,1)S(1)} %get-tuple-element.143), channel_id=1, source_target_pairs={{0,16},{8,24},{16,0},{24,8},{1,17},{9,25},{17,1},{25,9},{2,18},{10... | collective-permute-start | bytes 688136 | tf_op jit(solution)/shard_map/ppermute | solution.py:683
  178.1 16.3 %collective-permute-start.18 = (bf16[4,224,128]{2,1,0:T(8,128)(2,1)S(1)}, bf16[4,224,128]{2,1,0:T(8,128)(2,1)S(1)}, u32[]{:S(2)}, u32[]{:S(2)}) collective-permute-start(bf16[4,224,128]{2,1,0:T(8,128)(2,1)S(1)} %get-tuple-element.144), channel_id=1, source_target_pairs={{0,24},{8,16},{16,8},{24,0},{1,25},{9,17},{17,9},{25,1},{2,26},{10... | collective-permute-start | bytes 688136 | tf_op jit(solution)/shard_map/ppermute | solution.py:683
  178.6 15.8 %collective-permute-start.20 = (bf16[704,128]{1,0:T(8,128)(2,1)S(1)}, bf16[704,128]{1,0:T(8,128)(2,1)S(1)}, u32[]{:S(2)}, u32[]{:S(2)}) collective-permute-start(bf16[704,128]{1,0:T(8,128)(2,1)S(1)} %get-tuple-element.146), channel_id=1, source_target_pairs={{0,4},{2,6},{4,0},{6,2},{1,5},{3,7},{5,1},{7,3},{8,12},{10,14},{12... | collective-permute-start | bytes 540680 | tf_op jit(solution)/shard_map/ppermute | solution.py:683
  180.6 13.8 %collective-permute-start.21 = (bf16[704,128]{1,0:T(8,128)(2,1)S(1)}, bf16[704,128]{1,0:T(8,128)(2,1)S(1)}, u32[]{:S(2)}, u32[]{:S(2)}) collective-permute-start(bf16[704,128]{1,0:T(8,128)(2,1)S(1)} %get-tuple-element.147), channel_id=1, source_target_pairs={{0,6},{2,4},{4,2},{6,0},{1,7},{3,5},{5,3},{7,1},{8,14},{10,12},{12... | collective-permute-start | bytes 540680 | tf_op jit(solution)/shard_map/ppermute | solution.py:683
  195.2 7.9 %collective-permute-start.22 = (bf16[224,128]{1,0:T(8,128)(2,1)S(1)}, bf16[224,128]{1,0:T(8,128)(2,1)S(1)}, u32[]{:S(2)}, u32[]{:S(2)}) collective-permute-start(bf16[224,128]{1,0:T(8,128)(2,1)S(1)} %get-tuple-element.238), channel_id=1, source_target_pairs={{0,2},{2,0},{4,6},{6,4},{1,3},{3,1},{5,7},{7,5},{8,10},{10,8},{12,... | collective-permute-start | bytes 172040 | tf_op jit(solution)/shard_map/ppermute | solution.py:683
  198.2 6.5 %collective-permute-start.23 = (bf16[224,128]{1,0:T(8,128)(2,1)S(1)}, bf16[224,128]{1,0:T(8,128)(2,1)S(1)}, u32[]{:S(2)}, u32[]{:S(2)}) collective-permute-start(bf16[224,128]{1,0:T(8,128)(2,1)S(1)} %get-tuple-element.237), channel_id=1, source_target_pairs={{0,4},{2,6},{4,0},{6,2},{1,5},{3,7},{5,1},{7,3},{8,12},{10,14},{12... | collective-permute-start | bytes 172040 | tf_op jit(solution)/shard_map/ppermute | solution.py:683
  198.2 6.5 %collective-permute-start.24 = (bf16[224,128]{1,0:T(8,128)(2,1)S(1)}, bf16[224,128]{1,0:T(8,128)(2,1)S(1)}, u32[]{:S(2)}, u32[]{:S(2)}) collective-permute-start(bf16[224,128]{1,0:T(8,128)(2,1)S(1)} %get-tuple-element.236), channel_id=1, source_target_pairs={{0,6},{2,4},{4,2},{6,0},{1,7},{3,5},{5,3},{7,1},{8,14},{10,12},{12... | collective-permute-start | bytes 172040 | tf_op jit(solution)/shard_map/ppermute | solution.py:683
  200.5 6.6 %copy-start.1 = (s32[2,32]{1,0:T(2,128)S(1)}, s32[2,32]{1,0:T(2,128)}, u32[]{:S(2)}) copy-start(s32[2,32]{1,0:T(2,128)} %param.17) | copy-start | bytes 772
  203.1 1.6 copy-start.6
  204.7 0.6 copy-start.7
  204.7 0.6 copy-start.8

commit v7 on v6

--- a/solution.py
+++ b/solution.py
@@ -593,7 +593,7 @@
     ids, x_ref, mid_ref, r_ref, own_ref, other_ref, vec_ref, out_ref, w_ref, sems
 ):
     first = (pl.program_id(0) == 0) & (pl.program_id(1) == 0)
-    copies = half_copies(ids[0], sems, [(own_ref, other_ref, w_ref)])
+    copies = half_copies(ids[2], sems, [(own_ref, other_ref, w_ref)])
     start_all(first, copies)
 
     wait_all(first, copies)
@@ -1082,7 +1082,7 @@
         out_shape=state_s,
         compiler_params=params(),
         cost_estimate=cost(2 * tokens * model * all_rows, 0, 40 << 20),
-    )(ids[2:], states, mid, routed, proj, proj_other, vectors)
+    )(ids, states, mid, routed, proj, proj_other, vectors)
 
     def open_heads(value):
         return jnp.swapaxes(value.reshape(-1, own_experts, width), 0, 1)[None]

time: 208 us -> 206 us (level)
    unnamed x36 -> x34, local copies, waits for them, and re-layouts: 4.87 us -> 4.35 us
where the time goes in v7:
time: 206 us; the launch traced here: 205 us
  Pallas kernels  137 us (67%)
  starting transfers between devices  25.6 us (12%)
  other arithmetic  15 us (7%)
  waiting for transfers between devices  13.6 us (7%)
  local copies, waits for them, and re-layouts  12.4 us (6%)
    pallas_call x1, Pallas kernels, local(): pl.pallas_call(middle_kernel, name='middle', grid_spec=pltpu.PrefetchScal...  54.9 us
    pallas_call x1, Pallas kernels, local(): pl.pallas_call(backward_kernel, name='backward', grid_spec=pltpu.Prefetch...  36.5 us
    pallas_call x1, Pallas kernels, local(): pl.pallas_call(forward_kernel, name='forward', grid_spec=pltpu.PrefetchSc...  32.4 us
    ppermute x25, starting transfers between devices, exchange(): lax.ppermute(value, axis, [(at, at ^ distance) for at in range(count)])  25.6 us
    ppermute x25, waiting for transfers between devices, exchange(): lax.ppermute(value, axis, [(at, at ^ distance) for at in range(count)])  13.6 us
    pallas_call x1, Pallas kernels, local(): pl.pallas_call(input_kernel, name='input_back', grid_spec=pltpu.PrefetchS...  11.9 us
    convert_element_type x2, other arithmetic, core_stage(): (keep[at].astype(F32) + other[at].astype(F32)).astype(BF16)  5.7 us
    unnamed x34, local copies, waits for them, and re-layouts  4.35 us
  transfers between devices with their start and end apart: 25, of which 6 were waited for; matrix products, arithmetic and copies ran while one was open for 9% of the time, Pallas kernels for 39%

profile of v7, /device:TPU:0, one launch (start us, length us, event | category | flops | bytes accessed | tf_op | source)
XLA Modules:
  0.0 205.5 jit_solution(1080516978862771010)
XLA Ops:
  0.7 5.1 %collective-permute-start.3 = (bf16[384,256]{1,0:T(8,128)(2,1)}, bf16[384,256]{1,0:T(8,128)(2,1)S(1)}, u32[]{:S(2)}, u32[]{:S(2)}) collective-permute-start(bf16[384,256]{1,0:T(8,128)(2,1)} %bitcast.108), channel_id=1, source_target_pairs={{0,6},{2,4},{4,2},{6,0},{1,7},{3,5},{5,3},{7,1},{8,14},{10,12},{12... | collective-permute-start | bytes 589832 | tf_op jit(solution)/shard_map/ppermute | solution.py:683
  5.8 0.6 collective-permute-start.1
  6.4 0.7 reduce.1
  7.2 0.9 concatenate.47
  8.1 0.7 reshape_reshape.6
  8.8 0.7 reshape.227
  9.5 0.9 sign_compare_fusion
  10.4 0.9 broadcast_remainder_fusion
  11.4 0.7 select_select_fusion
  12.1 0.7 fusion.11.route_ref
  12.8 0.6 pad_add_fusion.ids
  13.3 0.8 concatenate.46
  14.1 0.9 copy.53
  15.1 0.7 dynamic-slice_reduce_fusion.lens
  15.8 0.6 fusion.13.vec_ref
  16.4 1.4 fusion.12.up_shift_ref
  17.8 4.9 %collective-permute-done.2 = bf16[384,256]{1,0:T(8,128)(2,1)S(1)} collective-permute-done((bf16[384,256]{1,0:T(8,128)(2,1)}, bf16[384,256]{1,0:T(8,128)(2,1)S(1)}, u32[]{:S(2)}, u32[]{:S(2)}) %collective-permute-start.2) | collective-permute-done | bytes 196640 | tf_op jit(solution)/shard_map/ppermute | solution.py:683
  22.7 0.9 constant_dynamic-update-slice_fusion.4
  23.8 0.5 collective-permute-start.9
  24.4 2.5 %collective-permute-start.7 = (bf16[384,256]{1,0:T(8,128)(2,1)S(1)}, bf16[384,256]{1,0:T(8,128)(2,1)S(1)}, u32[]{:S(2)}, u32[]{:S(2)}) collective-permute-start(bf16[384,256]{1,0:T(8,128)(2,1)S(1)} %bitcast.112), channel_id=1, source_target_pairs={{0,6},{2,4},{4,2},{6,0},{1,7},{3,5},{5,3},{7,1},{8,14},{10,12},{12... | collective-permute-start | bytes 589832 | tf_op jit(solution)/shard_map/ppermute | solution.py:683
  26.9 1.9 collective-permute-start.5
  28.8 32.4 %forward.1 = (bf16[2,4,256,512]{3,2,1,0:T(8,128)(2,1)}, bf16[2,4,256,128]{3,2,1,0:T(8,128)(2,1)}, bf16[2,4,256,128]{3,2,1,0:T(8,128)(2,1)}, bf16[2,4,1,64,256]{4...) custom-call(s32[2]{0:T(128)} %dynamic-slice_reduce_fusion.lens, ...), custom_call_target="tpu_custom_call" | custom-call | flops 20736638976 | bytes 67108864 | tf_op jit(solution)/shard_map/forward/pallas_call | solution.py:835
  61.4 2.3 %collective-permute-done.8.other_ref = bf16[1536,256]{1,0:T(8,128)(2,1)S(1)} collective-permute-done((bf16[1536,256]{1,0:T(8,128)(2,1)S(1)}, bf16[1536,256]{1,0:T(8,128)(2,1)S(1)}, u32[]{:S(2)}, u32[]{:S(2)}) %collective-permute-start.8) | collective-permute-done | bytes 786464 | tf_op jit(solution)/shard_map/ppermute | solution.py:683
  63.7 0.9 copy-done.10
  64.6 54.9 %middle.1 = (f32[2,4,256,512]{3,2,1,0:T(8,128)}, bf16[2,4,256,512]{3,2,1,0:T(8,128)(2,1)}, bf16[2,4,64,2048]{3,2,1,0:T(8,128)(2,1)}, f32[2,4,1,2048]{3,2,1,0:T(1...) custom-call(s32[2]{0:T(128)} %dynamic-slice_reduce_fusion.lens, ...), custom_call_target="tpu_custom_call" | custom-call | flops 35433480192 | bytes 209715200 | tf_op jit(solution)/shard_map/middle/pallas_call | solution.py:890
  119.5 0.2 collective-permute-start.11
  119.7 0.6 pad_convert_fusion.order_ref
  120.3 0.7 slice_bitcast_fusion.8
  121.0 0.8 reduce_sum.18
  121.9 0.9 reduce_sum.19
  122.7 0.1 reshape.236
  122.8 0.1 reshape.237
  123.0 0.1 copy.55
  123.1 0.9 pad.17.columns_ref
  124.0 1.1 collective-permute-done.11
  125.0 4.1 %fusion.3 = (bf16[4,704,128]{2,1,0:T(8,128)(2,1)}, bf16[4,704,128]{2,1,0:T(8,128)(2,1)}, bf16[4,704,128]{2,1,0:T(8,128)(2,1)}, bf16[4,704,128]{2,1,0:T(8,128)(2,1)}) fusion(bf16[4,4,704,128]{3,2,1,0:T(8,128)(2,1)S(1)} %collective-permute-done.11, bf16[4,4,704,128]{3,2,1,0:T(8,128)(2,1)} %get-tuple-element.118), kind=kLoop, calls=%fused_computation.8 | loop fusion | flops 5767168 | bytes 8650752 | tf_op jit(solution)/shard_map/convert_element_type | solution.py:714
  129.1 0.7 collective-permute-start.12
  129.9 2.3 %collective-permute-start.13 = (bf16[4,704,128]{2,1,0:T(8,128)(2,1)}, bf16[4,704,128]{2,1,0:T(8,128)(2,1)S(1)}, u32[]{:S(2)}, u32[]{:S(2)}) collective-permute-start(bf16[4,704,128]{2,1,0:T(8,128)(2,1)} %get-tuple-element.128), channel_id=1, source_target_pairs={{0,16},{8,24},{16,0},{24,8},{1,17},{9,25},{17,1},{25,9},{2,18},{10... | collective-permute-start | bytes 2162696 | tf_op jit(solution)/shard_map/ppermute | solution.py:683
  132.1 0.5 collective-permute-start.14
  132.6 36.5 %backward.1 = (bf16[2,2,1696,512]{3,2,1,0:T(8,128)(2,1)}, bf16[4,4,224,128]{3,2,1,0:T(8,128)(2,1)}, bf16[4,4,224,128]{3,2,1,0:T(8,128)(2,1)}) custom-call(s32[2]{0:T(128)} %dynamic-slice_reduce_fusion.lens, s32[3]{0:T(128)} %pad_add_fusion.ids, bf16[2,4,256,512]{3,2,1,0:T(8,128)(2,1)} %get-tuple-element.111.hid_ref, ...), custom_call_target="tpu_custom_call" | custom-call | flops 46506442752 | bytes 104857600 | tf_op jit(solution)/shard_map/backward/pallas_call | solution.py:990
  169.2 2.7 %collective-permute-done.15 = bf16[4,4,224,128]{3,2,1,0:T(8,128)(2,1)S(1)} collective-permute-done((bf16[4,4,224,128]{3,2,1,0:T(8,128)(2,1)}, bf16[4,4,224,128]{3,2,1,0:T(8,128)(2,1)S(1)}, u32[]{:S(2)}, u32[]{:S(2)}) %collective-permute-start.15) | collective-permute-done | bytes 917536 | tf_op jit(solution)/shard_map/ppermute | solution.py:683
  171.9 1.6 fusion.7
  173.5 0.4 add_convert_fusion
  174.1 4.3 %collective-permute-start.21 = (bf16[704,128]{1,0:T(8,128)(2,1)S(1)}, bf16[704,128]{1,0:T(8,128)(2,1)S(1)}, u32[]{:S(2)}, u32[]{:S(2)}) collective-permute-start(bf16[704,128]{1,0:T(8,128)(2,1)S(1)} %get-tuple-element.147), channel_id=1, source_target_pairs={{0,6},{2,4},{4,2},{6,0},{1,7},{3,5},{5,3},{7,1},{8,14},{10,12},{12... | collective-permute-start | bytes 540680 | tf_op jit(solution)/shard_map/ppermute | solution.py:683
  178.4 0.4 collective-permute-start.16
  178.8 0.5 collective-permute-start.17
  179.3 2.5 %collective-permute-done.19 = bf16[704,128]{1,0:T(8,128)(2,1)S(1)} collective-permute-done((bf16[704,128]{1,0:T(8,128)(2,1)S(1)}, bf16[704,128]{1,0:T(8,128)(2,1)S(1)}, u32[]{:S(2)}, u32[]{:S(2)}) %collective-permute-start.19) | collective-permute-done | bytes 180256 | tf_op jit(solution)/shard_map/ppermute | solution.py:683
  181.8 1.1 collective-permute-start.18
  182.9 11.9 %input_back.1 = f32[2,4,256,512]{3,2,1,0:T(8,128)} custom-call(s32[3]{0:T(128)} %pad_add_fusion.ids, bf16[2,4,256,512]{3,2,1,0:T(8,128)(2,1)} %bitcast.100, bf16[2,4,256,512]{3,2,1,0:T(8,128)(2,1)} %get-tuple-element.110.mid_ref, bf16[2,2,1696,512]{3,2,1,0:T(8,128)(2,1)} %get-tuple-element.141.r_ref, bf16[1696,256]{1,0:T(8,128)(2,1)} %copy-done.3, ...), custom_call_target="tpu_custom_call" | custom-call | flops 3556769792 | bytes 41943040 | tf_op jit(solution)/shard_map/input_back/pallas_call | solution.py:1062
  194.9 0.1 add_convert_fusion.5
  195.0 0.6 slice_bitcast_fusion.4
  195.7 1.0 collective-permute-start.24
  196.7 0.7 collective-permute-start.23
  197.4 2.6 %collective-permute-start.22 = (bf16[224,128]{1,0:T(8,128)(2,1)S(1)}, bf16[224,128]{1,0:T(8,128)(2,1)S(1)}, u32[]{:S(2)}, u32[]{:S(2)}) collective-permute-start(bf16[224,128]{1,0:T(8,128)(2,1)S(1)} %get-tuple-element.238), channel_id=1, source_target_pairs={{0,2},{2,0},{4,6},{6,4},{1,3},{3,1},{5,7},{7,5},{8,10},{10,8},{12,... | collective-permute-start | bytes 172040 | tf_op jit(solution)/shard_map/ppermute | solution.py:683
  200.0 0.1 convert_add_fusion
  200.2 0.1 copy.58
  200.3 0.7 broadcast_in_dim_reshape.7
  201.0 0.7 broadcast_in_dim_reshape.6
  201.7 0.1 copy.56
  201.8 0.8 copy.61
  202.6 0.2 collective-permute-done.23.refs_2_
  202.9 0.4 copy-done.6
  203.3 0.2 copy-done.7
  203.5 1.8 finish.1
  (74 shorter events, 1.0 us)
Async XLA Ops:
  0.6 14.4 %copy-start = (s32[2,32]{1,0:T(2,128)S(1)}, s32[2,32]{1,0:T(2,128)}, u32[]{:S(2)}) copy-start(s32[2,32]{1,0:T(2,128)} %param.17) | copy-start | bytes 772
  0.7 23.7 %copy-start.5 = (bf16[1,6,256,64]{2,3,1,0:T(8,128)(2,1)S(1)}, bf16[1,6,256,64]{2,3,1,0:T(8,128)(2,1)}, u32[]{:S(2)}) copy-start(bf16[1,6,256,64]{2,3,1,0:T(8,128)(2,1)} %param.24) | copy-start | bytes 589828
  0.7 17.1 %collective-permute-start.3 = (bf16[384,256]{1,0:T(8,128)(2,1)}, bf16[384,256]{1,0:T(8,128)(2,1)S(1)}, u32[]{:S(2)}, u32[]{:S(2)}) collective-permute-start(bf16[384,256]{1,0:T(8,128)(2,1)} %bitcast.108), channel_id=1, source_target_pairs={{0,6},{2,4},{4,2},{6,0},{1,7},{3,5},{5,3},{7,1},{8,14},{10,12},{12... | collective-permute-start | bytes 589832 | tf_op jit(solution)/shard_map/ppermute | solution.py:683
  5.8 16.9 %collective-permute-start.2 = (bf16[384,256]{1,0:T(8,128)(2,1)}, bf16[384,256]{1,0:T(8,128)(2,1)S(1)}, u32[]{:S(2)}, u32[]{:S(2)}) collective-permute-start(bf16[384,256]{1,0:T(8,128)(2,1)} %bitcast.109), channel_id=1, source_target_pairs={{0,4},{2,6},{4,0},{6,2},{1,5},{3,7},{5,1},{7,3},{8,12},{10,14},{12... | collective-permute-start | bytes 589832 | tf_op jit(solution)/shard_map/ppermute | solution.py:683
  5.8 16.9 %collective-permute-start.1 = (bf16[384,256]{1,0:T(8,128)(2,1)}, bf16[384,256]{1,0:T(8,128)(2,1)S(1)}, u32[]{:S(2)}, u32[]{:S(2)}) collective-permute-start(bf16[384,256]{1,0:T(8,128)(2,1)} %bitcast.110), channel_id=1, source_target_pairs={{0,2},{2,0},{4,6},{6,4},{1,3},{3,1},{5,7},{7,5},{8,10},{10,8},{12,... | collective-permute-start | bytes 589832 | tf_op jit(solution)/shard_map/ppermute | solution.py:683
  8.0 7.8 %collective-permute-start = (bf16[9,256]{1,0:T(8,128)(2,1)S(1)}, bf16[9,256]{1,0:T(8,128)(2,1)S(1)}, u32[]{:S(2)}, u32[]{:S(2)}) collective-permute-start(bf16[9,256]{1,0:T(8,128)(2,1)S(1)} %concatenate.47), channel_id=1, source_target_pairs={{0,1},{1,0},{2,3},{3,2},{4,5},{5,4},{6,7},{7,6},{8,9},{9,8},{10,11... | collective-permute-start | bytes 13832 | tf_op jit(solution)/shard_map/ppermute | solution.py:683
  23.7 5.1 %copy-start.3 = (bf16[1696,256]{1,0:T(8,128)(2,1)}, bf16[1696,256]{1,0:T(8,128)(2,1)S(1)}, u32[]{:S(2)}) copy-start(bf16[1696,256]{1,0:T(8,128)(2,1)S(1)} %constant_dynamic-update-slice_fusion.own_ref) | copy-start | bytes 2605060
  23.7 3.1 %collective-permute-start.4 = (bf16[1696,256]{1,0:T(8,128)(2,1)S(1)}, bf16[1696,256]{1,0:T(8,128)(2,1)S(1)}, u32[]{:S(2)}, u32[]{:S(2)}) collective-permute-start(bf16[1696,256]{1,0:T(8,128)(2,1)S(1)} %constant_dynamic-update-slice_fusion.own_ref), channel_id=1, source_target_pairs={{0,1},{1,0},{2,3},{3,2},{4,5},{5,4},{6,7},{7,6},{8,9},{9,8},{10,11... | collective-permute-start | bytes 2605064 | tf_op jit(solution)/shard_map/ppermute | solution.py:683
  23.8 37.6 %collective-permute-start.9 = (bf16[256,2048]{1,0:T(8,128)(2,1)}, bf16[256,2048]{1,0:T(8,128)(2,1)}, u32[]{:S(2)}, u32[]{:S(2)}) collective-permute-start(bf16[256,2048]{1,0:T(8,128)(2,1)} %bitcast.23.own_up_ref), channel_id=1, source_target_pairs={{0,1},{1,0},{2,3},{3,2},{4,5},{5,4},{6,7},{7,6},{8,9},{9,8},{10,11... | collective-permute-start | bytes 3145736 | tf_op jit(solution)/shard_map/ppermute | solution.py:683
  24.3 37.1 %collective-permute-start.10 = (bf16[1024,512]{1,0:T(8,128)(2,1)}, bf16[1024,512]{1,0:T(8,128)(2,1)}, u32[]{:S(2)}, u32[]{:S(2)}) collective-permute-start(bf16[1024,512]{1,0:T(8,128)(2,1)} %bitcast.24.own_down_ref), channel_id=1, source_target_pairs={{0,1},{1,0},{2,3},{3,2},{4,5},{5,4},{6,7},{7,6},{8,9},{9,8},{10,11... | collective-permute-start | bytes 3145736 | tf_op jit(solution)/shard_map/ppermute | solution.py:683
  24.4 36.8 %collective-permute-start.7 = (bf16[384,256]{1,0:T(8,128)(2,1)S(1)}, bf16[384,256]{1,0:T(8,128)(2,1)S(1)}, u32[]{:S(2)}, u32[]{:S(2)}) collective-permute-start(bf16[384,256]{1,0:T(8,128)(2,1)S(1)} %bitcast.112), channel_id=1, source_target_pairs={{0,6},{2,4},{4,2},{6,0},{1,7},{3,5},{5,3},{7,1},{8,14},{10,12},{12... | collective-permute-start | bytes 589832 | tf_op jit(solution)/shard_map/ppermute | solution.py:683
  26.9 34.3 %collective-permute-start.6 = (bf16[384,256]{1,0:T(8,128)(2,1)S(1)}, bf16[384,256]{1,0:T(8,128)(2,1)S(1)}, u32[]{:S(2)}, u32[]{:S(2)}) collective-permute-start(bf16[384,256]{1,0:T(8,128)(2,1)S(1)} %bitcast.113), channel_id=1, source_target_pairs={{0,4},{2,6},{4,0},{6,2},{1,5},{3,7},{5,1},{7,3},{8,12},{10,14},{12... | collective-permute-start | bytes 589832 | tf_op jit(solution)/shard_map/ppermute | solution.py:683
  26.9 1.9 copy-start.4
  26.9 34.3 %collective-permute-start.5 = (bf16[384,256]{1,0:T(8,128)(2,1)S(1)}, bf16[384,256]{1,0:T(8,128)(2,1)S(1)}, u32[]{:S(2)}, u32[]{:S(2)}) collective-permute-start(bf16[384,256]{1,0:T(8,128)(2,1)S(1)} %bitcast.114), channel_id=1, source_target_pairs={{0,2},{2,0},{4,6},{6,4},{1,3},{3,1},{5,7},{7,5},{8,10},{10,8},{12,... | collective-permute-start | bytes 589832 | tf_op jit(solution)/shard_map/ppermute | solution.py:683
  61.3 2.4 %copy-start.9 = (bf16[1536,256]{1,0:T(8,128)(2,1)}, bf16[1536,256]{1,0:T(8,128)(2,1)S(1)}, u32[]{:S(2)}) copy-start(bf16[1536,256]{1,0:T(8,128)(2,1)S(1)} %constant_dynamic-update-slice_fusion.5.own_ref) | copy-start | bytes 2359300
  61.3 2.4 %collective-permute-start.8 = (bf16[1536,256]{1,0:T(8,128)(2,1)S(1)}, bf16[1536,256]{1,0:T(8,128)(2,1)S(1)}, u32[]{:S(2)}, u32[]{:S(2)}) collective-permute-start(bf16[1536,256]{1,0:T(8,128)(2,1)S(1)} %constant_dynamic-update-slice_fusion.5.own_ref), channel_id=1, source_target_pairs={{0,1},{1,0},{2,3},{3,2},{4,5},{5,4},{6,7},{7,6},{8,9},{9,8},{10,11... | collective-permute-start | bytes 2359304 | tf_op jit(solution)/shard_map/ppermute | solution.py:683
  63.7 0.9 copy-start.10
  119.5 5.6 %collective-permute-start.11 = (bf16[4,4,704,128]{3,2,1,0:T(8,128)(2,1)}, bf16[4,4,704,128]{3,2,1,0:T(8,128)(2,1)S(1)}, u32[]{:S(2)}, u32[]{:S(2)}) collective-permute-start(bf16[4,4,704,128]{3,2,1,0:T(8,128)(2,1)} %get-tuple-element.119), channel_id=1, source_target_pairs={{0,1},{1,0},{2,3},{3,2},{4,5},{5,4},{6,7},{7,6},{8,9},{9,8},{10,11... | collective-permute-start | bytes 8650760 | tf_op jit(solution)/shard_map/ppermute | solution.py:683
  129.1 40.0 %collective-permute-start.12 = (bf16[4,704,128]{2,1,0:T(8,128)(2,1)}, bf16[4,704,128]{2,1,0:T(8,128)(2,1)S(1)}, u32[]{:S(2)}, u32[]{:S(2)}) collective-permute-start(bf16[4,704,128]{2,1,0:T(8,128)(2,1)} %get-tuple-element.127), channel_id=1, source_target_pairs={{0,8},{8,0},{16,24},{24,16},{1,9},{9,1},{17,25},{25,17},{2,10},{10... | collective-permute-start | bytes 2162696 | tf_op jit(solution)/shard_map/ppermute | solution.py:683
  129.9 39.2 %collective-permute-start.13 = (bf16[4,704,128]{2,1,0:T(8,128)(2,1)}, bf16[4,704,128]{2,1,0:T(8,128)(2,1)S(1)}, u32[]{:S(2)}, u32[]{:S(2)}) collective-permute-start(bf16[4,704,128]{2,1,0:T(8,128)(2,1)} %get-tuple-element.128), channel_id=1, source_target_pairs={{0,16},{8,24},{16,0},{24,8},{1,17},{9,25},{17,1},{25,9},{2,18},{10... | collective-permute-start | bytes 2162696 | tf_op jit(solution)/shard_map/ppermute | solution.py:683
  132.1 37.0 %collective-permute-start.14 = (bf16[4,704,128]{2,1,0:T(8,128)(2,1)}, bf16[4,704,128]{2,1,0:T(8,128)(2,1)S(1)}, u32[]{:S(2)}, u32[]{:S(2)}) collective-permute-start(bf16[4,704,128]{2,1,0:T(8,128)(2,1)} %get-tuple-element.129), channel_id=1, source_target_pairs={{0,24},{8,16},{16,8},{24,0},{1,25},{9,17},{17,9},{25,1},{2,26},{10... | collective-permute-start | bytes 2162696 | tf_op jit(solution)/shard_map/ppermute | solution.py:683
  169.1 4.4 %copy-start.2 = (bf16[4,704,128]{2,1,0:T(8,128)(2,1)S(1)}, bf16[4,704,128]{2,1,0:T(8,128)(2,1)}, u32[]{:S(2)}) copy-start(bf16[4,704,128]{2,1,0:T(8,128)(2,1)} %get-tuple-element.126) | copy-start | bytes 2162692
  169.1 2.7 %collective-permute-start.15 = (bf16[4,4,224,128]{3,2,1,0:T(8,128)(2,1)}, bf16[4,4,224,128]{3,2,1,0:T(8,128)(2,1)S(1)}, u32[]{:S(2)}, u32[]{:S(2)}) collective-permute-start(bf16[4,4,224,128]{3,2,1,0:T(8,128)(2,1)} %get-tuple-element.136), channel_id=1, source_target_pairs={{0,1},{1,0},{2,3},{3,2},{4,5},{5,4},{6,7},{7,6},{8,9},{9,8},{10,11... | collective-permute-start | bytes 2752520 | tf_op jit(solution)/shard_map/ppermute | solution.py:683
  173.9 7.9 %collective-permute-start.19 = (bf16[704,128]{1,0:T(8,128)(2,1)S(1)}, bf16[704,128]{1,0:T(8,128)(2,1)S(1)}, u32[]{:S(2)}, u32[]{:S(2)}) collective-permute-start(bf16[704,128]{1,0:T(8,128)(2,1)S(1)} %get-tuple-element.145), channel_id=1, source_target_pairs={{0,2},{2,0},{4,6},{6,4},{1,3},{3,1},{5,7},{7,5},{8,10},{10,8},{12,... | collective-permute-start | bytes 540680 | tf_op jit(solution)/shard_map/ppermute | solution.py:683
  174.0 20.8 %collective-permute-start.20 = (bf16[704,128]{1,0:T(8,128)(2,1)S(1)}, bf16[704,128]{1,0:T(8,128)(2,1)S(1)}, u32[]{:S(2)}, u32[]{:S(2)}) collective-permute-start(bf16[704,128]{1,0:T(8,128)(2,1)S(1)} %get-tuple-element.146), channel_id=1, source_target_pairs={{0,4},{2,6},{4,0},{6,2},{1,5},{3,7},{5,1},{7,3},{8,12},{10,14},{12... | collective-permute-start | bytes 540680 | tf_op jit(solution)/shard_map/ppermute | solution.py:683
  174.1 20.8 %collective-permute-start.21 = (bf16[704,128]{1,0:T(8,128)(2,1)S(1)}, bf16[704,128]{1,0:T(8,128)(2,1)S(1)}, u32[]{:S(2)}, u32[]{:S(2)}) collective-permute-start(bf16[704,128]{1,0:T(8,128)(2,1)S(1)} %get-tuple-element.147), channel_id=1, source_target_pairs={{0,6},{2,4},{4,2},{6,0},{1,7},{3,5},{5,3},{7,1},{8,14},{10,12},{12... | collective-permute-start | bytes 540680 | tf_op jit(solution)/shard_map/ppermute | solution.py:683
  178.4 16.5 %collective-permute-start.16 = (bf16[4,224,128]{2,1,0:T(8,128)(2,1)S(1)}, bf16[4,224,128]{2,1,0:T(8,128)(2,1)S(1)}, u32[]{:S(2)}, u32[]{:S(2)}) collective-permute-start(bf16[4,224,128]{2,1,0:T(8,128)(2,1)S(1)} %get-tuple-element.142), channel_id=1, source_target_pairs={{0,8},{8,0},{16,24},{24,16},{1,9},{9,1},{17,25},{25,17},{2,10},{10... | collective-permute-start | bytes 688136 | tf_op jit(solution)/shard_map/ppermute | solution.py:683
  178.8 16.0 %collective-permute-start.17 = (bf16[4,224,128]{2,1,0:T(8,128)(2,1)S(1)}, bf16[4,224,128]{2,1,0:T(8,128)(2,1)S(1)}, u32[]{:S(2)}, u32[]{:S(2)}) collective-permute-start(bf16[4,224,128]{2,1,0:T(8,128)(2,1)S(1)} %get-tuple-element.143), channel_id=1, source_target_pairs={{0,16},{8,24},{16,0},{24,8},{1,17},{9,25},{17,1},{25,9},{2,18},{10... | collective-permute-start | bytes 688136 | tf_op jit(solution)/shard_map/ppermute | solution.py:683
  181.8 13.1 %collective-permute-start.18 = (bf16[4,224,128]{2,1,0:T(8,128)(2,1)S(1)}, bf16[4,224,128]{2,1,0:T(8,128)(2,1)S(1)}, u32[]{:S(2)}, u32[]{:S(2)}) collective-permute-start(bf16[4,224,128]{2,1,0:T(8,128)(2,1)S(1)} %get-tuple-element.144), channel_id=1, source_target_pairs={{0,24},{8,16},{16,8},{24,0},{1,25},{9,17},{17,9},{25,1},{2,26},{10... | collective-permute-start | bytes 688136 | tf_op jit(solution)/shard_map/ppermute | solution.py:683
  195.7 7.0 %collective-permute-start.24 = (bf16[224,128]{1,0:T(8,128)(2,1)S(1)}, bf16[224,128]{1,0:T(8,128)(2,1)S(1)}, u32[]{:S(2)}, u32[]{:S(2)}) collective-permute-start(bf16[224,128]{1,0:T(8,128)(2,1)S(1)} %get-tuple-element.236), channel_id=1, source_target_pairs={{0,6},{2,4},{4,2},{6,0},{1,7},{3,5},{5,3},{7,1},{8,14},{10,12},{12... | collective-permute-start | bytes 172040 | tf_op jit(solution)/shard_map/ppermute | solution.py:683
  196.7 6.2 %collective-permute-start.23 = (bf16[224,128]{1,0:T(8,128)(2,1)S(1)}, bf16[224,128]{1,0:T(8,128)(2,1)S(1)}, u32[]{:S(2)}, u32[]{:S(2)}) collective-permute-start(bf16[224,128]{1,0:T(8,128)(2,1)S(1)} %get-tuple-element.237), channel_id=1, source_target_pairs={{0,4},{2,6},{4,0},{6,2},{1,5},{3,7},{5,1},{7,3},{8,12},{10,14},{12... | collective-permute-start | bytes 172040 | tf_op jit(solution)/shard_map/ppermute | solution.py:683
  197.4 5.5 %collective-permute-start.22 = (bf16[224,128]{1,0:T(8,128)(2,1)S(1)}, bf16[224,128]{1,0:T(8,128)(2,1)S(1)}, u32[]{:S(2)}, u32[]{:S(2)}) collective-permute-start(bf16[224,128]{1,0:T(8,128)(2,1)S(1)} %get-tuple-element.238), channel_id=1, source_target_pairs={{0,2},{2,0},{4,6},{6,4},{1,3},{3,1},{5,7},{7,5},{8,10},{10,8},{12,... | collective-permute-start | bytes 172040 | tf_op jit(solution)/shard_map/ppermute | solution.py:683
  200.0 5.2 %copy-start.1 = (s32[2,32]{1,0:T(2,128)S(1)}, s32[2,32]{1,0:T(2,128)}, u32[]{:S(2)}) copy-start(s32[2,32]{1,0:T(2,128)} %param.17) | copy-start | bytes 772
  202.6 0.6 copy-start.6
  202.9 0.6 copy-start.7
  202.9 0.6 copy-start.8
